TPU v7x, 32 devices: a whole 2x2x4 slice. The times are simulated.
32 devices in a mesh: users: 8 (over z, y), items: 4 (over x, core).
Axes of the slice: x: 2, y: 2, z: 4, core: 2. Of those that a mesh axis runs over, the one named last changes fastest.
Arguments:
- tile_rows: int32 [8, 4, 512], P('users', 'items'), may hold values from 0 to 63, as said below
- tile_cols: int32 [8, 4, 512], P('users', 'items'), may hold values from 0 to 63, as said below
- tile_count: int32 [8, 4], P('users', 'items'), may hold values from 64 to 512, as said below
- tile_vals: bfloat16 [8, 4, 512, 128, 128], P('users', 'items'), may hold values from -6 to 6
- user_degree: int32 [65536], P(('users', 'items')), may hold values from 16 to 575
- item_degree: int32 [32768], P(('items', 'users')), may hold values from 16 to 575
- start_items: bfloat16 [64, 32768], P(None, ('items', 'users')), may hold values from -6 to 6
Outputs:
- user_panel: float32 [64, 65536], P(None, ('users', 'items'))
- item_panel: float32 [64, 32768], P(None, ('items', 'users'))
Inputs may be any that keep to these rules, and one draw needn't show every extreme that they name: Within one user block and item block, the pairs (tile_rows, tile_cols) of all 512 slots are distinct. `tile_cols`: paired with tile_rows slot by slot. Only the first tile_count slots of a block are live; some block is full in every draw.
All inputs are finite; a program needn't handle non-finite values.
Results may differ from a plain program's by a relative error of at most 0.0003.
Values sent between devices are 32-bit elements; how exact they have to be, the bound alone decides.
No kernel may reach another device: no remote copies, remote signals or barrier semaphores. Data moves between devices by JAX's collectives and lax.ppermute only.
A program may use at most 128 MiB of HBM per device.

v0:
```python
import jax
import jax.numpy as jnp
from jax import lax
from jax.sharding import PartitionSpec as P

K = 64
TILE = 128
ITERS = 2
UT = 64
IT = 64


def local_gram(raw):
    return jnp.einsum(
        "kr,jr->kj", raw, raw, precision=lax.Precision.HIGHEST, preferred_element_type=jnp.float32
    )


def solve_panel(gram, raw):
    lower = jnp.linalg.cholesky(gram)
    return lax.linalg.triangular_solve(lower, raw, left_side=True, lower=True)


def user_partial(full_items, rows, cols, values, live_weight):
    picked = jnp.take(full_items.reshape(K, IT, TILE), cols, axis=1)
    product = jnp.einsum(
        "ktc,trc->ktr",
        picked,
        values,
        precision=lax.Precision.HIGHEST,
        preferred_element_type=jnp.float32,
    )
    product = product * live_weight[None, :, None]
    summed = jnp.zeros((K, UT, TILE), jnp.float32).at[:, rows, :].add(product)
    return summed.reshape(K, UT * TILE)


def item_partial(full_users, rows, cols, values, live_weight):
    picked = jnp.take(full_users.reshape(K, UT, TILE), rows, axis=1)
    product = jnp.einsum(
        "ktr,trc->ktc",
        picked,
        values,
        precision=lax.Precision.HIGHEST,
        preferred_element_type=jnp.float32,
    )
    product = product * live_weight[None, :, None]
    summed = jnp.zeros((K, IT, TILE), jnp.float32).at[:, cols, :].add(product)
    return summed.reshape(K, IT * TILE)


def gather_items(sent):
    return lax.all_gather(sent, "users", axis=1, tiled=True)


def body(tile_rows, tile_cols, tile_count, tile_vals, user_degree, item_degree, start_items):
    rows = tile_rows[0, 0]
    cols = tile_cols[0, 0]
    values = tile_vals[0, 0].astype(jnp.float32)
    slots = values.shape[0]
    live_weight = (jnp.arange(slots, dtype=jnp.int32) < tile_count[0, 0]).astype(jnp.float32)
    user_scale = lax.rsqrt(user_degree.astype(jnp.float32))
    item_scale = lax.rsqrt(item_degree.astype(jnp.float32))
    user_groups = lax.axis_size("users")
    item_groups = lax.axis_size("items")
    user_total = UT * TILE * user_groups
    item_total = IT * TILE * item_groups
    user_width = UT * TILE // item_groups
    item_width = IT * TILE // user_groups
    item_scale_block = lax.all_gather(item_scale, "users", axis=0, tiled=True)
    panel = start_items.astype(jnp.float32)
    user_panel = jnp.zeros((K, user_width), jnp.float32)
    for step in range(ITERS):
        if step == 0:
            full_items = gather_items(item_scale[None, :] * panel)
        else:
            full_items = item_scale_block[None, :] * panel
        partial_users = user_partial(full_items, rows, cols, values, live_weight)
        user_raw = user_scale[None, :] * lax.psum_scatter(
            partial_users, "items", scatter_dimension=1, tiled=True
        )
        user_gram = lax.psum(local_gram(user_raw), ("users", "items"))
        user_panel = solve_panel(user_gram / user_total, user_raw)
        full_users = lax.all_gather(user_scale[None, :] * user_panel, "items", axis=1, tiled=True)
        partial_items = item_partial(full_users, rows, cols, values, live_weight)
        item_raw = item_scale_block[None, :] * lax.psum(partial_items, "users")
        item_gram = lax.psum(local_gram(item_raw), "items")
        panel = solve_panel(item_gram / item_total, item_raw)
    item_out = lax.dynamic_slice_in_dim(panel, lax.axis_index("users") * item_width, item_width, 1)
    return (user_panel, item_out)


def solution(mesh):
    in_specs = (
        P("users", "items", None),
        P("users", "items", None),
        P("users", "items"),
        P("users", "items", None, None, None),
        P(("users", "items")),
        P(("items", "users")),
        P(None, ("items", "users")),
    )
    out_specs = (P(None, ("users", "items")), P(None, ("items", "users")))
    return jax.shard_map(body, mesh=mesh, in_specs=in_specs, out_specs=out_specs, check_vma=False)
```

profile of v0, /device:TPU:0, one launch (start us, length us, event | category | flops | bytes accessed | tf_op | source)
XLA Modules:
  0.0 920.6 jit_solution(12152243749214164985)
XLA Ops:
  7.9 1.6 convert_multiply_fusion
  12.3 50.2 %all-gather.4.cloned.1.call-done = f32[64,8192]{1,0:T(8,128)} async-done(((f32[64,1024]{1,0:T(8,128)}), f32[64,8192]{1,0:T(8,128)}) %all-gather.4.cloned.1.call-update) | async-done | bytes 2097168 | tf_op jit(solution)/shard_map/all_gather | solution.py:53
  62.6 1.9 copy_bitcast_fusion.7
  64.4 7.0 gather_fusion
  71.4 37.3 %broadcast_multiply_fusion.3 = f32[512,64,128]{2,1,0:T(8,128)} fusion(f32[512]{0:T(512)S(1)} %get-tuple-element.8, bf16[1,1,512,128,128]{4,3,2,1,0:T(8,128)(2,1)} %param.17, f32[512,64,128]{2,1,0:T(8,128)} %gather_fusion, pred[512]{0:T(512)(128)(4,1)S(1)} %get-tuple-element.9), kind=kOutput, calls=%fused_computation.32 | convolution fusion | flops 6450839552 | bytes 50334208 | tf_op jit(solution)/shard_map/ktc,trc->ktr/dot_general | solution.py:26
  108.9 51.9 %scatter_fusion = f32[64,64,128]{2,0,1:T(8,128)S(1)} fusion(f32[64,64,128]{2,0,1:T(8,128)S(1)} %broadcast.101.clone.2, s32[512]{0:T(512)S(1)} %bitcast.126, f32[512,64,128]{2,1,0:T(8,128)} %broadcast_multiply_fusion.3), kind=kCustom, calls=%fused_computation.4 | custom fusion | flops 4194304 | bytes 50333696 | tf_op jit(solution)/shard_map/scatter-add | solution.py:34
  160.8 1.5 copy_bitcast_fusion.3
  163.0 29.2 %reduce-scatter.3.cloned.1.call-done = f32[64,2048]{1,0:T(8,128)} async-done(((f32[64,8192]{1,0:T(8,128)}), f32[64,2048]{1,0:T(8,128)}) %reduce-scatter.3.cloned.1.call-update) | async-done | bytes 524304 | tf_op jit(solution)/shard_map/reduce_scatter | solution.py:79
  192.2 1.8 fusion.59
  194.0 39.4 %psum.42 = f32[64,64]{0,1:T(8,128)S(1)} all-reduce(f32[64,64]{0,1:T(8,128)S(1)} %fusion.59), channel_id=1, replica_groups=mesh['users'=8,'items'=4] {'users','items'}, use_global_device_ids=true, to_apply=%region_2.4 | all-reduce | flops 4096 | bytes 32768 | tf_op jit(solution)/shard_map/psum | solution.py:82
  233.5 5.8 cholesky.74
  240.7 4.9 custom-call.10
  245.6 2.5 convolution_multiply_fusion.1
  248.4 23.1 %all-gather.6.cloned.1.call-done = f32[64,8192]{1,0:T(8,128)} async-done(((f32[64,2048]{1,0:T(8,128)}), f32[64,8192]{1,0:T(8,128)}) %all-gather.6.cloned.1.call-update) | async-done | bytes 2097168 | tf_op jit(solution)/shard_map/all_gather | solution.py:84
  271.6 1.9 copy_bitcast_fusion.6
  273.5 7.0 gather_fusion.1
  280.4 22.0 %broadcast_multiply_fusion.2 = f32[512,64,128]{2,1,0:T(8,128)} fusion(f32[512]{0:T(512)S(1)} %get-tuple-element.8, bf16[1,1,512,128,128]{4,3,2,1,0:T(8,128)(2,1)} %param.17, f32[512,64,128]{2,1,0:T(8,128)} %gather_fusion.1, pred[512]{0:T(512)(128)(4,1)S(1)} %compare_and_fusion.1), kind=kOutput, calls=%fused_computation.31 | convolution fusion | flops 6450839552 | bytes 50334208 | tf_op jit(solution)/shard_map/ktr,trc->ktc/dot_general | solution.py:40
  302.7 51.8 %scatter_fusion.1 = f32[64,64,128]{2,0,1:T(8,128)S(1)} fusion(f32[64,64,128]{2,0,1:T(8,128)S(1)} %broadcast.101.clone.1, s32[512]{0:T(512)S(1)} %bitcast.128, f32[512,64,128]{2,1,0:T(8,128)} %broadcast_multiply_fusion.2), kind=kCustom, calls=%fused_computation.5 | custom fusion | flops 4194304 | bytes 50333696 | tf_op jit(solution)/shard_map/scatter-add | solution.py:48
  354.6 1.4 copy_bitcast_fusion.2
  356.1 31.6 %all_gather.12 = f32[8192]{0:T(1024)S(1)} all-gather(f32[1024]{0:T(1024)S(1)} %convert_rsqrt_fusion.1), channel_id=1, replica_groups=mesh['users'=8,'items'=4] {'users'}, dimensions={0}, use_global_device_ids=true | all-gather | bytes 36864 | tf_op jit(solution)/shard_map/all_gather | solution.py:70
  387.6 71.1 %all-reduce.3.cloned.1.call-done = f32[64,8192]{1,0:T(8,128)} async-done(((f32[64,8192]{1,0:T(8,128)}), f32[64,8192]{1,0:T(8,128)}) %all-reduce.3.cloned.1.call-update) | async-done | bytes 2097168 | tf_op jit(solution)/shard_map/psum | solution.py:86
  458.7 4.3 fusion.45
  463.0 11.1 %psum.44 = f32[64,64]{0,1:T(8,128)S(1)} all-reduce(f32[64,64]{0,1:T(8,128)S(1)} %fusion.45), channel_id=1, replica_groups=mesh['users'=8,'items'=4] {'items'}, use_global_device_ids=true, to_apply=%region_7.0 | all-reduce | flops 4096 | bytes 32768 | tf_op jit(solution)/shard_map/psum | solution.py:87
  474.3 5.8 cholesky.85
  481.4 4.9 custom-call.11
  486.4 2.0 fusion.47
  488.6 7.0 gather_fusion.2
  495.6 37.3 %broadcast_multiply_fusion.1 = f32[512,64,128]{2,1,0:T(8,128)} fusion(f32[512]{0:T(512)S(1)} %get-tuple-element.8, bf16[1,1,512,128,128]{4,3,2,1,0:T(8,128)(2,1)} %param.17, f32[512,64,128]{2,1,0:T(8,128)} %gather_fusion.2, pred[512]{0:T(512)(128)(4,1)S(1)} %get-tuple-element.9), kind=kOutput, calls=%fused_computation.30 | convolution fusion | flops 6450839552 | bytes 50334208 | tf_op jit(solution)/shard_map/ktc,trc->ktr/dot_general | solution.py:26
  533.2 51.9 %scatter_fusion.2 = f32[64,64,128]{2,0,1:T(8,128)S(1)} fusion(f32[64,64,128]{2,0,1:T(8,128)S(1)} %broadcast.101.clone, s32[512]{0:T(512)S(1)} %bitcast.127, f32[512,64,128]{2,1,0:T(8,128)} %broadcast_multiply_fusion.1), kind=kCustom, calls=%fused_computation.6 | custom fusion | flops 4194304 | bytes 50333696 | tf_op jit(solution)/shard_map/scatter-add | solution.py:34
  585.0 1.5 copy_bitcast_fusion.1
  586.8 30.2 %reduce-scatter.5.cloned.1.call-done = f32[64,2048]{1,0:T(8,128)} async-done(((f32[64,8192]{1,0:T(8,128)}), f32[64,2048]{1,0:T(8,128)}) %reduce-scatter.5.cloned.1.call-update) | async-done | bytes 524304 | tf_op jit(solution)/shard_map/reduce_scatter | solution.py:79
  616.9 1.8 fusion.56
  618.7 39.4 %psum.45 = f32[64,64]{0,1:T(8,128)S(1)} all-reduce(f32[64,64]{0,1:T(8,128)S(1)} %fusion.56), channel_id=1, replica_groups=mesh['users'=8,'items'=4] {'users','items'}, use_global_device_ids=true, to_apply=%region_10.15 | all-reduce | flops 4096 | bytes 32768 | tf_op jit(solution)/shard_map/psum | solution.py:82
  658.3 5.8 cholesky.96
  665.5 4.9 custom-call.12
  670.3 2.7 broadcast_multiply_fusion.4
  673.1 23.4 %all-gather.8.cloned.1.call-done = f32[64,8192]{1,0:T(8,128)} async-done(((f32[64,2048]{1,0:T(8,128)}), f32[64,8192]{1,0:T(8,128)}) %all-gather.8.cloned.1.call-update) | async-done | bytes 2097168 | tf_op jit(solution)/shard_map/all_gather | solution.py:84
  696.5 1.9 copy_bitcast_fusion.4
  698.3 7.0 gather_fusion.3
  705.3 22.0 %broadcast_multiply_fusion = f32[512,64,128]{2,1,0:T(8,128)} fusion(f32[512]{0:T(512)S(1)} %get-tuple-element.8, bf16[1,1,512,128,128]{4,3,2,1,0:T(8,128)(2,1)} %param.17, f32[512,64,128]{2,1,0:T(8,128)} %gather_fusion.3, pred[512]{0:T(512)(128)(4,1)S(1)} %compare_and_fusion.1), kind=kOutput, calls=%fused_computation.29 | convolution fusion | flops 6450839552 | bytes 50334208 | tf_op jit(solution)/shard_map/ktr,trc->ktc/dot_general | solution.py:40
  727.6 51.8 %scatter_fusion.3 = f32[64,64,128]{2,0,1:T(8,128)S(1)} fusion(f32[64,64,128]{2,0,1:T(8,128)S(1)} %broadcast.101, s32[512]{0:T(512)S(1)} %bitcast.129, f32[512,64,128]{2,1,0:T(8,128)} %broadcast_multiply_fusion), kind=kCustom, calls=%fused_computation.7 | custom fusion | flops 4194304 | bytes 50333696 | tf_op jit(solution)/shard_map/scatter-add | solution.py:48
  779.4 1.4 copy_bitcast_fusion
  780.9 102.4 %all-reduce.5.cloned.1.call-done = f32[64,8192]{1,0:T(8,128)} async-done(((f32[64,8192]{1,0:T(8,128)}), f32[64,8192]{1,0:T(8,128)}) %all-reduce.5.cloned.1.call-update) | async-done | bytes 2097168 | tf_op jit(solution)/shard_map/psum | solution.py:86
  883.3 4.3 fusion.42
  887.7 10.9 %psum.47 = f32[64,64]{0,1:T(8,128)S(1)} all-reduce(f32[64,64]{0,1:T(8,128)S(1)} %fusion.42), channel_id=1, replica_groups=mesh['users'=8,'items'=4] {'items'}, use_global_device_ids=true, to_apply=%region_13.18 | all-reduce | flops 4096 | bytes 32768 | tf_op jit(solution)/shard_map/psum | solution.py:87
  898.7 5.8 cholesky.107
  905.9 4.9 custom-call.13
  910.8 2.0 fusion.40
  (64 shorter events, 11.8 us)
Async XLA Ops:
  7.2 55.4 %all-gather.4.cloned.1.call-start = ((), (), s32[]{:S(2)}) async-start(), calls=%async_computation.2 | async-start | bytes 2359296 | tf_op jit(solution)/shard_map/all_gather | solution.py:53
  9.6 182.6 %reduce-scatter.3.cloned.1.call-start = ((), (), s32[]{:S(2)}) async-start(), calls=%async_computation.3 | async-start | bytes 2621440 | tf_op jit(solution)/shard_map/reduce_scatter | solution.py:79
  162.3 0.7 copy-start.4
  162.3 86.1 %copy-start.2 = (s32[1,1,512]{2,1,0:T(1,128)S(1)}, s32[1,1,512]{2,1,0:T(1,128)}, u32[]{:S(2)}) copy-start(s32[1,1,512]{2,1,0:T(1,128)} %param.14) | copy-start | bytes 6148
  162.3 86.1 %copy-start.3 = (s32[1,1,512]{2,1,0:T(1,128)S(1)}, s32[1,1,512]{2,1,0:T(1,128)}, u32[]{:S(2)}) copy-start(s32[1,1,512]{2,1,0:T(1,128)} %param.15) | copy-start | bytes 6148
  162.3 109.3 %all-gather.6.cloned.1.call-start = ((), (), s32[]{:S(2)}) async-start(), calls=%async_computation.4 | async-start | bytes 2621440 | tf_op jit(solution)/shard_map/all_gather | solution.py:84
  248.1 210.6 %all-reduce.3.cloned.1.call-start = ((), (), s32[]{:S(2)}) async-start(), calls=%async_computation.5 | async-start | bytes 4194304 | tf_op jit(solution)/shard_map/psum | solution.py:86
  356.0 260.9 %reduce-scatter.5.cloned.1.call-start = ((), (), s32[]{:S(2)}) async-start(), calls=%async_computation.6 | async-start | bytes 2621440 | tf_op jit(solution)/shard_map/reduce_scatter | solution.py:79
  458.7 27.7 %copy-start.1 = (f32[64,8192]{1,0:T(8,128)S(1)}, f32[64,8192]{1,0:T(8,128)}, u32[]{:S(2)}) copy-start(f32[64,8192]{1,0:T(8,128)} %all-reduce.3.cloned.1.call-done) | copy-start | bytes 6291460
  586.5 109.9 %all-gather.8.cloned.1.call-start = ((), (), s32[]{:S(2)}) async-start(), calls=%async_computation.7 | async-start | bytes 2621440 | tf_op jit(solution)/shard_map/all_gather | solution.py:84
  673.0 210.3 %all-reduce.5.cloned.1.call-start = ((), (), s32[]{:S(2)}) async-start(), calls=%async_computation.8 | async-start | bytes 4194304 | tf_op jit(solution)/shard_map/psum | solution.py:86
  883.3 27.5 %copy-start = (f32[64,8192]{1,0:T(8,128)S(1)}, f32[64,8192]{1,0:T(8,128)}, u32[]{:S(2)}) copy-start(f32[64,8192]{1,0:T(8,128)} %all-reduce.5.cloned.1.call-done) | copy-start | bytes 6291460
Sparse Core Ops, SparseCore 0:
  10.7 51.7 all-gather.3
  162.4 29.6 reduce-scatter.2
  248.2 23.3 all-gather.5
  356.1 102.5 all-reduce.2
  586.7 30.2 reduce-scatter.4
  673.2 23.2 all-gather.7
  781.0 102.2 all-reduce.4
where the time goes:
time: 936 us; the launch traced here: 921 us
  waiting for transfers between devices  330 us (35%)
  other arithmetic  260 us (28%)
  matrix products  140 us (15%)
  blocking collectives  132 us (14%)
  local copies, waits for them, and re-layouts  42.2 us (5%)
  between operations  15.4 us (2%)
    psum x2, waiting for transfers between devices, body(): item_raw = item_scale_block[None, :] * lax.psum(partial_items, 'users')  173 us
    scatter-add x2, other arithmetic, user_partial(): summed = jnp.zeros((K, UT, TILE), jnp.float32).at[:, rows, :].add(product)  104 us
    scatter-add x2, other arithmetic, item_partial(): summed = jnp.zeros((K, IT, TILE), jnp.float32).at[:, cols, :].add(product)  104 us
    psum x2, blocking collectives, body(): user_gram = lax.psum(local_gram(user_raw), ('users', 'items'))  78.9 us
    dot_general x2, matrix products, user_partial(): jnp.einsum('ktc,trc->ktr', picked, values, precision=lax.Precision.HIGHES...  74.6 us
    reduce_scatter x2, waiting for transfers between devices, body(): lax.psum_scatter(partial_users, 'items', scatter_dimension=1, tiled=True)  59.3 us
    all_gather x1, waiting for transfers between devices, gather_items(): return lax.all_gather(sent, 'users', axis=1, tiled=True)  50.2 us
    all_gather x2, waiting for transfers between devices, body(): lax.all_gather(user_scale[None, :] * user_panel, 'items', axis=1, tiled=T...  46.5 us
  transfers between devices with their start and end apart: 7, of which 7 were waited for; matrix products, arithmetic and copies ran while one was open for 0% of the time, Pallas kernels for 0%

commit v1 on v0

v1 whole, which is shorter than its diff:
```python
import functools

import jax
import jax.numpy as jnp
from jax import lax
from jax.experimental import pallas as pl
from jax.experimental.pallas import tpu as pltpu
from jax.sharding import PartitionSpec as P

K = 64
TILE = 128
ITERS = 2
UT = 64
IT = 64
BATCH = 64
UNROLL = 32
HIGHEST = lax.Precision.HIGHEST


def gather_order(size):
    bits = []
    bit = size >> 1
    while bit:
        bits.append(bit)
        bit >>= 1
    return bits


def exchange(value, axis, bit):
    size = lax.axis_size(axis)
    return lax.ppermute(value, axis, [(at, at ^ bit) for at in range(size)])


def relative_position(shard, axis):
    apart = shard ^ lax.axis_index(axis)
    place = jnp.zeros_like(apart)
    for level, bit in enumerate(gather_order(lax.axis_size(axis))):
        place = place + jnp.where(apart & bit != 0, 1 << level, 0)
    return place


def all_gather_halves(shard, axis):
    held = shard
    order = gather_order(lax.axis_size(axis))
    for bit in order[:-1]:
        held = jnp.concatenate([held, exchange(held, axis, bit)], axis=0)
    return held, exchange(held, axis, order[-1])


def reduce_scatter_halves(kept, sent, axis):
    order = gather_order(lax.axis_size(axis))[::-1]
    received = exchange(sent, axis, order[0])
    for bit in order[1:]:
        half = kept.shape[0] // 2
        sent = kept[half:] + received[half:]
        kept = kept[:half] + received[:half]
        received = exchange(sent, axis, bit)
    return kept + received


def all_sum(value):
    for axis in ("items", "users"):
        for bit in gather_order(lax.axis_size(axis))[::-1]:
            value = value + exchange(value, axis, bit)
    return value


def tiles_kernel(count, source, target, low_ref, high_ref, tile_ref, keep_ref, send_ref, pieces, total, *, transposed):
    step = pl.program_id(0)
    half = low_ref.shape[0]

    @pl.when(step == 0)
    def _():
        def prepare(at, carry):
            for offset, ref in ((0, low_ref), (half, high_ref)):
                value = ref[at]
                top = value.astype(jnp.bfloat16)
                pieces[offset + at, :K] = top
                pieces[offset + at, K:] = (value - top.astype(jnp.float32)).astype(jnp.bfloat16)
                total[offset + at] = jnp.zeros((2 * K, TILE), jnp.float32)
            return carry

        lax.fori_loop(0, half, prepare, 0, unroll=4)

    live = jnp.clip(count[0] - step * BATCH, 0, BATCH)
    contract = 1 if transposed else 0

    def group(at, carry):
        first = at * UNROLL
        products = []
        for slot in range(UNROLL):
            products.append(
                lax.dot_general(
                    pieces[source[step * BATCH + first + slot]],
                    tile_ref[first + slot],
                    (((1,), (contract,)), ((), ())),
                    preferred_element_type=jnp.float32,
                )
            )
        for slot in range(UNROLL):
            total[target[step * BATCH + first + slot]] += products[slot]
        return carry

    lax.fori_loop(0, (live + UNROLL - 1) // UNROLL, group, 0)

    @pl.when(step == pl.num_programs(0) - 1)
    def _():
        def finish(at, carry):
            for offset, ref in ((0, keep_ref), (half, send_ref)):
                ref[at] = total[offset + at, :K] + total[offset + at, K:]
            return carry

        lax.fori_loop(0, half, finish, 0, unroll=4)


def tiles_product(count, source, target, low, high, tiles, blocks_out, transposed):
    half_in = low.shape[0]
    half_out = blocks_out // 2
    whole = lambda step, *refs: (0, 0, 0)

    def tile_block(step, count, source, target):
        return (jnp.minimum(step, (count[0] + BATCH - 1) // BATCH - 1), 0, 0)

    return pl.pallas_call(
        functools.partial(tiles_kernel, transposed=transposed),
        out_shape=[jax.ShapeDtypeStruct((half_out, K, TILE), jnp.float32)] * 2,
        grid_spec=pltpu.PrefetchScalarGridSpec(
            num_scalar_prefetch=3,
            grid=(tiles.shape[0] // BATCH,),
            in_specs=[
                pl.BlockSpec((half_in, K, TILE), whole),
                pl.BlockSpec((half_in, K, TILE), whole),
                pl.BlockSpec((BATCH, TILE, TILE), tile_block),
            ],
            out_specs=[pl.BlockSpec((half_out, K, TILE), whole)] * 2,
            scratch_shapes=[
                pltpu.VMEM((2 * half_in, 2 * K, TILE), jnp.bfloat16),
                pltpu.VMEM((2 * half_out + 1, 2 * K, TILE), jnp.float32),
            ],
        ),
        name="user_tiles" if transposed else "item_tiles",
    )(count, source, target, low, high, tiles)


def dot_full(left, right, contract):
    return lax.dot_general(
        left, right, ((contract[:1], contract[1:]), ((), ())), precision=HIGHEST, preferred_element_type=jnp.float32
    )


def scale_kernel(inverse_ref, raw_ref, scale_ref, panel_ref, sent_ref, gram_ref):
    gram = jnp.zeros((K, K), jnp.float32)
    for at in range(raw_ref.shape[0]):
        scale = scale_ref[at][None, :]
        panel = raw_ref[at]
        if inverse_ref is not None:
            panel = dot_full(inverse_ref[...], panel, (1, 0))
        panel = scale * panel
        panel_ref[at] = panel
        sent_ref[at] = scale * panel
        gram = gram + dot_full(panel, panel, (1, 1))
    gram_ref[...] = gram


def scale_panel(inverse, raw, scale):
    kernel = scale_kernel if inverse is not None else functools.partial(scale_kernel, None)
    operands = (raw, scale) if inverse is None else (inverse, raw, scale)
    shape = jax.ShapeDtypeStruct(raw.shape, jnp.float32)
    return pl.pallas_call(
        kernel,
        out_shape=[shape, shape, jax.ShapeDtypeStruct((K, K), jnp.float32)],
        name="scale_panel",
    )(*operands)


def finish_kernel(inverse_ref, panel_ref, out_ref):
    for at in range(panel_ref.shape[0]):
        out_ref[:, at * TILE : (at + 1) * TILE] = dot_full(inverse_ref[...], panel_ref[at], (1, 0))


def finish_panel(inverse, panel):
    return pl.pallas_call(
        finish_kernel,
        out_shape=jax.ShapeDtypeStruct((K, panel.shape[0] * TILE), jnp.float32),
        name="finish_panel",
    )(inverse, panel)


def inverse_factor(gram, total):
    lower = jnp.linalg.cholesky(gram / total)
    return lax.linalg.triangular_solve(lower, jnp.eye(K, dtype=jnp.float32), left_side=True, lower=True)


def body(tile_rows, tile_cols, tile_count, tile_vals, user_degree, item_degree, start_items):
    user_groups = lax.axis_size("users")
    item_groups = lax.axis_size("items")
    user_blocks = UT // item_groups
    item_blocks = IT // user_groups
    user_total = UT * TILE * user_groups
    item_total = IT * TILE * item_groups

    rows = tile_rows[0, 0]
    cols = tile_cols[0, 0]
    tiles = tile_vals[0, 0]
    count = tile_count[0]
    live = jnp.arange(rows.shape[0], dtype=jnp.int32) < count[0]
    row_place = relative_position(rows // user_blocks, "items") * user_blocks + rows % user_blocks
    col_place = relative_position(cols // item_blocks, "users") * item_blocks + cols % item_blocks
    row_target = jnp.where(live, row_place, UT)
    col_target = jnp.where(live, col_place, IT)

    user_scale = lax.rsqrt(user_degree.astype(jnp.float32)).reshape(user_blocks, TILE)
    item_scale = lax.rsqrt(item_degree.astype(jnp.float32)).reshape(item_blocks, TILE)
    start = start_items.astype(jnp.float32).reshape(K, item_blocks, TILE).transpose(1, 0, 2)
    sent_items = item_scale[:, None, :] * start
    item_inverse = None
    for step in range(ITERS):
        low, high = all_gather_halves(sent_items, "users")
        kept, sent = tiles_product(count, col_place, row_target, low, high, tiles, UT, True)
        user_sum = reduce_scatter_halves(kept, sent, "items")
        user_raw, sent_users, user_gram = scale_panel(item_inverse, user_sum, user_scale)

        low, high = all_gather_halves(sent_users, "items")
        user_inverse = inverse_factor(all_sum(user_gram), user_total)
        kept, sent = tiles_product(count, row_place, col_target, low, high, tiles, IT, False)
        item_sum = reduce_scatter_halves(kept, sent, "users")
        item_raw, sent_items, item_gram = scale_panel(user_inverse, item_sum, item_scale)
        item_inverse = inverse_factor(all_sum(item_gram), item_total)
    return finish_panel(user_inverse, user_raw), finish_panel(item_inverse, item_raw)


def solution(mesh):
    in_specs = (
        P("users", "items", None),
        P("users", "items", None),
        P("users", "items"),
        P("users", "items", None, None, None),
        P(("users", "items")),
        P(("items", "users")),
        P(None, ("items", "users")),
    )
    out_specs = (P(None, ("users", "items")), P(None, ("items", "users")))
    return jax.shard_map(body, mesh=mesh, in_specs=in_specs, out_specs=out_specs, check_vma=False)
```

time: 936 us -> 422 us (0.45); the launches traced: 921 us -> 420 us
  other arithmetic: 260 us -> 63.4 us
  matrix products: 140 us -> 3.48 us
  blocking collectives: 132 us -> 0 us
  waiting for transfers between devices: 330 us -> 228 us
  Pallas kernels: 0 us -> 85.4 us
  local copies, waits for them, and re-layouts: 42.2 us -> 8.66 us
  starting transfers between devices: 0.67 us -> 29.7 us
  between operations: 15.4 us -> 1.72 us
    ppermute x0 -> x40, waiting for transfers between devices: none -> 228 us  [exchange(): return lax.ppermute(value, axis, [(at, at ^ bit) for at in range(size)])]
    scatter-add x4 -> x0, other arithmetic: 207 us -> none  [the longest x2 104 us: user_partial(): summed = jnp.zeros((K, UT, TILE), jnp.float32).at[:, rows, :].add(product)]
    psum x2 -> x0, waiting for transfers between devices: 173 us -> none  [body(): item_raw = item_scale_block[None, :] * lax.psum(partial_items, 'users')]
    dot_general x8 -> x0, matrix products: 131 us -> none  [the longest x2 74.6 us: user_partial(): jnp.einsum('ktc,trc->ktr', picked, values, precision=lax.Precision.HIGHES...]
    psum x4 -> x0, blocking collectives: 101 us -> none  [the longest x2 78.9 us: body(): user_gram = lax.psum(local_gram(user_raw), ('users', 'items'))]
    all_gather x3 -> x0, waiting for transfers between devices: 96.8 us -> none  [the longest x1 50.2 us: gather_items(): return lax.all_gather(sent, 'users', axis=1, tiled=True)]
    pallas_call x0 -> x10, Pallas kernels: none -> 85.4 us  [the longest x4 68.1 us: tiles_product(): pl.pallas_call(functools.partial(tiles_kernel, transposed=transposed), ou...]
    reduce_scatter x2 -> x0, waiting for transfers between devices: 59.3 us -> none  [body(): lax.psum_scatter(partial_users, 'items', scatter_dimension=1, tiled=True)]
  transfers between devices with their start and end apart: 7 -> 40, of which waited for: 7 -> 37; matrix products, arithmetic and copies ran while one was open for 0% -> 11% of each run, Pallas kernels for 0% -> 1%
where the time goes in v1:
time: 422 us; the launch traced here: 420 us
  waiting for transfers between devices  228 us (54%)
  Pallas kernels  85.4 us (20%)
  other arithmetic  63.4 us (15%)
  starting transfers between devices  29.7 us (7%)
  local copies, waits for them, and re-layouts  8.66 us (2%)
    ppermute x40, waiting for transfers between devices, exchange(): return lax.ppermute(value, axis, [(at, at ^ bit) for at in range(size)])  228 us
    pallas_call x4, Pallas kernels, tiles_product(): pl.pallas_call(functools.partial(tiles_kernel, transposed=transposed), ou...  68.1 us
    ppermute x40, starting transfers between devices, exchange(): return lax.ppermute(value, axis, [(at, at ^ bit) for at in range(size)])  29.7 us
    another operation x12, other arithmetic, inverse_factor(): lower = jnp.linalg.cholesky(gram / total)  26.1 us
    another operation x8, other arithmetic, inverse_factor(): lax.linalg.triangular_solve(lower, jnp.eye(K, dtype=jnp.float32), left_si...  22.2 us
    pallas_call x4, Pallas kernels, scale_panel(): pl.pallas_call(kernel, out_shape=[shape, shape, jax.ShapeDtypeStruct((K,...  12.9 us
  transfers between devices with their start and end apart: 40, of which 37 were waited for; matrix products, arithmetic and copies ran while one was open for 11% of the time, Pallas kernels for 1%

profile of v1, /device:TPU:0, one launch (start us, length us, event | category | flops | bytes accessed | tf_op | source)
XLA Modules:
  0.0 420.0 jit_solution(2560120908916758636)
XLA Ops:
  2.3 4.1 collective-permute-start
  6.4 11.9 %collective-permute-done = f32[8,64,128]{2,1,0:T(8,128)S(1)} collective-permute-done((f32[8,64,128]{2,1,0:T(8,128)S(1)}, f32[8,64,128]{2,1,0:T(8,128)S(1)}, u32[]{:S(2)}, u32[]{:S(2)}) %collective-permute-start) | collective-permute-done | bytes 262176 | tf_op jit(solution)/shard_map/ppermute | solution.py:31
  19.2 12.4 %collective-permute-done.1 = f32[16,64,128]{2,1,0:T(8,128)S(1)} collective-permute-done((f32[16,64,128]{2,1,0:T(8,128)S(1)}, f32[16,64,128]{2,1,0:T(8,128)S(1)}, u32[]{:S(2)}, u32[]{:S(2)}) %collective-permute-start.1) | collective-permute-done | bytes 524320 | tf_op jit(solution)/shard_map/ppermute | solution.py:31
  35.0 20.2 %collective-permute-done.2.high_ref = f32[32,64,128]{2,1,0:T(8,128)S(1)} collective-permute-done((f32[32,64,128]{2,1,0:T(8,128)S(1)}, f32[32,64,128]{2,1,0:T(8,128)S(1)}, u32[]{:S(2)}, u32[]{:S(2)}) %collective-permute-start.2) | collective-permute-done | bytes 1048608 | tf_op jit(solution)/shard_map/ppermute | solution.py:31
  56.2 19.0 %user_tiles.2 = (f32[32,64,128]{2,1,0:T(8,128)}, f32[32,64,128]{2,1,0:T(8,128)}) custom-call(s32[1]{0:T(128)} %bitcast.54.count, s32[512]{0:T(512)} %get-tuple-element.39.source, s32[512]{0:T(512)} %get-tuple-element.46.target, f32[32,64,128]{2,1,0:T(8,128)} %copy-done, f32[32,64,128]{2,1,0:T(8,128)} %copy-done.4, bf16[512,128,128]{2,1,0:T(8,128)(2,1)} %bitcast.59), custom_call_target="tpu_custom_call" | custom-call | tf_op jit(solution)/shard_map/user_tiles/pallas_call | solution.py:124
  75.2 2.9 collective-permute-done.3
  79.8 13.3 %collective-permute-done.4 = f32[16,64,128]{2,1,0:T(8,128)S(1)} collective-permute-done((f32[16,64,128]{2,1,0:T(8,128)S(1)}, f32[16,64,128]{2,1,0:T(8,128)S(1)}, u32[]{:S(2)}, u32[]{:S(2)}) %collective-permute-start.4) | collective-permute-done | bytes 524320 | tf_op jit(solution)/shard_map/ppermute | solution.py:31
  95.1 2.7 scale_panel.4
  99.2 11.9 %collective-permute-done.10 = f32[16,64,128]{2,1,0:T(8,128)S(1)} collective-permute-done((f32[16,64,128]{2,1,0:T(8,128)}, f32[16,64,128]{2,1,0:T(8,128)S(1)}, u32[]{:S(2)}, u32[]{:S(2)}) %collective-permute-start.10) | collective-permute-done | bytes 524320 | tf_op jit(solution)/shard_map/ppermute | solution.py:31
  111.2 2.6 collective-permute-done.11.high_ref
  114.9 15.0 %item_tiles.2 = (f32[32,64,128]{2,1,0:T(8,128)}, f32[32,64,128]{2,1,0:T(8,128)}) custom-call(s32[1]{0:T(128)} %bitcast.55.count, s32[512]{0:T(512)} %get-tuple-element.47.source, s32[512]{0:T(512)} %get-tuple-element.38.target, f32[32,64,128]{2,1,0:T(8,128)} %copy-done.1, f32[32,64,128]{2,1,0:T(8,128)} %copy-done.7, bf16[512,128,128]{2,1,0:T(8,128)(2,1)} %bitcast.60), custom_call_target="tpu_custom_call" | custom-call | tf_op jit(solution)/shard_map/item_tiles/pallas_call | solution.py:124
  131.5 3.6 collective-permute-done.6
  137.1 10.2 %collective-permute-done.7 = f32[64,64]{0,1:T(8,128)S(1)} collective-permute-done((f32[64,64]{0,1:T(8,128)S(1)}, f32[64,64]{0,1:T(8,128)S(1)}, u32[]{:S(2)}, u32[]{:S(2)}) %collective-permute-start.7) | collective-permute-done | bytes 16416 | tf_op jit(solution)/shard_map/ppermute | solution.py:31
  147.3 3.9 collective-permute-done.8
  151.2 7.5 %collective-permute-start.9 = (f32[64,64]{0,1:T(8,128)S(1)}, f32[64,64]{0,1:T(8,128)S(1)}, u32[]{:S(2)}, u32[]{:S(2)}) collective-permute-start(f32[64,64]{0,1:T(8,128)S(1)} %add.156), channel_id=1, source_target_pairs={{0,16},{4,20},{8,24},{12,28},{16,0},{20,4},{24,8},{28,12},{1,17},{... | collective-permute-start | bytes 49160 | tf_op jit(solution)/shard_map/ppermute | solution.py:31
  160.9 5.8 %cholesky.74 = f32[64,64]{1,0:T(8,128)S(1)} custom-call(f32[64,64]{1,0:T(8,128)S(1)} %fusion.24), custom_call_target="Cholesky" | custom-call | tf_op jit(solution)/shard_map/jit(cholesky)/cholesky | solution.py:190
  167.4 4.2 collective-permute-done.13
  172.4 4.9 %custom-call.8 = f32[1,64,64]{1,2,0:T(8,128)S(1)} custom-call(f32[1,64,64]{2,1,0:T(8,128)S(1)} %fusion.13), custom_call_target="InvertDiagBlocksLowerTriangular" | custom-call | tf_op jit(solution)/shard_map/triangular_solve/custom-call.0 | solution.py:191
  178.2 5.5 %collective-permute-done.14 = f32[8,64,128]{2,1,0:T(8,128)S(1)} collective-permute-done((f32[8,64,128]{2,1,0:T(8,128)S(1)}, f32[8,64,128]{2,1,0:T(8,128)S(1)}, u32[]{:S(2)}, u32[]{:S(2)}) %collective-permute-start.14) | collective-permute-done | bytes 262176 | tf_op jit(solution)/shard_map/ppermute | solution.py:31
  184.4 3.0 scale_panel.5
  187.4 13.0 %collective-permute-done.20 = f32[8,64,128]{2,1,0:T(8,128)S(1)} collective-permute-done((f32[8,64,128]{2,1,0:T(8,128)}, f32[8,64,128]{2,1,0:T(8,128)S(1)}, u32[]{:S(2)}, u32[]{:S(2)}) %collective-permute-start.20) | collective-permute-done | bytes 262176 | tf_op jit(solution)/shard_map/ppermute | solution.py:31
  202.5 12.0 %collective-permute-done.21 = f32[16,64,128]{2,1,0:T(8,128)S(1)} collective-permute-done((f32[16,64,128]{2,1,0:T(8,128)S(1)}, f32[16,64,128]{2,1,0:T(8,128)S(1)}, u32[]{:S(2)}, u32[]{:S(2)}) %collective-permute-start.21) | collective-permute-done | bytes 524320 | tf_op jit(solution)/shard_map/ppermute | solution.py:31
  216.7 21.4 %collective-permute-done.22.high_ref = f32[32,64,128]{2,1,0:T(8,128)S(1)} collective-permute-done((f32[32,64,128]{2,1,0:T(8,128)S(1)}, f32[32,64,128]{2,1,0:T(8,128)S(1)}, u32[]{:S(2)}, u32[]{:S(2)}) %collective-permute-start.22) | collective-permute-done | bytes 1048608 | tf_op jit(solution)/shard_map/ppermute | solution.py:31
  239.1 19.0 %user_tiles.3 = (f32[32,64,128]{2,1,0:T(8,128)}, f32[32,64,128]{2,1,0:T(8,128)}) custom-call(s32[1]{0:T(128)} %bitcast.56.count, s32[512]{0:T(512)} %get-tuple-element.39.source, s32[512]{0:T(512)} %get-tuple-element.46.target, f32[32,64,128]{2,1,0:T(8,128)} %copy-done.3, f32[32,64,128]{2,1,0:T(8,128)} %copy-done.6, bf16[512,128,128]{2,1,0:T(8,128)(2,1)} %bitcast.61), custom_call_target="tpu_custom_call" | custom-call | tf_op jit(solution)/shard_map/user_tiles/pallas_call | solution.py:124
  261.0 3.9 collective-permute-done.16
  265.0 3.9 collective-permute-done.17
  268.9 3.9 collective-permute-done.18
  275.0 2.6 collective-permute-done.19
  277.7 5.8 %cholesky.85 = f32[64,64]{1,0:T(8,128)S(1)} custom-call(f32[64,64]{1,0:T(8,128)S(1)} %fusion.22), custom_call_target="Cholesky" | custom-call | tf_op jit(solution)/shard_map/jit(cholesky)/cholesky | solution.py:190
  286.1 4.9 %custom-call.9 = f32[1,64,64]{1,2,0:T(8,128)S(1)} custom-call(f32[1,64,64]{2,1,0:T(8,128)S(1)} %fusion.14), custom_call_target="InvertDiagBlocksLowerTriangular" | custom-call | tf_op jit(solution)/shard_map/triangular_solve/custom-call.0 | solution.py:191
  296.1 4.3 %scale_panel.6 = (f32[16,64,128]{2,1,0:T(8,128)}, f32[16,64,128]{2,1,0:T(8,128)}, f32[64,64]{1,0:T(8,128)}) custom-call(f32[64,64]{1,0:T(8,128)} %fusion.9.inverse_ref, f32[16,64,128]{2,1,0:T(8,128)} %fusion.raw_ref, f32[16,128]{1,0:T(8,128)} %rsqrt_bitcast_fusion.scale_ref), custom_call_target="tpu_custom_call" | custom-call | tf_op jit(solution)/shard_map/scale_panel/pallas_call | solution.py:169
  301.8 8.0 %collective-permute-done.30 = f32[16,64,128]{2,1,0:T(8,128)S(1)} collective-permute-done((f32[16,64,128]{2,1,0:T(8,128)}, f32[16,64,128]{2,1,0:T(8,128)S(1)}, u32[]{:S(2)}, u32[]{:S(2)}) %collective-permute-start.30) | collective-permute-done | bytes 524320 | tf_op jit(solution)/shard_map/ppermute | solution.py:31
  309.9 2.6 collective-permute-done.31.high_ref
  313.6 15.2 %item_tiles.3 = (f32[32,64,128]{2,1,0:T(8,128)}, f32[32,64,128]{2,1,0:T(8,128)}) custom-call(s32[1]{0:T(128)} %bitcast.57.count, s32[512]{0:T(512)} %get-tuple-element.47.source, s32[512]{0:T(512)} %get-tuple-element.38.target, f32[32,64,128]{2,1,0:T(8,128)} %copy-done.2, f32[32,64,128]{2,1,0:T(8,128)} %copy-done.5, bf16[512,128,128]{2,1,0:T(8,128)(2,1)} %bitcast.62), custom_call_target="tpu_custom_call" | custom-call | tf_op jit(solution)/shard_map/item_tiles/pallas_call | solution.py:124
  330.1 3.8 collective-permute-done.26
  336.0 13.6 %collective-permute-done.27 = f32[64,64]{0,1:T(8,128)S(1)} collective-permute-done((f32[64,64]{0,1:T(8,128)S(1)}, f32[64,64]{0,1:T(8,128)S(1)}, u32[]{:S(2)}, u32[]{:S(2)}) %collective-permute-start.27) | collective-permute-done | bytes 16416 | tf_op jit(solution)/shard_map/ppermute | solution.py:31
  349.6 3.9 collective-permute-done.28
  353.5 2.6 collective-permute-start.29
  358.5 5.8 %cholesky.96 = f32[64,64]{1,0:T(8,128)S(1)} custom-call(f32[64,64]{1,0:T(8,128)S(1)} %fusion.20), custom_call_target="Cholesky" | custom-call | tf_op jit(solution)/shard_map/jit(cholesky)/cholesky | solution.py:190
  365.0 4.4 %collective-permute-done.33 = f32[16,64,128]{2,1,0:T(8,128)S(1)} collective-permute-done((f32[16,64,128]{2,1,0:T(8,128)S(1)}, f32[16,64,128]{2,1,0:T(8,128)S(1)}, u32[]{:S(2)}, u32[]{:S(2)}) %collective-permute-start.33) | collective-permute-done | bytes 524320 | tf_op jit(solution)/shard_map/ppermute | solution.py:31
  370.3 4.9 %custom-call.10 = f32[1,64,64]{1,2,0:T(8,128)S(1)} custom-call(f32[1,64,64]{2,1,0:T(8,128)S(1)} %fusion.15), custom_call_target="InvertDiagBlocksLowerTriangular" | custom-call | tf_op jit(solution)/shard_map/triangular_solve/custom-call.0 | solution.py:191
  376.1 6.5 %collective-permute-done.34 = f32[8,64,128]{2,1,0:T(8,128)S(1)} collective-permute-done((f32[8,64,128]{2,1,0:T(8,128)S(1)}, f32[8,64,128]{2,1,0:T(8,128)S(1)}, u32[]{:S(2)}, u32[]{:S(2)}) %collective-permute-start.34) | collective-permute-done | bytes 262176 | tf_op jit(solution)/shard_map/ppermute | solution.py:31
  383.3 3.0 scale_panel.7
  388.4 3.9 collective-permute-done.36
  396.2 3.9 collective-permute-done.38
  400.7 2.4 finish_panel.2
  405.0 5.8 %cholesky.107 = f32[64,64]{1,0:T(8,128)S(1)} custom-call(f32[64,64]{1,0:T(8,128)S(1)} %fusion.18), custom_call_target="Cholesky" | custom-call | tf_op jit(solution)/shard_map/jit(cholesky)/cholesky | solution.py:190
  412.2 4.9 %custom-call.11 = f32[1,64,64]{1,2,0:T(8,128)S(1)} custom-call(f32[1,64,64]{2,1,0:T(8,128)S(1)} %fusion.16), custom_call_target="InvertDiagBlocksLowerTriangular" | custom-call | tf_op jit(solution)/shard_map/triangular_solve/custom-call.0 | solution.py:191
  (148 shorter events, 63.6 us)
Async XLA Ops:
  0.6 78.6 %copy-start.12 = (s32[2048]{0:T(1024)S(1)}, s32[2048]{0:T(1024)}, u32[]{:S(2)}) copy-start(s32[2048]{0:T(1024)} %param.14) | copy-start | bytes 24580
  1.3 128.5 %copy-start.8 = (f32[8,128]{1,0:T(8,128)}, f32[8,128]{1,0:T(8,128)S(1)}, u32[]{:S(2)}) copy-start(f32[8,128]{1,0:T(8,128)S(1)} %rsqrt_bitcast_fusion.1.scale_ref) | copy-start | bytes 12292
  2.3 16.1 %collective-permute-start = (f32[8,64,128]{2,1,0:T(8,128)S(1)}, f32[8,64,128]{2,1,0:T(8,128)S(1)}, u32[]{:S(2)}, u32[]{:S(2)}) collective-permute-start(f32[8,64,128]{2,1,0:T(8,128)S(1)} %fusion.2), channel_id=1, source_target_pairs={{0,16},{4,20},{8,24},{12,28},{16,0},{20,4},{24,8},{28,12},{1,17},{... | collective-permute-start | bytes 786440 | tf_op jit(solution)/shard_map/ppermute | solution.py:31
  18.4 13.2 %collective-permute-start.1 = (f32[16,64,128]{2,1,0:T(8,128)S(1)}, f32[16,64,128]{2,1,0:T(8,128)S(1)}, u32[]{:S(2)}, u32[]{:S(2)}) collective-permute-start(f32[16,64,128]{2,1,0:T(8,128)S(1)} %pad_maximum_fusion.1), channel_id=1, source_target_pairs={{0,8},{4,12},{8,0},{12,4},{16,24},{20,28},{24,16},{28,20},{1,9},{5... | collective-permute-start | bytes 1572872 | tf_op jit(solution)/shard_map/ppermute | solution.py:31
  31.6 23.5 %copy-start = (f32[32,64,128]{2,1,0:T(8,128)}, f32[32,64,128]{2,1,0:T(8,128)S(1)}, u32[]{:S(2)}) copy-start(f32[32,64,128]{2,1,0:T(8,128)S(1)} %pad_maximum_fusion.low_ref) | copy-start | bytes 3145732
  31.6 23.5 %collective-permute-start.2 = (f32[32,64,128]{2,1,0:T(8,128)S(1)}, f32[32,64,128]{2,1,0:T(8,128)S(1)}, u32[]{:S(2)}, u32[]{:S(2)}) collective-permute-start(f32[32,64,128]{2,1,0:T(8,128)S(1)} %pad_maximum_fusion.low_ref), channel_id=1, source_target_pairs={{0,4},{4,0},{8,12},{12,8},{16,20},{20,16},{24,28},{28,24},{1,5},{5... | collective-permute-start | bytes 3145736 | tf_op jit(solution)/shard_map/ppermute | solution.py:31
  75.2 2.9 collective-permute-start.3
  79.1 14.0 %collective-permute-start.4 = (f32[16,64,128]{2,1,0:T(8,128)S(1)}, f32[16,64,128]{2,1,0:T(8,128)S(1)}, u32[]{:S(2)}, u32[]{:S(2)}) collective-permute-start(f32[16,64,128]{2,1,0:T(8,128)S(1)} %slice_add_fusion.6), channel_id=1, source_target_pairs={{0,2},{1,3},{2,0},{3,1},{4,6},{5,7},{6,4},{7,5},{8,10},{9,11},{10,... | collective-permute-start | bytes 1572872 | tf_op jit(solution)/shard_map/ppermute | solution.py:31
  97.8 32.1 %copy-start.11 = (f32[64,64]{1,0:T(8,128)S(1)}, f32[64,64]{1,0:T(8,128)}, u32[]{:S(2)}) copy-start(f32[64,64]{1,0:T(8,128)} %get-tuple-element.23) | copy-start | bytes 49156
  97.8 13.3 %collective-permute-start.10 = (f32[16,64,128]{2,1,0:T(8,128)}, f32[16,64,128]{2,1,0:T(8,128)S(1)}, u32[]{:S(2)}, u32[]{:S(2)}) collective-permute-start(f32[16,64,128]{2,1,0:T(8,128)} %get-tuple-element.24), channel_id=1, source_target_pairs={{0,2},{1,3},{2,0},{3,1},{4,6},{5,7},{6,4},{7,5},{8,10},{9,11},{10,... | collective-permute-start | bytes 1572872 | tf_op jit(solution)/shard_map/ppermute | solution.py:31
  111.2 2.7 copy-start.1
  111.2 2.7 collective-permute-start.11
  129.8 28.9 %collective-permute-start.12 = (f32[32,64,128]{2,1,0:T(8,128)}, f32[32,64,128]{2,1,0:T(8,128)S(1)}, u32[]{:S(2)}, u32[]{:S(2)}) collective-permute-start(f32[32,64,128]{2,1,0:T(8,128)} %get-tuple-element.26), channel_id=1, source_target_pairs={{0,4},{4,0},{8,12},{12,8},{16,20},{20,16},{24,28},{28,24},{1,5},{5... | collective-permute-start | bytes 3145736 | tf_op jit(solution)/shard_map/ppermute | solution.py:31
  129.9 1.2 collective-permute-start.5
  131.2 3.9 collective-permute-start.6
  135.1 12.2 %collective-permute-start.7 = (f32[64,64]{0,1:T(8,128)S(1)}, f32[64,64]{0,1:T(8,128)S(1)}, u32[]{:S(2)}, u32[]{:S(2)}) collective-permute-start(f32[64,64]{0,1:T(8,128)S(1)} %add.154), channel_id=1, source_target_pairs={{0,4},{4,0},{8,12},{12,8},{16,20},{20,16},{24,28},{28,24},{1,5},{5... | collective-permute-start | bytes 49160 | tf_op jit(solution)/shard_map/ppermute | solution.py:31
  147.3 3.9 collective-permute-start.8
  151.2 9.6 %collective-permute-start.9 = (f32[64,64]{0,1:T(8,128)S(1)}, f32[64,64]{0,1:T(8,128)S(1)}, u32[]{:S(2)}, u32[]{:S(2)}) collective-permute-start(f32[64,64]{0,1:T(8,128)S(1)} %add.156), channel_id=1, source_target_pairs={{0,16},{4,20},{8,24},{12,28},{16,0},{20,4},{24,8},{28,12},{1,17},{... | collective-permute-start | bytes 49160 | tf_op jit(solution)/shard_map/ppermute | solution.py:31
  160.1 11.5 %collective-permute-start.13 = (f32[16,64,128]{2,1,0:T(8,128)S(1)}, f32[16,64,128]{2,1,0:T(8,128)S(1)}, u32[]{:S(2)}, u32[]{:S(2)}) collective-permute-start(f32[16,64,128]{2,1,0:T(8,128)S(1)} %get-tuple-element.45), channel_id=1, source_target_pairs={{0,8},{4,12},{8,0},{12,4},{16,24},{20,28},{24,16},{28,20},{1,9},{5... | collective-permute-start | bytes 1572872 | tf_op jit(solution)/shard_map/ppermute | solution.py:31
  171.6 12.0 %collective-permute-start.14 = (f32[8,64,128]{2,1,0:T(8,128)S(1)}, f32[8,64,128]{2,1,0:T(8,128)S(1)}, u32[]{:S(2)}, u32[]{:S(2)}) collective-permute-start(f32[8,64,128]{2,1,0:T(8,128)S(1)} %slice_add_fusion.10), channel_id=1, source_target_pairs={{0,16},{4,20},{8,24},{12,28},{16,0},{20,4},{24,8},{28,12},{1,17},{... | collective-permute-start | bytes 786440 | tf_op jit(solution)/shard_map/ppermute | solution.py:31
  187.4 70.7 %copy-start.9 = (f32[64,64]{1,0:T(8,128)S(1)}, f32[64,64]{1,0:T(8,128)}, u32[]{:S(2)}) copy-start(f32[64,64]{1,0:T(8,128)} %get-tuple-element.27) | copy-start | bytes 49156
  187.4 13.0 %collective-permute-start.20 = (f32[8,64,128]{2,1,0:T(8,128)}, f32[8,64,128]{2,1,0:T(8,128)S(1)}, u32[]{:S(2)}, u32[]{:S(2)}) collective-permute-start(f32[8,64,128]{2,1,0:T(8,128)} %get-tuple-element.28), channel_id=1, source_target_pairs={{0,16},{4,20},{8,24},{12,28},{16,0},{20,4},{24,8},{28,12},{1,17},{... | collective-permute-start | bytes 786440 | tf_op jit(solution)/shard_map/ppermute | solution.py:31
  201.4 13.1 %collective-permute-start.21 = (f32[16,64,128]{2,1,0:T(8,128)S(1)}, f32[16,64,128]{2,1,0:T(8,128)S(1)}, u32[]{:S(2)}, u32[]{:S(2)}) collective-permute-start(f32[16,64,128]{2,1,0:T(8,128)S(1)} %pad_maximum_fusion.2), channel_id=1, source_target_pairs={{0,8},{4,12},{8,0},{12,4},{16,24},{20,28},{24,16},{28,20},{1,9},{5... | collective-permute-start | bytes 1572872 | tf_op jit(solution)/shard_map/ppermute | solution.py:31
  214.6 23.5 %copy-start.3 = (f32[32,64,128]{2,1,0:T(8,128)}, f32[32,64,128]{2,1,0:T(8,128)S(1)}, u32[]{:S(2)}) copy-start(f32[32,64,128]{2,1,0:T(8,128)S(1)} %constant_dynamic-update-slice_fusion.2.low_ref) | copy-start | bytes 3145732
  214.6 23.5 %collective-permute-start.22 = (f32[32,64,128]{2,1,0:T(8,128)S(1)}, f32[32,64,128]{2,1,0:T(8,128)S(1)}, u32[]{:S(2)}, u32[]{:S(2)}) collective-permute-start(f32[32,64,128]{2,1,0:T(8,128)S(1)} %constant_dynamic-update-slice_fusion.2.low_ref), channel_id=1, source_target_pairs={{0,4},{4,0},{8,12},{12,8},{16,20},{20,16},{24,28},{28,24},{1,5},{5... | collective-permute-start | bytes 3145736 | tf_op jit(solution)/shard_map/ppermute | solution.py:31
  258.1 25.5 %collective-permute-start.23 = (f32[32,64,128]{2,1,0:T(8,128)}, f32[32,64,128]{2,1,0:T(8,128)S(1)}, u32[]{:S(2)}, u32[]{:S(2)}) collective-permute-start(f32[32,64,128]{2,1,0:T(8,128)} %get-tuple-element.30), channel_id=1, source_target_pairs={{0,1},{1,0},{2,3},{3,2},{4,5},{5,4},{6,7},{7,6},{8,9},{9,8},{10,11... | collective-permute-start | bytes 3145736 | tf_op jit(solution)/shard_map/ppermute | solution.py:31
  258.2 2.8 collective-permute-start.15
  261.0 3.9 collective-permute-start.16
  264.9 3.9 collective-permute-start.17
  268.9 3.9 collective-permute-start.18
  272.8 4.8 %collective-permute-start.19 = (f32[64,64]{0,1:T(8,128)S(1)}, f32[64,64]{0,1:T(8,128)S(1)}, u32[]{:S(2)}, u32[]{:S(2)}) collective-permute-start(f32[64,64]{0,1:T(8,128)S(1)} %add.166), channel_id=1, source_target_pairs={{0,16},{4,20},{8,24},{12,28},{16,0},{20,4},{24,8},{28,12},{1,17},{... | collective-permute-start | bytes 49160 | tf_op jit(solution)/shard_map/ppermute | solution.py:31
  284.7 9.5 %collective-permute-start.24 = (f32[16,64,128]{2,1,0:T(8,128)S(1)}, f32[16,64,128]{2,1,0:T(8,128)S(1)}, u32[]{:S(2)}, u32[]{:S(2)}) collective-permute-start(f32[16,64,128]{2,1,0:T(8,128)S(1)} %slice_add_fusion.2), channel_id=1, source_target_pairs={{0,2},{1,3},{2,0},{3,1},{4,6},{5,7},{6,4},{7,5},{8,10},{9,11},{10,... | collective-permute-start | bytes 1572872 | tf_op jit(solution)/shard_map/ppermute | solution.py:31
  300.4 28.3 %copy-start.10 = (f32[64,64]{1,0:T(8,128)S(1)}, f32[64,64]{1,0:T(8,128)}, u32[]{:S(2)}) copy-start(f32[64,64]{1,0:T(8,128)} %get-tuple-element.31) | copy-start | bytes 49156
  300.4 9.4 %collective-permute-start.30 = (f32[16,64,128]{2,1,0:T(8,128)}, f32[16,64,128]{2,1,0:T(8,128)S(1)}, u32[]{:S(2)}, u32[]{:S(2)}) collective-permute-start(f32[16,64,128]{2,1,0:T(8,128)} %get-tuple-element.33), channel_id=1, source_target_pairs={{0,2},{1,3},{2,0},{3,1},{4,6},{5,7},{6,4},{7,5},{8,10},{9,11},{10,... | collective-permute-start | bytes 1572872 | tf_op jit(solution)/shard_map/ppermute | solution.py:31
  309.8 2.7 collective-permute-start.31
  328.7 27.4 %collective-permute-start.32 = (f32[32,64,128]{2,1,0:T(8,128)}, f32[32,64,128]{2,1,0:T(8,128)S(1)}, u32[]{:S(2)}, u32[]{:S(2)}) collective-permute-start(f32[32,64,128]{2,1,0:T(8,128)} %get-tuple-element.35), channel_id=1, source_target_pairs={{0,4},{4,0},{8,12},{12,8},{16,20},{20,16},{24,28},{28,24},{1,5},{5... | collective-permute-start | bytes 3145736 | tf_op jit(solution)/shard_map/ppermute | solution.py:31
  328.8 1.2 collective-permute-start.25
  330.1 3.9 collective-permute-start.26
  334.0 15.6 %collective-permute-start.27 = (f32[64,64]{0,1:T(8,128)S(1)}, f32[64,64]{0,1:T(8,128)S(1)}, u32[]{:S(2)}, u32[]{:S(2)}) collective-permute-start(f32[64,64]{0,1:T(8,128)S(1)} %add.172), channel_id=1, source_target_pairs={{0,4},{4,0},{8,12},{12,8},{16,20},{20,16},{24,28},{28,24},{1,5},{5... | collective-permute-start | bytes 49160 | tf_op jit(solution)/shard_map/ppermute | solution.py:31
  349.6 3.9 collective-permute-start.28
  353.5 4.9 %collective-permute-start.29 = (f32[64,64]{0,1:T(8,128)S(1)}, f32[64,64]{0,1:T(8,128)S(1)}, u32[]{:S(2)}, u32[]{:S(2)}) collective-permute-start(f32[64,64]{0,1:T(8,128)S(1)} %add.174), channel_id=1, source_target_pairs={{0,16},{4,20},{8,24},{12,28},{16,0},{20,4},{24,8},{28,12},{1,17},{... | collective-permute-start | bytes 49160 | tf_op jit(solution)/shard_map/ppermute | solution.py:31
  357.4 12.0 %collective-permute-start.33 = (f32[16,64,128]{2,1,0:T(8,128)S(1)}, f32[16,64,128]{2,1,0:T(8,128)S(1)}, u32[]{:S(2)}, u32[]{:S(2)}) collective-permute-start(f32[16,64,128]{2,1,0:T(8,128)S(1)} %get-tuple-element.43), channel_id=1, source_target_pairs={{0,8},{4,12},{8,0},{12,4},{16,24},{20,28},{24,16},{28,20},{1,9},{5... | collective-permute-start | bytes 1572872 | tf_op jit(solution)/shard_map/ppermute | solution.py:31
  369.5 13.1 %collective-permute-start.34 = (f32[8,64,128]{2,1,0:T(8,128)S(1)}, f32[8,64,128]{2,1,0:T(8,128)S(1)}, u32[]{:S(2)}, u32[]{:S(2)}) collective-permute-start(f32[8,64,128]{2,1,0:T(8,128)S(1)} %slice_add_fusion.8), channel_id=1, source_target_pairs={{0,16},{4,20},{8,24},{12,28},{16,0},{20,4},{24,8},{28,12},{1,17},{... | collective-permute-start | bytes 786440 | tf_op jit(solution)/shard_map/ppermute | solution.py:31
  387.1 1.3 collective-permute-start.35
  388.4 3.9 collective-permute-start.36
  392.3 3.9 collective-permute-start.37
  396.2 3.9 collective-permute-start.38
  400.1 4.8 %collective-permute-start.39 = (f32[64,64]{0,1:T(8,128)S(1)}, f32[64,64]{0,1:T(8,128)S(1)}, u32[]{:S(2)}, u32[]{:S(2)}) collective-permute-start(f32[64,64]{0,1:T(8,128)S(1)} %add.184), channel_id=1, source_target_pairs={{0,16},{4,20},{8,24},{12,28},{16,0},{20,4},{24,8},{28,12},{1,17},{... | collective-permute-start | bytes 49160 | tf_op jit(solution)/shard_map/ppermute | solution.py:31
  (5 other events, 6.7 us)

commit v2 on v1

v2 whole, which is shorter than its diff:
```python
import functools

import jax
import jax.numpy as jnp
from jax import lax
from jax.experimental import pallas as pl
from jax.experimental.pallas import tpu as pltpu
from jax.sharding import PartitionSpec as P

K = 64
PARTS = 2
ROWS = K // PARTS
TILE = 128
ITERS = 2
UT = 64
IT = 64
BATCH = 64
UNROLL = 64
HIGHEST = lax.Precision.HIGHEST


def gather_order(axis, part):
    order = []
    bit = lax.axis_size(axis) >> 1
    while bit:
        order.append(bit)
        bit >>= 1
    if axis == "users" and part == 1:
        order[-2:] = order[-2:][::-1]
    return order


def exchange(value, axis, bit):
    return lax.ppermute(value, axis, [(at, at ^ bit) for at in range(lax.axis_size(axis))])


def relative_position(shard, axis, part):
    apart = shard ^ lax.axis_index(axis)
    place = jnp.zeros_like(apart)
    for level, bit in enumerate(gather_order(axis, part)):
        place = place + jnp.where(apart & bit != 0, 1 << level, 0)
    return place


def gather(held, axis):
    levels = len(gather_order(axis, 0))
    for level in range(levels - 1):
        got = [exchange(held[part], axis, gather_order(axis, part)[level]) for part in range(PARTS)]
        held = [
            jnp.concatenate([have[:-1], more[:-1], have[-1:] + more[-1:]], axis=0) for have, more in zip(held, got)
        ]
    got = [exchange(held[part], axis, gather_order(axis, part)[-1]) for part in range(PARTS)]
    return held, got


def reduce_scatter(kept, sent, axis):
    levels = len(gather_order(axis, 0))
    for level in range(levels - 1, 0, -1):
        got = [exchange(sent[part], axis, gather_order(axis, part)[level]) for part in range(PARTS)]
        half = kept[0].shape[0] // 2
        sent = [have[half:] + more[half:] for have, more in zip(kept, got)]
        if level > 1:
            kept = [
                jnp.concatenate([have[:half] + more[:half], out[-1:]], axis=0)
                for have, more, out in zip(kept, got, sent)
            ]
        else:
            kept = [have[:half] + more[:half] for have, more in zip(kept, got)]
    bit = gather_order(axis, 0)[0]
    gram = jnp.concatenate([out[-1] for out in sent], axis=0)
    gram = gram + exchange(gram, axis, bit)
    got = [exchange(out[:-1], axis, bit) for out in sent]
    return [have + more for have, more in zip(kept, got)], gram


def all_sum(value):
    for axis in ("items", "users"):
        for bit in gather_order(axis, 0)[::-1]:
            value = value + exchange(value, axis, bit)
    return value


def part_places(axis, part, blocks):
    swapped = gather_order(axis, part) != gather_order(axis, 0)
    quarter = blocks // 4
    return [at * quarter for at in ((0, 2, 1, 3) if swapped else (0, 1, 2, 3))], quarter


def tiles_kernel(count, source, target, *refs, transposed, places_in, places_out):
    low_refs, high_refs, refs = refs[:PARTS], refs[PARTS : 2 * PARTS], refs[2 * PARTS :]
    tile_ref, keep_refs, send_refs = refs[0], refs[1 : 1 + PARTS], refs[1 + PARTS : 1 + 2 * PARTS]
    pieces, total = refs[1 + 2 * PARTS :]
    step = pl.program_id(0)
    half_in = low_refs[0].shape[0] - 1
    half_out = keep_refs[0].shape[0] - 1

    @pl.when(step == 0)
    def _():
        for part in range(PARTS):
            starts, quarter = places_in[part]
            band = slice(part * ROWS, (part + 1) * ROWS)
            for at, place in enumerate(starts):
                ref = (low_refs, low_refs, high_refs, high_refs)[at][part]
                first = at % 2 * quarter

                def prepare(block, carry):
                    value = ref[first + block]
                    top = value.astype(jnp.bfloat16)
                    pieces[place + block, band, :TILE] = top
                    pieces[place + block, band, TILE:] = (value - top.astype(jnp.float32)).astype(jnp.bfloat16)
                    return carry

                lax.fori_loop(0, quarter, prepare, 0, unroll=4)

        def clear(at, carry):
            total[at] = jnp.zeros((K, TILE), jnp.float32)
            return carry

        lax.fori_loop(0, 2 * half_out, clear, 0, unroll=4)

    live = jnp.clip(count[0] - step * BATCH, 0, BATCH)
    contract = 1 if transposed else 0

    def group(at, carry):
        first = at * UNROLL
        products = []
        for slot in range(UNROLL):
            tile = tile_ref[first + slot]
            products.append(
                lax.dot_general(
                    pieces[source[step * BATCH + first + slot]],
                    jnp.concatenate([tile, tile], axis=contract),
                    (((1,), (contract,)), ((), ())),
                    preferred_element_type=jnp.float32,
                )
            )
        for slot in range(UNROLL):
            total[target[step * BATCH + first + slot]] += products[slot]
        return carry

    lax.fori_loop(0, (live + UNROLL - 1) // UNROLL, group, 0)

    @pl.when(step == pl.num_programs(0) - 1)
    def _():
        for part in range(PARTS):
            starts, quarter = places_out[part]
            band = slice(part * ROWS, (part + 1) * ROWS)
            for at, place in enumerate(starts):
                ref = (keep_refs, keep_refs, send_refs, send_refs)[at][part]
                first = at % 2 * quarter

                def finish(block, carry):
                    ref[first + block] = total[place + block, band]
                    return carry

                lax.fori_loop(0, quarter, finish, 0, unroll=4)
            gram = low_refs[part][half_in] + high_refs[part][half_in]
            keep_refs[part][half_out] = gram
            send_refs[part][half_out] = gram


def tiles_product(count, source, target, low, high, tiles, blocks_out, axis_in, axis_out, transposed):
    half_in = low[0].shape[0] - 1
    half_out = blocks_out // 2
    whole = lambda step, *refs: (0, 0, 0)

    def tile_block(step, count, source, target):
        return (jnp.minimum(step, (count[0] + BATCH - 1) // BATCH - 1), 0, 0)

    kernel = functools.partial(
        tiles_kernel,
        transposed=transposed,
        places_in=[part_places(axis_in, part, 2 * half_in) for part in range(PARTS)],
        places_out=[part_places(axis_out, part, 2 * half_out) for part in range(PARTS)],
    )
    out = pl.pallas_call(
        kernel,
        out_shape=[jax.ShapeDtypeStruct((half_out + 1, ROWS, TILE), jnp.float32)] * (2 * PARTS),
        grid_spec=pltpu.PrefetchScalarGridSpec(
            num_scalar_prefetch=3,
            grid=(tiles.shape[0] // BATCH,),
            in_specs=[pl.BlockSpec((half_in + 1, ROWS, TILE), whole)] * (2 * PARTS)
            + [pl.BlockSpec((BATCH, TILE, TILE), tile_block)],
            out_specs=[pl.BlockSpec((half_out + 1, ROWS, TILE), whole)] * (2 * PARTS),
            scratch_shapes=[
                pltpu.VMEM((2 * half_in, K, 2 * TILE), jnp.bfloat16),
                pltpu.VMEM((2 * half_out + 1, K, TILE), jnp.float32),
            ],
        ),
        name="user_tiles" if transposed else "item_tiles",
    )(count, source, target, *low, *high, tiles)
    return out[:PARTS], out[PARTS:]


def dot_full(left, right, contract):
    return lax.dot_general(
        left, right, ((contract[:1], contract[1:]), ((), ())), precision=HIGHEST, preferred_element_type=jnp.float32
    )


def factor_kernel(gram_ref, out_ref, *, total):
    row = lax.broadcasted_iota(jnp.int32, (K, K), 0)
    col = lax.broadcasted_iota(jnp.int32, (K, K), 1)
    work = jnp.concatenate([gram_ref[:, :K] * (1.0 / total), (row == col).astype(jnp.float32)], axis=1)
    below = lax.broadcasted_iota(jnp.int32, (K, 1), 0)
    for at in range(K):
        pivot_row = work[at : at + 1, :]
        factor = work[:, at : at + 1] / pivot_row[:, at : at + 1]
        work = work - jnp.where(below > at, factor, 0.0) * pivot_row
    pivots = jnp.sum(jnp.where(row == col, work[:, :K], 0.0), axis=1, keepdims=True)
    out_ref[...] = work[:, K:] * lax.rsqrt(pivots)


def inverse_factor(gram, total):
    return pl.pallas_call(
        functools.partial(factor_kernel, total=total),
        out_shape=jax.ShapeDtypeStruct((K, K), jnp.float32),
        name="factor",
    )(gram)


def scale_kernel(*refs, factored):
    refs = list(refs)
    inverse = refs.pop(0)[...] if factored else None
    raw_refs, refs = refs[:PARTS], refs[PARTS:]
    scale_ref, panel_ref, sent_refs = refs[0], refs[1], refs[2:]
    blocks = scale_ref.shape[0]
    gram = jnp.zeros((K, K), jnp.float32)
    for at in range(blocks):
        scale = scale_ref[at][None, :]
        panel = jnp.concatenate([ref[at] for ref in raw_refs], axis=0)
        if factored:
            panel = dot_full(inverse, panel, (1, 0))
        panel = scale * panel
        panel_ref[at] = panel
        for part in range(PARTS):
            sent_refs[part][at] = scale * panel[part * ROWS : (part + 1) * ROWS]
        gram = gram + dot_full(panel, panel, (1, 1))
    gram = jnp.concatenate([gram, jnp.zeros((K, TILE - K), jnp.float32)], axis=1)
    for part in range(PARTS):
        sent_refs[part][blocks] = gram[part * ROWS : (part + 1) * ROWS]


def scale_panel(inverse, raws, scale):
    factored = inverse is not None
    operands = ([inverse] if factored else []) + list(raws) + [scale]
    blocks = scale.shape[0]
    panel, *sent = pl.pallas_call(
        functools.partial(scale_kernel, factored=factored),
        out_shape=[jax.ShapeDtypeStruct((blocks, K, TILE), jnp.float32)]
        + [jax.ShapeDtypeStruct((blocks + 1, ROWS, TILE), jnp.float32)] * PARTS,
        name="scale_panel",
    )(*operands)
    return panel, sent


def finish_kernel(inverse_ref, panel_ref, out_ref):
    for at in range(panel_ref.shape[0]):
        out_ref[:, at * TILE : (at + 1) * TILE] = dot_full(inverse_ref[...], panel_ref[at], (1, 0))


def finish_panel(inverse, panel):
    return pl.pallas_call(
        finish_kernel,
        out_shape=jax.ShapeDtypeStruct((K, panel.shape[0] * TILE), jnp.float32),
        name="finish_panel",
    )(inverse, panel)


def body(tile_rows, tile_cols, tile_count, tile_vals, user_degree, item_degree, start_items):
    user_groups = lax.axis_size("users")
    item_groups = lax.axis_size("items")
    user_blocks = UT // item_groups
    item_blocks = IT // user_groups
    user_total = UT * TILE * user_groups
    item_total = IT * TILE * item_groups

    rows = tile_rows[0, 0]
    cols = tile_cols[0, 0]
    tiles = tile_vals[0, 0]
    count = tile_count[0]
    live = jnp.arange(rows.shape[0], dtype=jnp.int32) < count[0]
    row_at = relative_position(rows // user_blocks, "items", 0) * user_blocks + rows % user_blocks
    col_at = relative_position(cols // item_blocks, "users", 0) * item_blocks + cols % item_blocks
    row_to = jnp.where(live, row_at, UT)
    col_to = jnp.where(live, col_at, IT)

    user_scale = lax.rsqrt(user_degree.astype(jnp.float32)).reshape(user_blocks, TILE)
    item_scale = lax.rsqrt(item_degree.astype(jnp.float32)).reshape(item_blocks, TILE)
    start = start_items.astype(jnp.float32).reshape(PARTS, ROWS, item_blocks, TILE).transpose(0, 2, 1, 3)
    start = item_scale[None, :, None, :] * start
    start = jnp.concatenate([start, jnp.zeros_like(start[:, :1])], axis=1)
    sent = [start[part] for part in range(PARTS)]

    item_inverse = None
    for step in range(ITERS):
        low, high = gather(sent, "users")
        kept, out = tiles_product(count, col_at, row_to, low, high, tiles, UT, "users", "items", True)
        raws, gram = reduce_scatter(kept, out, "items")
        if step:
            item_inverse = inverse_factor(gram, item_total)
        user_raw, sent = scale_panel(item_inverse, raws, user_scale)
        low, high = gather(sent, "items")
        kept, out = tiles_product(count, row_at, col_to, low, high, tiles, IT, "items", "users", False)
        raws, gram = reduce_scatter(kept, out, "users")
        user_inverse = inverse_factor(gram, user_total)
        item_raw, sent = scale_panel(user_inverse, raws, item_scale)
    gram = all_sum(jnp.concatenate([part[-1] for part in sent], axis=0))
    return finish_panel(user_inverse, user_raw), finish_panel(inverse_factor(gram, item_total), item_raw)


def solution(mesh):
    in_specs = (
        P("users", "items", None),
        P("users", "items", None),
        P("users", "items"),
        P("users", "items", None, None, None),
        P(("users", "items")),
        P(("items", "users")),
        P(None, ("items", "users")),
    )
    out_specs = (P(None, ("users", "items")), P(None, ("items", "users")))
    return jax.shard_map(body, mesh=mesh, in_specs=in_specs, out_specs=out_specs, check_vma=False)
```

time: 422 us -> 347 us (0.82)
  waiting for transfers between devices: 228 us -> 128 us
  starting transfers between devices: 29.7 us -> 80.3 us
  other arithmetic: 63.4 us -> 30.5 us
  local copies, waits for them, and re-layouts: 8.66 us -> 12.9 us
    ppermute x40 -> x48, waiting for transfers between devices: 228 us -> 128 us  [exchange(): lax.ppermute(value, axis, [(at, at ^ bit) for at in range(lax.axis_size(a...]
    ppermute x40 -> x48, starting transfers between devices: 29.7 us -> 80.3 us  [exchange(): lax.ppermute(value, axis, [(at, at ^ bit) for at in range(lax.axis_size(a...]
    another operation x20 -> x0, other arithmetic: 48.3 us -> none  [the longest x12 26.1 us: inverse_factor(): lower = jnp.linalg.cholesky(gram / total)]
    add x10 -> x37, other arithmetic: 10.3 us -> 25.9 us  [the longest x8 9.54 us: reduce_scatter(): return ([have + more for have, more in zip(kept, got)], gram)]
    slice x0 -> x33, local copies, waits for them, and re-layouts: none -> 8.08 us  [the longest x7 5.82 us: gather(): have[:-1]]
    pallas_call x8 -> x12, Pallas kernels: 81 us -> 83.1 us  [the longest x4 42.4 us: tiles_product(): pl.pallas_call(kernel, out_shape=[jax.ShapeDtypeStruct((half_out + 1, ROW...]
  transfers between devices with their start and end apart: 40 -> 48, of which waited for: 37 -> 33; matrix products, arithmetic and copies ran while one was open for 11% -> 9% of each run, Pallas kernels for 1% -> 7%
where the time goes in v2:
time: 347 us; the launch traced here: 341 us
  waiting for transfers between devices  128 us (37%)
  Pallas kernels  87.6 us (25%)
  starting transfers between devices  80.3 us (23%)
  other arithmetic  30.5 us (9%)
  local copies, waits for them, and re-layouts  12.9 us (4%)
    ppermute x48, waiting for transfers between devices, exchange(): lax.ppermute(value, axis, [(at, at ^ bit) for at in range(lax.axis_size(a...  128 us
    ppermute x48, starting transfers between devices, exchange(): lax.ppermute(value, axis, [(at, at ^ bit) for at in range(lax.axis_size(a...  80.3 us
    pallas_call x4, Pallas kernels, tiles_product(): pl.pallas_call(kernel, out_shape=[jax.ShapeDtypeStruct((half_out + 1, ROW...  42.4 us
    pallas_call x4, Pallas kernels, inverse_factor(): pl.pallas_call(functools.partial(factor_kernel, total=total), out_shape=j...  27.3 us
    pallas_call x4, Pallas kernels, scale_panel(): pl.pallas_call(functools.partial(scale_kernel, factored=factored), out_sh...  13.4 us
    add x8, other arithmetic, reduce_scatter(): return ([have + more for have, more in zip(kept, got)], gram)  9.54 us
  transfers between devices with their start and end apart: 48, of which 33 were waited for; matrix products, arithmetic and copies ran while one was open for 9% of the time, Pallas kernels for 7%

profile of v2, /device:TPU:0, one launch (start us, length us, event | category | flops | bytes accessed | tf_op | source)
XLA Modules:
  0.0 341.5 jit_solution(15117496306084674584)
XLA Ops:
  2.4 4.1 %collective-permute-start = (f32[9,32,128]{2,1,0:T(8,128)S(1)}, f32[9,32,128]{2,1,0:T(8,128)S(1)}, u32[]{:S(2)}, u32[]{:S(2)}) collective-permute-start(f32[9,32,128]{2,1,0:T(8,128)S(1)} %get-tuple-element.61), channel_id=1, source_target_pairs={{0,16},{4,20},{8,24},{12,28},{16,0},{20,4},{24,8},{28,12},{1,17},{... | collective-permute-start | bytes 442376 | tf_op jit(solution)/shard_map/ppermute | solution.py:34
  6.6 7.0 %collective-permute-done = f32[9,32,128]{2,1,0:T(8,128)S(1)} collective-permute-done((f32[9,32,128]{2,1,0:T(8,128)S(1)}, f32[9,32,128]{2,1,0:T(8,128)S(1)}, u32[]{:S(2)}, u32[]{:S(2)}) %collective-permute-start) | collective-permute-done | bytes 147488 | tf_op jit(solution)/shard_map/ppermute | solution.py:34
  14.4 3.4 collective-permute-start.2
  17.7 5.9 %collective-permute-done.2 = f32[9,32,128]{2,1,0:T(8,128)S(1)} collective-permute-done((f32[9,32,128]{2,1,0:T(8,128)S(1)}, f32[9,32,128]{2,1,0:T(8,128)S(1)}, u32[]{:S(2)}, u32[]{:S(2)}) %collective-permute-start.2) | collective-permute-done | bytes 147488 | tf_op jit(solution)/shard_map/ppermute | solution.py:34
  26.1 7.1 %collective-permute-done.3 = f32[17,32,128]{2,1,0:T(8,128)S(1)} collective-permute-done((f32[17,32,128]{2,1,0:T(8,128)S(1)}, f32[17,32,128]{2,1,0:T(8,128)S(1)}, u32[]{:S(2)}, u32[]{:S(2)}) %collective-permute-start.3) | collective-permute-done | bytes 278560 | tf_op jit(solution)/shard_map/ppermute | solution.py:34
  33.3 4.2 %collective-permute-start.5 = (f32[33,32,128]{2,1,0:T(8,128)S(1)}, f32[33,32,128]{2,1,0:T(8,128)S(1)}, u32[]{:S(2)}, u32[]{:S(2)}) collective-permute-start(f32[33,32,128]{2,1,0:T(8,128)S(1)} %pad_maximum_fusion.1.refs_1_), channel_id=1, source_target_pairs={{0,8},{4,12},{8,0},{12,4},{16,24},{20,28},{24,16},{28,20},{1,9},{5... | collective-permute-start | bytes 1622024 | tf_op jit(solution)/shard_map/ppermute | solution.py:34
  39.5 3.5 %collective-permute-done.4.refs_2_ = f32[33,32,128]{2,1,0:T(8,128)S(1)} collective-permute-done((f32[33,32,128]{2,1,0:T(8,128)S(1)}, f32[33,32,128]{2,1,0:T(8,128)S(1)}, u32[]{:S(2)}, u32[]{:S(2)}) %collective-permute-start.4) | collective-permute-done | bytes 540704 | tf_op jit(solution)/shard_map/ppermute | solution.py:34
  43.0 4.0 %collective-permute-done.5.refs_3_ = f32[33,32,128]{2,1,0:T(8,128)S(1)} collective-permute-done((f32[33,32,128]{2,1,0:T(8,128)S(1)}, f32[33,32,128]{2,1,0:T(8,128)S(1)}, u32[]{:S(2)}, u32[]{:S(2)}) %collective-permute-start.5) | collective-permute-done | bytes 540704 | tf_op jit(solution)/shard_map/ppermute | solution.py:34
  47.8 11.8 %user_tiles.2 = (f32[33,32,128]{2,1,0:T(8,128)}, f32[33,32,128]{2,1,0:T(8,128)}, f32[33,32,128]{2,1,0:T(8,128)}, f32[33,32,128]{2,1,0:T(8,128)}) custom-call(s32[1]{0:T(128)} %bitcast.39.count, s32[512]{0:T(512)} %get-tuple-element.63.source, s32[512]{0:T(512)} %get-tuple-element.54.target, f32[33,32,128]{2,1,0:T(8,128)} %copy-done, ...), custom_call_target="tpu_custom_call" | custom-call | tf_op jit(solution)/shard_map/user_tiles/pallas_call | solution.py:176
  65.0 6.4 %collective-permute-done.7 = f32[16,32,128]{2,1,0:T(8,128)S(1)} collective-permute-done((f32[16,32,128]{2,1,0:T(8,128)S(1)}, f32[16,32,128]{2,1,0:T(8,128)S(1)}, u32[]{:S(2)}, u32[]{:S(2)}) %collective-permute-start.7) | collective-permute-done | bytes 262176 | tf_op jit(solution)/shard_map/ppermute | solution.py:34
  73.1 2.9 collective-permute-done.9
  77.8 2.8 scale_panel.4
  84.6 5.7 %collective-permute-done.11 = f32[17,32,128]{2,1,0:T(8,128)S(1)} collective-permute-done((f32[17,32,128]{2,1,0:T(8,128)}, f32[17,32,128]{2,1,0:T(8,128)S(1)}, u32[]{:S(2)}, u32[]{:S(2)}) %collective-permute-start.11) | collective-permute-done | bytes 278560 | tf_op jit(solution)/shard_map/ppermute | solution.py:34
  91.2 3.3 collective-permute-done.10
  98.1 9.4 %item_tiles.2 = (f32[33,32,128]{2,1,0:T(8,128)}, f32[33,32,128]{2,1,0:T(8,128)}, f32[33,32,128]{2,1,0:T(8,128)}, f32[33,32,128]{2,1,0:T(8,128)}) custom-call(s32[1]{0:T(128)} %bitcast.40.count, s32[512]{0:T(512)} %get-tuple-element.55.source, s32[512]{0:T(512)} %get-tuple-element.62.target, f32[33,32,128]{2,1,0:T(8,128)} %copy-done.7, ...), custom_call_target="tpu_custom_call" | custom-call | tf_op jit(solution)/shard_map/item_tiles/pallas_call | solution.py:176
  107.4 7.5 %collective-permute-start.14 = (f32[33,32,128]{2,1,0:T(8,128)}, f32[33,32,128]{2,1,0:T(8,128)S(1)}, u32[]{:S(2)}, u32[]{:S(2)}) collective-permute-start(f32[33,32,128]{2,1,0:T(8,128)} %get-tuple-element.35), channel_id=1, source_target_pairs={{0,4},{4,0},{8,12},{12,8},{16,20},{20,16},{24,28},{28,24},{1,5},{5... | collective-permute-start | bytes 1622024 | tf_op jit(solution)/shard_map/ppermute | solution.py:34
  114.9 5.0 %collective-permute-done.16 = f32[33,32,128]{2,1,0:T(8,128)S(1)} collective-permute-done((f32[33,32,128]{2,1,0:T(8,128)}, f32[33,32,128]{2,1,0:T(8,128)S(1)}, u32[]{:S(2)}, u32[]{:S(2)}) %collective-permute-start.16) | collective-permute-done | bytes 540704 | tf_op jit(solution)/shard_map/ppermute | solution.py:34
  120.9 4.3 %collective-permute-start.17 = (f32[17,32,128]{2,1,0:T(8,128)S(1)}, f32[17,32,128]{2,1,0:T(8,128)S(1)}, u32[]{:S(2)}, u32[]{:S(2)}) collective-permute-start(f32[17,32,128]{2,1,0:T(8,128)S(1)} %slice_add_fusion.4), channel_id=1, source_target_pairs={{0,4},{4,0},{8,12},{12,8},{16,20},{20,16},{24,28},{28,24},{1,5},{5... | collective-permute-start | bytes 835592 | tf_op jit(solution)/shard_map/ppermute | solution.py:34
  126.2 2.4 collective-permute-start.15
  130.6 2.6 collective-permute-done.15
  133.3 5.7 %collective-permute-start.18 = (f32[64,128]{1,0:T(8,128)S(1)}, f32[64,128]{1,0:T(8,128)S(1)}, u32[]{:S(2)}, u32[]{:S(2)}) collective-permute-start(f32[64,128]{1,0:T(8,128)S(1)} %pad_maximum_fusion.16), channel_id=1, source_target_pairs={{0,16},{4,20},{8,24},{12,28},{16,0},{20,4},{24,8},{28,12},{1,17},{... | collective-permute-start | bytes 98312 | tf_op jit(solution)/shard_map/ppermute | solution.py:34
  139.1 2.9 collective-permute-start.20
  143.8 6.8 %factor.4.refs_0_ = f32[64,64]{1,0:T(8,128)} custom-call(f32[64,128]{1,0:T(8,128)} %fusion.24.gram_ref), custom_call_target="tpu_custom_call" | custom-call | tf_op jit(solution)/shard_map/factor/pallas_call | solution.py:215
  153.3 3.1 scale_panel.5
  158.3 3.0 collective-permute-start.21
  161.2 8.2 %collective-permute-done.23 = f32[9,32,128]{2,1,0:T(8,128)S(1)} collective-permute-done((f32[9,32,128]{2,1,0:T(8,128)}, f32[9,32,128]{2,1,0:T(8,128)S(1)}, u32[]{:S(2)}, u32[]{:S(2)}) %collective-permute-start.23) | collective-permute-done | bytes 147488 | tf_op jit(solution)/shard_map/ppermute | solution.py:34
  173.1 6.5 %collective-permute-done.24 = f32[17,32,128]{2,1,0:T(8,128)S(1)} collective-permute-done((f32[17,32,128]{2,1,0:T(8,128)S(1)}, f32[17,32,128]{2,1,0:T(8,128)S(1)}, u32[]{:S(2)}, u32[]{:S(2)}) %collective-permute-start.24) | collective-permute-done | bytes 278560 | tf_op jit(solution)/shard_map/ppermute | solution.py:34
  182.7 11.0 %collective-permute-done.26.refs_3_ = f32[33,32,128]{2,1,0:T(8,128)S(1)} collective-permute-done((f32[33,32,128]{2,1,0:T(8,128)S(1)}, f32[33,32,128]{2,1,0:T(8,128)S(1)}, u32[]{:S(2)}, u32[]{:S(2)}) %collective-permute-start.26) | collective-permute-done | bytes 540704 | tf_op jit(solution)/shard_map/ppermute | solution.py:34
  196.4 11.9 %user_tiles.3 = (f32[33,32,128]{2,1,0:T(8,128)}, f32[33,32,128]{2,1,0:T(8,128)}, f32[33,32,128]{2,1,0:T(8,128)}, f32[33,32,128]{2,1,0:T(8,128)}) custom-call(s32[1]{0:T(128)} %bitcast.41.count, s32[512]{0:T(512)} %get-tuple-element.63.source, s32[512]{0:T(512)} %get-tuple-element.54.target, f32[33,32,128]{2,1,0:T(8,128)} %copy-done.5, ...), custom_call_target="tpu_custom_call" | custom-call | tf_op jit(solution)/shard_map/user_tiles/pallas_call | solution.py:176
  214.7 6.6 %collective-permute-done.29 = f32[64,128]{1,0:T(8,128)S(1)} collective-permute-done((f32[64,128]{1,0:T(8,128)S(1)}, f32[64,128]{1,0:T(8,128)S(1)}, u32[]{:S(2)}, u32[]{:S(2)}) %collective-permute-start.29) | collective-permute-done | bytes 32800 | tf_op jit(solution)/shard_map/ppermute | solution.py:34
  222.0 6.8 %factor.5.refs_0_ = f32[64,64]{1,0:T(8,128)} custom-call(f32[64,128]{1,0:T(8,128)} %fusion.23.gram_ref), custom_call_target="tpu_custom_call" | custom-call | tf_op jit(solution)/shard_map/factor/pallas_call | solution.py:215
  232.2 4.4 %scale_panel.6 = (f32[16,64,128]{2,1,0:T(8,128)}, f32[17,32,128]{2,1,0:T(8,128)}, f32[17,32,128]{2,1,0:T(8,128)}) custom-call(f32[64,64]{1,0:T(8,128)} %factor.5.refs_0_, f32[16,32,128]{2,1,0:T(8,128)} %fusion.1.refs_1_, f32[16,32,128]{2,1,0:T(8,128)} %fusion.refs_2_, f32[16,128]{1,0:T(8,128)} %rsqrt_bitcast_fusion.refs_2_.refs_3_), custom_call_target="tpu_custom_call" | custom-call | tf_op jit(solution)/shard_map/scale_panel/pallas_call | solution.py:248
  240.7 5.7 %collective-permute-done.33 = f32[17,32,128]{2,1,0:T(8,128)S(1)} collective-permute-done((f32[17,32,128]{2,1,0:T(8,128)}, f32[17,32,128]{2,1,0:T(8,128)S(1)}, u32[]{:S(2)}, u32[]{:S(2)}) %collective-permute-start.33) | collective-permute-done | bytes 278560 | tf_op jit(solution)/shard_map/ppermute | solution.py:34
  247.3 2.6 collective-permute-done.32
  253.4 9.4 %item_tiles.3 = (f32[33,32,128]{2,1,0:T(8,128)}, f32[33,32,128]{2,1,0:T(8,128)}, f32[33,32,128]{2,1,0:T(8,128)}, f32[33,32,128]{2,1,0:T(8,128)}) custom-call(s32[1]{0:T(128)} %bitcast.42.count, s32[512]{0:T(512)} %get-tuple-element.55.source, s32[512]{0:T(512)} %get-tuple-element.62.target, f32[33,32,128]{2,1,0:T(8,128)} %copy-done.6, ...), custom_call_target="tpu_custom_call" | custom-call | tf_op jit(solution)/shard_map/item_tiles/pallas_call | solution.py:176
  262.8 6.9 %collective-permute-start.36 = (f32[33,32,128]{2,1,0:T(8,128)}, f32[33,32,128]{2,1,0:T(8,128)S(1)}, u32[]{:S(2)}, u32[]{:S(2)}) collective-permute-start(f32[33,32,128]{2,1,0:T(8,128)} %get-tuple-element.47), channel_id=1, source_target_pairs={{0,4},{4,0},{8,12},{12,8},{16,20},{20,16},{24,28},{28,24},{1,5},{5... | collective-permute-start | bytes 1622024 | tf_op jit(solution)/shard_map/ppermute | solution.py:34
  269.7 5.3 %collective-permute-done.38 = f32[33,32,128]{2,1,0:T(8,128)S(1)} collective-permute-done((f32[33,32,128]{2,1,0:T(8,128)}, f32[33,32,128]{2,1,0:T(8,128)S(1)}, u32[]{:S(2)}, u32[]{:S(2)}) %collective-permute-start.38) | collective-permute-done | bytes 540704 | tf_op jit(solution)/shard_map/ppermute | solution.py:34
  276.0 3.5 %collective-permute-start.39 = (f32[17,32,128]{2,1,0:T(8,128)S(1)}, f32[17,32,128]{2,1,0:T(8,128)S(1)}, u32[]{:S(2)}, u32[]{:S(2)}) collective-permute-start(f32[17,32,128]{2,1,0:T(8,128)S(1)} %slice_add_fusion), channel_id=1, source_target_pairs={{0,4},{4,0},{8,12},{12,8},{16,20},{20,16},{24,28},{28,24},{1,5},{5... | collective-permute-start | bytes 835592 | tf_op jit(solution)/shard_map/ppermute | solution.py:34
  280.6 2.4 collective-permute-start.37
  285.0 2.5 collective-permute-done.37
  287.6 5.2 %collective-permute-start.40 = (f32[64,128]{1,0:T(8,128)S(1)}, f32[64,128]{1,0:T(8,128)S(1)}, u32[]{:S(2)}, u32[]{:S(2)}) collective-permute-start(f32[64,128]{1,0:T(8,128)S(1)} %pad_maximum_fusion.18), channel_id=1, source_target_pairs={{0,16},{4,20},{8,24},{12,28},{16,0},{20,4},{24,8},{28,12},{1,17},{... | collective-permute-start | bytes 98312 | tf_op jit(solution)/shard_map/ppermute | solution.py:34
  293.0 2.9 collective-permute-start.42
  296.5 6.8 %factor.6.inverse_ref.refs_0_ = f32[64,64]{1,0:T(8,128)} custom-call(f32[64,128]{1,0:T(8,128)} %fusion.22.gram_ref), custom_call_target="tpu_custom_call" | custom-call | tf_op jit(solution)/shard_map/factor/pallas_call | solution.py:215
  307.9 3.1 scale_panel.7
  313.7 3.9 %collective-permute-done.44 = f32[64,128]{1,0:T(8,128)S(1)} collective-permute-done((f32[64,128]{1,0:T(8,128)S(1)}, f32[64,128]{1,0:T(8,128)S(1)}, u32[]{:S(2)}, u32[]{:S(2)}) %collective-permute-start.44) | collective-permute-done | bytes 32800 | tf_op jit(solution)/shard_map/ppermute | solution.py:34
  325.5 4.1 %collective-permute-start.47 = (f32[64,128]{1,0:T(8,128)S(1)}, f32[64,128]{1,0:T(8,128)S(1)}, u32[]{:S(2)}, u32[]{:S(2)}) collective-permute-start(f32[64,128]{1,0:T(8,128)S(1)} %add.236), channel_id=1, source_target_pairs={{0,16},{4,20},{8,24},{12,28},{16,0},{20,4},{24,8},{28,12},{1,17},{... | collective-permute-start | bytes 98312 | tf_op jit(solution)/shard_map/ppermute | solution.py:34
  329.6 2.4 finish_panel.2
  332.6 6.8 %factor.7.inverse_ref = f32[64,64]{1,0:T(8,128)} custom-call(f32[64,128]{1,0:T(8,128)} %add.237.gram_ref), custom_call_target="tpu_custom_call" | custom-call | tf_op jit(solution)/shard_map/factor/pallas_call | solution.py:215
  (204 shorter events, 85.6 us)
Async XLA Ops:
  2.4 11.1 %collective-permute-start = (f32[9,32,128]{2,1,0:T(8,128)S(1)}, f32[9,32,128]{2,1,0:T(8,128)S(1)}, u32[]{:S(2)}, u32[]{:S(2)}) collective-permute-start(f32[9,32,128]{2,1,0:T(8,128)S(1)} %get-tuple-element.61), channel_id=1, source_target_pairs={{0,16},{4,20},{8,24},{12,28},{16,0},{20,4},{24,8},{28,12},{1,17},{... | collective-permute-start | bytes 442376 | tf_op jit(solution)/shard_map/ppermute | solution.py:34
  13.6 11.7 %collective-permute-start.1 = (f32[17,32,128]{2,1,0:T(8,128)S(1)}, f32[17,32,128]{2,1,0:T(8,128)S(1)}, u32[]{:S(2)}, u32[]{:S(2)}) collective-permute-start(f32[17,32,128]{2,1,0:T(8,128)S(1)} %pad_maximum_fusion.8), channel_id=1, source_target_pairs={{0,8},{4,12},{8,0},{12,4},{16,24},{20,28},{24,16},{28,20},{1,9},{5... | collective-permute-start | bytes 835592 | tf_op jit(solution)/shard_map/ppermute | solution.py:34
  14.4 9.3 %collective-permute-start.2 = (f32[9,32,128]{2,1,0:T(8,128)S(1)}, f32[9,32,128]{2,1,0:T(8,128)S(1)}, u32[]{:S(2)}, u32[]{:S(2)}) collective-permute-start(f32[9,32,128]{2,1,0:T(8,128)S(1)} %get-tuple-element.60), channel_id=1, source_target_pairs={{0,16},{4,20},{8,24},{12,28},{16,0},{20,4},{24,8},{28,12},{1,17},{... | collective-permute-start | bytes 442376 | tf_op jit(solution)/shard_map/ppermute | solution.py:34
  23.6 9.6 %collective-permute-start.3 = (f32[17,32,128]{2,1,0:T(8,128)S(1)}, f32[17,32,128]{2,1,0:T(8,128)S(1)}, u32[]{:S(2)}, u32[]{:S(2)}) collective-permute-start(f32[17,32,128]{2,1,0:T(8,128)S(1)} %pad_maximum_fusion.9), channel_id=1, source_target_pairs={{0,4},{4,0},{8,12},{12,8},{16,20},{20,16},{24,28},{28,24},{1,5},{5... | collective-permute-start | bytes 835592 | tf_op jit(solution)/shard_map/ppermute | solution.py:34
  25.4 17.7 %collective-permute-start.4 = (f32[33,32,128]{2,1,0:T(8,128)S(1)}, f32[33,32,128]{2,1,0:T(8,128)S(1)}, u32[]{:S(2)}, u32[]{:S(2)}) collective-permute-start(f32[33,32,128]{2,1,0:T(8,128)S(1)} %pad_maximum_fusion.refs_0_), channel_id=1, source_target_pairs={{0,4},{4,0},{8,12},{12,8},{16,20},{20,16},{24,28},{28,24},{1,5},{5... | collective-permute-start | bytes 1622024 | tf_op jit(solution)/shard_map/ppermute | solution.py:34
  33.3 13.7 %collective-permute-start.5 = (f32[33,32,128]{2,1,0:T(8,128)S(1)}, f32[33,32,128]{2,1,0:T(8,128)S(1)}, u32[]{:S(2)}, u32[]{:S(2)}) collective-permute-start(f32[33,32,128]{2,1,0:T(8,128)S(1)} %pad_maximum_fusion.1.refs_1_), channel_id=1, source_target_pairs={{0,8},{4,12},{8,0},{12,4},{16,24},{20,28},{24,16},{28,20},{1,9},{5... | collective-permute-start | bytes 1622024 | tf_op jit(solution)/shard_map/ppermute | solution.py:34
  59.6 2.5 collective-permute-start.6
  59.6 4.1 %collective-permute-start.8 = (f32[33,32,128]{2,1,0:T(8,128)}, f32[33,32,128]{2,1,0:T(8,128)S(1)}, u32[]{:S(2)}, u32[]{:S(2)}) collective-permute-start(f32[33,32,128]{2,1,0:T(8,128)} %get-tuple-element.31), channel_id=1, source_target_pairs={{0,1},{1,0},{2,3},{3,2},{4,5},{5,4},{6,7},{7,6},{8,9},{9,8},{10,11... | collective-permute-start | bytes 1622024 | tf_op jit(solution)/shard_map/ppermute | solution.py:34
  62.2 9.2 %collective-permute-start.7 = (f32[16,32,128]{2,1,0:T(8,128)S(1)}, f32[16,32,128]{2,1,0:T(8,128)S(1)}, u32[]{:S(2)}, u32[]{:S(2)}) collective-permute-start(f32[16,32,128]{2,1,0:T(8,128)S(1)} %slice_add_fusion.14), channel_id=1, source_target_pairs={{0,2},{1,3},{2,0},{3,1},{4,6},{5,7},{6,4},{7,5},{8,10},{9,11},{10,... | collective-permute-start | bytes 786440 | tf_op jit(solution)/shard_map/ppermute | solution.py:34
  63.8 12.3 %collective-permute-start.9 = (f32[16,32,128]{2,1,0:T(8,128)S(1)}, f32[16,32,128]{2,1,0:T(8,128)S(1)}, u32[]{:S(2)}, u32[]{:S(2)}) collective-permute-start(f32[16,32,128]{2,1,0:T(8,128)S(1)} %slice_add_fusion.12), channel_id=1, source_target_pairs={{0,2},{1,3},{2,0},{3,1},{4,6},{5,7},{6,4},{7,5},{8,10},{9,11},{10,... | collective-permute-start | bytes 786440 | tf_op jit(solution)/shard_map/ppermute | solution.py:34
  80.6 9.7 %collective-permute-start.11 = (f32[17,32,128]{2,1,0:T(8,128)}, f32[17,32,128]{2,1,0:T(8,128)S(1)}, u32[]{:S(2)}, u32[]{:S(2)}) collective-permute-start(f32[17,32,128]{2,1,0:T(8,128)} %get-tuple-element.33), channel_id=1, source_target_pairs={{0,2},{1,3},{2,0},{3,1},{4,6},{5,7},{6,4},{7,5},{8,10},{9,11},{10,... | collective-permute-start | bytes 835592 | tf_op jit(solution)/shard_map/ppermute | solution.py:34
  84.0 10.4 %collective-permute-start.10 = (f32[17,32,128]{2,1,0:T(8,128)}, f32[17,32,128]{2,1,0:T(8,128)S(1)}, u32[]{:S(2)}, u32[]{:S(2)}) collective-permute-start(f32[17,32,128]{2,1,0:T(8,128)} %get-tuple-element.32), channel_id=1, source_target_pairs={{0,2},{1,3},{2,0},{3,1},{4,6},{5,7},{6,4},{7,5},{8,10},{9,11},{10,... | collective-permute-start | bytes 835592 | tf_op jit(solution)/shard_map/ppermute | solution.py:34
  91.1 4.2 %collective-permute-start.13 = (f32[33,32,128]{2,1,0:T(8,128)S(1)}, f32[33,32,128]{2,1,0:T(8,128)S(1)}, u32[]{:S(2)}, u32[]{:S(2)}) collective-permute-start(f32[33,32,128]{2,1,0:T(8,128)S(1)} %pad_maximum_fusion.3.refs_1_), channel_id=1, source_target_pairs={{0,1},{1,0},{2,3},{3,2},{4,5},{5,4},{6,7},{7,6},{8,9},{9,8},{10,11... | collective-permute-start | bytes 1622024 | tf_op jit(solution)/shard_map/ppermute | solution.py:34
  95.2 2.0 collective-permute-start.12
  107.4 12.5 %collective-permute-start.16 = (f32[33,32,128]{2,1,0:T(8,128)}, f32[33,32,128]{2,1,0:T(8,128)S(1)}, u32[]{:S(2)}, u32[]{:S(2)}) collective-permute-start(f32[33,32,128]{2,1,0:T(8,128)} %get-tuple-element.37), channel_id=1, source_target_pairs={{0,8},{4,12},{8,0},{12,4},{16,24},{20,28},{24,16},{28,20},{1,9},{5... | collective-permute-start | bytes 1622024 | tf_op jit(solution)/shard_map/ppermute | solution.py:34
  107.4 17.8 %collective-permute-start.14 = (f32[33,32,128]{2,1,0:T(8,128)}, f32[33,32,128]{2,1,0:T(8,128)S(1)}, u32[]{:S(2)}, u32[]{:S(2)}) collective-permute-start(f32[33,32,128]{2,1,0:T(8,128)} %get-tuple-element.35), channel_id=1, source_target_pairs={{0,4},{4,0},{8,12},{12,8},{16,20},{20,16},{24,28},{28,24},{1,5},{5... | collective-permute-start | bytes 1622024 | tf_op jit(solution)/shard_map/ppermute | solution.py:34
  120.9 12.3 %collective-permute-start.17 = (f32[17,32,128]{2,1,0:T(8,128)S(1)}, f32[17,32,128]{2,1,0:T(8,128)S(1)}, u32[]{:S(2)}, u32[]{:S(2)}) collective-permute-start(f32[17,32,128]{2,1,0:T(8,128)S(1)} %slice_add_fusion.4), channel_id=1, source_target_pairs={{0,4},{4,0},{8,12},{12,8},{16,20},{20,16},{24,28},{28,24},{1,5},{5... | collective-permute-start | bytes 835592 | tf_op jit(solution)/shard_map/ppermute | solution.py:34
  126.2 7.0 %collective-permute-start.15 = (f32[17,32,128]{2,1,0:T(8,128)S(1)}, f32[17,32,128]{2,1,0:T(8,128)S(1)}, u32[]{:S(2)}, u32[]{:S(2)}) collective-permute-start(f32[17,32,128]{2,1,0:T(8,128)S(1)} %slice_add_fusion.5), channel_id=1, source_target_pairs={{0,8},{4,12},{8,0},{12,4},{16,24},{20,28},{24,16},{28,20},{1,9},{5... | collective-permute-start | bytes 835592 | tf_op jit(solution)/shard_map/ppermute | solution.py:34
  133.3 9.9 %collective-permute-start.18 = (f32[64,128]{1,0:T(8,128)S(1)}, f32[64,128]{1,0:T(8,128)S(1)}, u32[]{:S(2)}, u32[]{:S(2)}) collective-permute-start(f32[64,128]{1,0:T(8,128)S(1)} %pad_maximum_fusion.16), channel_id=1, source_target_pairs={{0,16},{4,20},{8,24},{12,28},{16,0},{20,4},{24,8},{28,12},{1,17},{... | collective-permute-start | bytes 98312 | tf_op jit(solution)/shard_map/ppermute | solution.py:34
  139.1 11.6 %collective-permute-start.19 = (f32[8,32,128]{2,1,0:T(8,128)S(1)}, f32[8,32,128]{2,1,0:T(8,128)S(1)}, u32[]{:S(2)}, u32[]{:S(2)}) collective-permute-start(f32[8,32,128]{2,1,0:T(8,128)S(1)} %slice.494), channel_id=1, source_target_pairs={{0,16},{4,20},{8,24},{12,28},{16,0},{20,4},{24,8},{28,12},{1,17},{... | collective-permute-start | bytes 393224 | tf_op jit(solution)/shard_map/ppermute | solution.py:34
  139.1 13.5 %collective-permute-start.20 = (f32[8,32,128]{2,1,0:T(8,128)S(1)}, f32[8,32,128]{2,1,0:T(8,128)S(1)}, u32[]{:S(2)}, u32[]{:S(2)}) collective-permute-start(f32[8,32,128]{2,1,0:T(8,128)S(1)} %slice.497), channel_id=1, source_target_pairs={{0,16},{4,20},{8,24},{12,28},{16,0},{20,4},{24,8},{28,12},{1,17},{... | collective-permute-start | bytes 393224 | tf_op jit(solution)/shard_map/ppermute | solution.py:34
  156.4 13.1 %collective-permute-start.23 = (f32[9,32,128]{2,1,0:T(8,128)}, f32[9,32,128]{2,1,0:T(8,128)S(1)}, u32[]{:S(2)}, u32[]{:S(2)}) collective-permute-start(f32[9,32,128]{2,1,0:T(8,128)} %get-tuple-element.39), channel_id=1, source_target_pairs={{0,16},{4,20},{8,24},{12,28},{16,0},{20,4},{24,8},{28,12},{1,17},{... | collective-permute-start | bytes 442376 | tf_op jit(solution)/shard_map/ppermute | solution.py:34
  158.3 14.0 %collective-permute-start.21 = (f32[9,32,128]{2,1,0:T(8,128)}, f32[9,32,128]{2,1,0:T(8,128)S(1)}, u32[]{:S(2)}, u32[]{:S(2)}) collective-permute-start(f32[9,32,128]{2,1,0:T(8,128)} %get-tuple-element.38), channel_id=1, source_target_pairs={{0,16},{4,20},{8,24},{12,28},{16,0},{20,4},{24,8},{28,12},{1,17},{... | collective-permute-start | bytes 442376 | tf_op jit(solution)/shard_map/ppermute | solution.py:34
  170.2 9.3 %collective-permute-start.24 = (f32[17,32,128]{2,1,0:T(8,128)S(1)}, f32[17,32,128]{2,1,0:T(8,128)S(1)}, u32[]{:S(2)}, u32[]{:S(2)}) collective-permute-start(f32[17,32,128]{2,1,0:T(8,128)S(1)} %pad_maximum_fusion.11), channel_id=1, source_target_pairs={{0,4},{4,0},{8,12},{12,8},{16,20},{20,16},{24,28},{28,24},{1,5},{5... | collective-permute-start | bytes 835592 | tf_op jit(solution)/shard_map/ppermute | solution.py:34
  173.0 8.9 %collective-permute-start.22 = (f32[17,32,128]{2,1,0:T(8,128)S(1)}, f32[17,32,128]{2,1,0:T(8,128)S(1)}, u32[]{:S(2)}, u32[]{:S(2)}) collective-permute-start(f32[17,32,128]{2,1,0:T(8,128)S(1)} %pad_maximum_fusion.10), channel_id=1, source_target_pairs={{0,8},{4,12},{8,0},{12,4},{16,24},{20,28},{24,16},{28,20},{1,9},{5... | collective-permute-start | bytes 835592 | tf_op jit(solution)/shard_map/ppermute | solution.py:34
  179.7 14.1 %collective-permute-start.26 = (f32[33,32,128]{2,1,0:T(8,128)S(1)}, f32[33,32,128]{2,1,0:T(8,128)S(1)}, u32[]{:S(2)}, u32[]{:S(2)}) collective-permute-start(f32[33,32,128]{2,1,0:T(8,128)S(1)} %pad_maximum_fusion.5.refs_1_), channel_id=1, source_target_pairs={{0,8},{4,12},{8,0},{12,4},{16,24},{20,28},{24,16},{28,20},{1,9},{5... | collective-permute-start | bytes 1622024 | tf_op jit(solution)/shard_map/ppermute | solution.py:34
  181.9 13.6 %collective-permute-start.25 = (f32[33,32,128]{2,1,0:T(8,128)S(1)}, f32[33,32,128]{2,1,0:T(8,128)S(1)}, u32[]{:S(2)}, u32[]{:S(2)}) collective-permute-start(f32[33,32,128]{2,1,0:T(8,128)S(1)} %pad_maximum_fusion.4.refs_0_), channel_id=1, source_target_pairs={{0,4},{4,0},{8,12},{12,8},{16,20},{20,16},{24,28},{28,24},{1,5},{5... | collective-permute-start | bytes 1622024 | tf_op jit(solution)/shard_map/ppermute | solution.py:34
  208.2 2.1 collective-permute-start.27
  208.2 3.3 collective-permute-start.28
  211.4 17.4 %collective-permute-start.30 = (f32[16,32,128]{2,1,0:T(8,128)S(1)}, f32[16,32,128]{2,1,0:T(8,128)S(1)}, u32[]{:S(2)}, u32[]{:S(2)}) collective-permute-start(f32[16,32,128]{2,1,0:T(8,128)S(1)} %slice.511), channel_id=1, source_target_pairs={{0,2},{1,3},{2,0},{3,1},{4,6},{5,7},{6,4},{7,5},{8,10},{9,11},{10,... | collective-permute-start | bytes 786440 | tf_op jit(solution)/shard_map/ppermute | solution.py:34
  212.5 8.8 %collective-permute-start.29 = (f32[64,128]{1,0:T(8,128)S(1)}, f32[64,128]{1,0:T(8,128)S(1)}, u32[]{:S(2)}, u32[]{:S(2)}) collective-permute-start(f32[64,128]{1,0:T(8,128)S(1)} %pad_maximum_fusion.17), channel_id=1, source_target_pairs={{0,2},{1,3},{2,0},{3,1},{4,6},{5,7},{6,4},{7,5},{8,10},{9,11},{10,... | collective-permute-start | bytes 98312 | tf_op jit(solution)/shard_map/ppermute | solution.py:34
  214.6 15.9 %collective-permute-start.31 = (f32[16,32,128]{2,1,0:T(8,128)S(1)}, f32[16,32,128]{2,1,0:T(8,128)S(1)}, u32[]{:S(2)}, u32[]{:S(2)}) collective-permute-start(f32[16,32,128]{2,1,0:T(8,128)S(1)} %slice.513), channel_id=1, source_target_pairs={{0,2},{1,3},{2,0},{3,1},{4,6},{5,7},{6,4},{7,5},{8,10},{9,11},{10,... | collective-permute-start | bytes 786440 | tf_op jit(solution)/shard_map/ppermute | solution.py:34
  236.6 9.7 %collective-permute-start.33 = (f32[17,32,128]{2,1,0:T(8,128)}, f32[17,32,128]{2,1,0:T(8,128)S(1)}, u32[]{:S(2)}, u32[]{:S(2)}) collective-permute-start(f32[17,32,128]{2,1,0:T(8,128)} %get-tuple-element.45), channel_id=1, source_target_pairs={{0,2},{1,3},{2,0},{3,1},{4,6},{5,7},{6,4},{7,5},{8,10},{9,11},{10,... | collective-permute-start | bytes 835592 | tf_op jit(solution)/shard_map/ppermute | solution.py:34
  238.6 11.2 %collective-permute-start.32 = (f32[17,32,128]{2,1,0:T(8,128)}, f32[17,32,128]{2,1,0:T(8,128)S(1)}, u32[]{:S(2)}, u32[]{:S(2)}) collective-permute-start(f32[17,32,128]{2,1,0:T(8,128)} %get-tuple-element.44), channel_id=1, source_target_pairs={{0,2},{1,3},{2,0},{3,1},{4,6},{5,7},{6,4},{7,5},{8,10},{9,11},{10,... | collective-permute-start | bytes 835592 | tf_op jit(solution)/shard_map/ppermute | solution.py:34
  247.2 3.5 %collective-permute-start.35 = (f32[33,32,128]{2,1,0:T(8,128)S(1)}, f32[33,32,128]{2,1,0:T(8,128)S(1)}, u32[]{:S(2)}, u32[]{:S(2)}) collective-permute-start(f32[33,32,128]{2,1,0:T(8,128)S(1)} %pad_maximum_fusion.7.refs_1_), channel_id=1, source_target_pairs={{0,1},{1,0},{2,3},{3,2},{4,5},{5,4},{6,7},{7,6},{8,9},{9,8},{10,11... | collective-permute-start | bytes 1622024 | tf_op jit(solution)/shard_map/ppermute | solution.py:34
  250.6 2.0 collective-permute-start.34
  262.8 12.2 %collective-permute-start.38 = (f32[33,32,128]{2,1,0:T(8,128)}, f32[33,32,128]{2,1,0:T(8,128)S(1)}, u32[]{:S(2)}, u32[]{:S(2)}) collective-permute-start(f32[33,32,128]{2,1,0:T(8,128)} %get-tuple-element.49), channel_id=1, source_target_pairs={{0,8},{4,12},{8,0},{12,4},{16,24},{20,28},{24,16},{28,20},{1,9},{5... | collective-permute-start | bytes 1622024 | tf_op jit(solution)/shard_map/ppermute | solution.py:34
  262.8 16.7 %collective-permute-start.36 = (f32[33,32,128]{2,1,0:T(8,128)}, f32[33,32,128]{2,1,0:T(8,128)S(1)}, u32[]{:S(2)}, u32[]{:S(2)}) collective-permute-start(f32[33,32,128]{2,1,0:T(8,128)} %get-tuple-element.47), channel_id=1, source_target_pairs={{0,4},{4,0},{8,12},{12,8},{16,20},{20,16},{24,28},{28,24},{1,5},{5... | collective-permute-start | bytes 1622024 | tf_op jit(solution)/shard_map/ppermute | solution.py:34
  276.0 11.5 %collective-permute-start.39 = (f32[17,32,128]{2,1,0:T(8,128)S(1)}, f32[17,32,128]{2,1,0:T(8,128)S(1)}, u32[]{:S(2)}, u32[]{:S(2)}) collective-permute-start(f32[17,32,128]{2,1,0:T(8,128)S(1)} %slice_add_fusion), channel_id=1, source_target_pairs={{0,4},{4,0},{8,12},{12,8},{16,20},{20,16},{24,28},{28,24},{1,5},{5... | collective-permute-start | bytes 835592 | tf_op jit(solution)/shard_map/ppermute | solution.py:34
  280.6 7.0 %collective-permute-start.37 = (f32[17,32,128]{2,1,0:T(8,128)S(1)}, f32[17,32,128]{2,1,0:T(8,128)S(1)}, u32[]{:S(2)}, u32[]{:S(2)}) collective-permute-start(f32[17,32,128]{2,1,0:T(8,128)S(1)} %slice_add_fusion.1), channel_id=1, source_target_pairs={{0,8},{4,12},{8,0},{12,4},{16,24},{20,28},{24,16},{28,20},{1,9},{5... | collective-permute-start | bytes 835592 | tf_op jit(solution)/shard_map/ppermute | solution.py:34
  287.6 8.3 %collective-permute-start.40 = (f32[64,128]{1,0:T(8,128)S(1)}, f32[64,128]{1,0:T(8,128)S(1)}, u32[]{:S(2)}, u32[]{:S(2)}) collective-permute-start(f32[64,128]{1,0:T(8,128)S(1)} %pad_maximum_fusion.18), channel_id=1, source_target_pairs={{0,16},{4,20},{8,24},{12,28},{16,0},{20,4},{24,8},{28,12},{1,17},{... | collective-permute-start | bytes 98312 | tf_op jit(solution)/shard_map/ppermute | solution.py:34
  292.9 11.5 %collective-permute-start.41 = (f32[8,32,128]{2,1,0:T(8,128)S(1)}, f32[8,32,128]{2,1,0:T(8,128)S(1)}, u32[]{:S(2)}, u32[]{:S(2)}) collective-permute-start(f32[8,32,128]{2,1,0:T(8,128)S(1)} %slice.530), channel_id=1, source_target_pairs={{0,16},{4,20},{8,24},{12,28},{16,0},{20,4},{24,8},{28,12},{1,17},{... | collective-permute-start | bytes 393224 | tf_op jit(solution)/shard_map/ppermute | solution.py:34
  293.0 14.3 %collective-permute-start.42 = (f32[8,32,128]{2,1,0:T(8,128)S(1)}, f32[8,32,128]{2,1,0:T(8,128)S(1)}, u32[]{:S(2)}, u32[]{:S(2)}) collective-permute-start(f32[8,32,128]{2,1,0:T(8,128)S(1)} %slice.533), channel_id=1, source_target_pairs={{0,16},{4,20},{8,24},{12,28},{16,0},{20,4},{24,8},{28,12},{1,17},{... | collective-permute-start | bytes 393224 | tf_op jit(solution)/shard_map/ppermute | solution.py:34
  312.5 1.2 collective-permute-start.43
  313.7 3.9 %collective-permute-start.44 = (f32[64,128]{1,0:T(8,128)S(1)}, f32[64,128]{1,0:T(8,128)S(1)}, u32[]{:S(2)}, u32[]{:S(2)}) collective-permute-start(f32[64,128]{1,0:T(8,128)S(1)} %fusion.21), channel_id=1, source_target_pairs={{0,2},{1,3},{2,0},{3,1},{4,6},{5,7},{6,4},{7,5},{8,10},{9,11},{10,... | collective-permute-start | bytes 98312 | tf_op jit(solution)/shard_map/ppermute | solution.py:34
  317.6 3.9 %collective-permute-start.45 = (f32[64,128]{1,0:T(8,128)S(1)}, f32[64,128]{1,0:T(8,128)S(1)}, u32[]{:S(2)}, u32[]{:S(2)}) collective-permute-start(f32[64,128]{1,0:T(8,128)S(1)} %add.234), channel_id=1, source_target_pairs={{0,4},{4,0},{8,12},{12,8},{16,20},{20,16},{24,28},{28,24},{1,5},{5... | collective-permute-start | bytes 98312 | tf_op jit(solution)/shard_map/ppermute | solution.py:34
  321.5 3.9 %collective-permute-start.46 = (f32[64,128]{1,0:T(8,128)S(1)}, f32[64,128]{1,0:T(8,128)S(1)}, u32[]{:S(2)}, u32[]{:S(2)}) collective-permute-start(f32[64,128]{1,0:T(8,128)S(1)} %add.235), channel_id=1, source_target_pairs={{0,8},{4,12},{8,0},{12,4},{16,24},{20,28},{24,16},{28,20},{1,9},{5... | collective-permute-start | bytes 98312 | tf_op jit(solution)/shard_map/ppermute | solution.py:34
  325.5 6.5 %collective-permute-start.47 = (f32[64,128]{1,0:T(8,128)S(1)}, f32[64,128]{1,0:T(8,128)S(1)}, u32[]{:S(2)}, u32[]{:S(2)}) collective-permute-start(f32[64,128]{1,0:T(8,128)S(1)} %add.236), channel_id=1, source_target_pairs={{0,16},{4,20},{8,24},{12,28},{16,0},{20,4},{24,8},{28,12},{1,17},{... | collective-permute-start | bytes 98312 | tf_op jit(solution)/shard_map/ppermute | solution.py:34
  (18 other events, 240.0 us)

commit v3 on v2

--- a/solution.py
+++ b/solution.py
@@ -46,9 +46,8 @@
     levels = len(gather_order(axis, 0))
     for level in range(levels - 1):
         got = [exchange(held[part], axis, gather_order(axis, part)[level]) for part in range(PARTS)]
-        held = [
-            jnp.concatenate([have[:-1], more[:-1], have[-1:] + more[-1:]], axis=0) for have, more in zip(held, got)
-        ]
+        first = jnp.concatenate([held[0][:-1], got[0][:-1], held[0][-1:] + got[0][-1:]], axis=0)
+        held = [first] + [jnp.concatenate([have, more], axis=0) for have, more in zip(held[1:], got[1:])]
     got = [exchange(held[part], axis, gather_order(axis, part)[-1]) for part in range(PARTS)]
     return held, got
 
@@ -57,20 +56,19 @@
     levels = len(gather_order(axis, 0))
     for level in range(levels - 1, 0, -1):
         got = [exchange(sent[part], axis, gather_order(axis, part)[level]) for part in range(PARTS)]
-        half = kept[0].shape[0] // 2
-        sent = [have[half:] + more[half:] for have, more in zip(kept, got)]
-        if level > 1:
-            kept = [
-                jnp.concatenate([have[:half] + more[:half], out[-1:]], axis=0)
-                for have, more, out in zip(kept, got, sent)
-            ]
+        half = kept[-1].shape[0] // 2
+        if level == 1:
+            gram = kept[0][-1] + got[0][-1]
+            sent = [have[half : 2 * half] + more[half : 2 * half] for have, more in zip(kept, got)]
+            kept = [have[:half] + more[:half] for have, more in zip(kept, got)]
         else:
+            sent = [have[half:] + more[half:] for have, more in zip(kept, got)]
             kept = [have[:half] + more[:half] for have, more in zip(kept, got)]
+            kept[0] = jnp.concatenate([kept[0], sent[0][-1:]], axis=0)
     bit = gather_order(axis, 0)[0]
-    gram = jnp.concatenate([out[-1] for out in sent], axis=0)
     gram = gram + exchange(gram, axis, bit)
-    got = [exchange(out[:-1], axis, bit) for out in sent]
-    return [have + more for have, more in zip(kept, got)], gram
+    got = [exchange(out, axis, bit) for out in sent]
+    return kept, got, gram
 
 
 def all_sum(value):
@@ -86,13 +84,13 @@
     return [at * quarter for at in ((0, 2, 1, 3) if swapped else (0, 1, 2, 3))], quarter
 
 
-def tiles_kernel(count, source, target, *refs, transposed, places_in, places_out):
+def tiles_kernel(count, source, target, *refs, places_in, places_out):
     low_refs, high_refs, refs = refs[:PARTS], refs[PARTS : 2 * PARTS], refs[2 * PARTS :]
     tile_ref, keep_refs, send_refs = refs[0], refs[1 : 1 + PARTS], refs[1 + PARTS : 1 + 2 * PARTS]
     pieces, total = refs[1 + 2 * PARTS :]
     step = pl.program_id(0)
-    half_in = low_refs[0].shape[0] - 1
-    half_out = keep_refs[0].shape[0] - 1
+    half_in = low_refs[-1].shape[0]
+    half_out = keep_refs[-1].shape[0]
 
     @pl.when(step == 0)
     def _():
@@ -119,7 +117,6 @@
         lax.fori_loop(0, 2 * half_out, clear, 0, unroll=4)
 
     live = jnp.clip(count[0] - step * BATCH, 0, BATCH)
-    contract = 1 if transposed else 0
 
     def group(at, carry):
         first = at * UNROLL
@@ -129,8 +126,8 @@
             products.append(
                 lax.dot_general(
                     pieces[source[step * BATCH + first + slot]],
-                    jnp.concatenate([tile, tile], axis=contract),
-                    (((1,), (contract,)), ((), ())),
+                    jnp.concatenate([tile, tile], axis=0),
+                    (((1,), (0,)), ((), ())),
                     preferred_element_type=jnp.float32,
                 )
             )
@@ -154,40 +151,40 @@
                     return carry
 
                 lax.fori_loop(0, quarter, finish, 0, unroll=4)
-            gram = low_refs[part][half_in] + high_refs[part][half_in]
-            keep_refs[part][half_out] = gram
-            send_refs[part][half_out] = gram
-
-
-def tiles_product(count, source, target, low, high, tiles, blocks_out, axis_in, axis_out, transposed):
-    half_in = low[0].shape[0] - 1
+        gram = low_refs[0][half_in] + high_refs[0][half_in]
+        keep_refs[0][half_out] = gram
+        send_refs[0][half_out] = gram
+
+
+def tiles_product(count, source, target, low, high, tiles, blocks_out, axis_in, axis_out):
+    half_in = low[-1].shape[0]
     half_out = blocks_out // 2
     whole = lambda step, *refs: (0, 0, 0)
+    shapes = lambda blocks: [(blocks + (part == 0), ROWS, TILE) for part in range(PARTS)]
 
     def tile_block(step, count, source, target):
         return (jnp.minimum(step, (count[0] + BATCH - 1) // BATCH - 1), 0, 0)
 
     kernel = functools.partial(
         tiles_kernel,
-        transposed=transposed,
         places_in=[part_places(axis_in, part, 2 * half_in) for part in range(PARTS)],
         places_out=[part_places(axis_out, part, 2 * half_out) for part in range(PARTS)],
     )
     out = pl.pallas_call(
         kernel,
-        out_shape=[jax.ShapeDtypeStruct((half_out + 1, ROWS, TILE), jnp.float32)] * (2 * PARTS),
+        out_shape=[jax.ShapeDtypeStruct(shape, jnp.float32) for shape in shapes(half_out)] * 2,
         grid_spec=pltpu.PrefetchScalarGridSpec(
             num_scalar_prefetch=3,
             grid=(tiles.shape[0] // BATCH,),
-            in_specs=[pl.BlockSpec((half_in + 1, ROWS, TILE), whole)] * (2 * PARTS)
+            in_specs=[pl.BlockSpec(shape, whole) for shape in shapes(half_in)] * 2
             + [pl.BlockSpec((BATCH, TILE, TILE), tile_block)],
-            out_specs=[pl.BlockSpec((half_out + 1, ROWS, TILE), whole)] * (2 * PARTS),
+            out_specs=[pl.BlockSpec(shape, whole) for shape in shapes(half_out)] * 2,
             scratch_shapes=[
                 pltpu.VMEM((2 * half_in, K, 2 * TILE), jnp.bfloat16),
                 pltpu.VMEM((2 * half_out + 1, K, TILE), jnp.float32),
             ],
         ),
-        name="user_tiles" if transposed else "item_tiles",
+        name=axis_out + "_tiles",
     )(count, source, target, *low, *high, tiles)
     return out[:PARTS], out[PARTS:]
 
@@ -201,14 +198,39 @@
 def factor_kernel(gram_ref, out_ref, *, total):
     row = lax.broadcasted_iota(jnp.int32, (K, K), 0)
     col = lax.broadcasted_iota(jnp.int32, (K, K), 1)
-    work = jnp.concatenate([gram_ref[:, :K] * (1.0 / total), (row == col).astype(jnp.float32)], axis=1)
+    gram = jnp.concatenate([gram_ref[:, :K], gram_ref[:, K:]], axis=0) * (1.0 / total)
+    work = jnp.concatenate([gram, (row == col).astype(jnp.float32)], axis=1)
     below = lax.broadcasted_iota(jnp.int32, (K, 1), 0)
-    for at in range(K):
-        pivot_row = work[at : at + 1, :]
-        factor = work[:, at : at + 1] / pivot_row[:, at : at + 1]
-        work = work - jnp.where(below > at, factor, 0.0) * pivot_row
+    for at in range(0, K, 2):
+        first, second = work[at : at + 1, :], work[at + 1 : at + 2, :]
+        beside = first[:, at + 1 : at + 2]
+        inverse = 1.0 / first[:, at : at + 1]
+        multiple = beside * inverse
+        pivot = second[:, at + 1 : at + 2] - multiple * beside
+        second = second - multiple * first
+        column = work[:, at : at + 1] * inverse
+        next_column = (work[:, at + 1 : at + 2] - column * beside) * (1.0 / pivot)
+        work = work - jnp.where(below > at, column, 0.0) * first
+        work = work - jnp.where(below > at + 1, next_column, 0.0) * second
     pivots = jnp.sum(jnp.where(row == col, work[:, :K], 0.0), axis=1, keepdims=True)
     out_ref[...] = work[:, K:] * lax.rsqrt(pivots)
+
+
+def turn_kernel(tile_ref, out_ref):
+    for at in range(tile_ref.shape[0]):
+        out_ref[at] = tile_ref[at].T
+
+
+def turned_tiles(tiles):
+    block = pl.BlockSpec((32, TILE, TILE), lambda step: (step, 0, 0))
+    return pl.pallas_call(
+        turn_kernel,
+        out_shape=jax.ShapeDtypeStruct(tiles.shape, tiles.dtype),
+        grid=(tiles.shape[0] // 32,),
+        in_specs=[block],
+        out_specs=block,
+        name="turned_tiles",
+    )(tiles)
 
 
 def inverse_factor(gram, total):
@@ -222,13 +244,13 @@
 def scale_kernel(*refs, factored):
     refs = list(refs)
     inverse = refs.pop(0)[...] if factored else None
-    raw_refs, refs = refs[:PARTS], refs[PARTS:]
+    raw_refs, refs = list(zip(refs[:PARTS], refs[PARTS : 2 * PARTS])), refs[2 * PARTS :]
     scale_ref, panel_ref, sent_refs = refs[0], refs[1], refs[2:]
     blocks = scale_ref.shape[0]
     gram = jnp.zeros((K, K), jnp.float32)
     for at in range(blocks):
         scale = scale_ref[at][None, :]
-        panel = jnp.concatenate([ref[at] for ref in raw_refs], axis=0)
+        panel = jnp.concatenate([kept[at] + got[at] for kept, got in raw_refs], axis=0)
         if factored:
             panel = dot_full(inverse, panel, (1, 0))
         panel = scale * panel
@@ -236,19 +258,17 @@
         for part in range(PARTS):
             sent_refs[part][at] = scale * panel[part * ROWS : (part + 1) * ROWS]
         gram = gram + dot_full(panel, panel, (1, 1))
-    gram = jnp.concatenate([gram, jnp.zeros((K, TILE - K), jnp.float32)], axis=1)
-    for part in range(PARTS):
-        sent_refs[part][blocks] = gram[part * ROWS : (part + 1) * ROWS]
-
-
-def scale_panel(inverse, raws, scale):
+    sent_refs[0][blocks] = jnp.concatenate([gram[:ROWS], gram[ROWS:]], axis=1)
+
+
+def scale_panel(inverse, kept, got, scale):
     factored = inverse is not None
-    operands = ([inverse] if factored else []) + list(raws) + [scale]
+    operands = ([inverse] if factored else []) + list(kept) + list(got) + [scale]
     blocks = scale.shape[0]
     panel, *sent = pl.pallas_call(
         functools.partial(scale_kernel, factored=factored),
         out_shape=[jax.ShapeDtypeStruct((blocks, K, TILE), jnp.float32)]
-        + [jax.ShapeDtypeStruct((blocks + 1, ROWS, TILE), jnp.float32)] * PARTS,
+        + [jax.ShapeDtypeStruct((blocks + (part == 0), ROWS, TILE), jnp.float32) for part in range(PARTS)],
         name="scale_panel",
     )(*operands)
     return panel, sent
@@ -289,24 +309,26 @@
     item_scale = lax.rsqrt(item_degree.astype(jnp.float32)).reshape(item_blocks, TILE)
     start = start_items.astype(jnp.float32).reshape(PARTS, ROWS, item_blocks, TILE).transpose(0, 2, 1, 3)
     start = item_scale[None, :, None, :] * start
-    start = jnp.concatenate([start, jnp.zeros_like(start[:, :1])], axis=1)
-    sent = [start[part] for part in range(PARTS)]
-
+    sent = [jnp.concatenate([start[0], jnp.zeros_like(start[0][:1])], axis=0), start[1]]
+    turned = turned_tiles(tiles)
     item_inverse = None
     for step in range(ITERS):
         low, high = gather(sent, "users")
-        kept, out = tiles_product(count, col_at, row_to, low, high, tiles, UT, "users", "items", True)
-        raws, gram = reduce_scatter(kept, out, "items")
+        kept, out = tiles_product(count, col_at, row_to, low, high, turned, UT, "users", "items")
+        kept, got, gram = reduce_scatter(kept, out, "items")
         if step:
             item_inverse = inverse_factor(gram, item_total)
-        user_raw, sent = scale_panel(item_inverse, raws, user_scale)
+        user_raw, sent = scale_panel(item_inverse, kept, got, user_scale)
         low, high = gather(sent, "items")
-        kept, out = tiles_product(count, row_at, col_to, low, high, tiles, IT, "items", "users", False)
-        raws, gram = reduce_scatter(kept, out, "users")
+        kept, out = tiles_product(count, row_at, col_to, low, high, tiles, IT, "items", "users")
+        kept, got, gram = reduce_scatter(kept, out, "users")
         user_inverse = inverse_factor(gram, user_total)
-        item_raw, sent = scale_panel(user_inverse, raws, item_scale)
-    gram = all_sum(jnp.concatenate([part[-1] for part in sent], axis=0))
-    return finish_panel(user_inverse, user_raw), finish_panel(inverse_factor(gram, item_total), item_raw)
+        if step == ITERS - 1:
+            user_panel = finish_panel(user_inverse, user_raw)
+            user_panel, got = lax.optimization_barrier((user_panel, got))
+        item_raw, sent = scale_panel(user_inverse, kept, got, item_scale)
+    item_inverse = inverse_factor(all_sum(sent[0][-1]), item_total)
+    return user_panel, finish_panel(item_inverse, item_raw)
 
 
 def solution(mesh):

time: 347 us -> 365 us (1.052)
  waiting for transfers between devices: 128 us -> 141 us
  Pallas kernels: 87.6 us -> 98.5 us
  other arithmetic: 30.5 us -> 26.4 us
    ppermute x48, waiting for transfers between devices: 128 us -> 141 us  [exchange(): lax.ppermute(value, axis, [(at, at ^ bit) for at in range(lax.axis_size(a...]
    unnamed x37 -> x61, local copies, waits for them, and re-layouts: 3.29 us -> 9.78 us
    pallas_call x4, Pallas kernels: 27.3 us -> 32.7 us  [inverse_factor(): pl.pallas_call(functools.partial(factor_kernel, total=total), out_shape=j...]
    slice x33 -> x8, local copies, waits for them, and re-layouts: 8.08 us -> 3.03 us  [the longest x3 2.95 us: gather(): held[0][:-1]]
    pallas_call x4 -> x5, Pallas kernels: 42.4 us -> 47.1 us  [the longest x4 28 us: tiles_product(): pl.pallas_call(kernel, out_shape=[jax.ShapeDtypeStruct(shape, jnp.float32...]
    add x12 -> x2, other arithmetic: 6.16 us -> 2.01 us  [reduce_scatter(): sent = [have[half:] + more[half:] for have, more in zip(kept, got)]]
    add x22 -> x20, other arithmetic: 17.9 us -> 17.1 us  [the longest x6 8.65 us: reduce_scatter(): have[half:2 * half] + more[half:2 * half]]
  transfers between devices with their start and end apart: 48 -> 48, of which waited for: 33 -> 33; matrix products, arithmetic and copies ran while one was open for 9% -> 8% of each run, Pallas kernels for 7% -> 13%
where the time goes in v3:
time: 365 us; the launch traced here: 362 us
  waiting for transfers between devices  141 us (39%)
  Pallas kernels  98.5 us (27%)
  starting transfers between devices  80.5 us (22%)
  other arithmetic  26.4 us (7%)
  local copies, waits for them, and re-layouts  13.6 us (4%)
    ppermute x48, waiting for transfers between devices, exchange(): lax.ppermute(value, axis, [(at, at ^ bit) for at in range(lax.axis_size(a...  141 us
    ppermute x48, starting transfers between devices, exchange(): lax.ppermute(value, axis, [(at, at ^ bit) for at in range(lax.axis_size(a...  80.5 us
    pallas_call x4, Pallas kernels, inverse_factor(): pl.pallas_call(functools.partial(factor_kernel, total=total), out_shape=j...  32.7 us
    pallas_call x4, Pallas kernels, tiles_product(): pl.pallas_call(kernel, out_shape=[jax.ShapeDtypeStruct(shape, jnp.float32...  28 us
    pallas_call x1, Pallas kernels, turned_tiles(): pl.pallas_call(turn_kernel, out_shape=jax.ShapeDtypeStruct(tiles.shape, t...  19.1 us
    pallas_call x4, Pallas kernels, scale_panel(): pl.pallas_call(functools.partial(scale_kernel, factored=factored), out_sh...  14.3 us
    unnamed x61, local copies, waits for them, and re-layouts  9.78 us
    add x6, other arithmetic, reduce_scatter(): have[half:2 * half] + more[half:2 * half]  8.65 us
  transfers between devices with their start and end apart: 48, of which 33 were waited for; matrix products, arithmetic and copies ran while one was open for 8% of the time, Pallas kernels for 13%

profile of v3, /device:TPU:0, one launch (start us, length us, event | category | flops | bytes accessed | tf_op | source)
XLA Modules:
  0.0 362.1 jit_solution(4696478938583683687)
XLA Ops:
  2.4 4.1 %collective-permute-start = (f32[9,32,128]{2,1,0:T(8,128)S(1)}, f32[9,32,128]{2,1,0:T(8,128)S(1)}, u32[]{:S(2)}, u32[]{:S(2)}) collective-permute-start(f32[9,32,128]{2,1,0:T(8,128)S(1)} %concatenate.44), channel_id=1, source_target_pairs={{0,16},{4,20},{8,24},{12,28},{16,0},{20,4},{24,8},{28,12},{1,17},{... | collective-permute-start | bytes 442376 | tf_op jit(solution)/shard_map/ppermute | solution.py:34
  6.6 10.6 %collective-permute-done = f32[9,32,128]{2,1,0:T(8,128)S(1)} collective-permute-done((f32[9,32,128]{2,1,0:T(8,128)S(1)}, f32[9,32,128]{2,1,0:T(8,128)S(1)}, u32[]{:S(2)}, u32[]{:S(2)}) %collective-permute-start) | collective-permute-done | bytes 147488 | tf_op jit(solution)/shard_map/ppermute | solution.py:34
  17.3 1.9 collective-permute-done.2
  21.0 4.2 %collective-permute-done.1 = f32[17,32,128]{2,1,0:T(8,128)S(1)} collective-permute-done((f32[17,32,128]{2,1,0:T(8,128)S(1)}, f32[17,32,128]{2,1,0:T(8,128)S(1)}, u32[]{:S(2)}, u32[]{:S(2)}) %collective-permute-start.1) | collective-permute-done | bytes 278560 | tf_op jit(solution)/shard_map/ppermute | solution.py:34
  29.7 19.1 %turned_tiles.1.refs_4_ = bf16[512,128,128]{2,1,0:T(8,128)(2,1)} custom-call(bf16[512,128,128]{2,1,0:T(8,128)(2,1)} %bitcast.34), custom_call_target="tpu_custom_call" | custom-call | tf_op jit(solution)/shard_map/turned_tiles/pallas_call | solution.py:226
  50.5 7.0 %items_tiles.2 = (f32[33,32,128]{2,1,0:T(8,128)}, f32[32,32,128]{2,1,0:T(8,128)}, f32[33,32,128]{2,1,0:T(8,128)}, f32[32,32,128]{2,1,0:T(8,128)}) custom-call(s32[1]{0:T(128)} %bitcast.29.count, s32[512]{0:T(512)} %get-tuple-element.85.source, s32[512]{0:T(512)} %get-tuple-element.58.target, f32[33,32,128]{2,1,0:T(8,128)} %copy-done, ...), custom_call_target="tpu_custom_call" | custom-call | tf_op jit(solution)/shard_map/items_tiles/pallas_call | solution.py:173
  65.9 4.7 %collective-permute-done.9.refs_3_ = f32[16,32,128]{2,1,0:T(8,128)S(1)} collective-permute-done((f32[16,32,128]{2,1,0:T(8,128)S(1)}, f32[16,32,128]{2,1,0:T(8,128)S(1)}, u32[]{:S(2)}, u32[]{:S(2)}) %collective-permute-start.9) | collective-permute-done | bytes 262176 | tf_op jit(solution)/shard_map/ppermute | solution.py:34
  70.6 4.8 %collective-permute-done.8.refs_2_ = f32[16,32,128]{2,1,0:T(8,128)S(1)} collective-permute-done((f32[16,32,128]{2,1,0:T(8,128)S(1)}, f32[16,32,128]{2,1,0:T(8,128)S(1)}, u32[]{:S(2)}, u32[]{:S(2)}) %collective-permute-start.8) | collective-permute-done | bytes 262176 | tf_op jit(solution)/shard_map/ppermute | solution.py:34
  76.1 3.0 scale_panel.4
  83.3 5.6 %collective-permute-done.10 = f32[17,32,128]{2,1,0:T(8,128)S(1)} collective-permute-done((f32[17,32,128]{2,1,0:T(8,128)}, f32[17,32,128]{2,1,0:T(8,128)S(1)}, u32[]{:S(2)}, u32[]{:S(2)}) %collective-permute-start.10) | collective-permute-done | bytes 278560 | tf_op jit(solution)/shard_map/ppermute | solution.py:34
  89.8 3.1 collective-permute-done.11
  95.9 7.0 %users_tiles.2 = (f32[33,32,128]{2,1,0:T(8,128)}, f32[32,32,128]{2,1,0:T(8,128)}, f32[33,32,128]{2,1,0:T(8,128)}, f32[32,32,128]{2,1,0:T(8,128)}) custom-call(s32[1]{0:T(128)} %bitcast.30.count, s32[512]{0:T(512)} %get-tuple-element.59.source, s32[512]{0:T(512)} %get-tuple-element.84.target, f32[33,32,128]{2,1,0:T(8,128)} %copy-done.3, ...), custom_call_target="tpu_custom_call" | custom-call | tf_op jit(solution)/shard_map/users_tiles/pallas_call | solution.py:173
  102.8 7.4 %collective-permute-start.17 = (f32[32,32,128]{2,1,0:T(8,128)}, f32[32,32,128]{2,1,0:T(8,128)S(1)}, u32[]{:S(2)}, u32[]{:S(2)}) collective-permute-start(f32[32,32,128]{2,1,0:T(8,128)} %get-tuple-element.39), channel_id=1, source_target_pairs={{0,8},{4,12},{8,0},{12,4},{16,24},{20,28},{24,16},{28,20},{1,9},{5... | collective-permute-start | bytes 1572872 | tf_op jit(solution)/shard_map/ppermute | solution.py:34
  110.2 3.9 %collective-permute-start.14 = (f32[33,32,128]{2,1,0:T(8,128)}, f32[33,32,128]{2,1,0:T(8,128)S(1)}, u32[]{:S(2)}, u32[]{:S(2)}) collective-permute-start(f32[33,32,128]{2,1,0:T(8,128)} %get-tuple-element.37), channel_id=1, source_target_pairs={{0,4},{4,0},{8,12},{12,8},{16,20},{20,16},{24,28},{28,24},{1,5},{5... | collective-permute-start | bytes 1622024 | tf_op jit(solution)/shard_map/ppermute | solution.py:34
  114.1 7.9 %collective-permute-done.17 = f32[32,32,128]{2,1,0:T(8,128)S(1)} collective-permute-done((f32[32,32,128]{2,1,0:T(8,128)}, f32[32,32,128]{2,1,0:T(8,128)S(1)}, u32[]{:S(2)}, u32[]{:S(2)}) %collective-permute-start.17) | collective-permute-done | bytes 524320 | tf_op jit(solution)/shard_map/ppermute | solution.py:34
  130.9 2.9 collective-permute-start.20
  137.5 9.5 %collective-permute-done.16 = f32[32,128]{1,0:T(8,128)S(1)} collective-permute-done((f32[32,128]{1,0:T(8,128)S(1)}, f32[32,128]{1,0:T(8,128)S(1)}, u32[]{:S(2)}, u32[]{:S(2)}) %collective-permute-start.16) | collective-permute-done | bytes 16416 | tf_op jit(solution)/shard_map/ppermute | solution.py:34
  147.6 8.2 %factor.4.refs_0_ = f32[64,64]{1,0:T(8,128)} custom-call(f32[32,128]{1,0:T(8,128)} %add.174.gram_ref), custom_call_target="tpu_custom_call" | custom-call | tf_op jit(solution)/shard_map/factor/pallas_call | solution.py:237
  156.5 3.3 scale_panel.5
  160.7 3.0 collective-permute-start.23
  163.7 9.9 %collective-permute-done.21 = f32[9,32,128]{2,1,0:T(8,128)S(1)} collective-permute-done((f32[9,32,128]{2,1,0:T(8,128)}, f32[9,32,128]{2,1,0:T(8,128)S(1)}, u32[]{:S(2)}, u32[]{:S(2)}) %collective-permute-start.21) | collective-permute-done | bytes 147488 | tf_op jit(solution)/shard_map/ppermute | solution.py:34
  178.0 4.1 %collective-permute-done.22 = f32[17,32,128]{2,1,0:T(8,128)S(1)} collective-permute-done((f32[17,32,128]{2,1,0:T(8,128)S(1)}, f32[17,32,128]{2,1,0:T(8,128)S(1)}, u32[]{:S(2)}, u32[]{:S(2)}) %collective-permute-start.22) | collective-permute-done | bytes 278560 | tf_op jit(solution)/shard_map/ppermute | solution.py:34
  183.3 2.8 collective-permute-done.24
  187.2 10.2 %collective-permute-done.26.refs_3_ = f32[32,32,128]{2,1,0:T(8,128)S(1)} collective-permute-done((f32[32,32,128]{2,1,0:T(8,128)S(1)}, f32[32,32,128]{2,1,0:T(8,128)S(1)}, u32[]{:S(2)}, u32[]{:S(2)}) %collective-permute-start.26) | collective-permute-done | bytes 524320 | tf_op jit(solution)/shard_map/ppermute | solution.py:34
  198.4 7.0 %items_tiles.3 = (f32[33,32,128]{2,1,0:T(8,128)}, f32[32,32,128]{2,1,0:T(8,128)}, f32[33,32,128]{2,1,0:T(8,128)}, f32[32,32,128]{2,1,0:T(8,128)}) custom-call(s32[1]{0:T(128)} %bitcast.31.count, s32[512]{0:T(512)} %get-tuple-element.85.source, s32[512]{0:T(512)} %get-tuple-element.58.target, f32[33,32,128]{2,1,0:T(8,128)} %copy-done.1, ...), custom_call_target="tpu_custom_call" | custom-call | tf_op jit(solution)/shard_map/items_tiles/pallas_call | solution.py:173
  209.4 7.1 %collective-permute-start.31 = (f32[16,32,128]{2,1,0:T(8,128)S(1)}, f32[16,32,128]{2,1,0:T(8,128)S(1)}, u32[]{:S(2)}, u32[]{:S(2)}) collective-permute-start(f32[16,32,128]{2,1,0:T(8,128)S(1)} %get-tuple-element.68), channel_id=1, source_target_pairs={{0,2},{1,3},{2,0},{3,1},{4,6},{5,7},{6,4},{7,5},{8,10},{9,11},{10,... | collective-permute-start | bytes 786440 | tf_op jit(solution)/shard_map/ppermute | solution.py:34
  219.0 2.0 collective-permute-start.28
  221.0 8.0 %collective-permute-done.28 = f32[32,128]{1,0:T(8,128)S(1)} collective-permute-done((f32[32,128]{1,0:T(8,128)S(1)}, f32[32,128]{1,0:T(8,128)S(1)}, u32[]{:S(2)}, u32[]{:S(2)}) %collective-permute-start.28) | collective-permute-done | bytes 16416 | tf_op jit(solution)/shard_map/ppermute | solution.py:34
  229.7 8.2 %factor.5.refs_0_ = f32[64,64]{1,0:T(8,128)} custom-call(f32[32,128]{1,0:T(8,128)} %add.186.gram_ref), custom_call_target="tpu_custom_call" | custom-call | tf_op jit(solution)/shard_map/factor/pallas_call | solution.py:237
  238.6 4.7 %scale_panel.6 = (f32[16,64,128]{2,1,0:T(8,128)}, f32[17,32,128]{2,1,0:T(8,128)}, f32[16,32,128]{2,1,0:T(8,128)}) custom-call(f32[64,64]{1,0:T(8,128)} %factor.5.refs_0_, f32[16,32,128]{2,1,0:T(8,128)} %get-tuple-element.63.refs_1_, f32[16,32,128]{2,1,0:T(8,128)} %get-tuple-element.69.refs_2_, f32[16,32,128]{2,1,0:T(8,128)} %copy-done.17, ...), custom_call_target="tpu_custom_call" | custom-call | tf_op jit(solution)/shard_map/scale_panel/pallas_call | solution.py:268
  247.4 5.6 %collective-permute-done.32 = f32[17,32,128]{2,1,0:T(8,128)S(1)} collective-permute-done((f32[17,32,128]{2,1,0:T(8,128)}, f32[17,32,128]{2,1,0:T(8,128)S(1)}, u32[]{:S(2)}, u32[]{:S(2)}) %collective-permute-start.32) | collective-permute-done | bytes 278560 | tf_op jit(solution)/shard_map/ppermute | solution.py:34
  253.9 3.3 collective-permute-done.33
  260.2 7.0 %users_tiles.3 = (f32[33,32,128]{2,1,0:T(8,128)}, f32[32,32,128]{2,1,0:T(8,128)}, f32[33,32,128]{2,1,0:T(8,128)}, f32[32,32,128]{2,1,0:T(8,128)}) custom-call(s32[1]{0:T(128)} %bitcast.32.count, s32[512]{0:T(512)} %get-tuple-element.59.source, s32[512]{0:T(512)} %get-tuple-element.84.target, f32[33,32,128]{2,1,0:T(8,128)} %copy-done.2, ...), custom_call_target="tpu_custom_call" | custom-call | tf_op jit(solution)/shard_map/users_tiles/pallas_call | solution.py:173
  267.3 8.0 %collective-permute-start.40 = (f32[32,32,128]{2,1,0:T(8,128)}, f32[32,32,128]{2,1,0:T(8,128)S(1)}, u32[]{:S(2)}, u32[]{:S(2)}) collective-permute-start(f32[32,32,128]{2,1,0:T(8,128)} %get-tuple-element.52), channel_id=1, source_target_pairs={{0,8},{4,12},{8,0},{12,4},{16,24},{20,28},{24,16},{28,20},{1,9},{5... | collective-permute-start | bytes 1572872 | tf_op jit(solution)/shard_map/ppermute | solution.py:34
  275.3 2.9 collective-permute-start.36
  278.2 8.8 %collective-permute-done.40 = f32[32,32,128]{2,1,0:T(8,128)S(1)} collective-permute-done((f32[32,32,128]{2,1,0:T(8,128)}, f32[32,32,128]{2,1,0:T(8,128)S(1)}, u32[]{:S(2)}, u32[]{:S(2)}) %collective-permute-start.40) | collective-permute-done | bytes 524320 | tf_op jit(solution)/shard_map/ppermute | solution.py:34
  292.6 2.7 collective-permute-done.41
  297.4 2.2 collective-permute-start.39
  300.3 11.6 %collective-permute-done.38 = f32[32,128]{1,0:T(8,128)S(1)} collective-permute-done((f32[32,128]{1,0:T(8,128)S(1)}, f32[32,128]{1,0:T(8,128)S(1)}, u32[]{:S(2)}, u32[]{:S(2)}) %collective-permute-start.38) | collective-permute-done | bytes 16416 | tf_op jit(solution)/shard_map/ppermute | solution.py:34
  312.6 8.2 %factor.6.inverse_ref.refs_0_ = f32[64,64]{1,0:T(8,128)} custom-call(f32[32,128]{1,0:T(8,128)} %add.195.gram_ref), custom_call_target="tpu_custom_call" | custom-call | tf_op jit(solution)/shard_map/factor/pallas_call | solution.py:237
  320.7 2.4 finish_panel.2
  323.8 3.3 scale_panel.7
  329.7 7.7 %collective-permute-start.44 = (f32[32,128]{1,0:T(8,128)S(1)}, f32[32,128]{1,0:T(8,128)S(1)}, u32[]{:S(2)}, u32[]{:S(2)}) collective-permute-start(f32[32,128]{1,0:T(8,128)S(1)} %fusion.15), channel_id=1, source_target_pairs={{0,2},{1,3},{2,0},{3,1},{4,6},{5,7},{6,4},{7,5},{8,10},{9,11},{10,... | collective-permute-start | bytes 49160 | tf_op jit(solution)/shard_map/ppermute | solution.py:34
  339.7 3.2 collective-permute-done.45
  343.4 3.3 collective-permute-done.46
  348.6 2.7 collective-permute-done.47
  351.9 8.2 %factor.7.inverse_ref = f32[64,64]{1,0:T(8,128)} custom-call(f32[32,128]{1,0:T(8,128)} %add.207.gram_ref), custom_call_target="tpu_custom_call" | custom-call | tf_op jit(solution)/shard_map/factor/pallas_call | solution.py:237
  360.1 2.0 finish_panel.3
  (183 shorter events, 82.0 us)
Async XLA Ops:
  2.4 14.8 %collective-permute-start = (f32[9,32,128]{2,1,0:T(8,128)S(1)}, f32[9,32,128]{2,1,0:T(8,128)S(1)}, u32[]{:S(2)}, u32[]{:S(2)}) collective-permute-start(f32[9,32,128]{2,1,0:T(8,128)S(1)} %concatenate.44), channel_id=1, source_target_pairs={{0,16},{4,20},{8,24},{12,28},{16,0},{20,4},{24,8},{28,12},{1,17},{... | collective-permute-start | bytes 442376 | tf_op jit(solution)/shard_map/ppermute | solution.py:34
  6.5 12.7 %collective-permute-start.2 = (f32[8,32,128]{2,1,0:T(8,128)S(1)}, f32[8,32,128]{2,1,0:T(8,128)S(1)}, u32[]{:S(2)}, u32[]{:S(2)}) collective-permute-start(f32[8,32,128]{2,1,0:T(8,128)S(1)} %get-tuple-element.82), channel_id=1, source_target_pairs={{0,16},{4,20},{8,24},{12,28},{16,0},{20,4},{24,8},{28,12},{1,17},{... | collective-permute-start | bytes 393224 | tf_op jit(solution)/shard_map/ppermute | solution.py:34
  17.2 7.9 %collective-permute-start.1 = (f32[17,32,128]{2,1,0:T(8,128)S(1)}, f32[17,32,128]{2,1,0:T(8,128)S(1)}, u32[]{:S(2)}, u32[]{:S(2)}) collective-permute-start(f32[17,32,128]{2,1,0:T(8,128)S(1)} %pad_maximum_fusion.5), channel_id=1, source_target_pairs={{0,8},{4,12},{8,0},{12,4},{16,24},{20,28},{24,16},{28,20},{1,9},{5... | collective-permute-start | bytes 835592 | tf_op jit(solution)/shard_map/ppermute | solution.py:34
  19.3 7.9 %collective-permute-start.3 = (f32[16,32,128]{2,1,0:T(8,128)S(1)}, f32[16,32,128]{2,1,0:T(8,128)S(1)}, u32[]{:S(2)}, u32[]{:S(2)}) collective-permute-start(f32[16,32,128]{2,1,0:T(8,128)S(1)} %pad_maximum_fusion.7), channel_id=1, source_target_pairs={{0,4},{4,0},{8,12},{12,8},{16,20},{20,16},{24,28},{28,24},{1,5},{5... | collective-permute-start | bytes 786440 | tf_op jit(solution)/shard_map/ppermute | solution.py:34
  25.2 24.3 %collective-permute-start.4 = (f32[33,32,128]{2,1,0:T(8,128)S(1)}, f32[33,32,128]{2,1,0:T(8,128)S(1)}, u32[]{:S(2)}, u32[]{:S(2)}) collective-permute-start(f32[33,32,128]{2,1,0:T(8,128)S(1)} %pad_maximum_fusion.refs_0_), channel_id=1, source_target_pairs={{0,4},{4,0},{8,12},{12,8},{16,20},{20,16},{24,28},{28,24},{1,5},{5... | collective-permute-start | bytes 1622024 | tf_op jit(solution)/shard_map/ppermute | solution.py:34
  27.2 22.3 %collective-permute-start.5 = (f32[32,32,128]{2,1,0:T(8,128)S(1)}, f32[32,32,128]{2,1,0:T(8,128)S(1)}, u32[]{:S(2)}, u32[]{:S(2)}) collective-permute-start(f32[32,32,128]{2,1,0:T(8,128)S(1)} %pad_maximum_fusion.4.refs_1_), channel_id=1, source_target_pairs={{0,8},{4,12},{8,0},{12,4},{16,24},{20,28},{24,16},{28,20},{1,9},{5... | collective-permute-start | bytes 1572872 | tf_op jit(solution)/shard_map/ppermute | solution.py:34
  57.5 2.1 collective-permute-start.7
  57.5 5.0 %collective-permute-start.6 = (f32[33,32,128]{2,1,0:T(8,128)}, f32[33,32,128]{2,1,0:T(8,128)S(1)}, u32[]{:S(2)}, u32[]{:S(2)}) collective-permute-start(f32[33,32,128]{2,1,0:T(8,128)} %get-tuple-element.31), channel_id=1, source_target_pairs={{0,1},{1,0},{2,3},{3,2},{4,5},{5,4},{6,7},{7,6},{8,9},{9,8},{10,11... | collective-permute-start | bytes 1622024 | tf_op jit(solution)/shard_map/ppermute | solution.py:34
  61.5 9.2 %collective-permute-start.9 = (f32[16,32,128]{2,1,0:T(8,128)S(1)}, f32[16,32,128]{2,1,0:T(8,128)S(1)}, u32[]{:S(2)}, u32[]{:S(2)}) collective-permute-start(f32[16,32,128]{2,1,0:T(8,128)S(1)} %get-tuple-element.72), channel_id=1, source_target_pairs={{0,2},{1,3},{2,0},{3,1},{4,6},{5,7},{6,4},{7,5},{8,10},{9,11},{10,... | collective-permute-start | bytes 786440 | tf_op jit(solution)/shard_map/ppermute | solution.py:34
  64.3 11.1 %collective-permute-start.8 = (f32[16,32,128]{2,1,0:T(8,128)S(1)}, f32[16,32,128]{2,1,0:T(8,128)S(1)}, u32[]{:S(2)}, u32[]{:S(2)}) collective-permute-start(f32[16,32,128]{2,1,0:T(8,128)S(1)} %get-tuple-element.64), channel_id=1, source_target_pairs={{0,2},{1,3},{2,0},{3,1},{4,6},{5,7},{6,4},{7,5},{8,10},{9,11},{10,... | collective-permute-start | bytes 786440 | tf_op jit(solution)/shard_map/ppermute | solution.py:34
  79.2 9.7 %collective-permute-start.10 = (f32[17,32,128]{2,1,0:T(8,128)}, f32[17,32,128]{2,1,0:T(8,128)S(1)}, u32[]{:S(2)}, u32[]{:S(2)}) collective-permute-start(f32[17,32,128]{2,1,0:T(8,128)} %get-tuple-element.34), channel_id=1, source_target_pairs={{0,2},{1,3},{2,0},{3,1},{4,6},{5,7},{6,4},{7,5},{8,10},{9,11},{10,... | collective-permute-start | bytes 835592 | tf_op jit(solution)/shard_map/ppermute | solution.py:34
  81.2 11.6 %collective-permute-start.11 = (f32[16,32,128]{2,1,0:T(8,128)}, f32[16,32,128]{2,1,0:T(8,128)S(1)}, u32[]{:S(2)}, u32[]{:S(2)}) collective-permute-start(f32[16,32,128]{2,1,0:T(8,128)} %get-tuple-element.35), channel_id=1, source_target_pairs={{0,2},{1,3},{2,0},{3,1},{4,6},{5,7},{6,4},{7,5},{8,10},{9,11},{10,... | collective-permute-start | bytes 786440 | tf_op jit(solution)/shard_map/ppermute | solution.py:34
  89.7 5.2 %collective-permute-start.12 = (f32[33,32,128]{2,1,0:T(8,128)S(1)}, f32[33,32,128]{2,1,0:T(8,128)S(1)}, u32[]{:S(2)}, u32[]{:S(2)}) collective-permute-start(f32[33,32,128]{2,1,0:T(8,128)S(1)} %pad_maximum_fusion.1.refs_0_), channel_id=1, source_target_pairs={{0,1},{1,0},{2,3},{3,2},{4,5},{5,4},{6,7},{7,6},{8,9},{9,8},{10,11... | collective-permute-start | bytes 1622024 | tf_op jit(solution)/shard_map/ppermute | solution.py:34
  92.9 2.0 collective-permute-start.13
  102.8 19.1 %collective-permute-start.17 = (f32[32,32,128]{2,1,0:T(8,128)}, f32[32,32,128]{2,1,0:T(8,128)S(1)}, u32[]{:S(2)}, u32[]{:S(2)}) collective-permute-start(f32[32,32,128]{2,1,0:T(8,128)} %get-tuple-element.39), channel_id=1, source_target_pairs={{0,8},{4,12},{8,0},{12,4},{16,24},{20,28},{24,16},{28,20},{1,9},{5... | collective-permute-start | bytes 1572872 | tf_op jit(solution)/shard_map/ppermute | solution.py:34
  110.2 14.4 %collective-permute-start.14 = (f32[33,32,128]{2,1,0:T(8,128)}, f32[33,32,128]{2,1,0:T(8,128)S(1)}, u32[]{:S(2)}, u32[]{:S(2)}) collective-permute-start(f32[33,32,128]{2,1,0:T(8,128)} %get-tuple-element.37), channel_id=1, source_target_pairs={{0,4},{4,0},{8,12},{12,8},{16,20},{20,16},{24,28},{28,24},{1,5},{5... | collective-permute-start | bytes 1622024 | tf_op jit(solution)/shard_map/ppermute | solution.py:34
  123.1 7.1 %collective-permute-start.18 = (f32[16,32,128]{2,1,0:T(8,128)S(1)}, f32[16,32,128]{2,1,0:T(8,128)S(1)}, u32[]{:S(2)}, u32[]{:S(2)}) collective-permute-start(f32[16,32,128]{2,1,0:T(8,128)S(1)} %get-tuple-element.71), channel_id=1, source_target_pairs={{0,4},{4,0},{8,12},{12,8},{16,20},{20,16},{24,28},{28,24},{1,5},{5... | collective-permute-start | bytes 786440 | tf_op jit(solution)/shard_map/ppermute | solution.py:34
  125.7 8.2 %collective-permute-start.15 = (f32[17,32,128]{2,1,0:T(8,128)S(1)}, f32[17,32,128]{2,1,0:T(8,128)S(1)}, u32[]{:S(2)}, u32[]{:S(2)}) collective-permute-start(f32[17,32,128]{2,1,0:T(8,128)S(1)} %slice_add_fusion.1), channel_id=1, source_target_pairs={{0,8},{4,12},{8,0},{12,4},{16,24},{20,28},{24,16},{28,20},{1,9},{5... | collective-permute-start | bytes 835592 | tf_op jit(solution)/shard_map/ppermute | solution.py:34
  130.9 24.8 %collective-permute-start.20 = (f32[8,32,128]{2,1,0:T(8,128)S(1)}, f32[8,32,128]{2,1,0:T(8,128)S(1)}, u32[]{:S(2)}, u32[]{:S(2)}) collective-permute-start(f32[8,32,128]{2,1,0:T(8,128)S(1)} %get-tuple-element.80), channel_id=1, source_target_pairs={{0,16},{4,20},{8,24},{12,28},{16,0},{20,4},{24,8},{28,12},{1,17},{... | collective-permute-start | bytes 393224 | tf_op jit(solution)/shard_map/ppermute | solution.py:34
  134.5 21.2 %collective-permute-start.19 = (f32[8,32,128]{2,1,0:T(8,128)S(1)}, f32[8,32,128]{2,1,0:T(8,128)S(1)}, u32[]{:S(2)}, u32[]{:S(2)}) collective-permute-start(f32[8,32,128]{2,1,0:T(8,128)S(1)} %get-tuple-element.76), channel_id=1, source_target_pairs={{0,16},{4,20},{8,24},{12,28},{16,0},{20,4},{24,8},{28,12},{1,17},{... | collective-permute-start | bytes 393224 | tf_op jit(solution)/shard_map/ppermute | solution.py:34
  136.4 10.6 %collective-permute-start.16 = (f32[32,128]{1,0:T(8,128)S(1)}, f32[32,128]{1,0:T(8,128)S(1)}, u32[]{:S(2)}, u32[]{:S(2)}) collective-permute-start(f32[32,128]{1,0:T(8,128)S(1)} %fusion.4), channel_id=1, source_target_pairs={{0,16},{4,20},{8,24},{12,28},{16,0},{20,4},{24,8},{28,12},{1,17},{... | collective-permute-start | bytes 49160 | tf_op jit(solution)/shard_map/ppermute | solution.py:34
  159.7 13.8 %collective-permute-start.21 = (f32[9,32,128]{2,1,0:T(8,128)}, f32[9,32,128]{2,1,0:T(8,128)S(1)}, u32[]{:S(2)}, u32[]{:S(2)}) collective-permute-start(f32[9,32,128]{2,1,0:T(8,128)} %get-tuple-element.40), channel_id=1, source_target_pairs={{0,16},{4,20},{8,24},{12,28},{16,0},{20,4},{24,8},{28,12},{1,17},{... | collective-permute-start | bytes 442376 | tf_op jit(solution)/shard_map/ppermute | solution.py:34
  160.7 15.2 %collective-permute-start.23 = (f32[8,32,128]{2,1,0:T(8,128)}, f32[8,32,128]{2,1,0:T(8,128)S(1)}, u32[]{:S(2)}, u32[]{:S(2)}) collective-permute-start(f32[8,32,128]{2,1,0:T(8,128)} %get-tuple-element.41), channel_id=1, source_target_pairs={{0,16},{4,20},{8,24},{12,28},{16,0},{20,4},{24,8},{28,12},{1,17},{... | collective-permute-start | bytes 393224 | tf_op jit(solution)/shard_map/ppermute | solution.py:34
  174.3 7.8 %collective-permute-start.22 = (f32[17,32,128]{2,1,0:T(8,128)S(1)}, f32[17,32,128]{2,1,0:T(8,128)S(1)}, u32[]{:S(2)}, u32[]{:S(2)}) collective-permute-start(f32[17,32,128]{2,1,0:T(8,128)S(1)} %pad_maximum_fusion.6), channel_id=1, source_target_pairs={{0,8},{4,12},{8,0},{12,4},{16,24},{20,28},{24,16},{28,20},{1,9},{5... | collective-permute-start | bytes 835592 | tf_op jit(solution)/shard_map/ppermute | solution.py:34
  176.8 9.2 %collective-permute-start.24 = (f32[16,32,128]{2,1,0:T(8,128)S(1)}, f32[16,32,128]{2,1,0:T(8,128)S(1)}, u32[]{:S(2)}, u32[]{:S(2)}) collective-permute-start(f32[16,32,128]{2,1,0:T(8,128)S(1)} %pad_maximum_fusion.8), channel_id=1, source_target_pairs={{0,4},{4,0},{8,12},{12,8},{16,20},{20,16},{24,28},{28,24},{1,5},{5... | collective-permute-start | bytes 786440 | tf_op jit(solution)/shard_map/ppermute | solution.py:34
  182.2 15.2 %collective-permute-start.25 = (f32[33,32,128]{2,1,0:T(8,128)S(1)}, f32[33,32,128]{2,1,0:T(8,128)S(1)}, u32[]{:S(2)}, u32[]{:S(2)}) collective-permute-start(f32[33,32,128]{2,1,0:T(8,128)S(1)} %pad_maximum_fusion.2.refs_0_), channel_id=1, source_target_pairs={{0,4},{4,0},{8,12},{12,8},{16,20},{20,16},{24,28},{28,24},{1,5},{5... | collective-permute-start | bytes 1622024 | tf_op jit(solution)/shard_map/ppermute | solution.py:34
  186.1 11.3 %collective-permute-start.26 = (f32[32,32,128]{2,1,0:T(8,128)S(1)}, f32[32,32,128]{2,1,0:T(8,128)S(1)}, u32[]{:S(2)}, u32[]{:S(2)}) collective-permute-start(f32[32,32,128]{2,1,0:T(8,128)S(1)} %constant_dynamic-update-slice_fusion.2.refs_1_), channel_id=1, source_target_pairs={{0,8},{4,12},{8,0},{12,4},{16,24},{20,28},{24,16},{28,20},{1,9},{5... | collective-permute-start | bytes 1572872 | tf_op jit(solution)/shard_map/ppermute | solution.py:34
  205.4 2.1 collective-permute-start.29
  205.4 11.1 %collective-permute-start.27 = (f32[33,32,128]{2,1,0:T(8,128)}, f32[33,32,128]{2,1,0:T(8,128)S(1)}, u32[]{:S(2)}, u32[]{:S(2)}) collective-permute-start(f32[33,32,128]{2,1,0:T(8,128)} %get-tuple-element.43), channel_id=1, source_target_pairs={{0,1},{1,0},{2,3},{3,2},{4,5},{5,4},{6,7},{7,6},{8,9},{9,8},{10,11... | collective-permute-start | bytes 1622024 | tf_op jit(solution)/shard_map/ppermute | solution.py:34
  209.4 28.5 %collective-permute-start.31 = (f32[16,32,128]{2,1,0:T(8,128)S(1)}, f32[16,32,128]{2,1,0:T(8,128)S(1)}, u32[]{:S(2)}, u32[]{:S(2)}) collective-permute-start(f32[16,32,128]{2,1,0:T(8,128)S(1)} %get-tuple-element.68), channel_id=1, source_target_pairs={{0,2},{1,3},{2,0},{3,1},{4,6},{5,7},{6,4},{7,5},{8,10},{9,11},{10,... | collective-permute-start | bytes 786440 | tf_op jit(solution)/shard_map/ppermute | solution.py:34
  218.3 19.5 %collective-permute-start.30 = (f32[16,32,128]{2,1,0:T(8,128)S(1)}, f32[16,32,128]{2,1,0:T(8,128)S(1)}, u32[]{:S(2)}, u32[]{:S(2)}) collective-permute-start(f32[16,32,128]{2,1,0:T(8,128)S(1)} %get-tuple-element.62), channel_id=1, source_target_pairs={{0,2},{1,3},{2,0},{3,1},{4,6},{5,7},{6,4},{7,5},{8,10},{9,11},{10,... | collective-permute-start | bytes 786440 | tf_op jit(solution)/shard_map/ppermute | solution.py:34
  219.0 10.0 %collective-permute-start.28 = (f32[32,128]{1,0:T(8,128)S(1)}, f32[32,128]{1,0:T(8,128)S(1)}, u32[]{:S(2)}, u32[]{:S(2)}) collective-permute-start(f32[32,128]{1,0:T(8,128)S(1)} %fusion.3), channel_id=1, source_target_pairs={{0,2},{1,3},{2,0},{3,1},{4,6},{5,7},{6,4},{7,5},{8,10},{9,11},{10,... | collective-permute-start | bytes 49160 | tf_op jit(solution)/shard_map/ppermute | solution.py:34
  243.3 9.7 %collective-permute-start.32 = (f32[17,32,128]{2,1,0:T(8,128)}, f32[17,32,128]{2,1,0:T(8,128)S(1)}, u32[]{:S(2)}, u32[]{:S(2)}) collective-permute-start(f32[17,32,128]{2,1,0:T(8,128)} %get-tuple-element.46), channel_id=1, source_target_pairs={{0,2},{1,3},{2,0},{3,1},{4,6},{5,7},{6,4},{7,5},{8,10},{9,11},{10,... | collective-permute-start | bytes 835592 | tf_op jit(solution)/shard_map/ppermute | solution.py:34
  246.1 11.2 %collective-permute-start.33 = (f32[16,32,128]{2,1,0:T(8,128)}, f32[16,32,128]{2,1,0:T(8,128)S(1)}, u32[]{:S(2)}, u32[]{:S(2)}) collective-permute-start(f32[16,32,128]{2,1,0:T(8,128)} %get-tuple-element.47), channel_id=1, source_target_pairs={{0,2},{1,3},{2,0},{3,1},{4,6},{5,7},{6,4},{7,5},{8,10},{9,11},{10,... | collective-permute-start | bytes 786440 | tf_op jit(solution)/shard_map/ppermute | solution.py:34
  253.9 5.4 %collective-permute-start.34 = (f32[33,32,128]{2,1,0:T(8,128)S(1)}, f32[33,32,128]{2,1,0:T(8,128)S(1)}, u32[]{:S(2)}, u32[]{:S(2)}) collective-permute-start(f32[33,32,128]{2,1,0:T(8,128)S(1)} %pad_maximum_fusion.3.refs_0_), channel_id=1, source_target_pairs={{0,1},{1,0},{2,3},{3,2},{4,5},{5,4},{6,7},{7,6},{8,9},{9,8},{10,11... | collective-permute-start | bytes 1622024 | tf_op jit(solution)/shard_map/ppermute | solution.py:34
  257.3 2.0 collective-permute-start.35
  267.3 19.8 %collective-permute-start.40 = (f32[32,32,128]{2,1,0:T(8,128)}, f32[32,32,128]{2,1,0:T(8,128)S(1)}, u32[]{:S(2)}, u32[]{:S(2)}) collective-permute-start(f32[32,32,128]{2,1,0:T(8,128)} %get-tuple-element.52), channel_id=1, source_target_pairs={{0,8},{4,12},{8,0},{12,4},{16,24},{20,28},{24,16},{28,20},{1,9},{5... | collective-permute-start | bytes 1572872 | tf_op jit(solution)/shard_map/ppermute | solution.py:34
  275.3 13.5 %collective-permute-start.36 = (f32[33,32,128]{2,1,0:T(8,128)}, f32[33,32,128]{2,1,0:T(8,128)S(1)}, u32[]{:S(2)}, u32[]{:S(2)}) collective-permute-start(f32[33,32,128]{2,1,0:T(8,128)} %get-tuple-element.49), channel_id=1, source_target_pairs={{0,4},{4,0},{8,12},{12,8},{16,20},{20,16},{24,28},{28,24},{1,5},{5... | collective-permute-start | bytes 1622024 | tf_op jit(solution)/shard_map/ppermute | solution.py:34
  288.1 7.1 %collective-permute-start.41 = (f32[16,32,128]{2,1,0:T(8,128)S(1)}, f32[16,32,128]{2,1,0:T(8,128)S(1)}, u32[]{:S(2)}, u32[]{:S(2)}) collective-permute-start(f32[16,32,128]{2,1,0:T(8,128)S(1)} %get-tuple-element.67), channel_id=1, source_target_pairs={{0,4},{4,0},{8,12},{12,8},{16,20},{20,16},{24,28},{28,24},{1,5},{5... | collective-permute-start | bytes 786440 | tf_op jit(solution)/shard_map/ppermute | solution.py:34
  289.8 6.9 %collective-permute-start.37 = (f32[17,32,128]{2,1,0:T(8,128)S(1)}, f32[17,32,128]{2,1,0:T(8,128)S(1)}, u32[]{:S(2)}, u32[]{:S(2)}) collective-permute-start(f32[17,32,128]{2,1,0:T(8,128)S(1)} %slice_add_fusion), channel_id=1, source_target_pairs={{0,8},{4,12},{8,0},{12,4},{16,24},{20,28},{24,16},{28,20},{1,9},{5... | collective-permute-start | bytes 835592 | tf_op jit(solution)/shard_map/ppermute | solution.py:34
  296.0 27.2 %collective-permute-start.42 = (f32[8,32,128]{2,1,0:T(8,128)S(1)}, f32[8,32,128]{2,1,0:T(8,128)S(1)}, u32[]{:S(2)}, u32[]{:S(2)}) collective-permute-start(f32[8,32,128]{2,1,0:T(8,128)S(1)} %get-tuple-element.79), channel_id=1, source_target_pairs={{0,16},{4,20},{8,24},{12,28},{16,0},{20,4},{24,8},{28,12},{1,17},{... | collective-permute-start | bytes 393224 | tf_op jit(solution)/shard_map/ppermute | solution.py:34
  297.4 25.7 %collective-permute-start.39 = (f32[8,32,128]{2,1,0:T(8,128)S(1)}, f32[8,32,128]{2,1,0:T(8,128)S(1)}, u32[]{:S(2)}, u32[]{:S(2)}) collective-permute-start(f32[8,32,128]{2,1,0:T(8,128)S(1)} %get-tuple-element.75), channel_id=1, source_target_pairs={{0,16},{4,20},{8,24},{12,28},{16,0},{20,4},{24,8},{28,12},{1,17},{... | collective-permute-start | bytes 393224 | tf_op jit(solution)/shard_map/ppermute | solution.py:34
  299.6 12.4 %collective-permute-start.38 = (f32[32,128]{1,0:T(8,128)S(1)}, f32[32,128]{1,0:T(8,128)S(1)}, u32[]{:S(2)}, u32[]{:S(2)}) collective-permute-start(f32[32,128]{1,0:T(8,128)S(1)} %fusion.2), channel_id=1, source_target_pairs={{0,16},{4,20},{8,24},{12,28},{16,0},{20,4},{24,8},{28,12},{1,17},{... | collective-permute-start | bytes 49160 | tf_op jit(solution)/shard_map/ppermute | solution.py:34
  327.8 1.2 collective-permute-start.43
  329.7 9.4 %collective-permute-start.44 = (f32[32,128]{1,0:T(8,128)S(1)}, f32[32,128]{1,0:T(8,128)S(1)}, u32[]{:S(2)}, u32[]{:S(2)}) collective-permute-start(f32[32,128]{1,0:T(8,128)S(1)} %fusion.15), channel_id=1, source_target_pairs={{0,2},{1,3},{2,0},{3,1},{4,6},{5,7},{6,4},{7,5},{8,10},{9,11},{10,... | collective-permute-start | bytes 49160 | tf_op jit(solution)/shard_map/ppermute | solution.py:34
  339.2 3.7 %collective-permute-start.45 = (f32[32,128]{1,0:T(8,128)S(1)}, f32[32,128]{1,0:T(8,128)S(1)}, u32[]{:S(2)}, u32[]{:S(2)}) collective-permute-start(f32[32,128]{1,0:T(8,128)S(1)} %add.204), channel_id=1, source_target_pairs={{0,4},{4,0},{8,12},{12,8},{16,20},{20,16},{24,28},{28,24},{1,5},{5... | collective-permute-start | bytes 49160 | tf_op jit(solution)/shard_map/ppermute | solution.py:34
  342.9 3.7 %collective-permute-start.46 = (f32[32,128]{1,0:T(8,128)S(1)}, f32[32,128]{1,0:T(8,128)S(1)}, u32[]{:S(2)}, u32[]{:S(2)}) collective-permute-start(f32[32,128]{1,0:T(8,128)S(1)} %add.205), channel_id=1, source_target_pairs={{0,8},{4,12},{8,0},{12,4},{16,24},{20,28},{24,16},{28,20},{1,9},{5... | collective-permute-start | bytes 49160 | tf_op jit(solution)/shard_map/ppermute | solution.py:34
  346.7 4.6 %collective-permute-start.47 = (f32[32,128]{1,0:T(8,128)S(1)}, f32[32,128]{1,0:T(8,128)S(1)}, u32[]{:S(2)}, u32[]{:S(2)}) collective-permute-start(f32[32,128]{1,0:T(8,128)S(1)} %add.206), channel_id=1, source_target_pairs={{0,16},{4,20},{8,24},{12,28},{16,0},{20,4},{24,8},{28,12},{1,17},{... | collective-permute-start | bytes 49160 | tf_op jit(solution)/shard_map/ppermute | solution.py:34
  (28 other events, 205.7 us)

commit v4 on v3

--- a/solution.py
+++ b/solution.py
@@ -6,6 +6,7 @@
 from jax.experimental import pallas as pl
 from jax.experimental.pallas import tpu as pltpu
 from jax.sharding import PartitionSpec as P
+
 
 K = 64
 PARTS = 2
@@ -17,6 +18,7 @@
 BATCH = 64
 UNROLL = 64
 HIGHEST = lax.Precision.HIGHEST
+VMEM_SPEC = pl.BlockSpec(memory_space=pltpu.VMEM)
 
 
 def gather_order(axis, part):
@@ -43,13 +45,17 @@
 
 
 def gather(held, axis):
+    held = list(held)
     levels = len(gather_order(axis, 0))
-    for level in range(levels - 1):
+    for level in range(levels - 2):
         got = [exchange(held[part], axis, gather_order(axis, part)[level]) for part in range(PARTS)]
         first = jnp.concatenate([held[0][:-1], got[0][:-1], held[0][-1:] + got[0][-1:]], axis=0)
         held = [first] + [jnp.concatenate([have, more], axis=0) for have, more in zip(held[1:], got[1:])]
-    got = [exchange(held[part], axis, gather_order(axis, part)[-1]) for part in range(PARTS)]
-    return held, got
+    order = [gather_order(axis, part)[-2:] for part in range(PARTS)]
+    near = [exchange(held[part], axis, order[part][0]) for part in range(PARTS)]
+    own = [exchange(held[part], axis, order[part][1]) for part in range(PARTS)]
+    far = [exchange(near[part], axis, order[part][1]) for part in range(PARTS)]
+    return [[held[part], near[part], own[part], far[part]] for part in range(PARTS)]
 
 
 def reduce_scatter(kept, sent, axis):
@@ -85,11 +91,10 @@
 
 
 def tiles_kernel(count, source, target, *refs, places_in, places_out):
-    low_refs, high_refs, refs = refs[:PARTS], refs[PARTS : 2 * PARTS], refs[2 * PARTS :]
+    piece_refs, refs = [refs[4 * part : 4 * part + 4] for part in range(PARTS)], refs[4 * PARTS :]
     tile_ref, keep_refs, send_refs = refs[0], refs[1 : 1 + PARTS], refs[1 + PARTS : 1 + 2 * PARTS]
     pieces, total = refs[1 + 2 * PARTS :]
     step = pl.program_id(0)
-    half_in = low_refs[-1].shape[0]
     half_out = keep_refs[-1].shape[0]
 
     @pl.when(step == 0)
@@ -98,11 +103,10 @@
             starts, quarter = places_in[part]
             band = slice(part * ROWS, (part + 1) * ROWS)
             for at, place in enumerate(starts):
-                ref = (low_refs, low_refs, high_refs, high_refs)[at][part]
-                first = at % 2 * quarter
+                ref = piece_refs[part][at]
 
                 def prepare(block, carry):
-                    value = ref[first + block]
+                    value = ref[block]
                     top = value.astype(jnp.bfloat16)
                     pieces[place + block, band, :TILE] = top
                     pieces[place + block, band, TILE:] = (value - top.astype(jnp.float32)).astype(jnp.bfloat16)
@@ -151,15 +155,15 @@
                     return carry
 
                 lax.fori_loop(0, quarter, finish, 0, unroll=4)
-        gram = low_refs[0][half_in] + high_refs[0][half_in]
+        near, own = piece_refs[0][0].shape[0] - 1, piece_refs[0][2].shape[0] - 1
+        gram = (piece_refs[0][0][near] + piece_refs[0][1][near]) + (piece_refs[0][2][own] + piece_refs[0][3][own])
         keep_refs[0][half_out] = gram
         send_refs[0][half_out] = gram
 
 
-def tiles_product(count, source, target, low, high, tiles, blocks_out, axis_in, axis_out):
-    half_in = low[-1].shape[0]
+def tiles_product(count, source, target, pieces, tiles, blocks_out, axis_in, axis_out):
+    quarter_in = pieces[-1][0].shape[0]
     half_out = blocks_out // 2
-    whole = lambda step, *refs: (0, 0, 0)
     shapes = lambda blocks: [(blocks + (part == 0), ROWS, TILE) for part in range(PARTS)]
 
     def tile_block(step, count, source, target):
@@ -167,7 +171,7 @@
 
     kernel = functools.partial(
         tiles_kernel,
-        places_in=[part_places(axis_in, part, 2 * half_in) for part in range(PARTS)],
+        places_in=[part_places(axis_in, part, 4 * quarter_in) for part in range(PARTS)],
         places_out=[part_places(axis_out, part, 2 * half_out) for part in range(PARTS)],
     )
     out = pl.pallas_call(
@@ -176,16 +180,15 @@
         grid_spec=pltpu.PrefetchScalarGridSpec(
             num_scalar_prefetch=3,
             grid=(tiles.shape[0] // BATCH,),
-            in_specs=[pl.BlockSpec(shape, whole) for shape in shapes(half_in)] * 2
+            in_specs=[VMEM_SPEC] * (4 * PARTS)
             + [pl.BlockSpec((BATCH, TILE, TILE), tile_block)],
-            out_specs=[pl.BlockSpec(shape, whole) for shape in shapes(half_out)] * 2,
+            out_specs=[VMEM_SPEC] * (2 * PARTS),
             scratch_shapes=[
-                pltpu.VMEM((2 * half_in, K, 2 * TILE), jnp.bfloat16),
+                pltpu.VMEM((4 * quarter_in, K, 2 * TILE), jnp.bfloat16),
                 pltpu.VMEM((2 * half_out + 1, K, TILE), jnp.float32),
             ],
         ),
-        name=axis_out + "_tiles",
-    )(count, source, target, *low, *high, tiles)
+    )(count, source, target, *pieces[0], *pieces[1], tiles)
     return out[:PARTS], out[PARTS:]
 
 
@@ -200,43 +203,48 @@
     col = lax.broadcasted_iota(jnp.int32, (K, K), 1)
     gram = jnp.concatenate([gram_ref[:, :K], gram_ref[:, K:]], axis=0) * (1.0 / total)
     work = jnp.concatenate([gram, (row == col).astype(jnp.float32)], axis=1)
-    below = lax.broadcasted_iota(jnp.int32, (K, 1), 0)
-    for at in range(0, K, 2):
-        first, second = work[at : at + 1, :], work[at + 1 : at + 2, :]
-        beside = first[:, at + 1 : at + 2]
-        inverse = 1.0 / first[:, at : at + 1]
-        multiple = beside * inverse
-        pivot = second[:, at + 1 : at + 2] - multiple * beside
-        second = second - multiple * first
-        column = work[:, at : at + 1] * inverse
-        next_column = (work[:, at + 1 : at + 2] - column * beside) * (1.0 / pivot)
-        work = work - jnp.where(below > at, column, 0.0) * first
-        work = work - jnp.where(below > at + 1, next_column, 0.0) * second
+    bands = [work[8 * at : 8 * at + 8] for at in range(K // 8)]
+    place = lax.broadcasted_iota(jnp.int32, (8, 1), 0)
+    for at in range(K):
+        band, inside = divmod(at, 8)
+        pivot_row = bands[band][inside : inside + 1, :]
+        inverse = 1.0 / pivot_row[:, at : at + 1]
+        for under in range(band, K // 8):
+            factor = bands[under][:, at : at + 1] * inverse
+            if under == band:
+                factor = jnp.where(place > inside, factor, 0.0)
+            bands[under] = bands[under] - factor * pivot_row
+    work = jnp.concatenate(bands, axis=0)
     pivots = jnp.sum(jnp.where(row == col, work[:, :K], 0.0), axis=1, keepdims=True)
     out_ref[...] = work[:, K:] * lax.rsqrt(pivots)
 
 
-def turn_kernel(tile_ref, out_ref):
+def turn_kernel(tile_ref, *refs):
+    out_ref = refs[-1]
     for at in range(tile_ref.shape[0]):
         out_ref[at] = tile_ref[at].T
 
 
-def turned_tiles(tiles):
-    block = pl.BlockSpec((32, TILE, TILE), lambda step: (step, 0, 0))
+def turned_tiles(tiles, first, blocks, into):
+    size = tiles.shape[0] // 16
+    block = pl.BlockSpec((size, TILE, TILE), lambda step: (step + first, 0, 0))
     return pl.pallas_call(
         turn_kernel,
         out_shape=jax.ShapeDtypeStruct(tiles.shape, tiles.dtype),
-        grid=(tiles.shape[0] // 32,),
-        in_specs=[block],
+        grid=(blocks,),
+        in_specs=[block] + ([] if into is None else [pl.BlockSpec(memory_space=pl.ANY)]),
         out_specs=block,
+        input_output_aliases={} if into is None else {1: 0},
         name="turned_tiles",
-    )(tiles)
+    )(*([tiles] if into is None else [tiles, into]))
 
 
 def inverse_factor(gram, total):
     return pl.pallas_call(
         functools.partial(factor_kernel, total=total),
         out_shape=jax.ShapeDtypeStruct((K, K), jnp.float32),
+        in_specs=[VMEM_SPEC],
+        out_specs=VMEM_SPEC,
         name="factor",
     )(gram)
 
@@ -269,6 +277,8 @@
         functools.partial(scale_kernel, factored=factored),
         out_shape=[jax.ShapeDtypeStruct((blocks, K, TILE), jnp.float32)]
         + [jax.ShapeDtypeStruct((blocks + (part == 0), ROWS, TILE), jnp.float32) for part in range(PARTS)],
+        in_specs=[VMEM_SPEC] * len(operands),
+        out_specs=[VMEM_SPEC] * (1 + PARTS),
         name="scale_panel",
     )(*operands)
     return panel, sent
@@ -283,6 +293,8 @@
     return pl.pallas_call(
         finish_kernel,
         out_shape=jax.ShapeDtypeStruct((K, panel.shape[0] * TILE), jnp.float32),
+        in_specs=[VMEM_SPEC] * 2,
+        out_specs=VMEM_SPEC,
         name="finish_panel",
     )(inverse, panel)
 
@@ -310,17 +322,18 @@
     start = start_items.astype(jnp.float32).reshape(PARTS, ROWS, item_blocks, TILE).transpose(0, 2, 1, 3)
     start = item_scale[None, :, None, :] * start
     sent = [jnp.concatenate([start[0], jnp.zeros_like(start[0][:1])], axis=0), start[1]]
-    turned = turned_tiles(tiles)
+    turned = turned_tiles(tiles, 0, 8, None)
+    turned = turned_tiles(tiles, 8, 8, turned)
     item_inverse = None
     for step in range(ITERS):
-        low, high = gather(sent, "users")
-        kept, out = tiles_product(count, col_at, row_to, low, high, turned, UT, "users", "items")
+        pieces = gather(sent, "users")
+        kept, out = tiles_product(count, col_at, row_to, pieces, turned, UT, "users", "items")
         kept, got, gram = reduce_scatter(kept, out, "items")
         if step:
             item_inverse = inverse_factor(gram, item_total)
         user_raw, sent = scale_panel(item_inverse, kept, got, user_scale)
-        low, high = gather(sent, "items")
-        kept, out = tiles_product(count, row_at, col_to, low, high, tiles, IT, "items", "users")
+        pieces = gather(sent, "items")
+        kept, out = tiles_product(count, row_at, col_to, pieces, tiles, IT, "items", "users")
         kept, got, gram = reduce_scatter(kept, out, "users")
         user_inverse = inverse_factor(gram, user_total)
         if step == ITERS - 1:

time: 365 us -> 356 us (0.975)
  waiting for transfers between devices: 141 us -> 146 us
  Pallas kernels: 98.5 us -> 93.6 us
  local copies, waits for them, and re-layouts: 13.6 us -> 8.82 us
    pallas_call x4, Pallas kernels: 32.7 us -> 27.1 us  [inverse_factor(): pl.pallas_call(functools.partial(factor_kernel, total=total), out_shape=j...]
    ppermute x48 -> x56, waiting for transfers between devices: 141 us -> 146 us  [exchange(): lax.ppermute(value, axis, [(at, at ^ bit) for at in range(lax.axis_size(a...]
    unnamed x61 -> x82, local copies, waits for them, and re-layouts: 9.78 us -> 7.1 us
    ppermute x48 -> x56, starting transfers between devices: 80.5 us -> 79.9 us  [exchange(): lax.ppermute(value, axis, [(at, at ^ bit) for at in range(lax.axis_size(a...]
    pallas_call x1 -> x2, Pallas kernels: 19.1 us -> 19.8 us  [turned_tiles(): pl.pallas_call(turn_kernel, out_shape=jax.ShapeDtypeStruct(tiles.shape, t...]
  transfers between devices with their start and end apart: 48 -> 56, of which waited for: 33 -> 32; matrix products, arithmetic and copies ran while one was open for 8% -> 6% of each run, Pallas kernels for 13% -> 12%
where the time goes in v4:
time: 356 us; the launch traced here: 354 us
  waiting for transfers between devices  146 us (41%)
  Pallas kernels  93.6 us (26%)
  starting transfers between devices  79.9 us (22%)
  other arithmetic  23.8 us (7%)
  local copies, waits for them, and re-layouts  8.82 us (2%)
    ppermute x56, waiting for transfers between devices, exchange(): lax.ppermute(value, axis, [(at, at ^ bit) for at in range(lax.axis_size(a...  146 us
    ppermute x56, starting transfers between devices, exchange(): lax.ppermute(value, axis, [(at, at ^ bit) for at in range(lax.axis_size(a...  79.9 us
    pallas_call x4, Pallas kernels, tiles_product(): pl.pallas_call(kernel, out_shape=[jax.ShapeDtypeStruct(shape, jnp.float32...  28 us
    pallas_call x4, Pallas kernels, inverse_factor(): pl.pallas_call(functools.partial(factor_kernel, total=total), out_shape=j...  27.1 us
    pallas_call x2, Pallas kernels, turned_tiles(): pl.pallas_call(turn_kernel, out_shape=jax.ShapeDtypeStruct(tiles.shape, t...  19.8 us
    pallas_call x4, Pallas kernels, scale_panel(): pl.pallas_call(functools.partial(scale_kernel, factored=factored), out_sh...  14.2 us
    add x6, other arithmetic, reduce_scatter(): have[half:2 * half] + more[half:2 * half]  8.63 us
  transfers between devices with their start and end apart: 56, of which 32 were waited for; matrix products, arithmetic and copies ran while one was open for 6% of the time, Pallas kernels for 12%

profile of v4, /device:TPU:0, one launch (start us, length us, event | category | flops | bytes accessed | tf_op | source)
XLA Modules:
  0.0 353.6 jit_solution(8548166618790066945)
XLA Ops:
  2.4 4.1 %collective-permute-start = (f32[9,32,128]{2,1,0:T(8,128)S(1)}, f32[9,32,128]{2,1,0:T(8,128)S(1)}, u32[]{:S(2)}, u32[]{:S(2)}) collective-permute-start(f32[9,32,128]{2,1,0:T(8,128)S(1)} %concatenate.15), channel_id=1, source_target_pairs={{0,16},{4,20},{8,24},{12,28},{16,0},{20,4},{24,8},{28,12},{1,17},{... | collective-permute-start | bytes 442376 | tf_op jit(solution)/shard_map/ppermute | solution.py:36
  6.6 10.6 %collective-permute-done = f32[9,32,128]{2,1,0:T(8,128)S(1)} collective-permute-done((f32[9,32,128]{2,1,0:T(8,128)S(1)}, f32[9,32,128]{2,1,0:T(8,128)S(1)}, u32[]{:S(2)}, u32[]{:S(2)}) %collective-permute-start) | collective-permute-done | bytes 147488 | tf_op jit(solution)/shard_map/ppermute | solution.py:36
  17.3 1.9 collective-permute-done.4
  21.4 3.7 %collective-permute-done.1.refs_1_ = f32[17,32,128]{2,1,0:T(8,128)S(1)} collective-permute-done((f32[17,32,128]{2,1,0:T(8,128)S(1)}, f32[17,32,128]{2,1,0:T(8,128)S(1)}, u32[]{:S(2)}, u32[]{:S(2)}) %collective-permute-start.1) | collective-permute-done | bytes 278560 | tf_op jit(solution)/shard_map/ppermute | solution.py:36
  29.8 9.9 %turned_tiles.2.refs_0_ = bf16[512,128,128]{2,1,0:T(8,128)(2,1)} custom-call(bf16[512,128,128]{2,1,0:T(8,128)(2,1)} %bitcast.34), custom_call_target="tpu_custom_call" | custom-call | tf_op jit(solution)/shard_map/turned_tiles/pallas_call | solution.py:231
  39.8 9.9 %turned_tiles.3.refs_8_ = bf16[512,128,128]{2,1,0:T(8,128)(2,1)} custom-call(bf16[512,128,128]{2,1,0:T(8,128)(2,1)} %bitcast.35, bf16[512,128,128]{2,1,0:T(8,128)(2,1)} %turned_tiles.2.refs_0_), custom_call_target="tpu_custom_call", output_to_operand_aliasing={{}: (1, {})} | custom-call | tf_op jit(solution)/shard_map/turned_tiles/pallas_call | solution.py:231
  51.3 7.0 %shard_map.86 = (f32[33,32,128]{2,1,0:T(8,128)}, f32[32,32,128]{2,1,0:T(8,128)}, f32[33,32,128]{2,1,0:T(8,128)}, f32[32,32,128]{2,1,0:T(8,128)}) custom-call(s32[1]{0:T(128)} %bitcast.29.count, s32[512]{0:T(512)} %get-tuple-element.85.source, s32[512]{0:T(512)} %get-tuple-element.58.target, f32[17,32,128]{2,1,0:T(8,128)} %copy-done, ...), custom_call_target="tpu_custom_call" | custom-call | tf_op jit(solution)/shard_map/pallas_call | solution.py:177
  62.2 8.5 %collective-permute-start.11 = (f32[16,32,128]{2,1,0:T(8,128)S(1)}, f32[16,32,128]{2,1,0:T(8,128)S(1)}, u32[]{:S(2)}, u32[]{:S(2)}) collective-permute-start(f32[16,32,128]{2,1,0:T(8,128)S(1)} %get-tuple-element.72), channel_id=1, source_target_pairs={{0,2},{1,3},{2,0},{3,1},{4,6},{5,7},{6,4},{7,5},{8,10},{9,11},{10,... | collective-permute-start | bytes 786440 | tf_op jit(solution)/shard_map/ppermute | solution.py:36
  73.1 4.7 %collective-permute-done.11.refs_3_ = f32[16,32,128]{2,1,0:T(8,128)S(1)} collective-permute-done((f32[16,32,128]{2,1,0:T(8,128)S(1)}, f32[16,32,128]{2,1,0:T(8,128)S(1)}, u32[]{:S(2)}, u32[]{:S(2)}) %collective-permute-start.11) | collective-permute-done | bytes 262176 | tf_op jit(solution)/shard_map/ppermute | solution.py:36
  77.9 5.1 %collective-permute-done.10.refs_2_ = f32[16,32,128]{2,1,0:T(8,128)S(1)} collective-permute-done((f32[16,32,128]{2,1,0:T(8,128)S(1)}, f32[16,32,128]{2,1,0:T(8,128)S(1)}, u32[]{:S(2)}, u32[]{:S(2)}) %collective-permute-start.10) | collective-permute-done | bytes 262176 | tf_op jit(solution)/shard_map/ppermute | solution.py:36
  83.6 3.0 scale_panel.4
  88.7 7.7 %collective-permute-done.12.refs_1_ = f32[17,32,128]{2,1,0:T(8,128)S(1)} collective-permute-done((f32[17,32,128]{2,1,0:T(8,128)}, f32[17,32,128]{2,1,0:T(8,128)S(1)}, u32[]{:S(2)}, u32[]{:S(2)}) %collective-permute-start.12) | collective-permute-done | bytes 278560 | tf_op jit(solution)/shard_map/ppermute | solution.py:36
  96.9 3.7 %collective-permute-done.15.refs_5_ = f32[16,32,128]{2,1,0:T(8,128)S(1)} collective-permute-done((f32[16,32,128]{2,1,0:T(8,128)}, f32[16,32,128]{2,1,0:T(8,128)S(1)}, u32[]{:S(2)}, u32[]{:S(2)}) %collective-permute-start.15) | collective-permute-done | bytes 262176 | tf_op jit(solution)/shard_map/ppermute | solution.py:36
  103.0 7.0 %shard_map.87 = (f32[33,32,128]{2,1,0:T(8,128)}, f32[32,32,128]{2,1,0:T(8,128)}, f32[33,32,128]{2,1,0:T(8,128)}, f32[32,32,128]{2,1,0:T(8,128)}) custom-call(s32[1]{0:T(128)} %bitcast.30.count, s32[512]{0:T(512)} %get-tuple-element.59.source, s32[512]{0:T(512)} %get-tuple-element.84.target, f32[17,32,128]{2,1,0:T(8,128)} %get-tuple-element.34.refs_0_, ...), custom_call_target="tpu_custom_call" | custom-call | tf_op jit(solution)/shard_map/pallas_call | solution.py:177
  110.0 12.2 %collective-permute-done.21 = f32[32,32,128]{2,1,0:T(8,128)S(1)} collective-permute-done((f32[32,32,128]{2,1,0:T(8,128)}, f32[32,32,128]{2,1,0:T(8,128)S(1)}, u32[]{:S(2)}, u32[]{:S(2)}) %collective-permute-start.21) | collective-permute-done | bytes 524320 | tf_op jit(solution)/shard_map/ppermute | solution.py:36
  125.7 5.3 %collective-permute-done.22 = f32[16,32,128]{2,1,0:T(8,128)S(1)} collective-permute-done((f32[16,32,128]{2,1,0:T(8,128)S(1)}, f32[16,32,128]{2,1,0:T(8,128)S(1)}, u32[]{:S(2)}, u32[]{:S(2)}) %collective-permute-start.22) | collective-permute-done | bytes 262176 | tf_op jit(solution)/shard_map/ppermute | solution.py:36
  131.7 12.2 %collective-permute-start.24 = (f32[8,32,128]{2,1,0:T(8,128)S(1)}, f32[8,32,128]{2,1,0:T(8,128)S(1)}, u32[]{:S(2)}, u32[]{:S(2)}) collective-permute-start(f32[8,32,128]{2,1,0:T(8,128)S(1)} %get-tuple-element.80), channel_id=1, source_target_pairs={{0,16},{4,20},{8,24},{12,28},{16,0},{20,4},{24,8},{28,12},{1,17},{... | collective-permute-start | bytes 393224 | tf_op jit(solution)/shard_map/ppermute | solution.py:36
  147.5 7.5 %collective-permute-done.20 = f32[32,128]{1,0:T(8,128)S(1)} collective-permute-done((f32[32,128]{1,0:T(8,128)S(1)}, f32[32,128]{1,0:T(8,128)S(1)}, u32[]{:S(2)}, u32[]{:S(2)}) %collective-permute-start.20) | collective-permute-done | bytes 16416 | tf_op jit(solution)/shard_map/ppermute | solution.py:36
  155.6 6.8 %factor.4.refs_0_ = f32[64,64]{1,0:T(8,128)} custom-call(f32[32,128]{1,0:T(8,128)} %add.160.gram_ref), custom_call_target="tpu_custom_call" | custom-call | tf_op jit(solution)/shard_map/factor/pallas_call | solution.py:243
  163.1 3.3 scale_panel.5
  167.3 3.0 collective-permute-start.29
  171.3 6.9 %collective-permute-done.25 = f32[9,32,128]{2,1,0:T(8,128)S(1)} collective-permute-done((f32[9,32,128]{2,1,0:T(8,128)}, f32[9,32,128]{2,1,0:T(8,128)S(1)}, u32[]{:S(2)}, u32[]{:S(2)}) %collective-permute-start.25) | collective-permute-done | bytes 147488 | tf_op jit(solution)/shard_map/ppermute | solution.py:36
  182.9 4.4 %collective-permute-done.26.refs_1_ = f32[17,32,128]{2,1,0:T(8,128)S(1)} collective-permute-done((f32[17,32,128]{2,1,0:T(8,128)S(1)}, f32[17,32,128]{2,1,0:T(8,128)S(1)}, u32[]{:S(2)}, u32[]{:S(2)}) %collective-permute-start.26) | collective-permute-done | bytes 278560 | tf_op jit(solution)/shard_map/ppermute | solution.py:36
  190.4 7.1 %collective-permute-done.31.refs_6_ = f32[16,32,128]{2,1,0:T(8,128)S(1)} collective-permute-done((f32[16,32,128]{2,1,0:T(8,128)S(1)}, f32[16,32,128]{2,1,0:T(8,128)S(1)}, u32[]{:S(2)}, u32[]{:S(2)}) %collective-permute-start.31) | collective-permute-done | bytes 262176 | tf_op jit(solution)/shard_map/ppermute | solution.py:36
  197.5 3.4 collective-permute-done.32.refs_7_
  201.7 7.0 %shard_map.88 = (f32[33,32,128]{2,1,0:T(8,128)}, f32[32,32,128]{2,1,0:T(8,128)}, f32[33,32,128]{2,1,0:T(8,128)}, f32[32,32,128]{2,1,0:T(8,128)}) custom-call(s32[1]{0:T(128)} %bitcast.31.count, s32[512]{0:T(512)} %get-tuple-element.85.source, s32[512]{0:T(512)} %get-tuple-element.58.target, f32[17,32,128]{2,1,0:T(8,128)} %copy-done.1, ...), custom_call_target="tpu_custom_call" | custom-call | tf_op jit(solution)/shard_map/pallas_call | solution.py:177
  212.6 6.6 %collective-permute-start.37 = (f32[16,32,128]{2,1,0:T(8,128)S(1)}, f32[16,32,128]{2,1,0:T(8,128)S(1)}, u32[]{:S(2)}, u32[]{:S(2)}) collective-permute-start(f32[16,32,128]{2,1,0:T(8,128)S(1)} %get-tuple-element.68), channel_id=1, source_target_pairs={{0,2},{1,3},{2,0},{3,1},{4,6},{5,7},{6,4},{7,5},{8,10},{9,11},{10,... | collective-permute-start | bytes 786440 | tf_op jit(solution)/shard_map/ppermute | solution.py:36
  221.8 2.0 collective-permute-start.34
  223.8 8.0 %collective-permute-done.34 = f32[32,128]{1,0:T(8,128)S(1)} collective-permute-done((f32[32,128]{1,0:T(8,128)S(1)}, f32[32,128]{1,0:T(8,128)S(1)}, u32[]{:S(2)}, u32[]{:S(2)}) %collective-permute-start.34) | collective-permute-done | bytes 16416 | tf_op jit(solution)/shard_map/ppermute | solution.py:36
  232.4 6.8 %factor.5.refs_0_ = f32[64,64]{1,0:T(8,128)} custom-call(f32[32,128]{1,0:T(8,128)} %add.171.gram_ref), custom_call_target="tpu_custom_call" | custom-call | tf_op jit(solution)/shard_map/factor/pallas_call | solution.py:243
  240.0 4.6 %scale_panel.6 = (f32[16,64,128]{2,1,0:T(8,128)}, f32[17,32,128]{2,1,0:T(8,128)}, f32[16,32,128]{2,1,0:T(8,128)}) custom-call(f32[64,64]{1,0:T(8,128)} %factor.5.refs_0_, f32[16,32,128]{2,1,0:T(8,128)} %get-tuple-element.63.refs_1_, f32[16,32,128]{2,1,0:T(8,128)} %get-tuple-element.69.refs_2_, f32[16,32,128]{2,1,0:T(8,128)} %copy-done.29, ...), custom_call_target="tpu_custom_call" | custom-call | tf_op jit(solution)/shard_map/scale_panel/pallas_call | solution.py:276
  246.7 7.7 %collective-permute-done.38.refs_1_ = f32[17,32,128]{2,1,0:T(8,128)S(1)} collective-permute-done((f32[17,32,128]{2,1,0:T(8,128)}, f32[17,32,128]{2,1,0:T(8,128)S(1)}, u32[]{:S(2)}, u32[]{:S(2)}) %collective-permute-start.38) | collective-permute-done | bytes 278560 | tf_op jit(solution)/shard_map/ppermute | solution.py:36
  254.9 3.7 %collective-permute-done.41.refs_5_ = f32[16,32,128]{2,1,0:T(8,128)S(1)} collective-permute-done((f32[16,32,128]{2,1,0:T(8,128)}, f32[16,32,128]{2,1,0:T(8,128)S(1)}, u32[]{:S(2)}, u32[]{:S(2)}) %collective-permute-start.41) | collective-permute-done | bytes 262176 | tf_op jit(solution)/shard_map/ppermute | solution.py:36
  261.0 7.0 %shard_map.89 = (f32[33,32,128]{2,1,0:T(8,128)}, f32[32,32,128]{2,1,0:T(8,128)}, f32[33,32,128]{2,1,0:T(8,128)}, f32[32,32,128]{2,1,0:T(8,128)}) custom-call(s32[1]{0:T(128)} %bitcast.32.count, s32[512]{0:T(512)} %get-tuple-element.59.source, s32[512]{0:T(512)} %get-tuple-element.84.target, f32[17,32,128]{2,1,0:T(8,128)} %get-tuple-element.46.refs_0_, ...), custom_call_target="tpu_custom_call" | custom-call | tf_op jit(solution)/shard_map/pallas_call | solution.py:177
  268.0 2.1 collective-permute-start.44
  270.1 7.7 %collective-permute-done.48 = f32[32,32,128]{2,1,0:T(8,128)S(1)} collective-permute-done((f32[32,32,128]{2,1,0:T(8,128)}, f32[32,32,128]{2,1,0:T(8,128)S(1)}, u32[]{:S(2)}, u32[]{:S(2)}) %collective-permute-start.48) | collective-permute-done | bytes 524320 | tf_op jit(solution)/shard_map/ppermute | solution.py:36
  282.7 4.3 %collective-permute-done.49 = f32[16,32,128]{2,1,0:T(8,128)S(1)} collective-permute-done((f32[16,32,128]{2,1,0:T(8,128)S(1)}, f32[16,32,128]{2,1,0:T(8,128)S(1)}, u32[]{:S(2)}, u32[]{:S(2)}) %collective-permute-start.49) | collective-permute-done | bytes 262176 | tf_op jit(solution)/shard_map/ppermute | solution.py:36
  287.7 13.0 %collective-permute-start.50 = (f32[8,32,128]{2,1,0:T(8,128)S(1)}, f32[8,32,128]{2,1,0:T(8,128)S(1)}, u32[]{:S(2)}, u32[]{:S(2)}) collective-permute-start(f32[8,32,128]{2,1,0:T(8,128)S(1)} %get-tuple-element.79), channel_id=1, source_target_pairs={{0,16},{4,20},{8,24},{12,28},{16,0},{20,4},{24,8},{28,12},{1,17},{... | collective-permute-start | bytes 393224 | tf_op jit(solution)/shard_map/ppermute | solution.py:36
  304.3 7.6 %collective-permute-done.46 = f32[32,128]{1,0:T(8,128)S(1)} collective-permute-done((f32[32,128]{1,0:T(8,128)S(1)}, f32[32,128]{1,0:T(8,128)S(1)}, u32[]{:S(2)}, u32[]{:S(2)}) %collective-permute-start.46) | collective-permute-done | bytes 16416 | tf_op jit(solution)/shard_map/ppermute | solution.py:36
  312.5 6.8 %factor.6.inverse_ref.refs_0_ = f32[64,64]{1,0:T(8,128)} custom-call(f32[32,128]{1,0:T(8,128)} %add.179.gram_ref), custom_call_target="tpu_custom_call" | custom-call | tf_op jit(solution)/shard_map/factor/pallas_call | solution.py:243
  319.3 2.4 finish_panel.2
  322.4 3.3 scale_panel.7
  332.8 3.1 collective-permute-done.53
  336.6 3.0 collective-permute-done.54
  339.6 2.1 collective-permute-start.55
  341.7 2.6 collective-permute-done.55
  344.8 6.8 %factor.7.inverse_ref = f32[64,64]{1,0:T(8,128)} custom-call(f32[32,128]{1,0:T(8,128)} %add.191.gram_ref), custom_call_target="tpu_custom_call" | custom-call | tf_op jit(solution)/shard_map/factor/pallas_call | solution.py:243
  351.6 2.0 finish_panel.3
  (202 shorter events, 72.6 us)
Async XLA Ops:
  2.4 14.8 %collective-permute-start = (f32[9,32,128]{2,1,0:T(8,128)S(1)}, f32[9,32,128]{2,1,0:T(8,128)S(1)}, u32[]{:S(2)}, u32[]{:S(2)}) collective-permute-start(f32[9,32,128]{2,1,0:T(8,128)S(1)} %concatenate.15), channel_id=1, source_target_pairs={{0,16},{4,20},{8,24},{12,28},{16,0},{20,4},{24,8},{28,12},{1,17},{... | collective-permute-start | bytes 442376 | tf_op jit(solution)/shard_map/ppermute | solution.py:36
  6.5 12.7 %collective-permute-start.4 = (f32[8,32,128]{2,1,0:T(8,128)S(1)}, f32[8,32,128]{2,1,0:T(8,128)S(1)}, u32[]{:S(2)}, u32[]{:S(2)}) collective-permute-start(f32[8,32,128]{2,1,0:T(8,128)S(1)} %get-tuple-element.82), channel_id=1, source_target_pairs={{0,16},{4,20},{8,24},{12,28},{16,0},{20,4},{24,8},{28,12},{1,17},{... | collective-permute-start | bytes 393224 | tf_op jit(solution)/shard_map/ppermute | solution.py:36
  17.2 7.9 %collective-permute-start.1 = (f32[17,32,128]{2,1,0:T(8,128)S(1)}, f32[17,32,128]{2,1,0:T(8,128)S(1)}, u32[]{:S(2)}, u32[]{:S(2)}) collective-permute-start(f32[17,32,128]{2,1,0:T(8,128)S(1)} %pad_maximum_fusion.refs_0_), channel_id=1, source_target_pairs={{0,8},{4,12},{8,0},{12,4},{16,24},{20,28},{24,16},{28,20},{1,9},{5... | collective-permute-start | bytes 835592 | tf_op jit(solution)/shard_map/ppermute | solution.py:36
  19.3 9.2 %collective-permute-start.5 = (f32[16,32,128]{2,1,0:T(8,128)S(1)}, f32[16,32,128]{2,1,0:T(8,128)S(1)}, u32[]{:S(2)}, u32[]{:S(2)}) collective-permute-start(f32[16,32,128]{2,1,0:T(8,128)S(1)} %pad_maximum_fusion.2.refs_4_), channel_id=1, source_target_pairs={{0,4},{4,0},{8,12},{12,8},{16,20},{20,16},{24,28},{28,24},{1,5},{5... | collective-permute-start | bytes 786440 | tf_op jit(solution)/shard_map/ppermute | solution.py:36
  20.9 29.4 %collective-permute-start.2 = (f32[17,32,128]{2,1,0:T(8,128)S(1)}, f32[17,32,128]{2,1,0:T(8,128)S(1)}, u32[]{:S(2)}, u32[]{:S(2)}) collective-permute-start(f32[17,32,128]{2,1,0:T(8,128)S(1)} %pad_maximum_fusion.refs_0_), channel_id=1, source_target_pairs={{0,4},{4,0},{8,12},{12,8},{16,20},{20,16},{24,28},{28,24},{1,5},{5... | collective-permute-start | bytes 835592 | tf_op jit(solution)/shard_map/ppermute | solution.py:36
  25.1 25.2 %collective-permute-start.3 = (f32[17,32,128]{2,1,0:T(8,128)S(1)}, f32[17,32,128]{2,1,0:T(8,128)S(1)}, u32[]{:S(2)}, u32[]{:S(2)}) collective-permute-start(f32[17,32,128]{2,1,0:T(8,128)S(1)} %collective-permute-done.1.refs_1_), channel_id=1, source_target_pairs={{0,4},{4,0},{8,12},{12,8},{16,20},{20,16},{24,28},{28,24},{1,5},{5... | collective-permute-start | bytes 835592 | tf_op jit(solution)/shard_map/ppermute | solution.py:36
  26.7 23.6 %collective-permute-start.6 = (f32[16,32,128]{2,1,0:T(8,128)S(1)}, f32[16,32,128]{2,1,0:T(8,128)S(1)}, u32[]{:S(2)}, u32[]{:S(2)}) collective-permute-start(f32[16,32,128]{2,1,0:T(8,128)S(1)} %pad_maximum_fusion.2.refs_4_), channel_id=1, source_target_pairs={{0,8},{4,12},{8,0},{12,4},{16,24},{20,28},{24,16},{28,20},{1,9},{5... | collective-permute-start | bytes 786440 | tf_op jit(solution)/shard_map/ppermute | solution.py:36
  28.5 21.8 %collective-permute-start.7 = (f32[16,32,128]{2,1,0:T(8,128)S(1)}, f32[16,32,128]{2,1,0:T(8,128)S(1)}, u32[]{:S(2)}, u32[]{:S(2)}) collective-permute-start(f32[16,32,128]{2,1,0:T(8,128)S(1)} %collective-permute-done.5.refs_5_), channel_id=1, source_target_pairs={{0,8},{4,12},{8,0},{12,4},{16,24},{20,28},{24,16},{28,20},{1,9},{5... | collective-permute-start | bytes 786440 | tf_op jit(solution)/shard_map/ppermute | solution.py:36
  58.3 12.5 %collective-permute-start.8 = (f32[33,32,128]{2,1,0:T(8,128)}, f32[33,32,128]{2,1,0:T(8,128)S(1)}, u32[]{:S(2)}, u32[]{:S(2)}) collective-permute-start(f32[33,32,128]{2,1,0:T(8,128)} %get-tuple-element.31), channel_id=1, source_target_pairs={{0,1},{1,0},{2,3},{3,2},{4,5},{5,4},{6,7},{7,6},{8,9},{9,8},{10,11... | collective-permute-start | bytes 1622024 | tf_op jit(solution)/shard_map/ppermute | solution.py:36
  62.2 15.7 %collective-permute-start.11 = (f32[16,32,128]{2,1,0:T(8,128)S(1)}, f32[16,32,128]{2,1,0:T(8,128)S(1)}, u32[]{:S(2)}, u32[]{:S(2)}) collective-permute-start(f32[16,32,128]{2,1,0:T(8,128)S(1)} %get-tuple-element.72), channel_id=1, source_target_pairs={{0,2},{1,3},{2,0},{3,1},{4,6},{5,7},{6,4},{7,5},{8,10},{9,11},{10,... | collective-permute-start | bytes 786440 | tf_op jit(solution)/shard_map/ppermute | solution.py:36
  72.5 10.4 %collective-permute-start.10 = (f32[16,32,128]{2,1,0:T(8,128)S(1)}, f32[16,32,128]{2,1,0:T(8,128)S(1)}, u32[]{:S(2)}, u32[]{:S(2)}) collective-permute-start(f32[16,32,128]{2,1,0:T(8,128)S(1)} %get-tuple-element.64), channel_id=1, source_target_pairs={{0,2},{1,3},{2,0},{3,1},{4,6},{5,7},{6,4},{7,5},{8,10},{9,11},{10,... | collective-permute-start | bytes 786440 | tf_op jit(solution)/shard_map/ppermute | solution.py:36
  86.7 9.7 %collective-permute-start.12 = (f32[17,32,128]{2,1,0:T(8,128)}, f32[17,32,128]{2,1,0:T(8,128)S(1)}, u32[]{:S(2)}, u32[]{:S(2)}) collective-permute-start(f32[17,32,128]{2,1,0:T(8,128)} %get-tuple-element.34.refs_0_), channel_id=1, source_target_pairs={{0,2},{1,3},{2,0},{3,1},{4,6},{5,7},{6,4},{7,5},{8,10},{9,11},{10,... | collective-permute-start | bytes 835592 | tf_op jit(solution)/shard_map/ppermute | solution.py:36
  88.4 12.2 %collective-permute-start.15 = (f32[16,32,128]{2,1,0:T(8,128)}, f32[16,32,128]{2,1,0:T(8,128)S(1)}, u32[]{:S(2)}, u32[]{:S(2)}) collective-permute-start(f32[16,32,128]{2,1,0:T(8,128)} %get-tuple-element.35.refs_4_), channel_id=1, source_target_pairs={{0,2},{1,3},{2,0},{3,1},{4,6},{5,7},{6,4},{7,5},{8,10},{9,11},{10,... | collective-permute-start | bytes 786440 | tf_op jit(solution)/shard_map/ppermute | solution.py:36
  88.7 11.9 %collective-permute-start.13 = (f32[17,32,128]{2,1,0:T(8,128)}, f32[17,32,128]{2,1,0:T(8,128)S(1)}, u32[]{:S(2)}, u32[]{:S(2)}) collective-permute-start(f32[17,32,128]{2,1,0:T(8,128)} %get-tuple-element.34.refs_0_), channel_id=1, source_target_pairs={{0,1},{1,0},{2,3},{3,2},{4,5},{5,4},{6,7},{7,6},{8,9},{9,8},{10,11... | collective-permute-start | bytes 835592 | tf_op jit(solution)/shard_map/ppermute | solution.py:36
  96.4 5.8 %collective-permute-start.14 = (f32[17,32,128]{2,1,0:T(8,128)S(1)}, f32[17,32,128]{2,1,0:T(8,128)S(1)}, u32[]{:S(2)}, u32[]{:S(2)}) collective-permute-start(f32[17,32,128]{2,1,0:T(8,128)S(1)} %collective-permute-done.12.refs_1_), channel_id=1, source_target_pairs={{0,1},{1,0},{2,3},{3,2},{4,5},{5,4},{6,7},{7,6},{8,9},{9,8},{10,11... | collective-permute-start | bytes 835592 | tf_op jit(solution)/shard_map/ppermute | solution.py:36
  96.4 4.2 %collective-permute-start.16 = (f32[16,32,128]{2,1,0:T(8,128)}, f32[16,32,128]{2,1,0:T(8,128)S(1)}, u32[]{:S(2)}, u32[]{:S(2)}) collective-permute-start(f32[16,32,128]{2,1,0:T(8,128)} %get-tuple-element.35.refs_4_), channel_id=1, source_target_pairs={{0,1},{1,0},{2,3},{3,2},{4,5},{5,4},{6,7},{7,6},{8,9},{9,8},{10,11... | collective-permute-start | bytes 786440 | tf_op jit(solution)/shard_map/ppermute | solution.py:36
  110.0 12.3 %collective-permute-start.21 = (f32[32,32,128]{2,1,0:T(8,128)}, f32[32,32,128]{2,1,0:T(8,128)S(1)}, u32[]{:S(2)}, u32[]{:S(2)}) collective-permute-start(f32[32,32,128]{2,1,0:T(8,128)} %get-tuple-element.39), channel_id=1, source_target_pairs={{0,8},{4,12},{8,0},{12,4},{16,24},{20,28},{24,16},{28,20},{1,9},{5... | collective-permute-start | bytes 1572872 | tf_op jit(solution)/shard_map/ppermute | solution.py:36
  110.0 13.5 %collective-permute-start.18 = (f32[33,32,128]{2,1,0:T(8,128)}, f32[33,32,128]{2,1,0:T(8,128)S(1)}, u32[]{:S(2)}, u32[]{:S(2)}) collective-permute-start(f32[33,32,128]{2,1,0:T(8,128)} %get-tuple-element.37), channel_id=1, source_target_pairs={{0,4},{4,0},{8,12},{12,8},{16,20},{20,16},{24,28},{28,24},{1,5},{5... | collective-permute-start | bytes 1622024 | tf_op jit(solution)/shard_map/ppermute | solution.py:36
  123.3 7.7 %collective-permute-start.22 = (f32[16,32,128]{2,1,0:T(8,128)S(1)}, f32[16,32,128]{2,1,0:T(8,128)S(1)}, u32[]{:S(2)}, u32[]{:S(2)}) collective-permute-start(f32[16,32,128]{2,1,0:T(8,128)S(1)} %get-tuple-element.71), channel_id=1, source_target_pairs={{0,4},{4,0},{8,12},{12,8},{16,20},{20,16},{24,28},{28,24},{1,5},{5... | collective-permute-start | bytes 786440 | tf_op jit(solution)/shard_map/ppermute | solution.py:36
  124.4 19.4 %collective-permute-start.19 = (f32[17,32,128]{2,1,0:T(8,128)S(1)}, f32[17,32,128]{2,1,0:T(8,128)S(1)}, u32[]{:S(2)}, u32[]{:S(2)}) collective-permute-start(f32[17,32,128]{2,1,0:T(8,128)S(1)} %slice_add_fusion.1), channel_id=1, source_target_pairs={{0,8},{4,12},{8,0},{12,4},{16,24},{20,28},{24,16},{28,20},{1,9},{5... | collective-permute-start | bytes 835592 | tf_op jit(solution)/shard_map/ppermute | solution.py:36
  131.7 30.7 %collective-permute-start.24 = (f32[8,32,128]{2,1,0:T(8,128)S(1)}, f32[8,32,128]{2,1,0:T(8,128)S(1)}, u32[]{:S(2)}, u32[]{:S(2)}) collective-permute-start(f32[8,32,128]{2,1,0:T(8,128)S(1)} %get-tuple-element.80), channel_id=1, source_target_pairs={{0,16},{4,20},{8,24},{12,28},{16,0},{20,4},{24,8},{28,12},{1,17},{... | collective-permute-start | bytes 393224 | tf_op jit(solution)/shard_map/ppermute | solution.py:36
  144.6 17.8 %collective-permute-start.23 = (f32[8,32,128]{2,1,0:T(8,128)S(1)}, f32[8,32,128]{2,1,0:T(8,128)S(1)}, u32[]{:S(2)}, u32[]{:S(2)}) collective-permute-start(f32[8,32,128]{2,1,0:T(8,128)S(1)} %get-tuple-element.76), channel_id=1, source_target_pairs={{0,16},{4,20},{8,24},{12,28},{16,0},{20,4},{24,8},{28,12},{1,17},{... | collective-permute-start | bytes 393224 | tf_op jit(solution)/shard_map/ppermute | solution.py:36
  146.5 8.5 %collective-permute-start.20 = (f32[32,128]{1,0:T(8,128)S(1)}, f32[32,128]{1,0:T(8,128)S(1)}, u32[]{:S(2)}, u32[]{:S(2)}) collective-permute-start(f32[32,128]{1,0:T(8,128)S(1)} %fusion.3), channel_id=1, source_target_pairs={{0,16},{4,20},{8,24},{12,28},{16,0},{20,4},{24,8},{28,12},{1,17},{... | collective-permute-start | bytes 49160 | tf_op jit(solution)/shard_map/ppermute | solution.py:36
  166.4 11.8 %collective-permute-start.25 = (f32[9,32,128]{2,1,0:T(8,128)}, f32[9,32,128]{2,1,0:T(8,128)S(1)}, u32[]{:S(2)}, u32[]{:S(2)}) collective-permute-start(f32[9,32,128]{2,1,0:T(8,128)} %get-tuple-element.40), channel_id=1, source_target_pairs={{0,16},{4,20},{8,24},{12,28},{16,0},{20,4},{24,8},{28,12},{1,17},{... | collective-permute-start | bytes 442376 | tf_op jit(solution)/shard_map/ppermute | solution.py:36
  167.3 13.5 %collective-permute-start.29 = (f32[8,32,128]{2,1,0:T(8,128)}, f32[8,32,128]{2,1,0:T(8,128)S(1)}, u32[]{:S(2)}, u32[]{:S(2)}) collective-permute-start(f32[8,32,128]{2,1,0:T(8,128)} %get-tuple-element.41), channel_id=1, source_target_pairs={{0,16},{4,20},{8,24},{12,28},{16,0},{20,4},{24,8},{28,12},{1,17},{... | collective-permute-start | bytes 393224 | tf_op jit(solution)/shard_map/ppermute | solution.py:36
  179.0 8.3 %collective-permute-start.26 = (f32[17,32,128]{2,1,0:T(8,128)S(1)}, f32[17,32,128]{2,1,0:T(8,128)S(1)}, u32[]{:S(2)}, u32[]{:S(2)}) collective-permute-start(f32[17,32,128]{2,1,0:T(8,128)S(1)} %pad_maximum_fusion.1.refs_0_), channel_id=1, source_target_pairs={{0,8},{4,12},{8,0},{12,4},{16,24},{20,28},{24,16},{28,20},{1,9},{5... | collective-permute-start | bytes 835592 | tf_op jit(solution)/shard_map/ppermute | solution.py:36
  180.8 9.2 %collective-permute-start.30 = (f32[16,32,128]{2,1,0:T(8,128)S(1)}, f32[16,32,128]{2,1,0:T(8,128)S(1)}, u32[]{:S(2)}, u32[]{:S(2)}) collective-permute-start(f32[16,32,128]{2,1,0:T(8,128)S(1)} %constant_dynamic-update-slice_fusion.refs_4_), channel_id=1, source_target_pairs={{0,4},{4,0},{8,12},{12,8},{16,20},{20,16},{24,28},{28,24},{1,5},{5... | collective-permute-start | bytes 786440 | tf_op jit(solution)/shard_map/ppermute | solution.py:36
  181.8 15.7 %collective-permute-start.27 = (f32[17,32,128]{2,1,0:T(8,128)S(1)}, f32[17,32,128]{2,1,0:T(8,128)S(1)}, u32[]{:S(2)}, u32[]{:S(2)}) collective-permute-start(f32[17,32,128]{2,1,0:T(8,128)S(1)} %pad_maximum_fusion.1.refs_0_), channel_id=1, source_target_pairs={{0,4},{4,0},{8,12},{12,8},{16,20},{20,16},{24,28},{28,24},{1,5},{5... | collective-permute-start | bytes 835592 | tf_op jit(solution)/shard_map/ppermute | solution.py:36
  187.3 13.6 %collective-permute-start.28 = (f32[17,32,128]{2,1,0:T(8,128)S(1)}, f32[17,32,128]{2,1,0:T(8,128)S(1)}, u32[]{:S(2)}, u32[]{:S(2)}) collective-permute-start(f32[17,32,128]{2,1,0:T(8,128)S(1)} %collective-permute-done.26.refs_1_), channel_id=1, source_target_pairs={{0,4},{4,0},{8,12},{12,8},{16,20},{20,16},{24,28},{28,24},{1,5},{5... | collective-permute-start | bytes 835592 | tf_op jit(solution)/shard_map/ppermute | solution.py:36
  188.3 9.2 %collective-permute-start.31 = (f32[16,32,128]{2,1,0:T(8,128)S(1)}, f32[16,32,128]{2,1,0:T(8,128)S(1)}, u32[]{:S(2)}, u32[]{:S(2)}) collective-permute-start(f32[16,32,128]{2,1,0:T(8,128)S(1)} %constant_dynamic-update-slice_fusion.refs_4_), channel_id=1, source_target_pairs={{0,8},{4,12},{8,0},{12,4},{16,24},{20,28},{24,16},{28,20},{1,9},{5... | collective-permute-start | bytes 786440 | tf_op jit(solution)/shard_map/ppermute | solution.py:36
  190.1 10.8 %collective-permute-start.32 = (f32[16,32,128]{2,1,0:T(8,128)S(1)}, f32[16,32,128]{2,1,0:T(8,128)S(1)}, u32[]{:S(2)}, u32[]{:S(2)}) collective-permute-start(f32[16,32,128]{2,1,0:T(8,128)S(1)} %collective-permute-done.30.refs_5_), channel_id=1, source_target_pairs={{0,8},{4,12},{8,0},{12,4},{16,24},{20,28},{24,16},{28,20},{1,9},{5... | collective-permute-start | bytes 786440 | tf_op jit(solution)/shard_map/ppermute | solution.py:36
  208.7 10.5 %collective-permute-start.33 = (f32[33,32,128]{2,1,0:T(8,128)}, f32[33,32,128]{2,1,0:T(8,128)S(1)}, u32[]{:S(2)}, u32[]{:S(2)}) collective-permute-start(f32[33,32,128]{2,1,0:T(8,128)} %get-tuple-element.43), channel_id=1, source_target_pairs={{0,1},{1,0},{2,3},{3,2},{4,5},{5,4},{6,7},{7,6},{8,9},{9,8},{10,11... | collective-permute-start | bytes 1622024 | tf_op jit(solution)/shard_map/ppermute | solution.py:36
  212.6 26.6 %collective-permute-start.37 = (f32[16,32,128]{2,1,0:T(8,128)S(1)}, f32[16,32,128]{2,1,0:T(8,128)S(1)}, u32[]{:S(2)}, u32[]{:S(2)}) collective-permute-start(f32[16,32,128]{2,1,0:T(8,128)S(1)} %get-tuple-element.68), channel_id=1, source_target_pairs={{0,2},{1,3},{2,0},{3,1},{4,6},{5,7},{6,4},{7,5},{8,10},{9,11},{10,... | collective-permute-start | bytes 786440 | tf_op jit(solution)/shard_map/ppermute | solution.py:36
  221.1 18.2 %collective-permute-start.36 = (f32[16,32,128]{2,1,0:T(8,128)S(1)}, f32[16,32,128]{2,1,0:T(8,128)S(1)}, u32[]{:S(2)}, u32[]{:S(2)}) collective-permute-start(f32[16,32,128]{2,1,0:T(8,128)S(1)} %get-tuple-element.62), channel_id=1, source_target_pairs={{0,2},{1,3},{2,0},{3,1},{4,6},{5,7},{6,4},{7,5},{8,10},{9,11},{10,... | collective-permute-start | bytes 786440 | tf_op jit(solution)/shard_map/ppermute | solution.py:36
  221.8 10.0 %collective-permute-start.34 = (f32[32,128]{1,0:T(8,128)S(1)}, f32[32,128]{1,0:T(8,128)S(1)}, u32[]{:S(2)}, u32[]{:S(2)}) collective-permute-start(f32[32,128]{1,0:T(8,128)S(1)} %fusion.2), channel_id=1, source_target_pairs={{0,2},{1,3},{2,0},{3,1},{4,6},{5,7},{6,4},{7,5},{8,10},{9,11},{10,... | collective-permute-start | bytes 49160 | tf_op jit(solution)/shard_map/ppermute | solution.py:36
  244.6 9.7 %collective-permute-start.38 = (f32[17,32,128]{2,1,0:T(8,128)}, f32[17,32,128]{2,1,0:T(8,128)S(1)}, u32[]{:S(2)}, u32[]{:S(2)}) collective-permute-start(f32[17,32,128]{2,1,0:T(8,128)} %get-tuple-element.46.refs_0_), channel_id=1, source_target_pairs={{0,2},{1,3},{2,0},{3,1},{4,6},{5,7},{6,4},{7,5},{8,10},{9,11},{10,... | collective-permute-start | bytes 835592 | tf_op jit(solution)/shard_map/ppermute | solution.py:36
  246.4 12.2 %collective-permute-start.41 = (f32[16,32,128]{2,1,0:T(8,128)}, f32[16,32,128]{2,1,0:T(8,128)S(1)}, u32[]{:S(2)}, u32[]{:S(2)}) collective-permute-start(f32[16,32,128]{2,1,0:T(8,128)} %get-tuple-element.47.refs_4_), channel_id=1, source_target_pairs={{0,2},{1,3},{2,0},{3,1},{4,6},{5,7},{6,4},{7,5},{8,10},{9,11},{10,... | collective-permute-start | bytes 786440 | tf_op jit(solution)/shard_map/ppermute | solution.py:36
  246.7 11.9 %collective-permute-start.39 = (f32[17,32,128]{2,1,0:T(8,128)}, f32[17,32,128]{2,1,0:T(8,128)S(1)}, u32[]{:S(2)}, u32[]{:S(2)}) collective-permute-start(f32[17,32,128]{2,1,0:T(8,128)} %get-tuple-element.46.refs_0_), channel_id=1, source_target_pairs={{0,1},{1,0},{2,3},{3,2},{4,5},{5,4},{6,7},{7,6},{8,9},{9,8},{10,11... | collective-permute-start | bytes 835592 | tf_op jit(solution)/shard_map/ppermute | solution.py:36
  254.4 5.8 %collective-permute-start.40 = (f32[17,32,128]{2,1,0:T(8,128)S(1)}, f32[17,32,128]{2,1,0:T(8,128)S(1)}, u32[]{:S(2)}, u32[]{:S(2)}) collective-permute-start(f32[17,32,128]{2,1,0:T(8,128)S(1)} %collective-permute-done.38.refs_1_), channel_id=1, source_target_pairs={{0,1},{1,0},{2,3},{3,2},{4,5},{5,4},{6,7},{7,6},{8,9},{9,8},{10,11... | collective-permute-start | bytes 835592 | tf_op jit(solution)/shard_map/ppermute | solution.py:36
  254.4 4.2 %collective-permute-start.42 = (f32[16,32,128]{2,1,0:T(8,128)}, f32[16,32,128]{2,1,0:T(8,128)S(1)}, u32[]{:S(2)}, u32[]{:S(2)}) collective-permute-start(f32[16,32,128]{2,1,0:T(8,128)} %get-tuple-element.47.refs_4_), channel_id=1, source_target_pairs={{0,1},{1,0},{2,3},{3,2},{4,5},{5,4},{6,7},{7,6},{8,9},{9,8},{10,11... | collective-permute-start | bytes 786440 | tf_op jit(solution)/shard_map/ppermute | solution.py:36
  268.0 9.8 %collective-permute-start.48 = (f32[32,32,128]{2,1,0:T(8,128)}, f32[32,32,128]{2,1,0:T(8,128)S(1)}, u32[]{:S(2)}, u32[]{:S(2)}) collective-permute-start(f32[32,32,128]{2,1,0:T(8,128)} %get-tuple-element.52), channel_id=1, source_target_pairs={{0,8},{4,12},{8,0},{12,4},{16,24},{20,28},{24,16},{28,20},{1,9},{5... | collective-permute-start | bytes 1572872 | tf_op jit(solution)/shard_map/ppermute | solution.py:36
  268.0 12.6 %collective-permute-start.44 = (f32[33,32,128]{2,1,0:T(8,128)}, f32[33,32,128]{2,1,0:T(8,128)S(1)}, u32[]{:S(2)}, u32[]{:S(2)}) collective-permute-start(f32[33,32,128]{2,1,0:T(8,128)} %get-tuple-element.49), channel_id=1, source_target_pairs={{0,4},{4,0},{8,12},{12,8},{16,20},{20,16},{24,28},{28,24},{1,5},{5... | collective-permute-start | bytes 1622024 | tf_op jit(solution)/shard_map/ppermute | solution.py:36
  278.9 8.1 %collective-permute-start.49 = (f32[16,32,128]{2,1,0:T(8,128)S(1)}, f32[16,32,128]{2,1,0:T(8,128)S(1)}, u32[]{:S(2)}, u32[]{:S(2)}) collective-permute-start(f32[16,32,128]{2,1,0:T(8,128)S(1)} %get-tuple-element.67), channel_id=1, source_target_pairs={{0,4},{4,0},{8,12},{12,8},{16,20},{20,16},{24,28},{28,24},{1,5},{5... | collective-permute-start | bytes 786440 | tf_op jit(solution)/shard_map/ppermute | solution.py:36
  281.6 19.1 %collective-permute-start.45 = (f32[17,32,128]{2,1,0:T(8,128)S(1)}, f32[17,32,128]{2,1,0:T(8,128)S(1)}, u32[]{:S(2)}, u32[]{:S(2)}) collective-permute-start(f32[17,32,128]{2,1,0:T(8,128)S(1)} %slice_add_fusion), channel_id=1, source_target_pairs={{0,8},{4,12},{8,0},{12,4},{16,24},{20,28},{24,16},{28,20},{1,9},{5... | collective-permute-start | bytes 835592 | tf_op jit(solution)/shard_map/ppermute | solution.py:36
  287.7 34.1 %collective-permute-start.50 = (f32[8,32,128]{2,1,0:T(8,128)S(1)}, f32[8,32,128]{2,1,0:T(8,128)S(1)}, u32[]{:S(2)}, u32[]{:S(2)}) collective-permute-start(f32[8,32,128]{2,1,0:T(8,128)S(1)} %get-tuple-element.79), channel_id=1, source_target_pairs={{0,16},{4,20},{8,24},{12,28},{16,0},{20,4},{24,8},{28,12},{1,17},{... | collective-permute-start | bytes 393224 | tf_op jit(solution)/shard_map/ppermute | solution.py:36
  301.4 20.3 %collective-permute-start.47 = (f32[8,32,128]{2,1,0:T(8,128)S(1)}, f32[8,32,128]{2,1,0:T(8,128)S(1)}, u32[]{:S(2)}, u32[]{:S(2)}) collective-permute-start(f32[8,32,128]{2,1,0:T(8,128)S(1)} %get-tuple-element.75), channel_id=1, source_target_pairs={{0,16},{4,20},{8,24},{12,28},{16,0},{20,4},{24,8},{28,12},{1,17},{... | collective-permute-start | bytes 393224 | tf_op jit(solution)/shard_map/ppermute | solution.py:36
  302.4 9.5 %collective-permute-start.46 = (f32[32,128]{1,0:T(8,128)S(1)}, f32[32,128]{1,0:T(8,128)S(1)}, u32[]{:S(2)}, u32[]{:S(2)}) collective-permute-start(f32[32,128]{1,0:T(8,128)S(1)} %fusion.1), channel_id=1, source_target_pairs={{0,16},{4,20},{8,24},{12,28},{16,0},{20,4},{24,8},{28,12},{1,17},{... | collective-permute-start | bytes 49160 | tf_op jit(solution)/shard_map/ppermute | solution.py:36
  339.6 4.6 %collective-permute-start.55 = (f32[32,128]{1,0:T(8,128)S(1)}, f32[32,128]{1,0:T(8,128)S(1)}, u32[]{:S(2)}, u32[]{:S(2)}) collective-permute-start(f32[32,128]{1,0:T(8,128)S(1)} %add.190), channel_id=1, source_target_pairs={{0,16},{4,20},{8,24},{12,28},{16,0},{20,4},{24,8},{28,12},{1,17},{... | collective-permute-start | bytes 49160 | tf_op jit(solution)/shard_map/ppermute | solution.py:36
  (48 other events, 280.9 us)

commit v5 on v4

--- a/solution.py
+++ b/solution.py
@@ -9,9 +9,10 @@
 
 
 K = 64
-PARTS = 2
+PARTS = 4
 ROWS = K // PARTS
 TILE = 128
+GRAM = K // 2 // ROWS
 ITERS = 2
 UT = 64
 IT = 64
@@ -27,7 +28,7 @@
     while bit:
         order.append(bit)
         bit >>= 1
-    if axis == "users" and part == 1:
+    if axis == "users" and part % 2 == 1:
         order[-2:] = order[-2:][::-1]
     return order
 
@@ -48,32 +49,32 @@
     held = list(held)
     levels = len(gather_order(axis, 0))
     for level in range(levels - 2):
-        got = [exchange(held[part], axis, gather_order(axis, part)[level]) for part in range(PARTS)]
-        first = jnp.concatenate([held[0][:-1], got[0][:-1], held[0][-1:] + got[0][-1:]], axis=0)
+        got = []
+        for part in range(PARTS):
+            got.append(exchange(held[part], axis, gather_order(axis, part)[level]))
+        first = jnp.concatenate([held[0][:-GRAM], got[0][:-GRAM], held[0][-GRAM:] + got[0][-GRAM:]], axis=0)
         held = [first] + [jnp.concatenate([have, more], axis=0) for have, more in zip(held[1:], got[1:])]
     order = [gather_order(axis, part)[-2:] for part in range(PARTS)]
-    near = [exchange(held[part], axis, order[part][0]) for part in range(PARTS)]
-    own = [exchange(held[part], axis, order[part][1]) for part in range(PARTS)]
-    far = [exchange(near[part], axis, order[part][1]) for part in range(PARTS)]
+    near, own, far = [], [], []
+    for part in range(PARTS):
+        near.append(exchange(held[part], axis, order[part][0]))
+        own.append(exchange(held[part], axis, order[part][1]))
+    for part in range(PARTS):
+        far.append(exchange(near[part], axis, order[part][1]))
     return [[held[part], near[part], own[part], far[part]] for part in range(PARTS)]
 
 
-def reduce_scatter(kept, sent, axis):
-    levels = len(gather_order(axis, 0))
-    for level in range(levels - 1, 0, -1):
-        got = [exchange(sent[part], axis, gather_order(axis, part)[level]) for part in range(PARTS)]
-        half = kept[-1].shape[0] // 2
-        if level == 1:
-            gram = kept[0][-1] + got[0][-1]
-            sent = [have[half : 2 * half] + more[half : 2 * half] for have, more in zip(kept, got)]
-            kept = [have[:half] + more[:half] for have, more in zip(kept, got)]
-        else:
+def reduce_scatter(kept, sent, gram, axis):
+    for level in range(len(gather_order(axis, 0)) - 1, -1, -1):
+        other = exchange(gram, axis, gather_order(axis, 0)[level])
+        got = []
+        for part in range(PARTS):
+            got.append(exchange(sent[part], axis, gather_order(axis, part)[level]))
+        gram = gram + other
+        if level:
+            half = kept[0].shape[0] // 2
             sent = [have[half:] + more[half:] for have, more in zip(kept, got)]
             kept = [have[:half] + more[:half] for have, more in zip(kept, got)]
-            kept[0] = jnp.concatenate([kept[0], sent[0][-1:]], axis=0)
-    bit = gather_order(axis, 0)[0]
-    gram = gram + exchange(gram, axis, bit)
-    got = [exchange(out, axis, bit) for out in sent]
     return kept, got, gram
 
 
@@ -93,7 +94,7 @@
 def tiles_kernel(count, source, target, *refs, places_in, places_out):
     piece_refs, refs = [refs[4 * part : 4 * part + 4] for part in range(PARTS)], refs[4 * PARTS :]
     tile_ref, keep_refs, send_refs = refs[0], refs[1 : 1 + PARTS], refs[1 + PARTS : 1 + 2 * PARTS]
-    pieces, total = refs[1 + 2 * PARTS :]
+    gram_ref, pieces, total = refs[1 + 2 * PARTS :]
     step = pl.program_id(0)
     half_out = keep_refs[-1].shape[0]
 
@@ -155,16 +156,14 @@
                     return carry
 
                 lax.fori_loop(0, quarter, finish, 0, unroll=4)
-        near, own = piece_refs[0][0].shape[0] - 1, piece_refs[0][2].shape[0] - 1
-        gram = (piece_refs[0][0][near] + piece_refs[0][1][near]) + (piece_refs[0][2][own] + piece_refs[0][3][own])
-        keep_refs[0][half_out] = gram
-        send_refs[0][half_out] = gram
+        for at in range(GRAM):
+            held, near, own, far = [ref[ref.shape[0] - GRAM + at] for ref in piece_refs[0]]
+            gram_ref[at * ROWS : (at + 1) * ROWS] = (held + near) + (own + far)
 
 
 def tiles_product(count, source, target, pieces, tiles, blocks_out, axis_in, axis_out):
     quarter_in = pieces[-1][0].shape[0]
     half_out = blocks_out // 2
-    shapes = lambda blocks: [(blocks + (part == 0), ROWS, TILE) for part in range(PARTS)]
 
     def tile_block(step, count, source, target):
         return (jnp.minimum(step, (count[0] + BATCH - 1) // BATCH - 1), 0, 0)
@@ -176,20 +175,21 @@
     )
     out = pl.pallas_call(
         kernel,
-        out_shape=[jax.ShapeDtypeStruct(shape, jnp.float32) for shape in shapes(half_out)] * 2,
+        out_shape=[jax.ShapeDtypeStruct((half_out, ROWS, TILE), jnp.float32)] * (2 * PARTS)
+        + [jax.ShapeDtypeStruct((K // 2, TILE), jnp.float32)],
         grid_spec=pltpu.PrefetchScalarGridSpec(
             num_scalar_prefetch=3,
             grid=(tiles.shape[0] // BATCH,),
             in_specs=[VMEM_SPEC] * (4 * PARTS)
             + [pl.BlockSpec((BATCH, TILE, TILE), tile_block)],
-            out_specs=[VMEM_SPEC] * (2 * PARTS),
+            out_specs=[VMEM_SPEC] * (2 * PARTS + 1),
             scratch_shapes=[
                 pltpu.VMEM((4 * quarter_in, K, 2 * TILE), jnp.bfloat16),
                 pltpu.VMEM((2 * half_out + 1, K, TILE), jnp.float32),
             ],
         ),
-    )(count, source, target, *pieces[0], *pieces[1], tiles)
-    return out[:PARTS], out[PARTS:]
+    )(count, source, target, *[piece for part in pieces for piece in part], tiles)
+    return out[:PARTS], out[PARTS : 2 * PARTS], out[-1]
 
 
 def dot_full(left, right, contract):
@@ -266,7 +266,9 @@
         for part in range(PARTS):
             sent_refs[part][at] = scale * panel[part * ROWS : (part + 1) * ROWS]
         gram = gram + dot_full(panel, panel, (1, 1))
-    sent_refs[0][blocks] = jnp.concatenate([gram[:ROWS], gram[ROWS:]], axis=1)
+    gram = jnp.concatenate([gram[: K // 2], gram[K // 2 :]], axis=1)
+    for at in range(GRAM):
+        sent_refs[0][blocks + at] = gram[at * ROWS : (at + 1) * ROWS]
 
 
 def scale_panel(inverse, kept, got, scale):
@@ -276,7 +278,7 @@
     panel, *sent = pl.pallas_call(
         functools.partial(scale_kernel, factored=factored),
         out_shape=[jax.ShapeDtypeStruct((blocks, K, TILE), jnp.float32)]
-        + [jax.ShapeDtypeStruct((blocks + (part == 0), ROWS, TILE), jnp.float32) for part in range(PARTS)],
+        + [jax.ShapeDtypeStruct((blocks + GRAM * (part == 0), ROWS, TILE), jnp.float32) for part in range(PARTS)],
         in_specs=[VMEM_SPEC] * len(operands),
         out_specs=[VMEM_SPEC] * (1 + PARTS),
         name="scale_panel",
@@ -321,26 +323,27 @@
     item_scale = lax.rsqrt(item_degree.astype(jnp.float32)).reshape(item_blocks, TILE)
     start = start_items.astype(jnp.float32).reshape(PARTS, ROWS, item_blocks, TILE).transpose(0, 2, 1, 3)
     start = item_scale[None, :, None, :] * start
-    sent = [jnp.concatenate([start[0], jnp.zeros_like(start[0][:1])], axis=0), start[1]]
+    sent = [start[part] for part in range(PARTS)]
+    sent[0] = jnp.concatenate([sent[0], jnp.zeros((GRAM, ROWS, TILE), jnp.float32)], axis=0)
     turned = turned_tiles(tiles, 0, 8, None)
     turned = turned_tiles(tiles, 8, 8, turned)
     item_inverse = None
     for step in range(ITERS):
         pieces = gather(sent, "users")
-        kept, out = tiles_product(count, col_at, row_to, pieces, turned, UT, "users", "items")
-        kept, got, gram = reduce_scatter(kept, out, "items")
+        kept, out, gram = tiles_product(count, col_at, row_to, pieces, turned, UT, "users", "items")
+        kept, got, gram = reduce_scatter(kept, out, gram, "items")
         if step:
             item_inverse = inverse_factor(gram, item_total)
         user_raw, sent = scale_panel(item_inverse, kept, got, user_scale)
         pieces = gather(sent, "items")
-        kept, out = tiles_product(count, row_at, col_to, pieces, tiles, IT, "items", "users")
-        kept, got, gram = reduce_scatter(kept, out, "users")
+        kept, out, gram = tiles_product(count, row_at, col_to, pieces, tiles, IT, "items", "users")
+        kept, got, gram = reduce_scatter(kept, out, gram, "users")
         user_inverse = inverse_factor(gram, user_total)
         if step == ITERS - 1:
             user_panel = finish_panel(user_inverse, user_raw)
             user_panel, got = lax.optimization_barrier((user_panel, got))
         item_raw, sent = scale_panel(user_inverse, kept, got, item_scale)
-    item_inverse = inverse_factor(all_sum(sent[0][-1]), item_total)
+    item_inverse = inverse_factor(all_sum(sent[0][-GRAM:].reshape(K // 2, TILE)), item_total)
     return user_panel, finish_panel(item_inverse, item_raw)
 
 

time: 356 us -> 364 us (1.022)
  waiting for transfers between devices: 146 us -> 77.2 us
  starting transfers between devices: 79.9 us -> 142 us
  other arithmetic: 23.8 us -> 34.7 us
    ppermute x56 -> x109, waiting for transfers between devices: 146 us -> 77.2 us  [exchange(): lax.ppermute(value, axis, [(at, at ^ bit) for at in range(lax.axis_size(a...]
    ppermute x56 -> x109, starting transfers between devices: 79.9 us -> 142 us  [exchange(): lax.ppermute(value, axis, [(at, at ^ bit) for at in range(lax.axis_size(a...]
    add x2 -> x12, other arithmetic: 2.01 us -> 15.8 us  [reduce_scatter(): sent = [have[half:] + more[half:] for have, more in zip(kept, got)]]
    add x13 -> x9, other arithmetic: 11.9 us -> 4.72 us  [the longest x8 4 us: reduce_scatter(): gram = gram + other]
    add x6 -> x12, other arithmetic: 5.59 us -> 10.6 us  [reduce_scatter(): kept = [have[:half] + more[:half] for have, more in zip(kept, got)]]
    unnamed x82 -> x156, local copies, waits for them, and re-layouts: 7.1 us -> 7.96 us
  transfers between devices with their start and end apart: 56 -> 109, of which waited for: 32 -> 44; matrix products, arithmetic and copies ran while one was open for 6% -> 10% of each run, Pallas kernels for 12% -> 12%
where the time goes in v5:
time: 364 us; the launch traced here: 362 us
  starting transfers between devices  142 us (39%)
  Pallas kernels  95.6 us (26%)
  waiting for transfers between devices  77.2 us (21%)
  other arithmetic  34.7 us (10%)
  local copies, waits for them, and re-layouts  9.6 us (3%)
    ppermute x109, starting transfers between devices, exchange(): lax.ppermute(value, axis, [(at, at ^ bit) for at in range(lax.axis_size(a...  142 us
    ppermute x109, waiting for transfers between devices, exchange(): lax.ppermute(value, axis, [(at, at ^ bit) for at in range(lax.axis_size(a...  77.2 us
    pallas_call x4, Pallas kernels, tiles_product(): pl.pallas_call(kernel, out_shape=[jax.ShapeDtypeStruct((half_out, ROWS, T...  30.2 us
    pallas_call x4, Pallas kernels, inverse_factor(): pl.pallas_call(functools.partial(factor_kernel, total=total), out_shape=j...  27.1 us
    pallas_call x2, Pallas kernels, turned_tiles(): pl.pallas_call(turn_kernel, out_shape=jax.ShapeDtypeStruct(tiles.shape, t...  19.8 us
    add x12, other arithmetic, reduce_scatter(): sent = [have[half:] + more[half:] for have, more in zip(kept, got)]  15.8 us
    pallas_call x4, Pallas kernels, scale_panel(): pl.pallas_call(functools.partial(scale_kernel, factored=factored), out_sh...  14.1 us
    add x12, other arithmetic, reduce_scatter(): kept = [have[:half] + more[:half] for have, more in zip(kept, got)]  10.6 us
  transfers between devices with their start and end apart: 109, of which 44 were waited for; matrix products, arithmetic and copies ran while one was open for 10% of the time, Pallas kernels for 12%

profile of v5, /device:TPU:0, one launch (start us, length us, event | category | flops | bytes accessed | tf_op | source)
XLA Modules:
  0.0 361.7 jit_solution(789966141381463497)
XLA Ops:
  2.4 4.1 %collective-permute-start.4 = (f32[8,16,128]{2,1,0:T(8,128)S(1)}, f32[8,16,128]{2,1,0:T(8,128)S(1)}, u32[]{:S(2)}, u32[]{:S(2)}) collective-permute-start(f32[8,16,128]{2,1,0:T(8,128)S(1)} %get-tuple-element.166), channel_id=1, source_target_pairs={{0,16},{4,20},{8,24},{12,28},{16,0},{20,4},{24,8},{28,12},{1,17},{... | collective-permute-start | bytes 196616 | tf_op jit(solution)/shard_map/ppermute | solution.py:37
  6.6 2.8 collective-permute-start.8
  12.3 4.7 %collective-permute-start.6 = (f32[16,16,128]{2,1,0:T(8,128)S(1)}, f32[16,16,128]{2,1,0:T(8,128)S(1)}, u32[]{:S(2)}, u32[]{:S(2)}) collective-permute-start(f32[16,16,128]{2,1,0:T(8,128)S(1)} %pad_maximum_fusion.2.refs_4_), channel_id=1, source_target_pairs={{0,8},{4,12},{8,0},{12,4},{16,24},{20,28},{24,16},{28,20},{1,9},{5... | collective-permute-start | bytes 393224 | tf_op jit(solution)/shard_map/ppermute | solution.py:37
  23.9 9.9 %turned_tiles.2.refs_0_ = bf16[512,128,128]{2,1,0:T(8,128)(2,1)} custom-call(bf16[512,128,128]{2,1,0:T(8,128)(2,1)} %bitcast.30), custom_call_target="tpu_custom_call" | custom-call | tf_op jit(solution)/shard_map/turned_tiles/pallas_call | solution.py:231
  33.9 9.9 %turned_tiles.3.refs_16_ = bf16[512,128,128]{2,1,0:T(8,128)(2,1)} custom-call(bf16[512,128,128]{2,1,0:T(8,128)(2,1)} %bitcast.31, bf16[512,128,128]{2,1,0:T(8,128)(2,1)} %turned_tiles.2.refs_0_), custom_call_target="tpu_custom_call", output_to_operand_aliasing={{}: (1, {})} | custom-call | tf_op jit(solution)/shard_map/turned_tiles/pallas_call | solution.py:231
  51.2 2.2 collective-permute-done.11.refs_11_
  55.6 7.5 %shard_map.86 = (f32[32,16,128]{2,1,0:T(8,128)}, f32[32,16,128]{2,1,0:T(8,128)}, f32[32,16,128]{2,1,0:T(8,128)}, f32[32,16,128]{2,1,0:T(8,128)}, f32[32,16,128]{...) custom-call(s32[1]{0:T(128)} %bitcast.25.count, ...), custom_call_target="tpu_custom_call" | custom-call | tf_op jit(solution)/shard_map/pallas_call | solution.py:176
  66.6 8.4 %collective-permute-start.20 = (f32[16,16,128]{2,1,0:T(8,128)S(1)}, f32[16,16,128]{2,1,0:T(8,128)S(1)}, u32[]{:S(2)}, u32[]{:S(2)}) collective-permute-start(f32[16,16,128]{2,1,0:T(8,128)S(1)} %get-tuple-element.146), channel_id=1, source_target_pairs={{0,2},{1,3},{2,0},{3,1},{4,6},{5,7},{6,4},{7,5},{8,10},{9,11},{10,... | collective-permute-start | bytes 393224 | tf_op jit(solution)/shard_map/ppermute | solution.py:37
  83.0 2.5 collective-permute-done.22.refs_6_
  88.2 3.0 scale_panel.4
  94.7 2.2 collective-permute-done.27.refs_5_
  96.8 2.3 collective-permute-start.33
  99.1 3.7 %collective-permute-done.30.refs_9_ = f32[16,16,128]{2,1,0:T(8,128)S(1)} collective-permute-done((f32[16,16,128]{2,1,0:T(8,128)}, f32[16,16,128]{2,1,0:T(8,128)S(1)}, u32[]{:S(2)}, u32[]{:S(2)}) %collective-permute-start.30) | collective-permute-done | bytes 131104 | tf_op jit(solution)/shard_map/ppermute | solution.py:37
  107.4 7.5 %shard_map.87 = (f32[32,16,128]{2,1,0:T(8,128)}, f32[32,16,128]{2,1,0:T(8,128)}, f32[32,16,128]{2,1,0:T(8,128)}, f32[32,16,128]{2,1,0:T(8,128)}, f32[32,16,128]{...) custom-call(s32[1]{0:T(128)} %bitcast.26.count, ...), custom_call_target="tpu_custom_call" | custom-call | tf_op jit(solution)/shard_map/pallas_call | solution.py:176
  119.1 2.5 collective-permute-done.39
  130.6 12.9 %collective-permute-start.47 = (f32[8,16,128]{2,1,0:T(8,128)S(1)}, f32[8,16,128]{2,1,0:T(8,128)S(1)}, u32[]{:S(2)}, u32[]{:S(2)}) collective-permute-start(f32[8,16,128]{2,1,0:T(8,128)S(1)} %get-tuple-element.162), channel_id=1, source_target_pairs={{0,16},{4,20},{8,24},{12,28},{16,0},{20,4},{24,8},{28,12},{1,17},{... | collective-permute-start | bytes 196616 | tf_op jit(solution)/shard_map/ppermute | solution.py:37
  144.8 2.9 collective-permute-start.49
  149.6 2.7 collective-permute-done.36
  154.0 2.8 collective-permute-done.37
  156.8 2.9 collective-permute-start.38
  162.1 6.8 %factor.4.refs_0_ = f32[64,64]{1,0:T(8,128)} custom-call(f32[32,128]{1,0:T(8,128)} %add.232.gram_ref), custom_call_target="tpu_custom_call" | custom-call | tf_op jit(solution)/shard_map/factor/pallas_call | solution.py:243
  169.5 3.2 scale_panel.5
  172.8 2.9 collective-permute-start.51
  178.3 2.9 collective-permute-start.59
  192.8 2.6 collective-permute-start.53
  195.9 2.5 collective-permute-start.54
  200.6 2.8 collective-permute-done.58.refs_7_
  205.5 7.7 %shard_map.88 = (f32[32,16,128]{2,1,0:T(8,128)}, f32[32,16,128]{2,1,0:T(8,128)}, f32[32,16,128]{2,1,0:T(8,128)}, f32[32,16,128]{2,1,0:T(8,128)}, f32[32,16,128]{...) custom-call(s32[1]{0:T(128)} %bitcast.27.count, ...), custom_call_target="tpu_custom_call" | custom-call | tf_op jit(solution)/shard_map/pallas_call | solution.py:176
  216.7 7.2 %collective-permute-start.73 = (f32[16,16,128]{2,1,0:T(8,128)S(1)}, f32[16,16,128]{2,1,0:T(8,128)S(1)}, u32[]{:S(2)}, u32[]{:S(2)}) collective-permute-start(f32[16,16,128]{2,1,0:T(8,128)S(1)} %get-tuple-element.130), channel_id=1, source_target_pairs={{0,2},{1,3},{2,0},{3,1},{4,6},{5,7},{6,4},{7,5},{8,10},{9,11},{10,... | collective-permute-start | bytes 393224 | tf_op jit(solution)/shard_map/ppermute | solution.py:37
  237.4 6.8 %factor.5.refs_0_ = f32[64,64]{1,0:T(8,128)} custom-call(f32[32,128]{1,0:T(8,128)} %add.251.gram_ref), custom_call_target="tpu_custom_call" | custom-call | tf_op jit(solution)/shard_map/factor/pallas_call | solution.py:243
  245.0 4.7 %scale_panel.6 = (f32[16,64,128]{2,1,0:T(8,128)}, f32[18,16,128]{2,1,0:T(8,128)}, f32[16,16,128]{2,1,0:T(8,128)}, f32[16,16,128]{2,1,0:T(8,128)}, f32[16,16,128]{2,1,0:T(8,128)}) custom-call(f32[64,64]{1,0:T(8,128)} %factor.5.refs_0_, f32[16,16,128]{2,1,0:T(8,128)} %get-tuple-element.131.refs_1_, f32[16,16,128]{2,1,0:T(8,128)} %get-tuple-element.129.refs_2_, ...), custom_call_target="tpu_custom_call" | custom-call | tf_op jit(solution)/shard_map/scale_panel/pallas_call | solution.py:278
  253.7 2.2 collective-permute-done.80.refs_5_
  255.9 2.4 collective-permute-start.86
  258.3 3.4 collective-permute-done.83.refs_9_
  266.0 7.5 %shard_map.89 = (f32[32,16,128]{2,1,0:T(8,128)}, f32[32,16,128]{2,1,0:T(8,128)}, f32[32,16,128]{2,1,0:T(8,128)}, f32[32,16,128]{2,1,0:T(8,128)}, f32[32,16,128]{...) custom-call(s32[1]{0:T(128)} %bitcast.28.count, ...), custom_call_target="tpu_custom_call" | custom-call | tf_op jit(solution)/shard_map/pallas_call | solution.py:176
  277.7 5.3 %collective-permute-done.92 = f32[32,16,128]{2,1,0:T(8,128)S(1)} collective-permute-done((f32[32,16,128]{2,1,0:T(8,128)}, f32[32,16,128]{2,1,0:T(8,128)S(1)}, u32[]{:S(2)}, u32[]{:S(2)}) %collective-permute-start.92) | collective-permute-done | bytes 262176 | tf_op jit(solution)/shard_map/ppermute | solution.py:37
  286.1 2.4 collective-permute-done.98
  292.4 10.5 %collective-permute-start.94 = (f32[8,16,128]{2,1,0:T(8,128)S(1)}, f32[8,16,128]{2,1,0:T(8,128)S(1)}, u32[]{:S(2)}, u32[]{:S(2)}) collective-permute-start(f32[8,16,128]{2,1,0:T(8,128)S(1)} %get-tuple-element.155), channel_id=1, source_target_pairs={{0,16},{4,20},{8,24},{12,28},{16,0},{20,4},{24,8},{28,12},{1,17},{... | collective-permute-start | bytes 196616 | tf_op jit(solution)/shard_map/ppermute | solution.py:37
  304.1 2.9 collective-permute-start.100
  313.3 2.9 collective-permute-done.90
  316.2 2.9 collective-permute-start.91
  321.4 6.8 %factor.6.inverse_ref.refs_0_ = f32[64,64]{1,0:T(8,128)} custom-call(f32[32,128]{1,0:T(8,128)} %add.262.gram_ref), custom_call_target="tpu_custom_call" | custom-call | tf_op jit(solution)/shard_map/factor/pallas_call | solution.py:243
  328.2 2.4 finish_panel.2
  331.3 3.2 scale_panel.7
  337.4 2.8 collective-permute-done.105
  344.8 2.9 collective-permute-done.107
  347.7 2.9 collective-permute-start.108
  352.9 6.8 %factor.7.inverse_ref = f32[64,64]{1,0:T(8,128)} custom-call(f32[32,128]{1,0:T(8,128)} %add.283.gram_ref), custom_call_target="tpu_custom_call" | custom-call | tf_op jit(solution)/shard_map/factor/pallas_call | solution.py:243
  (398 shorter events, 141.7 us)
Async XLA Ops:
  6.5 12.1 %collective-permute-start = (f32[10,16,128]{2,1,0:T(8,128)S(1)}, f32[10,16,128]{2,1,0:T(8,128)S(1)}, u32[]{:S(2)}, u32[]{:S(2)}) collective-permute-start(f32[10,16,128]{2,1,0:T(8,128)S(1)} %concatenate.27), channel_id=1, source_target_pairs={{0,16},{4,20},{8,24},{12,28},{16,0},{20,4},{24,8},{28,12},{1,17},{... | collective-permute-start | bytes 245768 | tf_op jit(solution)/shard_map/ppermute | solution.py:37
  6.6 11.9 %collective-permute-start.8 = (f32[8,16,128]{2,1,0:T(8,128)S(1)}, f32[8,16,128]{2,1,0:T(8,128)S(1)}, u32[]{:S(2)}, u32[]{:S(2)}) collective-permute-start(f32[8,16,128]{2,1,0:T(8,128)S(1)} %get-tuple-element.165), channel_id=1, source_target_pairs={{0,16},{4,20},{8,24},{12,28},{16,0},{20,4},{24,8},{28,12},{1,17},{... | collective-permute-start | bytes 196616 | tf_op jit(solution)/shard_map/ppermute | solution.py:37
  9.5 10.8 %collective-permute-start.12 = (f32[8,16,128]{2,1,0:T(8,128)S(1)}, f32[8,16,128]{2,1,0:T(8,128)S(1)}, u32[]{:S(2)}, u32[]{:S(2)}) collective-permute-start(f32[8,16,128]{2,1,0:T(8,128)S(1)} %get-tuple-element.164), channel_id=1, source_target_pairs={{0,16},{4,20},{8,24},{12,28},{16,0},{20,4},{24,8},{28,12},{1,17},{... | collective-permute-start | bytes 196616 | tf_op jit(solution)/shard_map/ppermute | solution.py:37
  10.3 12.0 %collective-permute-start.5 = (f32[16,16,128]{2,1,0:T(8,128)S(1)}, f32[16,16,128]{2,1,0:T(8,128)S(1)}, u32[]{:S(2)}, u32[]{:S(2)}) collective-permute-start(f32[16,16,128]{2,1,0:T(8,128)S(1)} %pad_maximum_fusion.2.refs_4_), channel_id=1, source_target_pairs={{0,4},{4,0},{8,12},{12,8},{16,20},{20,16},{24,28},{28,24},{1,5},{5... | collective-permute-start | bytes 393224 | tf_op jit(solution)/shard_map/ppermute | solution.py:37
  12.3 10.6 %collective-permute-start.6 = (f32[16,16,128]{2,1,0:T(8,128)S(1)}, f32[16,16,128]{2,1,0:T(8,128)S(1)}, u32[]{:S(2)}, u32[]{:S(2)}) collective-permute-start(f32[16,16,128]{2,1,0:T(8,128)S(1)} %pad_maximum_fusion.2.refs_4_), channel_id=1, source_target_pairs={{0,8},{4,12},{8,0},{12,4},{16,24},{20,28},{24,16},{28,20},{1,9},{5... | collective-permute-start | bytes 393224 | tf_op jit(solution)/shard_map/ppermute | solution.py:37
  18.5 25.2 %collective-permute-start.9 = (f32[16,16,128]{2,1,0:T(8,128)S(1)}, f32[16,16,128]{2,1,0:T(8,128)S(1)}, u32[]{:S(2)}, u32[]{:S(2)}) collective-permute-start(f32[16,16,128]{2,1,0:T(8,128)S(1)} %pad_maximum_fusion.3.refs_8_), channel_id=1, source_target_pairs={{0,8},{4,12},{8,0},{12,4},{16,24},{20,28},{24,16},{28,20},{1,9},{5... | collective-permute-start | bytes 393224 | tf_op jit(solution)/shard_map/ppermute | solution.py:37
  18.7 26.4 %collective-permute-start.10 = (f32[16,16,128]{2,1,0:T(8,128)S(1)}, f32[16,16,128]{2,1,0:T(8,128)S(1)}, u32[]{:S(2)}, u32[]{:S(2)}) collective-permute-start(f32[16,16,128]{2,1,0:T(8,128)S(1)} %pad_maximum_fusion.3.refs_8_), channel_id=1, source_target_pairs={{0,4},{4,0},{8,12},{12,8},{16,20},{20,16},{24,28},{28,24},{1,5},{5... | collective-permute-start | bytes 393224 | tf_op jit(solution)/shard_map/ppermute | solution.py:37
  20.2 27.7 %collective-permute-start.1 = (f32[18,16,128]{2,1,0:T(8,128)S(1)}, f32[18,16,128]{2,1,0:T(8,128)S(1)}, u32[]{:S(2)}, u32[]{:S(2)}) collective-permute-start(f32[18,16,128]{2,1,0:T(8,128)S(1)} %pad_maximum_fusion.refs_0_), channel_id=1, source_target_pairs={{0,8},{4,12},{8,0},{12,4},{16,24},{20,28},{24,16},{28,20},{1,9},{5... | collective-permute-start | bytes 442376 | tf_op jit(solution)/shard_map/ppermute | solution.py:37
  22.3 24.8 %collective-permute-start.13 = (f32[16,16,128]{2,1,0:T(8,128)S(1)}, f32[16,16,128]{2,1,0:T(8,128)S(1)}, u32[]{:S(2)}, u32[]{:S(2)}) collective-permute-start(f32[16,16,128]{2,1,0:T(8,128)S(1)} %pad_maximum_fusion.4.refs_12_), channel_id=1, source_target_pairs={{0,4},{4,0},{8,12},{12,8},{16,20},{20,16},{24,28},{28,24},{1,5},{5... | collective-permute-start | bytes 393224 | tf_op jit(solution)/shard_map/ppermute | solution.py:37
  22.9 24.7 %collective-permute-start.14 = (f32[16,16,128]{2,1,0:T(8,128)S(1)}, f32[16,16,128]{2,1,0:T(8,128)S(1)}, u32[]{:S(2)}, u32[]{:S(2)}) collective-permute-start(f32[16,16,128]{2,1,0:T(8,128)S(1)} %pad_maximum_fusion.4.refs_12_), channel_id=1, source_target_pairs={{0,8},{4,12},{8,0},{12,4},{16,24},{20,28},{24,16},{28,20},{1,9},{5... | collective-permute-start | bytes 393224 | tf_op jit(solution)/shard_map/ppermute | solution.py:37
  63.2 11.8 %collective-permute-start.17 = (f32[32,16,128]{2,1,0:T(8,128)}, f32[32,16,128]{2,1,0:T(8,128)S(1)}, u32[]{:S(2)}, u32[]{:S(2)}) collective-permute-start(f32[32,16,128]{2,1,0:T(8,128)} %get-tuple-element.60), channel_id=1, source_target_pairs={{0,1},{1,0},{2,3},{3,2},{4,5},{5,4},{6,7},{7,6},{8,9},{9,8},{10,11... | collective-permute-start | bytes 786440 | tf_op jit(solution)/shard_map/ppermute | solution.py:37
  63.7 12.9 %collective-permute-start.18 = (f32[32,16,128]{2,1,0:T(8,128)}, f32[32,16,128]{2,1,0:T(8,128)S(1)}, u32[]{:S(2)}, u32[]{:S(2)}) collective-permute-start(f32[32,16,128]{2,1,0:T(8,128)} %get-tuple-element.62), channel_id=1, source_target_pairs={{0,1},{1,0},{2,3},{3,2},{4,5},{5,4},{6,7},{7,6},{8,9},{9,8},{10,11... | collective-permute-start | bytes 786440 | tf_op jit(solution)/shard_map/ppermute | solution.py:37
  63.8 16.6 %collective-permute-start.19 = (f32[32,16,128]{2,1,0:T(8,128)}, f32[32,16,128]{2,1,0:T(8,128)S(1)}, u32[]{:S(2)}, u32[]{:S(2)}) collective-permute-start(f32[32,16,128]{2,1,0:T(8,128)} %get-tuple-element.64), channel_id=1, source_target_pairs={{0,1},{1,0},{2,3},{3,2},{4,5},{5,4},{6,7},{7,6},{8,9},{9,8},{10,11... | collective-permute-start | bytes 786440 | tf_op jit(solution)/shard_map/ppermute | solution.py:37
  66.6 16.0 %collective-permute-start.20 = (f32[16,16,128]{2,1,0:T(8,128)S(1)}, f32[16,16,128]{2,1,0:T(8,128)S(1)}, u32[]{:S(2)}, u32[]{:S(2)}) collective-permute-start(f32[16,16,128]{2,1,0:T(8,128)S(1)} %get-tuple-element.146), channel_id=1, source_target_pairs={{0,2},{1,3},{2,0},{3,1},{4,6},{5,7},{6,4},{7,5},{8,10},{9,11},{10,... | collective-permute-start | bytes 393224 | tf_op jit(solution)/shard_map/ppermute | solution.py:37
  92.6 10.2 %collective-permute-start.24 = (f32[18,16,128]{2,1,0:T(8,128)}, f32[18,16,128]{2,1,0:T(8,128)S(1)}, u32[]{:S(2)}, u32[]{:S(2)}) collective-permute-start(f32[18,16,128]{2,1,0:T(8,128)} %get-tuple-element.65.refs_0_), channel_id=1, source_target_pairs={{0,2},{1,3},{2,0},{3,1},{4,6},{5,7},{6,4},{7,5},{8,10},{9,11},{10,... | collective-permute-start | bytes 442376 | tf_op jit(solution)/shard_map/ppermute | solution.py:37
  93.2 9.6 %collective-permute-start.30 = (f32[16,16,128]{2,1,0:T(8,128)}, f32[16,16,128]{2,1,0:T(8,128)S(1)}, u32[]{:S(2)}, u32[]{:S(2)}) collective-permute-start(f32[16,16,128]{2,1,0:T(8,128)} %get-tuple-element.67.refs_8_), channel_id=1, source_target_pairs={{0,2},{1,3},{2,0},{3,1},{4,6},{5,7},{6,4},{7,5},{8,10},{9,11},{10,... | collective-permute-start | bytes 393224 | tf_op jit(solution)/shard_map/ppermute | solution.py:37
  115.1 10.6 %collective-permute-start.43 = (f32[32,16,128]{2,1,0:T(8,128)}, f32[32,16,128]{2,1,0:T(8,128)S(1)}, u32[]{:S(2)}, u32[]{:S(2)}) collective-permute-start(f32[32,16,128]{2,1,0:T(8,128)} %get-tuple-element.75), channel_id=1, source_target_pairs={{0,4},{4,0},{8,12},{12,8},{16,20},{20,16},{24,28},{28,24},{1,5},{5... | collective-permute-start | bytes 786440 | tf_op jit(solution)/shard_map/ppermute | solution.py:37
  117.0 9.8 %collective-permute-start.45 = (f32[32,16,128]{2,1,0:T(8,128)}, f32[32,16,128]{2,1,0:T(8,128)S(1)}, u32[]{:S(2)}, u32[]{:S(2)}) collective-permute-start(f32[32,16,128]{2,1,0:T(8,128)} %get-tuple-element.77), channel_id=1, source_target_pairs={{0,8},{4,12},{8,0},{12,4},{16,24},{20,28},{24,16},{28,20},{1,9},{5... | collective-permute-start | bytes 786440 | tf_op jit(solution)/shard_map/ppermute | solution.py:37
  123.7 19.8 %collective-permute-start.42 = (f32[16,16,128]{2,1,0:T(8,128)S(1)}, f32[16,16,128]{2,1,0:T(8,128)S(1)}, u32[]{:S(2)}, u32[]{:S(2)}) collective-permute-start(f32[16,16,128]{2,1,0:T(8,128)S(1)} %get-tuple-element.137), channel_id=1, source_target_pairs={{0,4},{4,0},{8,12},{12,8},{16,20},{20,16},{24,28},{28,24},{1,5},{5... | collective-permute-start | bytes 393224 | tf_op jit(solution)/shard_map/ppermute | solution.py:37
  126.7 17.4 %collective-permute-start.44 = (f32[16,16,128]{2,1,0:T(8,128)S(1)}, f32[16,16,128]{2,1,0:T(8,128)S(1)}, u32[]{:S(2)}, u32[]{:S(2)}) collective-permute-start(f32[16,16,128]{2,1,0:T(8,128)S(1)} %get-tuple-element.135), channel_id=1, source_target_pairs={{0,8},{4,12},{8,0},{12,4},{16,24},{20,28},{24,16},{28,20},{1,9},{5... | collective-permute-start | bytes 393224 | tf_op jit(solution)/shard_map/ppermute | solution.py:37
  127.9 19.9 %collective-permute-start.46 = (f32[16,16,128]{2,1,0:T(8,128)S(1)}, f32[16,16,128]{2,1,0:T(8,128)S(1)}, u32[]{:S(2)}, u32[]{:S(2)}) collective-permute-start(f32[16,16,128]{2,1,0:T(8,128)S(1)} %get-tuple-element.133), channel_id=1, source_target_pairs={{0,4},{4,0},{8,12},{12,8},{16,20},{20,16},{24,28},{28,24},{1,5},{5... | collective-permute-start | bytes 393224 | tf_op jit(solution)/shard_map/ppermute | solution.py:37
  130.6 38.3 %collective-permute-start.47 = (f32[8,16,128]{2,1,0:T(8,128)S(1)}, f32[8,16,128]{2,1,0:T(8,128)S(1)}, u32[]{:S(2)}, u32[]{:S(2)}) collective-permute-start(f32[8,16,128]{2,1,0:T(8,128)S(1)} %get-tuple-element.162), channel_id=1, source_target_pairs={{0,16},{4,20},{8,24},{12,28},{16,0},{20,4},{24,8},{28,12},{1,17},{... | collective-permute-start | bytes 196616 | tf_op jit(solution)/shard_map/ppermute | solution.py:37
  144.2 24.7 %collective-permute-start.48 = (f32[8,16,128]{2,1,0:T(8,128)S(1)}, f32[8,16,128]{2,1,0:T(8,128)S(1)}, u32[]{:S(2)}, u32[]{:S(2)}) collective-permute-start(f32[8,16,128]{2,1,0:T(8,128)S(1)} %get-tuple-element.160), channel_id=1, source_target_pairs={{0,16},{4,20},{8,24},{12,28},{16,0},{20,4},{24,8},{28,12},{1,17},{... | collective-permute-start | bytes 196616 | tf_op jit(solution)/shard_map/ppermute | solution.py:37
  144.8 24.0 %collective-permute-start.49 = (f32[8,16,128]{2,1,0:T(8,128)S(1)}, f32[8,16,128]{2,1,0:T(8,128)S(1)}, u32[]{:S(2)}, u32[]{:S(2)}) collective-permute-start(f32[8,16,128]{2,1,0:T(8,128)S(1)} %get-tuple-element.158), channel_id=1, source_target_pairs={{0,16},{4,20},{8,24},{12,28},{16,0},{20,4},{24,8},{28,12},{1,17},{... | collective-permute-start | bytes 196616 | tf_op jit(solution)/shard_map/ppermute | solution.py:37
  148.4 20.5 %collective-permute-start.50 = (f32[8,16,128]{2,1,0:T(8,128)S(1)}, f32[8,16,128]{2,1,0:T(8,128)S(1)}, u32[]{:S(2)}, u32[]{:S(2)}) collective-permute-start(f32[8,16,128]{2,1,0:T(8,128)S(1)} %get-tuple-element.156), channel_id=1, source_target_pairs={{0,16},{4,20},{8,24},{12,28},{16,0},{20,4},{24,8},{28,12},{1,17},{... | collective-permute-start | bytes 196616 | tf_op jit(solution)/shard_map/ppermute | solution.py:37
  172.8 14.5 %collective-permute-start.51 = (f32[10,16,128]{2,1,0:T(8,128)}, f32[10,16,128]{2,1,0:T(8,128)S(1)}, u32[]{:S(2)}, u32[]{:S(2)}) collective-permute-start(f32[10,16,128]{2,1,0:T(8,128)} %get-tuple-element.78), channel_id=1, source_target_pairs={{0,16},{4,20},{8,24},{12,28},{16,0},{20,4},{24,8},{28,12},{1,17},{... | collective-permute-start | bytes 245768 | tf_op jit(solution)/shard_map/ppermute | solution.py:37
  187.2 11.2 %collective-permute-start.61 = (f32[16,16,128]{2,1,0:T(8,128)S(1)}, f32[16,16,128]{2,1,0:T(8,128)S(1)}, u32[]{:S(2)}, u32[]{:S(2)}) collective-permute-start(f32[16,16,128]{2,1,0:T(8,128)S(1)} %constant_dynamic-update-slice_fusion.2.refs_8_), channel_id=1, source_target_pairs={{0,4},{4,0},{8,12},{12,8},{16,20},{20,16},{24,28},{28,24},{1,5},{5... | collective-permute-start | bytes 393224 | tf_op jit(solution)/shard_map/ppermute | solution.py:37
  195.9 8.9 %collective-permute-start.54 = (f32[18,16,128]{2,1,0:T(8,128)S(1)}, f32[18,16,128]{2,1,0:T(8,128)S(1)}, u32[]{:S(2)}, u32[]{:S(2)}) collective-permute-start(f32[18,16,128]{2,1,0:T(8,128)S(1)} %collective-permute-done.52.refs_1_), channel_id=1, source_target_pairs={{0,4},{4,0},{8,12},{12,8},{16,20},{20,16},{24,28},{28,24},{1,5},{5... | collective-permute-start | bytes 442376 | tf_op jit(solution)/shard_map/ppermute | solution.py:37
  213.3 10.6 %collective-permute-start.70 = (f32[32,16,128]{2,1,0:T(8,128)}, f32[32,16,128]{2,1,0:T(8,128)S(1)}, u32[]{:S(2)}, u32[]{:S(2)}) collective-permute-start(f32[32,16,128]{2,1,0:T(8,128)} %get-tuple-element.86), channel_id=1, source_target_pairs={{0,1},{1,0},{2,3},{3,2},{4,5},{5,4},{6,7},{7,6},{8,9},{9,8},{10,11... | collective-permute-start | bytes 786440 | tf_op jit(solution)/shard_map/ppermute | solution.py:37
  213.8 11.8 %collective-permute-start.71 = (f32[32,16,128]{2,1,0:T(8,128)}, f32[32,16,128]{2,1,0:T(8,128)S(1)}, u32[]{:S(2)}, u32[]{:S(2)}) collective-permute-start(f32[32,16,128]{2,1,0:T(8,128)} %get-tuple-element.88), channel_id=1, source_target_pairs={{0,1},{1,0},{2,3},{3,2},{4,5},{5,4},{6,7},{7,6},{8,9},{9,8},{10,11... | collective-permute-start | bytes 786440 | tf_op jit(solution)/shard_map/ppermute | solution.py:37
  213.9 15.4 %collective-permute-start.72 = (f32[32,16,128]{2,1,0:T(8,128)}, f32[32,16,128]{2,1,0:T(8,128)S(1)}, u32[]{:S(2)}, u32[]{:S(2)}) collective-permute-start(f32[32,16,128]{2,1,0:T(8,128)} %get-tuple-element.90), channel_id=1, source_target_pairs={{0,1},{1,0},{2,3},{3,2},{4,5},{5,4},{6,7},{7,6},{8,9},{9,8},{10,11... | collective-permute-start | bytes 786440 | tf_op jit(solution)/shard_map/ppermute | solution.py:37
  216.7 27.5 %collective-permute-start.73 = (f32[16,16,128]{2,1,0:T(8,128)S(1)}, f32[16,16,128]{2,1,0:T(8,128)S(1)}, u32[]{:S(2)}, u32[]{:S(2)}) collective-permute-start(f32[16,16,128]{2,1,0:T(8,128)S(1)} %get-tuple-element.130), channel_id=1, source_target_pairs={{0,2},{1,3},{2,0},{3,1},{4,6},{5,7},{6,4},{7,5},{8,10},{9,11},{10,... | collective-permute-start | bytes 393224 | tf_op jit(solution)/shard_map/ppermute | solution.py:37
  225.6 18.6 %collective-permute-start.74 = (f32[16,16,128]{2,1,0:T(8,128)S(1)}, f32[16,16,128]{2,1,0:T(8,128)S(1)}, u32[]{:S(2)}, u32[]{:S(2)}) collective-permute-start(f32[16,16,128]{2,1,0:T(8,128)S(1)} %get-tuple-element.128), channel_id=1, source_target_pairs={{0,2},{1,3},{2,0},{3,1},{4,6},{5,7},{6,4},{7,5},{8,10},{9,11},{10,... | collective-permute-start | bytes 393224 | tf_op jit(solution)/shard_map/ppermute | solution.py:37
  227.3 17.0 %collective-permute-start.75 = (f32[16,16,128]{2,1,0:T(8,128)S(1)}, f32[16,16,128]{2,1,0:T(8,128)S(1)}, u32[]{:S(2)}, u32[]{:S(2)}) collective-permute-start(f32[16,16,128]{2,1,0:T(8,128)S(1)} %get-tuple-element.126), channel_id=1, source_target_pairs={{0,2},{1,3},{2,0},{3,1},{4,6},{5,7},{6,4},{7,5},{8,10},{9,11},{10,... | collective-permute-start | bytes 393224 | tf_op jit(solution)/shard_map/ppermute | solution.py:37
  231.0 13.3 %collective-permute-start.76 = (f32[16,16,128]{2,1,0:T(8,128)S(1)}, f32[16,16,128]{2,1,0:T(8,128)S(1)}, u32[]{:S(2)}, u32[]{:S(2)}) collective-permute-start(f32[16,16,128]{2,1,0:T(8,128)S(1)} %get-tuple-element.124), channel_id=1, source_target_pairs={{0,2},{1,3},{2,0},{3,1},{4,6},{5,7},{6,4},{7,5},{8,10},{9,11},{10,... | collective-permute-start | bytes 393224 | tf_op jit(solution)/shard_map/ppermute | solution.py:37
  251.7 10.0 %collective-permute-start.77 = (f32[18,16,128]{2,1,0:T(8,128)}, f32[18,16,128]{2,1,0:T(8,128)S(1)}, u32[]{:S(2)}, u32[]{:S(2)}) collective-permute-start(f32[18,16,128]{2,1,0:T(8,128)} %get-tuple-element.91.refs_0_), channel_id=1, source_target_pairs={{0,2},{1,3},{2,0},{3,1},{4,6},{5,7},{6,4},{7,5},{8,10},{9,11},{10,... | collective-permute-start | bytes 442376 | tf_op jit(solution)/shard_map/ppermute | solution.py:37
  251.8 9.8 %collective-permute-start.83 = (f32[16,16,128]{2,1,0:T(8,128)}, f32[16,16,128]{2,1,0:T(8,128)S(1)}, u32[]{:S(2)}, u32[]{:S(2)}) collective-permute-start(f32[16,16,128]{2,1,0:T(8,128)} %get-tuple-element.93.refs_8_), channel_id=1, source_target_pairs={{0,2},{1,3},{2,0},{3,1},{4,6},{5,7},{6,4},{7,5},{8,10},{9,11},{10,... | collective-permute-start | bytes 393224 | tf_op jit(solution)/shard_map/ppermute | solution.py:37
  273.6 9.5 %collective-permute-start.92 = (f32[32,16,128]{2,1,0:T(8,128)}, f32[32,16,128]{2,1,0:T(8,128)S(1)}, u32[]{:S(2)}, u32[]{:S(2)}) collective-permute-start(f32[32,16,128]{2,1,0:T(8,128)} %get-tuple-element.98), channel_id=1, source_target_pairs={{0,4},{4,0},{8,12},{12,8},{16,20},{20,16},{24,28},{28,24},{1,5},{5... | collective-permute-start | bytes 786440 | tf_op jit(solution)/shard_map/ppermute | solution.py:37
  273.6 10.5 %collective-permute-start.95 = (f32[32,16,128]{2,1,0:T(8,128)}, f32[32,16,128]{2,1,0:T(8,128)S(1)}, u32[]{:S(2)}, u32[]{:S(2)}) collective-permute-start(f32[32,16,128]{2,1,0:T(8,128)} %get-tuple-element.100), channel_id=1, source_target_pairs={{0,8},{4,12},{8,0},{12,4},{16,24},{20,28},{24,16},{28,20},{1,9},{5... | collective-permute-start | bytes 786440 | tf_op jit(solution)/shard_map/ppermute | solution.py:37
  273.7 14.8 %collective-permute-start.98 = (f32[32,16,128]{2,1,0:T(8,128)}, f32[32,16,128]{2,1,0:T(8,128)S(1)}, u32[]{:S(2)}, u32[]{:S(2)}) collective-permute-start(f32[32,16,128]{2,1,0:T(8,128)} %get-tuple-element.102), channel_id=1, source_target_pairs={{0,4},{4,0},{8,12},{12,8},{16,20},{20,16},{24,28},{28,24},{1,5},{5... | collective-permute-start | bytes 786440 | tf_op jit(solution)/shard_map/ppermute | solution.py:37
  275.6 14.0 %collective-permute-start.101 = (f32[32,16,128]{2,1,0:T(8,128)}, f32[32,16,128]{2,1,0:T(8,128)S(1)}, u32[]{:S(2)}, u32[]{:S(2)}) collective-permute-start(f32[32,16,128]{2,1,0:T(8,128)} %get-tuple-element.104), channel_id=1, source_target_pairs={{0,8},{4,12},{8,0},{12,4},{16,24},{20,28},{24,16},{28,20},{1,9},{5... | collective-permute-start | bytes 786440 | tf_op jit(solution)/shard_map/ppermute | solution.py:37
  285.1 17.7 %collective-permute-start.96 = (f32[16,16,128]{2,1,0:T(8,128)S(1)}, f32[16,16,128]{2,1,0:T(8,128)S(1)}, u32[]{:S(2)}, u32[]{:S(2)}) collective-permute-start(f32[16,16,128]{2,1,0:T(8,128)S(1)} %get-tuple-element.121), channel_id=1, source_target_pairs={{0,4},{4,0},{8,12},{12,8},{16,20},{20,16},{24,28},{28,24},{1,5},{5... | collective-permute-start | bytes 393224 | tf_op jit(solution)/shard_map/ppermute | solution.py:37
  289.5 14.0 %collective-permute-start.99 = (f32[16,16,128]{2,1,0:T(8,128)S(1)}, f32[16,16,128]{2,1,0:T(8,128)S(1)}, u32[]{:S(2)}, u32[]{:S(2)}) collective-permute-start(f32[16,16,128]{2,1,0:T(8,128)S(1)} %get-tuple-element.119), channel_id=1, source_target_pairs={{0,8},{4,12},{8,0},{12,4},{16,24},{20,28},{24,16},{28,20},{1,9},{5... | collective-permute-start | bytes 393224 | tf_op jit(solution)/shard_map/ppermute | solution.py:37
  290.6 16.4 %collective-permute-start.102 = (f32[16,16,128]{2,1,0:T(8,128)S(1)}, f32[16,16,128]{2,1,0:T(8,128)S(1)}, u32[]{:S(2)}, u32[]{:S(2)}) collective-permute-start(f32[16,16,128]{2,1,0:T(8,128)S(1)} %get-tuple-element.117), channel_id=1, source_target_pairs={{0,4},{4,0},{8,12},{12,8},{16,20},{20,16},{24,28},{28,24},{1,5},{5... | collective-permute-start | bytes 393224 | tf_op jit(solution)/shard_map/ppermute | solution.py:37
  292.4 38.2 %collective-permute-start.94 = (f32[8,16,128]{2,1,0:T(8,128)S(1)}, f32[8,16,128]{2,1,0:T(8,128)S(1)}, u32[]{:S(2)}, u32[]{:S(2)}) collective-permute-start(f32[8,16,128]{2,1,0:T(8,128)S(1)} %get-tuple-element.155), channel_id=1, source_target_pairs={{0,16},{4,20},{8,24},{12,28},{16,0},{20,4},{24,8},{28,12},{1,17},{... | collective-permute-start | bytes 196616 | tf_op jit(solution)/shard_map/ppermute | solution.py:37
  303.5 27.1 %collective-permute-start.97 = (f32[8,16,128]{2,1,0:T(8,128)S(1)}, f32[8,16,128]{2,1,0:T(8,128)S(1)}, u32[]{:S(2)}, u32[]{:S(2)}) collective-permute-start(f32[8,16,128]{2,1,0:T(8,128)S(1)} %get-tuple-element.153), channel_id=1, source_target_pairs={{0,16},{4,20},{8,24},{12,28},{16,0},{20,4},{24,8},{28,12},{1,17},{... | collective-permute-start | bytes 196616 | tf_op jit(solution)/shard_map/ppermute | solution.py:37
  304.1 26.5 %collective-permute-start.100 = (f32[8,16,128]{2,1,0:T(8,128)S(1)}, f32[8,16,128]{2,1,0:T(8,128)S(1)}, u32[]{:S(2)}, u32[]{:S(2)}) collective-permute-start(f32[8,16,128]{2,1,0:T(8,128)S(1)} %get-tuple-element.151), channel_id=1, source_target_pairs={{0,16},{4,20},{8,24},{12,28},{16,0},{20,4},{24,8},{28,12},{1,17},{... | collective-permute-start | bytes 196616 | tf_op jit(solution)/shard_map/ppermute | solution.py:37
  307.7 23.0 %collective-permute-start.103 = (f32[8,16,128]{2,1,0:T(8,128)S(1)}, f32[8,16,128]{2,1,0:T(8,128)S(1)}, u32[]{:S(2)}, u32[]{:S(2)}) collective-permute-start(f32[8,16,128]{2,1,0:T(8,128)S(1)} %get-tuple-element.149), channel_id=1, source_target_pairs={{0,16},{4,20},{8,24},{12,28},{16,0},{20,4},{24,8},{28,12},{1,17},{... | collective-permute-start | bytes 196616 | tf_op jit(solution)/shard_map/ppermute | solution.py:37
  (137 other events, 820.2 us)

commit v6 on v5

--- a/solution.py
+++ b/solution.py
@@ -9,10 +9,9 @@
 
 
 K = 64
-PARTS = 4
+PARTS = 2
 ROWS = K // PARTS
 TILE = 128
-GRAM = K // 2 // ROWS
 ITERS = 2
 UT = 64
 IT = 64
@@ -52,8 +51,7 @@
         got = []
         for part in range(PARTS):
             got.append(exchange(held[part], axis, gather_order(axis, part)[level]))
-        first = jnp.concatenate([held[0][:-GRAM], got[0][:-GRAM], held[0][-GRAM:] + got[0][-GRAM:]], axis=0)
-        held = [first] + [jnp.concatenate([have, more], axis=0) for have, more in zip(held[1:], got[1:])]
+        held = [jnp.concatenate([have, more], axis=0) for have, more in zip(held, got)]
     order = [gather_order(axis, part)[-2:] for part in range(PARTS)]
     near, own, far = [], [], []
     for part in range(PARTS):
@@ -64,24 +62,22 @@
     return [[held[part], near[part], own[part], far[part]] for part in range(PARTS)]
 
 
-def reduce_scatter(kept, sent, gram, axis):
+def reduce_scatter(kept, sent, axis):
     for level in range(len(gather_order(axis, 0)) - 1, -1, -1):
-        other = exchange(gram, axis, gather_order(axis, 0)[level])
         got = []
         for part in range(PARTS):
             got.append(exchange(sent[part], axis, gather_order(axis, part)[level]))
-        gram = gram + other
         if level:
             half = kept[0].shape[0] // 2
             sent = [have[half:] + more[half:] for have, more in zip(kept, got)]
             kept = [have[:half] + more[:half] for have, more in zip(kept, got)]
-    return kept, got, gram
-
-
-def all_sum(value):
-    for axis in ("items", "users"):
-        for bit in gather_order(axis, 0)[::-1]:
-            value = value + exchange(value, axis, bit)
+    return kept, got
+
+
+def sum_over(value, axis):
+    for bit in gather_order(axis, 0)[::-1]:
+        other = exchange(value, axis, bit)
+        value = value + other
     return value
 
 
@@ -94,7 +90,7 @@
 def tiles_kernel(count, source, target, *refs, places_in, places_out):
     piece_refs, refs = [refs[4 * part : 4 * part + 4] for part in range(PARTS)], refs[4 * PARTS :]
     tile_ref, keep_refs, send_refs = refs[0], refs[1 : 1 + PARTS], refs[1 + PARTS : 1 + 2 * PARTS]
-    gram_ref, pieces, total = refs[1 + 2 * PARTS :]
+    pieces, total = refs[1 + 2 * PARTS :]
     step = pl.program_id(0)
     half_out = keep_refs[-1].shape[0]
 
@@ -156,9 +152,6 @@
                     return carry
 
                 lax.fori_loop(0, quarter, finish, 0, unroll=4)
-        for at in range(GRAM):
-            held, near, own, far = [ref[ref.shape[0] - GRAM + at] for ref in piece_refs[0]]
-            gram_ref[at * ROWS : (at + 1) * ROWS] = (held + near) + (own + far)
 
 
 def tiles_product(count, source, target, pieces, tiles, blocks_out, axis_in, axis_out):
@@ -173,23 +166,23 @@
         places_in=[part_places(axis_in, part, 4 * quarter_in) for part in range(PARTS)],
         places_out=[part_places(axis_out, part, 2 * half_out) for part in range(PARTS)],
     )
-    out = pl.pallas_call(
+    call = pl.pallas_call(
         kernel,
-        out_shape=[jax.ShapeDtypeStruct((half_out, ROWS, TILE), jnp.float32)] * (2 * PARTS)
-        + [jax.ShapeDtypeStruct((K // 2, TILE), jnp.float32)],
+        out_shape=[jax.ShapeDtypeStruct((half_out, ROWS, TILE), jnp.float32)] * (2 * PARTS),
         grid_spec=pltpu.PrefetchScalarGridSpec(
             num_scalar_prefetch=3,
             grid=(tiles.shape[0] // BATCH,),
             in_specs=[VMEM_SPEC] * (4 * PARTS)
             + [pl.BlockSpec((BATCH, TILE, TILE), tile_block)],
-            out_specs=[VMEM_SPEC] * (2 * PARTS + 1),
+            out_specs=[VMEM_SPEC] * (2 * PARTS),
             scratch_shapes=[
                 pltpu.VMEM((4 * quarter_in, K, 2 * TILE), jnp.bfloat16),
                 pltpu.VMEM((2 * half_out + 1, K, TILE), jnp.float32),
             ],
         ),
-    )(count, source, target, *[piece for part in pieces for piece in part], tiles)
-    return out[:PARTS], out[PARTS : 2 * PARTS], out[-1]
+    )
+    out = call(count, source, target, *[piece for part in pieces for piece in part], tiles)
+    return out[:PARTS], out[PARTS:]
 
 
 def dot_full(left, right, contract):
@@ -253,7 +246,7 @@
     refs = list(refs)
     inverse = refs.pop(0)[...] if factored else None
     raw_refs, refs = list(zip(refs[:PARTS], refs[PARTS : 2 * PARTS])), refs[2 * PARTS :]
-    scale_ref, panel_ref, sent_refs = refs[0], refs[1], refs[2:]
+    scale_ref, panel_ref, gram_ref, sent_refs = refs[0], refs[1], refs[2], refs[3:]
     blocks = scale_ref.shape[0]
     gram = jnp.zeros((K, K), jnp.float32)
     for at in range(blocks):
@@ -266,24 +259,23 @@
         for part in range(PARTS):
             sent_refs[part][at] = scale * panel[part * ROWS : (part + 1) * ROWS]
         gram = gram + dot_full(panel, panel, (1, 1))
-    gram = jnp.concatenate([gram[: K // 2], gram[K // 2 :]], axis=1)
-    for at in range(GRAM):
-        sent_refs[0][blocks + at] = gram[at * ROWS : (at + 1) * ROWS]
+    gram_ref[...] = jnp.concatenate([gram[: K // 2], gram[K // 2 :]], axis=1)
 
 
 def scale_panel(inverse, kept, got, scale):
     factored = inverse is not None
     operands = ([inverse] if factored else []) + list(kept) + list(got) + [scale]
     blocks = scale.shape[0]
-    panel, *sent = pl.pallas_call(
+    panel, gram, *sent = pl.pallas_call(
         functools.partial(scale_kernel, factored=factored),
         out_shape=[jax.ShapeDtypeStruct((blocks, K, TILE), jnp.float32)]
-        + [jax.ShapeDtypeStruct((blocks + GRAM * (part == 0), ROWS, TILE), jnp.float32) for part in range(PARTS)],
+        + [jax.ShapeDtypeStruct((K // 2, TILE), jnp.float32)]
+        + [jax.ShapeDtypeStruct((blocks, ROWS, TILE), jnp.float32)] * PARTS,
         in_specs=[VMEM_SPEC] * len(operands),
-        out_specs=[VMEM_SPEC] * (1 + PARTS),
+        out_specs=[VMEM_SPEC] * (2 + PARTS),
         name="scale_panel",
     )(*operands)
-    return panel, sent
+    return panel, sent, gram
 
 
 def finish_kernel(inverse_ref, panel_ref, out_ref):
@@ -324,27 +316,28 @@
     start = start_items.astype(jnp.float32).reshape(PARTS, ROWS, item_blocks, TILE).transpose(0, 2, 1, 3)
     start = item_scale[None, :, None, :] * start
     sent = [start[part] for part in range(PARTS)]
-    sent[0] = jnp.concatenate([sent[0], jnp.zeros((GRAM, ROWS, TILE), jnp.float32)], axis=0)
     turned = turned_tiles(tiles, 0, 8, None)
     turned = turned_tiles(tiles, 8, 8, turned)
-    item_inverse = None
+    item_inverse = item_gram = None
     for step in range(ITERS):
+        if step:
+            item_gram = sum_over(sum_over(item_gram, "items"), "users")
+            item_inverse = inverse_factor(item_gram, item_total)
         pieces = gather(sent, "users")
-        kept, out, gram = tiles_product(count, col_at, row_to, pieces, turned, UT, "users", "items")
-        kept, got, gram = reduce_scatter(kept, out, gram, "items")
-        if step:
-            item_inverse = inverse_factor(gram, item_total)
-        user_raw, sent = scale_panel(item_inverse, kept, got, user_scale)
+        kept, out = tiles_product(count, col_at, row_to, pieces, turned, UT, "users", "items")
+        kept, got = reduce_scatter(kept, out, "items")
+        user_raw, sent, user_gram = scale_panel(item_inverse, kept, got, user_scale)
+        user_gram = sum_over(sum_over(user_gram, "users"), "items")
+        user_inverse = inverse_factor(user_gram, user_total)
         pieces = gather(sent, "items")
-        kept, out, gram = tiles_product(count, row_at, col_to, pieces, tiles, IT, "items", "users")
-        kept, got, gram = reduce_scatter(kept, out, gram, "users")
-        user_inverse = inverse_factor(gram, user_total)
+        kept, out = tiles_product(count, row_at, col_to, pieces, tiles, IT, "items", "users")
+        kept, got = reduce_scatter(kept, out, "users")
         if step == ITERS - 1:
             user_panel = finish_panel(user_inverse, user_raw)
             user_panel, got = lax.optimization_barrier((user_panel, got))
-        item_raw, sent = scale_panel(user_inverse, kept, got, item_scale)
-    item_inverse = inverse_factor(all_sum(sent[0][-GRAM:].reshape(K // 2, TILE)), item_total)
-    return user_panel, finish_panel(item_inverse, item_raw)
+        item_raw, sent, item_gram = scale_panel(user_inverse, kept, got, item_scale)
+    item_gram = sum_over(sum_over(item_gram, "items"), "users")
+    return user_panel, finish_panel(inverse_factor(item_gram, item_total), item_raw)
 
 
 def solution(mesh):

time: 364 us -> 377 us (1.036)
  waiting for transfers between devices: 77.2 us -> 151 us
  starting transfers between devices: 142 us -> 101 us
  other arithmetic: 34.7 us -> 20.6 us
    ppermute x109 -> x68, waiting for transfers between devices: 77.2 us -> 151 us  [exchange(): lax.ppermute(value, axis, [(at, at ^ bit) for at in range(lax.axis_size(a...]
    ppermute x109 -> x68, starting transfers between devices: 142 us -> 101 us  [exchange(): lax.ppermute(value, axis, [(at, at ^ bit) for at in range(lax.axis_size(a...]
    add x12 -> x6, other arithmetic: 15.8 us -> 8.63 us  [reduce_scatter(): sent = [have[half:] + more[half:] for have, more in zip(kept, got)]]
    add x12 -> x6, other arithmetic: 10.6 us -> 5.85 us  [reduce_scatter(): kept = [have[:half] + more[:half] for have, more in zip(kept, got)]]
    unnamed x156 -> x89, local copies, waits for them, and re-layouts: 7.96 us -> 7.93 us
  transfers between devices with their start and end apart: 109 -> 68, of which waited for: 44 -> 43; matrix products, arithmetic and copies ran while one was open for 10% -> 5% of each run, Pallas kernels for 12% -> 11%
where the time goes in v6:
time: 377 us; the launch traced here: 376 us
  waiting for transfers between devices  151 us (40%)
  starting transfers between devices  101 us (27%)
  Pallas kernels  93.1 us (25%)
  other arithmetic  20.6 us (5%)
  local copies, waits for them, and re-layouts  7.97 us (2%)
    ppermute x68, waiting for transfers between devices, exchange(): lax.ppermute(value, axis, [(at, at ^ bit) for at in range(lax.axis_size(a...  151 us
    ppermute x68, starting transfers between devices, exchange(): lax.ppermute(value, axis, [(at, at ^ bit) for at in range(lax.axis_size(a...  101 us
    pallas_call x4, Pallas kernels, tiles_product(): call(count, source, target, *[piece for part in pieces for piece in part]...  27.9 us
    pallas_call x4, Pallas kernels, inverse_factor(): pl.pallas_call(functools.partial(factor_kernel, total=total), out_shape=j...  27.1 us
    pallas_call x2, Pallas kernels, turned_tiles(): pl.pallas_call(turn_kernel, out_shape=jax.ShapeDtypeStruct(tiles.shape, t...  19.8 us
    pallas_call x4, Pallas kernels, scale_panel(): pl.pallas_call(functools.partial(scale_kernel, factored=factored), out_sh...  14 us
    add x6, other arithmetic, reduce_scatter(): sent = [have[half:] + more[half:] for have, more in zip(kept, got)]  8.63 us
    unnamed x89, local copies, waits for them, and re-layouts  7.93 us
  transfers between devices with their start and end apart: 68, of which 43 were waited for; matrix products, arithmetic and copies ran while one was open for 5% of the time, Pallas kernels for 11%

profile of v6, /device:TPU:0, one launch (start us, length us, event | category | flops | bytes accessed | tf_op | source)
XLA Modules:
  0.0 375.8 jit_solution(2857898450414053301)
XLA Ops:
  2.4 4.1 %collective-permute-start.4 = (f32[8,32,128]{2,1,0:T(8,128)S(1)}, f32[8,32,128]{2,1,0:T(8,128)S(1)}, u32[]{:S(2)}, u32[]{:S(2)}) collective-permute-start(f32[8,32,128]{2,1,0:T(8,128)S(1)} %get-tuple-element.92), channel_id=1, source_target_pairs={{0,16},{4,20},{8,24},{12,28},{16,0},{20,4},{24,8},{28,12},{1,17},{... | collective-permute-start | bytes 393224 | tf_op jit(solution)/shard_map/ppermute | solution.py:36
  6.6 9.9 %collective-permute-done.4 = f32[8,32,128]{2,1,0:T(8,128)S(1)} collective-permute-done((f32[8,32,128]{2,1,0:T(8,128)S(1)}, f32[8,32,128]{2,1,0:T(8,128)S(1)}, u32[]{:S(2)}, u32[]{:S(2)}) %collective-permute-start.4) | collective-permute-done | bytes 131104 | tf_op jit(solution)/shard_map/ppermute | solution.py:36
  22.1 2.4 collective-permute-done.5.refs_5_
  30.0 9.9 %turned_tiles.2.refs_0_ = bf16[512,128,128]{2,1,0:T(8,128)(2,1)} custom-call(bf16[512,128,128]{2,1,0:T(8,128)(2,1)} %bitcast.24), custom_call_target="tpu_custom_call" | custom-call | tf_op jit(solution)/shard_map/turned_tiles/pallas_call | solution.py:224
  39.9 9.9 %turned_tiles.3.refs_8_ = bf16[512,128,128]{2,1,0:T(8,128)(2,1)} custom-call(bf16[512,128,128]{2,1,0:T(8,128)(2,1)} %bitcast.25, bf16[512,128,128]{2,1,0:T(8,128)(2,1)} %turned_tiles.2.refs_0_), custom_call_target="tpu_custom_call", output_to_operand_aliasing={{}: (1, {})} | custom-call | tf_op jit(solution)/shard_map/turned_tiles/pallas_call | solution.py:224
  51.4 7.0 %shard_map.86 = (f32[32,32,128]{2,1,0:T(8,128)}, f32[32,32,128]{2,1,0:T(8,128)}, f32[32,32,128]{2,1,0:T(8,128)}, f32[32,32,128]{2,1,0:T(8,128)}) custom-call(s32[1]{0:T(128)} %bitcast.19.count, s32[512]{0:T(512)} %get-tuple-element.65.source, s32[512]{0:T(512)} %get-tuple-element.94.target, f32[16,32,128]{2,1,0:T(8,128)} %copy-done.1, ...), custom_call_target="tpu_custom_call" | custom-call | tf_op jit(solution)/shard_map/pallas_call | solution.py:184
  62.3 8.5 %collective-permute-start.11 = (f32[16,32,128]{2,1,0:T(8,128)S(1)}, f32[16,32,128]{2,1,0:T(8,128)S(1)}, u32[]{:S(2)}, u32[]{:S(2)}) collective-permute-start(f32[16,32,128]{2,1,0:T(8,128)S(1)} %get-tuple-element.80), channel_id=1, source_target_pairs={{0,2},{1,3},{2,0},{3,1},{4,6},{5,7},{6,4},{7,5},{8,10},{9,11},{10,... | collective-permute-start | bytes 786440 | tf_op jit(solution)/shard_map/ppermute | solution.py:36
  73.2 4.7 %collective-permute-done.11.refs_3_ = f32[16,32,128]{2,1,0:T(8,128)S(1)} collective-permute-done((f32[16,32,128]{2,1,0:T(8,128)S(1)}, f32[16,32,128]{2,1,0:T(8,128)S(1)}, u32[]{:S(2)}, u32[]{:S(2)}) %collective-permute-start.11) | collective-permute-done | bytes 262176 | tf_op jit(solution)/shard_map/ppermute | solution.py:36
  78.0 5.1 %collective-permute-done.10.refs_2_ = f32[16,32,128]{2,1,0:T(8,128)S(1)} collective-permute-done((f32[16,32,128]{2,1,0:T(8,128)S(1)}, f32[16,32,128]{2,1,0:T(8,128)S(1)}, u32[]{:S(2)}, u32[]{:S(2)}) %collective-permute-start.10) | collective-permute-done | bytes 262176 | tf_op jit(solution)/shard_map/ppermute | solution.py:36
  83.7 2.9 scale_panel.4
  89.2 6.8 %collective-permute-done.17.refs_1_ = f32[16,32,128]{2,1,0:T(8,128)S(1)} collective-permute-done((f32[16,32,128]{2,1,0:T(8,128)}, f32[16,32,128]{2,1,0:T(8,128)S(1)}, u32[]{:S(2)}, u32[]{:S(2)}) %collective-permute-start.17) | collective-permute-done | bytes 262176 | tf_op jit(solution)/shard_map/ppermute | solution.py:36
  96.1 4.2 %collective-permute-done.20.refs_5_ = f32[16,32,128]{2,1,0:T(8,128)S(1)} collective-permute-done((f32[16,32,128]{2,1,0:T(8,128)}, f32[16,32,128]{2,1,0:T(8,128)S(1)}, u32[]{:S(2)}, u32[]{:S(2)}) %collective-permute-start.20) | collective-permute-done | bytes 262176 | tf_op jit(solution)/shard_map/ppermute | solution.py:36
  102.5 7.0 %shard_map.87 = (f32[32,32,128]{2,1,0:T(8,128)}, f32[32,32,128]{2,1,0:T(8,128)}, f32[32,32,128]{2,1,0:T(8,128)}, f32[32,32,128]{2,1,0:T(8,128)}) custom-call(s32[1]{0:T(128)} %bitcast.20.count, s32[512]{0:T(512)} %get-tuple-element.95.source, s32[512]{0:T(512)} %get-tuple-element.64.target, f32[16,32,128]{2,1,0:T(8,128)} %get-tuple-element.38.refs_0_, ...), custom_call_target="tpu_custom_call" | custom-call | tf_op jit(solution)/shard_map/pallas_call | solution.py:184
  109.6 11.8 %collective-permute-done.25 = f32[32,32,128]{2,1,0:T(8,128)S(1)} collective-permute-done((f32[32,32,128]{2,1,0:T(8,128)}, f32[32,32,128]{2,1,0:T(8,128)S(1)}, u32[]{:S(2)}, u32[]{:S(2)}) %collective-permute-start.25) | collective-permute-done | bytes 524320 | tf_op jit(solution)/shard_map/ppermute | solution.py:36
  124.8 5.0 %collective-permute-done.26 = f32[16,32,128]{2,1,0:T(8,128)S(1)} collective-permute-done((f32[16,32,128]{2,1,0:T(8,128)S(1)}, f32[16,32,128]{2,1,0:T(8,128)S(1)}, u32[]{:S(2)}, u32[]{:S(2)}) %collective-permute-start.26) | collective-permute-done | bytes 262176 | tf_op jit(solution)/shard_map/ppermute | solution.py:36
  130.5 12.1 %collective-permute-start.28 = (f32[8,32,128]{2,1,0:T(8,128)S(1)}, f32[8,32,128]{2,1,0:T(8,128)S(1)}, u32[]{:S(2)}, u32[]{:S(2)}) collective-permute-start(f32[8,32,128]{2,1,0:T(8,128)S(1)} %get-tuple-element.88), channel_id=1, source_target_pairs={{0,16},{4,20},{8,24},{12,28},{16,0},{20,4},{24,8},{28,12},{1,17},{... | collective-permute-start | bytes 393224 | tf_op jit(solution)/shard_map/ppermute | solution.py:36
  143.8 2.6 collective-permute-start.12
  149.0 3.6 collective-permute-done.13
  153.7 3.5 collective-permute-done.14
  158.8 3.3 collective-permute-done.16
  162.8 6.8 %factor.4.refs_0_ = f32[64,64]{1,0:T(8,128)} custom-call(f32[32,128]{1,0:T(8,128)} %add.174.gram_ref), custom_call_target="tpu_custom_call" | custom-call | tf_op jit(solution)/shard_map/factor/pallas_call | solution.py:236
  170.3 3.2 scale_panel.5
  178.4 6.4 %collective-permute-done.38 = f32[8,32,128]{2,1,0:T(8,128)S(1)} collective-permute-done((f32[8,32,128]{2,1,0:T(8,128)}, f32[8,32,128]{2,1,0:T(8,128)S(1)}, u32[]{:S(2)}, u32[]{:S(2)}) %collective-permute-start.38) | collective-permute-done | bytes 131104 | tf_op jit(solution)/shard_map/ppermute | solution.py:36
  190.9 2.8 collective-permute-done.39.refs_5_
  193.7 2.8 collective-permute-done.35.refs_1_
  198.1 4.0 %collective-permute-done.40.refs_6_ = f32[16,32,128]{2,1,0:T(8,128)S(1)} collective-permute-done((f32[16,32,128]{2,1,0:T(8,128)S(1)}, f32[16,32,128]{2,1,0:T(8,128)S(1)}, u32[]{:S(2)}, u32[]{:S(2)}) %collective-permute-start.40) | collective-permute-done | bytes 262176 | tf_op jit(solution)/shard_map/ppermute | solution.py:36
  202.1 4.3 %collective-permute-done.41.refs_7_ = f32[16,32,128]{2,1,0:T(8,128)S(1)} collective-permute-done((f32[16,32,128]{2,1,0:T(8,128)S(1)}, f32[16,32,128]{2,1,0:T(8,128)S(1)}, u32[]{:S(2)}, u32[]{:S(2)}) %collective-permute-start.41) | collective-permute-done | bytes 262176 | tf_op jit(solution)/shard_map/ppermute | solution.py:36
  207.2 7.0 %shard_map.88 = (f32[32,32,128]{2,1,0:T(8,128)}, f32[32,32,128]{2,1,0:T(8,128)}, f32[32,32,128]{2,1,0:T(8,128)}, f32[32,32,128]{2,1,0:T(8,128)}) custom-call(s32[1]{0:T(128)} %bitcast.21.count, s32[512]{0:T(512)} %get-tuple-element.65.source, s32[512]{0:T(512)} %get-tuple-element.94.target, f32[16,32,128]{2,1,0:T(8,128)} %copy-done.2, ...), custom_call_target="tpu_custom_call" | custom-call | tf_op jit(solution)/shard_map/pallas_call | solution.py:184
  218.1 7.1 %collective-permute-start.45 = (f32[16,32,128]{2,1,0:T(8,128)S(1)}, f32[16,32,128]{2,1,0:T(8,128)S(1)}, u32[]{:S(2)}, u32[]{:S(2)}) collective-permute-start(f32[16,32,128]{2,1,0:T(8,128)S(1)} %get-tuple-element.72), channel_id=1, source_target_pairs={{0,2},{1,3},{2,0},{3,1},{4,6},{5,7},{6,4},{7,5},{8,10},{9,11},{10,... | collective-permute-start | bytes 786440 | tf_op jit(solution)/shard_map/ppermute | solution.py:36
  230.2 7.5 %collective-permute-done.30 = f32[32,128]{1,0:T(8,128)S(1)} collective-permute-done((f32[32,128]{1,0:T(8,128)S(1)}, f32[32,128]{1,0:T(8,128)S(1)}, u32[]{:S(2)}, u32[]{:S(2)}) %collective-permute-start.30) | collective-permute-done | bytes 16416 | tf_op jit(solution)/shard_map/ppermute | solution.py:36
  242.5 2.8 collective-permute-done.32
  245.3 2.6 collective-permute-start.33
  250.5 6.8 %factor.5.refs_0_ = f32[64,64]{1,0:T(8,128)} custom-call(f32[32,128]{1,0:T(8,128)} %add.187.gram_ref), custom_call_target="tpu_custom_call" | custom-call | tf_op jit(solution)/shard_map/factor/pallas_call | solution.py:236
  258.1 4.5 %scale_panel.6 = (f32[16,64,128]{2,1,0:T(8,128)}, f32[32,128]{1,0:T(8,128)}, f32[16,32,128]{2,1,0:T(8,128)}, f32[16,32,128]{2,1,0:T(8,128)}) custom-call(f32[64,64]{1,0:T(8,128)} %factor.5.refs_0_, f32[16,32,128]{2,1,0:T(8,128)} %get-tuple-element.75.refs_1_, f32[16,32,128]{2,1,0:T(8,128)} %get-tuple-element.73.refs_2_, f32[16,32,128]{2,1,0:T(8,128)} %copy-done.29, ...), custom_call_target="tpu_custom_call" | custom-call | tf_op jit(solution)/shard_map/scale_panel/pallas_call | solution.py:269
  265.2 4.8 %collective-permute-done.51.refs_1_ = f32[16,32,128]{2,1,0:T(8,128)S(1)} collective-permute-done((f32[16,32,128]{2,1,0:T(8,128)}, f32[16,32,128]{2,1,0:T(8,128)S(1)}, u32[]{:S(2)}, u32[]{:S(2)}) %collective-permute-start.51) | collective-permute-done | bytes 262176 | tf_op jit(solution)/shard_map/ppermute | solution.py:36
  270.0 2.8 collective-permute-done.54.refs_5_
  275.0 7.0 %shard_map.89 = (f32[32,32,128]{2,1,0:T(8,128)}, f32[32,32,128]{2,1,0:T(8,128)}, f32[32,32,128]{2,1,0:T(8,128)}, f32[32,32,128]{2,1,0:T(8,128)}) custom-call(s32[1]{0:T(128)} %bitcast.22.count, s32[512]{0:T(512)} %get-tuple-element.95.source, s32[512]{0:T(512)} %get-tuple-element.64.target, f32[16,32,128]{2,1,0:T(8,128)} %get-tuple-element.53.refs_0_, ...), custom_call_target="tpu_custom_call" | custom-call | tf_op jit(solution)/shard_map/pallas_call | solution.py:184
  283.6 7.8 %collective-permute-done.60 = f32[32,32,128]{2,1,0:T(8,128)S(1)} collective-permute-done((f32[32,32,128]{2,1,0:T(8,128)}, f32[32,32,128]{2,1,0:T(8,128)S(1)}, u32[]{:S(2)}, u32[]{:S(2)}) %collective-permute-start.60) | collective-permute-done | bytes 524320 | tf_op jit(solution)/shard_map/ppermute | solution.py:36
  295.3 6.4 %collective-permute-done.61 = f32[16,32,128]{2,1,0:T(8,128)S(1)} collective-permute-done((f32[16,32,128]{2,1,0:T(8,128)S(1)}, f32[16,32,128]{2,1,0:T(8,128)S(1)}, u32[]{:S(2)}, u32[]{:S(2)}) %collective-permute-start.61) | collective-permute-done | bytes 262176 | tf_op jit(solution)/shard_map/ppermute | solution.py:36
  302.4 12.4 %collective-permute-start.62 = (f32[8,32,128]{2,1,0:T(8,128)S(1)}, f32[8,32,128]{2,1,0:T(8,128)S(1)}, u32[]{:S(2)}, u32[]{:S(2)}) collective-permute-start(f32[8,32,128]{2,1,0:T(8,128)S(1)} %get-tuple-element.85), channel_id=1, source_target_pairs={{0,16},{4,20},{8,24},{12,28},{16,0},{20,4},{24,8},{28,12},{1,17},{... | collective-permute-start | bytes 393224 | tf_op jit(solution)/shard_map/ppermute | solution.py:36
  316.1 2.4 collective-permute-start.46
  321.5 3.3 collective-permute-done.47
  326.0 3.5 collective-permute-done.48
  335.0 6.8 %factor.6.inverse_ref.refs_0_ = f32[64,64]{1,0:T(8,128)} custom-call(f32[32,128]{1,0:T(8,128)} %add.196.gram_ref), custom_call_target="tpu_custom_call" | custom-call | tf_op jit(solution)/shard_map/factor/pallas_call | solution.py:236
  341.8 2.4 finish_panel.2
  344.9 3.3 scale_panel.7
  361.7 2.9 collective-permute-start.67
  367.0 6.8 %factor.7.inverse_ref = f32[64,64]{1,0:T(8,128)} custom-call(f32[32,128]{1,0:T(8,128)} %add.209.gram_ref), custom_call_target="tpu_custom_call" | custom-call | tf_op jit(solution)/shard_map/factor/pallas_call | solution.py:236
  (235 shorter events, 108.3 us)
Async XLA Ops:
  2.4 14.1 %collective-permute-start.4 = (f32[8,32,128]{2,1,0:T(8,128)S(1)}, f32[8,32,128]{2,1,0:T(8,128)S(1)}, u32[]{:S(2)}, u32[]{:S(2)}) collective-permute-start(f32[8,32,128]{2,1,0:T(8,128)S(1)} %get-tuple-element.92), channel_id=1, source_target_pairs={{0,16},{4,20},{8,24},{12,28},{16,0},{20,4},{24,8},{28,12},{1,17},{... | collective-permute-start | bytes 393224 | tf_op jit(solution)/shard_map/ppermute | solution.py:36
  6.5 11.9 %collective-permute-start = (f32[8,32,128]{2,1,0:T(8,128)S(1)}, f32[8,32,128]{2,1,0:T(8,128)S(1)}, u32[]{:S(2)}, u32[]{:S(2)}) collective-permute-start(f32[8,32,128]{2,1,0:T(8,128)S(1)} %get-tuple-element.93), channel_id=1, source_target_pairs={{0,16},{4,20},{8,24},{12,28},{16,0},{20,4},{24,8},{28,12},{1,17},{... | collective-permute-start | bytes 393224 | tf_op jit(solution)/shard_map/ppermute | solution.py:36
  16.5 8.0 %collective-permute-start.5 = (f32[16,32,128]{2,1,0:T(8,128)S(1)}, f32[16,32,128]{2,1,0:T(8,128)S(1)}, u32[]{:S(2)}, u32[]{:S(2)}) collective-permute-start(f32[16,32,128]{2,1,0:T(8,128)S(1)} %pad_maximum_fusion.1.refs_4_), channel_id=1, source_target_pairs={{0,4},{4,0},{8,12},{12,8},{16,20},{20,16},{24,28},{28,24},{1,5},{5... | collective-permute-start | bytes 786440 | tf_op jit(solution)/shard_map/ppermute | solution.py:36
  18.5 9.2 %collective-permute-start.1 = (f32[16,32,128]{2,1,0:T(8,128)S(1)}, f32[16,32,128]{2,1,0:T(8,128)S(1)}, u32[]{:S(2)}, u32[]{:S(2)}) collective-permute-start(f32[16,32,128]{2,1,0:T(8,128)S(1)} %pad_maximum_fusion.refs_0_), channel_id=1, source_target_pairs={{0,8},{4,12},{8,0},{12,4},{16,24},{20,28},{24,16},{28,20},{1,9},{5... | collective-permute-start | bytes 786440 | tf_op jit(solution)/shard_map/ppermute | solution.py:36
  19.3 31.1 %collective-permute-start.6 = (f32[16,32,128]{2,1,0:T(8,128)S(1)}, f32[16,32,128]{2,1,0:T(8,128)S(1)}, u32[]{:S(2)}, u32[]{:S(2)}) collective-permute-start(f32[16,32,128]{2,1,0:T(8,128)S(1)} %pad_maximum_fusion.1.refs_4_), channel_id=1, source_target_pairs={{0,8},{4,12},{8,0},{12,4},{16,24},{20,28},{24,16},{28,20},{1,9},{5... | collective-permute-start | bytes 786440 | tf_op jit(solution)/shard_map/ppermute | solution.py:36
  20.6 29.8 %collective-permute-start.2 = (f32[16,32,128]{2,1,0:T(8,128)S(1)}, f32[16,32,128]{2,1,0:T(8,128)S(1)}, u32[]{:S(2)}, u32[]{:S(2)}) collective-permute-start(f32[16,32,128]{2,1,0:T(8,128)S(1)} %pad_maximum_fusion.refs_0_), channel_id=1, source_target_pairs={{0,4},{4,0},{8,12},{12,8},{16,20},{20,16},{24,28},{28,24},{1,5},{5... | collective-permute-start | bytes 786440 | tf_op jit(solution)/shard_map/ppermute | solution.py:36
  24.6 25.9 %collective-permute-start.7 = (f32[16,32,128]{2,1,0:T(8,128)S(1)}, f32[16,32,128]{2,1,0:T(8,128)S(1)}, u32[]{:S(2)}, u32[]{:S(2)}) collective-permute-start(f32[16,32,128]{2,1,0:T(8,128)S(1)} %collective-permute-done.5.refs_5_), channel_id=1, source_target_pairs={{0,8},{4,12},{8,0},{12,4},{16,24},{20,28},{24,16},{28,20},{1,9},{5... | collective-permute-start | bytes 786440 | tf_op jit(solution)/shard_map/ppermute | solution.py:36
  27.7 22.7 %collective-permute-start.3 = (f32[16,32,128]{2,1,0:T(8,128)S(1)}, f32[16,32,128]{2,1,0:T(8,128)S(1)}, u32[]{:S(2)}, u32[]{:S(2)}) collective-permute-start(f32[16,32,128]{2,1,0:T(8,128)S(1)} %collective-permute-done.1.refs_1_), channel_id=1, source_target_pairs={{0,4},{4,0},{8,12},{12,8},{16,20},{20,16},{24,28},{28,24},{1,5},{5... | collective-permute-start | bytes 786440 | tf_op jit(solution)/shard_map/ppermute | solution.py:36
  58.4 12.5 %collective-permute-start.8 = (f32[32,32,128]{2,1,0:T(8,128)}, f32[32,32,128]{2,1,0:T(8,128)S(1)}, u32[]{:S(2)}, u32[]{:S(2)}) collective-permute-start(f32[32,32,128]{2,1,0:T(8,128)} %get-tuple-element.34), channel_id=1, source_target_pairs={{0,1},{1,0},{2,3},{3,2},{4,5},{5,4},{6,7},{7,6},{8,9},{9,8},{10,11... | collective-permute-start | bytes 1572872 | tf_op jit(solution)/shard_map/ppermute | solution.py:36
  62.3 15.7 %collective-permute-start.11 = (f32[16,32,128]{2,1,0:T(8,128)S(1)}, f32[16,32,128]{2,1,0:T(8,128)S(1)}, u32[]{:S(2)}, u32[]{:S(2)}) collective-permute-start(f32[16,32,128]{2,1,0:T(8,128)S(1)} %get-tuple-element.80), channel_id=1, source_target_pairs={{0,2},{1,3},{2,0},{3,1},{4,6},{5,7},{6,4},{7,5},{8,10},{9,11},{10,... | collective-permute-start | bytes 786440 | tf_op jit(solution)/shard_map/ppermute | solution.py:36
  72.6 10.4 %collective-permute-start.10 = (f32[16,32,128]{2,1,0:T(8,128)S(1)}, f32[16,32,128]{2,1,0:T(8,128)S(1)}, u32[]{:S(2)}, u32[]{:S(2)}) collective-permute-start(f32[16,32,128]{2,1,0:T(8,128)S(1)} %get-tuple-element.82), channel_id=1, source_target_pairs={{0,2},{1,3},{2,0},{3,1},{4,6},{5,7},{6,4},{7,5},{8,10},{9,11},{10,... | collective-permute-start | bytes 786440 | tf_op jit(solution)/shard_map/ppermute | solution.py:36
  86.7 9.4 %collective-permute-start.17 = (f32[16,32,128]{2,1,0:T(8,128)}, f32[16,32,128]{2,1,0:T(8,128)S(1)}, u32[]{:S(2)}, u32[]{:S(2)}) collective-permute-start(f32[16,32,128]{2,1,0:T(8,128)} %get-tuple-element.38.refs_0_), channel_id=1, source_target_pairs={{0,2},{1,3},{2,0},{3,1},{4,6},{5,7},{6,4},{7,5},{8,10},{9,11},{10,... | collective-permute-start | bytes 786440 | tf_op jit(solution)/shard_map/ppermute | solution.py:36
  88.4 11.9 %collective-permute-start.20 = (f32[16,32,128]{2,1,0:T(8,128)}, f32[16,32,128]{2,1,0:T(8,128)S(1)}, u32[]{:S(2)}, u32[]{:S(2)}) collective-permute-start(f32[16,32,128]{2,1,0:T(8,128)} %get-tuple-element.39.refs_4_), channel_id=1, source_target_pairs={{0,2},{1,3},{2,0},{3,1},{4,6},{5,7},{6,4},{7,5},{8,10},{9,11},{10,... | collective-permute-start | bytes 786440 | tf_op jit(solution)/shard_map/ppermute | solution.py:36
  88.7 11.6 %collective-permute-start.18 = (f32[16,32,128]{2,1,0:T(8,128)}, f32[16,32,128]{2,1,0:T(8,128)S(1)}, u32[]{:S(2)}, u32[]{:S(2)}) collective-permute-start(f32[16,32,128]{2,1,0:T(8,128)} %get-tuple-element.38.refs_0_), channel_id=1, source_target_pairs={{0,1},{1,0},{2,3},{3,2},{4,5},{5,4},{6,7},{7,6},{8,9},{9,8},{10,11... | collective-permute-start | bytes 786440 | tf_op jit(solution)/shard_map/ppermute | solution.py:36
  88.7 11.6 %collective-permute-start.21 = (f32[16,32,128]{2,1,0:T(8,128)}, f32[16,32,128]{2,1,0:T(8,128)S(1)}, u32[]{:S(2)}, u32[]{:S(2)}) collective-permute-start(f32[16,32,128]{2,1,0:T(8,128)} %get-tuple-element.39.refs_4_), channel_id=1, source_target_pairs={{0,1},{1,0},{2,3},{3,2},{4,5},{5,4},{6,7},{7,6},{8,9},{9,8},{10,11... | collective-permute-start | bytes 786440 | tf_op jit(solution)/shard_map/ppermute | solution.py:36
  109.5 11.9 %collective-permute-start.25 = (f32[32,32,128]{2,1,0:T(8,128)}, f32[32,32,128]{2,1,0:T(8,128)S(1)}, u32[]{:S(2)}, u32[]{:S(2)}) collective-permute-start(f32[32,32,128]{2,1,0:T(8,128)} %get-tuple-element.43), channel_id=1, source_target_pairs={{0,8},{4,12},{8,0},{12,4},{16,24},{20,28},{24,16},{28,20},{1,9},{5... | collective-permute-start | bytes 1572872 | tf_op jit(solution)/shard_map/ppermute | solution.py:36
  109.5 13.1 %collective-permute-start.23 = (f32[32,32,128]{2,1,0:T(8,128)}, f32[32,32,128]{2,1,0:T(8,128)S(1)}, u32[]{:S(2)}, u32[]{:S(2)}) collective-permute-start(f32[32,32,128]{2,1,0:T(8,128)} %get-tuple-element.41), channel_id=1, source_target_pairs={{0,4},{4,0},{8,12},{12,8},{16,20},{20,16},{24,28},{28,24},{1,5},{5... | collective-permute-start | bytes 1572872 | tf_op jit(solution)/shard_map/ppermute | solution.py:36
  122.5 7.3 %collective-permute-start.26 = (f32[16,32,128]{2,1,0:T(8,128)S(1)}, f32[16,32,128]{2,1,0:T(8,128)S(1)}, u32[]{:S(2)}, u32[]{:S(2)}) collective-permute-start(f32[16,32,128]{2,1,0:T(8,128)S(1)} %get-tuple-element.77), channel_id=1, source_target_pairs={{0,4},{4,0},{8,12},{12,8},{16,20},{20,16},{24,28},{28,24},{1,5},{5... | collective-permute-start | bytes 786440 | tf_op jit(solution)/shard_map/ppermute | solution.py:36
  123.7 18.9 %collective-permute-start.24 = (f32[16,32,128]{2,1,0:T(8,128)S(1)}, f32[16,32,128]{2,1,0:T(8,128)S(1)}, u32[]{:S(2)}, u32[]{:S(2)}) collective-permute-start(f32[16,32,128]{2,1,0:T(8,128)S(1)} %get-tuple-element.79), channel_id=1, source_target_pairs={{0,8},{4,12},{8,0},{12,4},{16,24},{20,28},{24,16},{28,20},{1,9},{5... | collective-permute-start | bytes 786440 | tf_op jit(solution)/shard_map/ppermute | solution.py:36
  130.5 39.1 %collective-permute-start.28 = (f32[8,32,128]{2,1,0:T(8,128)S(1)}, f32[8,32,128]{2,1,0:T(8,128)S(1)}, u32[]{:S(2)}, u32[]{:S(2)}) collective-permute-start(f32[8,32,128]{2,1,0:T(8,128)S(1)} %get-tuple-element.88), channel_id=1, source_target_pairs={{0,16},{4,20},{8,24},{12,28},{16,0},{20,4},{24,8},{28,12},{1,17},{... | collective-permute-start | bytes 393224 | tf_op jit(solution)/shard_map/ppermute | solution.py:36
  143.3 26.3 %collective-permute-start.27 = (f32[8,32,128]{2,1,0:T(8,128)S(1)}, f32[8,32,128]{2,1,0:T(8,128)S(1)}, u32[]{:S(2)}, u32[]{:S(2)}) collective-permute-start(f32[8,32,128]{2,1,0:T(8,128)S(1)} %get-tuple-element.90), channel_id=1, source_target_pairs={{0,16},{4,20},{8,24},{12,28},{16,0},{20,4},{24,8},{28,12},{1,17},{... | collective-permute-start | bytes 393224 | tf_op jit(solution)/shard_map/ppermute | solution.py:36
  152.6 4.6 %collective-permute-start.14 = (f32[32,128]{1,0:T(8,128)S(1)}, f32[32,128]{1,0:T(8,128)S(1)}, u32[]{:S(2)}, u32[]{:S(2)}) collective-permute-start(f32[32,128]{1,0:T(8,128)S(1)} %add.171), channel_id=1, source_target_pairs={{0,16},{4,20},{8,24},{12,28},{16,0},{20,4},{24,8},{28,12},{1,17},{... | collective-permute-start | bytes 49160 | tf_op jit(solution)/shard_map/ppermute | solution.py:36
  173.5 11.3 %collective-permute-start.38 = (f32[8,32,128]{2,1,0:T(8,128)}, f32[8,32,128]{2,1,0:T(8,128)S(1)}, u32[]{:S(2)}, u32[]{:S(2)}) collective-permute-start(f32[8,32,128]{2,1,0:T(8,128)} %get-tuple-element.46), channel_id=1, source_target_pairs={{0,16},{4,20},{8,24},{12,28},{16,0},{20,4},{24,8},{28,12},{1,17},{... | collective-permute-start | bytes 393224 | tf_op jit(solution)/shard_map/ppermute | solution.py:36
  175.6 11.6 %collective-permute-start.34 = (f32[8,32,128]{2,1,0:T(8,128)}, f32[8,32,128]{2,1,0:T(8,128)S(1)}, u32[]{:S(2)}, u32[]{:S(2)}) collective-permute-start(f32[8,32,128]{2,1,0:T(8,128)} %get-tuple-element.45), channel_id=1, source_target_pairs={{0,16},{4,20},{8,24},{12,28},{16,0},{20,4},{24,8},{28,12},{1,17},{... | collective-permute-start | bytes 393224 | tf_op jit(solution)/shard_map/ppermute | solution.py:36
  184.8 8.9 %collective-permute-start.39 = (f32[16,32,128]{2,1,0:T(8,128)S(1)}, f32[16,32,128]{2,1,0:T(8,128)S(1)}, u32[]{:S(2)}, u32[]{:S(2)}) collective-permute-start(f32[16,32,128]{2,1,0:T(8,128)S(1)} %constant_dynamic-update-slice_fusion.2.refs_4_), channel_id=1, source_target_pairs={{0,4},{4,0},{8,12},{12,8},{16,20},{20,16},{24,28},{28,24},{1,5},{5... | collective-permute-start | bytes 786440 | tf_op jit(solution)/shard_map/ppermute | solution.py:36
  187.2 9.2 %collective-permute-start.35 = (f32[16,32,128]{2,1,0:T(8,128)S(1)}, f32[16,32,128]{2,1,0:T(8,128)S(1)}, u32[]{:S(2)}, u32[]{:S(2)}) collective-permute-start(f32[16,32,128]{2,1,0:T(8,128)S(1)} %constant_dynamic-update-slice_fusion.refs_0_), channel_id=1, source_target_pairs={{0,8},{4,12},{8,0},{12,4},{16,24},{20,28},{24,16},{28,20},{1,9},{5... | collective-permute-start | bytes 786440 | tf_op jit(solution)/shard_map/ppermute | solution.py:36
  187.3 14.8 %collective-permute-start.40 = (f32[16,32,128]{2,1,0:T(8,128)S(1)}, f32[16,32,128]{2,1,0:T(8,128)S(1)}, u32[]{:S(2)}, u32[]{:S(2)}) collective-permute-start(f32[16,32,128]{2,1,0:T(8,128)S(1)} %constant_dynamic-update-slice_fusion.2.refs_4_), channel_id=1, source_target_pairs={{0,8},{4,12},{8,0},{12,4},{16,24},{20,28},{24,16},{28,20},{1,9},{5... | collective-permute-start | bytes 786440 | tf_op jit(solution)/shard_map/ppermute | solution.py:36
  189.3 12.8 %collective-permute-start.36 = (f32[16,32,128]{2,1,0:T(8,128)S(1)}, f32[16,32,128]{2,1,0:T(8,128)S(1)}, u32[]{:S(2)}, u32[]{:S(2)}) collective-permute-start(f32[16,32,128]{2,1,0:T(8,128)S(1)} %constant_dynamic-update-slice_fusion.refs_0_), channel_id=1, source_target_pairs={{0,4},{4,0},{8,12},{12,8},{16,20},{20,16},{24,28},{28,24},{1,5},{5... | collective-permute-start | bytes 786440 | tf_op jit(solution)/shard_map/ppermute | solution.py:36
  193.7 12.7 %collective-permute-start.41 = (f32[16,32,128]{2,1,0:T(8,128)S(1)}, f32[16,32,128]{2,1,0:T(8,128)S(1)}, u32[]{:S(2)}, u32[]{:S(2)}) collective-permute-start(f32[16,32,128]{2,1,0:T(8,128)S(1)} %collective-permute-done.39.refs_5_), channel_id=1, source_target_pairs={{0,8},{4,12},{8,0},{12,4},{16,24},{20,28},{24,16},{28,20},{1,9},{5... | collective-permute-start | bytes 786440 | tf_op jit(solution)/shard_map/ppermute | solution.py:36
  196.5 10.0 %collective-permute-start.37 = (f32[16,32,128]{2,1,0:T(8,128)S(1)}, f32[16,32,128]{2,1,0:T(8,128)S(1)}, u32[]{:S(2)}, u32[]{:S(2)}) collective-permute-start(f32[16,32,128]{2,1,0:T(8,128)S(1)} %collective-permute-done.35.refs_1_), channel_id=1, source_target_pairs={{0,4},{4,0},{8,12},{12,8},{16,20},{20,16},{24,28},{28,24},{1,5},{5... | collective-permute-start | bytes 786440 | tf_op jit(solution)/shard_map/ppermute | solution.py:36
  214.2 11.0 %collective-permute-start.42 = (f32[32,32,128]{2,1,0:T(8,128)}, f32[32,32,128]{2,1,0:T(8,128)S(1)}, u32[]{:S(2)}, u32[]{:S(2)}) collective-permute-start(f32[32,32,128]{2,1,0:T(8,128)} %get-tuple-element.48), channel_id=1, source_target_pairs={{0,1},{1,0},{2,3},{3,2},{4,5},{5,4},{6,7},{7,6},{8,9},{9,8},{10,11... | collective-permute-start | bytes 1572872 | tf_op jit(solution)/shard_map/ppermute | solution.py:36
  218.1 39.2 %collective-permute-start.45 = (f32[16,32,128]{2,1,0:T(8,128)S(1)}, f32[16,32,128]{2,1,0:T(8,128)S(1)}, u32[]{:S(2)}, u32[]{:S(2)}) collective-permute-start(f32[16,32,128]{2,1,0:T(8,128)S(1)} %get-tuple-element.72), channel_id=1, source_target_pairs={{0,2},{1,3},{2,0},{3,1},{4,6},{5,7},{6,4},{7,5},{8,10},{9,11},{10,... | collective-permute-start | bytes 786440 | tf_op jit(solution)/shard_map/ppermute | solution.py:36
  227.0 30.3 %collective-permute-start.44 = (f32[16,32,128]{2,1,0:T(8,128)S(1)}, f32[16,32,128]{2,1,0:T(8,128)S(1)}, u32[]{:S(2)}, u32[]{:S(2)}) collective-permute-start(f32[16,32,128]{2,1,0:T(8,128)S(1)} %get-tuple-element.74), channel_id=1, source_target_pairs={{0,2},{1,3},{2,0},{3,1},{4,6},{5,7},{6,4},{7,5},{8,10},{9,11},{10,... | collective-permute-start | bytes 786440 | tf_op jit(solution)/shard_map/ppermute | solution.py:36
  228.2 9.6 %collective-permute-start.30 = (f32[32,128]{1,0:T(8,128)S(1)}, f32[32,128]{1,0:T(8,128)S(1)}, u32[]{:S(2)}, u32[]{:S(2)}) collective-permute-start(f32[32,128]{1,0:T(8,128)S(1)} %add.183), channel_id=1, source_target_pairs={{0,2},{1,3},{2,0},{3,1},{4,6},{5,7},{6,4},{7,5},{8,10},{9,11},{10,... | collective-permute-start | bytes 49160 | tf_op jit(solution)/shard_map/ppermute | solution.py:36
  245.3 4.6 %collective-permute-start.33 = (f32[32,128]{1,0:T(8,128)S(1)}, f32[32,128]{1,0:T(8,128)S(1)}, u32[]{:S(2)}, u32[]{:S(2)}) collective-permute-start(f32[32,128]{1,0:T(8,128)S(1)} %add.186), channel_id=1, source_target_pairs={{0,16},{4,20},{8,24},{12,28},{16,0},{20,4},{24,8},{28,12},{1,17},{... | collective-permute-start | bytes 49160 | tf_op jit(solution)/shard_map/ppermute | solution.py:36
  262.6 7.3 %collective-permute-start.51 = (f32[16,32,128]{2,1,0:T(8,128)}, f32[16,32,128]{2,1,0:T(8,128)S(1)}, u32[]{:S(2)}, u32[]{:S(2)}) collective-permute-start(f32[16,32,128]{2,1,0:T(8,128)} %get-tuple-element.53.refs_0_), channel_id=1, source_target_pairs={{0,2},{1,3},{2,0},{3,1},{4,6},{5,7},{6,4},{7,5},{8,10},{9,11},{10,... | collective-permute-start | bytes 786440 | tf_op jit(solution)/shard_map/ppermute | solution.py:36
  264.4 8.4 %collective-permute-start.54 = (f32[16,32,128]{2,1,0:T(8,128)}, f32[16,32,128]{2,1,0:T(8,128)S(1)}, u32[]{:S(2)}, u32[]{:S(2)}) collective-permute-start(f32[16,32,128]{2,1,0:T(8,128)} %get-tuple-element.54.refs_4_), channel_id=1, source_target_pairs={{0,2},{1,3},{2,0},{3,1},{4,6},{5,7},{6,4},{7,5},{8,10},{9,11},{10,... | collective-permute-start | bytes 786440 | tf_op jit(solution)/shard_map/ppermute | solution.py:36
  264.7 8.1 %collective-permute-start.52 = (f32[16,32,128]{2,1,0:T(8,128)}, f32[16,32,128]{2,1,0:T(8,128)S(1)}, u32[]{:S(2)}, u32[]{:S(2)}) collective-permute-start(f32[16,32,128]{2,1,0:T(8,128)} %get-tuple-element.53.refs_0_), channel_id=1, source_target_pairs={{0,1},{1,0},{2,3},{3,2},{4,5},{5,4},{6,7},{7,6},{8,9},{9,8},{10,11... | collective-permute-start | bytes 786440 | tf_op jit(solution)/shard_map/ppermute | solution.py:36
  264.7 8.1 %collective-permute-start.55 = (f32[16,32,128]{2,1,0:T(8,128)}, f32[16,32,128]{2,1,0:T(8,128)S(1)}, u32[]{:S(2)}, u32[]{:S(2)}) collective-permute-start(f32[16,32,128]{2,1,0:T(8,128)} %get-tuple-element.54.refs_4_), channel_id=1, source_target_pairs={{0,1},{1,0},{2,3},{3,2},{4,5},{5,4},{6,7},{7,6},{8,9},{9,8},{10,11... | collective-permute-start | bytes 786440 | tf_op jit(solution)/shard_map/ppermute | solution.py:36
  282.0 9.4 %collective-permute-start.60 = (f32[32,32,128]{2,1,0:T(8,128)}, f32[32,32,128]{2,1,0:T(8,128)S(1)}, u32[]{:S(2)}, u32[]{:S(2)}) collective-permute-start(f32[32,32,128]{2,1,0:T(8,128)} %get-tuple-element.58), channel_id=1, source_target_pairs={{0,8},{4,12},{8,0},{12,4},{16,24},{20,28},{24,16},{28,20},{1,9},{5... | collective-permute-start | bytes 1572872 | tf_op jit(solution)/shard_map/ppermute | solution.py:36
  282.7 11.4 %collective-permute-start.57 = (f32[32,32,128]{2,1,0:T(8,128)}, f32[32,32,128]{2,1,0:T(8,128)S(1)}, u32[]{:S(2)}, u32[]{:S(2)}) collective-permute-start(f32[32,32,128]{2,1,0:T(8,128)} %get-tuple-element.56), channel_id=1, source_target_pairs={{0,4},{4,0},{8,12},{12,8},{16,20},{20,16},{24,28},{28,24},{1,5},{5... | collective-permute-start | bytes 1572872 | tf_op jit(solution)/shard_map/ppermute | solution.py:36
  292.5 9.2 %collective-permute-start.61 = (f32[16,32,128]{2,1,0:T(8,128)S(1)}, f32[16,32,128]{2,1,0:T(8,128)S(1)}, u32[]{:S(2)}, u32[]{:S(2)}) collective-permute-start(f32[16,32,128]{2,1,0:T(8,128)S(1)} %get-tuple-element.69), channel_id=1, source_target_pairs={{0,4},{4,0},{8,12},{12,8},{16,20},{20,16},{24,28},{28,24},{1,5},{5... | collective-permute-start | bytes 786440 | tf_op jit(solution)/shard_map/ppermute | solution.py:36
  295.2 19.6 %collective-permute-start.58 = (f32[16,32,128]{2,1,0:T(8,128)S(1)}, f32[16,32,128]{2,1,0:T(8,128)S(1)}, u32[]{:S(2)}, u32[]{:S(2)}) collective-permute-start(f32[16,32,128]{2,1,0:T(8,128)S(1)} %get-tuple-element.71), channel_id=1, source_target_pairs={{0,8},{4,12},{8,0},{12,4},{16,24},{20,28},{24,16},{28,20},{1,9},{5... | collective-permute-start | bytes 786440 | tf_op jit(solution)/shard_map/ppermute | solution.py:36
  302.4 41.8 %collective-permute-start.62 = (f32[8,32,128]{2,1,0:T(8,128)S(1)}, f32[8,32,128]{2,1,0:T(8,128)S(1)}, u32[]{:S(2)}, u32[]{:S(2)}) collective-permute-start(f32[8,32,128]{2,1,0:T(8,128)S(1)} %get-tuple-element.85), channel_id=1, source_target_pairs={{0,16},{4,20},{8,24},{12,28},{16,0},{20,4},{24,8},{28,12},{1,17},{... | collective-permute-start | bytes 393224 | tf_op jit(solution)/shard_map/ppermute | solution.py:36
  315.5 28.7 %collective-permute-start.59 = (f32[8,32,128]{2,1,0:T(8,128)S(1)}, f32[8,32,128]{2,1,0:T(8,128)S(1)}, u32[]{:S(2)}, u32[]{:S(2)}) collective-permute-start(f32[8,32,128]{2,1,0:T(8,128)S(1)} %get-tuple-element.87), channel_id=1, source_target_pairs={{0,16},{4,20},{8,24},{12,28},{16,0},{20,4},{24,8},{28,12},{1,17},{... | collective-permute-start | bytes 393224 | tf_op jit(solution)/shard_map/ppermute | solution.py:36
  320.2 4.7 %collective-permute-start.47 = (f32[32,128]{1,0:T(8,128)S(1)}, f32[32,128]{1,0:T(8,128)S(1)}, u32[]{:S(2)}, u32[]{:S(2)}) collective-permute-start(f32[32,128]{1,0:T(8,128)S(1)} %add.192), channel_id=1, source_target_pairs={{0,8},{4,12},{8,0},{12,4},{16,24},{20,28},{24,16},{28,20},{1,9},{5... | collective-permute-start | bytes 49160 | tf_op jit(solution)/shard_map/ppermute | solution.py:36
  324.8 4.6 %collective-permute-start.48 = (f32[32,128]{1,0:T(8,128)S(1)}, f32[32,128]{1,0:T(8,128)S(1)}, u32[]{:S(2)}, u32[]{:S(2)}) collective-permute-start(f32[32,128]{1,0:T(8,128)S(1)} %add.193), channel_id=1, source_target_pairs={{0,16},{4,20},{8,24},{12,28},{16,0},{20,4},{24,8},{28,12},{1,17},{... | collective-permute-start | bytes 49160 | tf_op jit(solution)/shard_map/ppermute | solution.py:36
  361.7 4.6 %collective-permute-start.67 = (f32[32,128]{1,0:T(8,128)S(1)}, f32[32,128]{1,0:T(8,128)S(1)}, u32[]{:S(2)}, u32[]{:S(2)}) collective-permute-start(f32[32,128]{1,0:T(8,128)S(1)} %add.208), channel_id=1, source_target_pairs={{0,16},{4,20},{8,24},{12,28},{16,0},{20,4},{24,8},{28,12},{1,17},{... | collective-permute-start | bytes 49160 | tf_op jit(solution)/shard_map/ppermute | solution.py:36
  (63 other events, 486.8 us)

commit v7 on v5

--- a/solution.py
+++ b/solution.py
@@ -64,18 +64,30 @@
     return [[held[part], near[part], own[part], far[part]] for part in range(PARTS)]
 
 
-def reduce_scatter(kept, sent, gram, axis):
+def reduce_scatter(kept, sent, axis):
     for level in range(len(gather_order(axis, 0)) - 1, -1, -1):
-        other = exchange(gram, axis, gather_order(axis, 0)[level])
         got = []
         for part in range(PARTS):
             got.append(exchange(sent[part], axis, gather_order(axis, part)[level]))
-        gram = gram + other
         if level:
             half = kept[0].shape[0] // 2
             sent = [have[half:] + more[half:] for have, more in zip(kept, got)]
             kept = [have[:half] + more[:half] for have, more in zip(kept, got)]
-    return kept, got, gram
+    return kept, got
+
+
+def gram_sum(pieces, axis):
+    held, near, own, far = [piece[-GRAM:].reshape(K // 2, TILE) for piece in pieces[0]]
+    gram = (held + near) + (own + far)
+    first, *rest = [gather_order(axis, 0)[-2:]] + gather_order(axis, 0)[:-2]
+    others = []
+    for bit in (first[0], first[1], first[0] | first[1]):
+        others.append(exchange(gram, axis, bit))
+    gram = (gram + others[0]) + (others[1] + others[2])
+    for bit in rest:
+        other = exchange(gram, axis, bit)
+        gram = gram + other
+    return gram
 
 
 def all_sum(value):
@@ -94,7 +106,7 @@
 def tiles_kernel(count, source, target, *refs, places_in, places_out):
     piece_refs, refs = [refs[4 * part : 4 * part + 4] for part in range(PARTS)], refs[4 * PARTS :]
     tile_ref, keep_refs, send_refs = refs[0], refs[1 : 1 + PARTS], refs[1 + PARTS : 1 + 2 * PARTS]
-    gram_ref, pieces, total = refs[1 + 2 * PARTS :]
+    pieces, total = refs[1 + 2 * PARTS :]
     step = pl.program_id(0)
     half_out = keep_refs[-1].shape[0]
 
@@ -156,9 +168,6 @@
                     return carry
 
                 lax.fori_loop(0, quarter, finish, 0, unroll=4)
-        for at in range(GRAM):
-            held, near, own, far = [ref[ref.shape[0] - GRAM + at] for ref in piece_refs[0]]
-            gram_ref[at * ROWS : (at + 1) * ROWS] = (held + near) + (own + far)
 
 
 def tiles_product(count, source, target, pieces, tiles, blocks_out, axis_in, axis_out):
@@ -173,23 +182,23 @@
         places_in=[part_places(axis_in, part, 4 * quarter_in) for part in range(PARTS)],
         places_out=[part_places(axis_out, part, 2 * half_out) for part in range(PARTS)],
     )
-    out = pl.pallas_call(
+    call = pl.pallas_call(
         kernel,
-        out_shape=[jax.ShapeDtypeStruct((half_out, ROWS, TILE), jnp.float32)] * (2 * PARTS)
-        + [jax.ShapeDtypeStruct((K // 2, TILE), jnp.float32)],
+        out_shape=[jax.ShapeDtypeStruct((half_out, ROWS, TILE), jnp.float32)] * (2 * PARTS),
         grid_spec=pltpu.PrefetchScalarGridSpec(
             num_scalar_prefetch=3,
             grid=(tiles.shape[0] // BATCH,),
             in_specs=[VMEM_SPEC] * (4 * PARTS)
             + [pl.BlockSpec((BATCH, TILE, TILE), tile_block)],
-            out_specs=[VMEM_SPEC] * (2 * PARTS + 1),
+            out_specs=[VMEM_SPEC] * (2 * PARTS),
             scratch_shapes=[
                 pltpu.VMEM((4 * quarter_in, K, 2 * TILE), jnp.bfloat16),
                 pltpu.VMEM((2 * half_out + 1, K, TILE), jnp.float32),
             ],
         ),
-    )(count, source, target, *[piece for part in pieces for piece in part], tiles)
-    return out[:PARTS], out[PARTS : 2 * PARTS], out[-1]
+    )
+    out = call(count, source, target, *[piece for part in pieces for piece in part], tiles)
+    return out[:PARTS], out[PARTS:]
 
 
 def dot_full(left, right, contract):
@@ -330,15 +339,15 @@
     item_inverse = None
     for step in range(ITERS):
         pieces = gather(sent, "users")
-        kept, out, gram = tiles_product(count, col_at, row_to, pieces, turned, UT, "users", "items")
-        kept, got, gram = reduce_scatter(kept, out, gram, "items")
         if step:
-            item_inverse = inverse_factor(gram, item_total)
+            item_inverse = inverse_factor(gram_sum(pieces, "items"), item_total)
+        kept, out = tiles_product(count, col_at, row_to, pieces, turned, UT, "users", "items")
+        kept, got = reduce_scatter(kept, out, "items")
         user_raw, sent = scale_panel(item_inverse, kept, got, user_scale)
         pieces = gather(sent, "items")
-        kept, out, gram = tiles_product(count, row_at, col_to, pieces, tiles, IT, "items", "users")
-        kept, got, gram = reduce_scatter(kept, out, gram, "users")
-        user_inverse = inverse_factor(gram, user_total)
+        user_inverse = inverse_factor(gram_sum(pieces, "users"), user_total)
+        kept, out = tiles_product(count, row_at, col_to, pieces, tiles, IT, "items", "users")
+        kept, got = reduce_scatter(kept, out, "users")
         if step == ITERS - 1:
             user_panel = finish_panel(user_inverse, user_raw)
             user_panel, got = lax.optimization_barrier((user_panel, got))

time: 364 us -> 362 us (level)
  starting transfers between devices: 142 us -> 130 us
  waiting for transfers between devices: 77.2 us -> 88.4 us
    ppermute x109 -> x112, starting transfers between devices: 142 us -> 130 us  [exchange(): lax.ppermute(value, axis, [(at, at ^ bit) for at in range(lax.axis_size(a...]
    ppermute x109 -> x112, waiting for transfers between devices: 77.2 us -> 88.4 us  [exchange(): lax.ppermute(value, axis, [(at, at ^ bit) for at in range(lax.axis_size(a...]
  transfers between devices with their start and end apart: 109 -> 112, of which waited for: 44 -> 48; matrix products, arithmetic and copies ran while one was open for 10% -> 10% of each run, Pallas kernels for 12% -> 12%
where the time goes in v7:
time: 362 us; the launch traced here: 360 us
  starting transfers between devices  130 us (36%)
  Pallas kernels  95.4 us (26%)
  waiting for transfers between devices  88.4 us (24%)
  other arithmetic  34.9 us (10%)
  local copies, waits for them, and re-layouts  9.55 us (3%)
    ppermute x112, starting transfers between devices, exchange(): lax.ppermute(value, axis, [(at, at ^ bit) for at in range(lax.axis_size(a...  130 us
    ppermute x112, waiting for transfers between devices, exchange(): lax.ppermute(value, axis, [(at, at ^ bit) for at in range(lax.axis_size(a...  88.4 us
    pallas_call x4, Pallas kernels, tiles_product(): call(count, source, target, *[piece for part in pieces for piece in part]...  30.1 us
    pallas_call x4, Pallas kernels, inverse_factor(): pl.pallas_call(functools.partial(factor_kernel, total=total), out_shape=j...  27.1 us
    pallas_call x2, Pallas kernels, turned_tiles(): pl.pallas_call(turn_kernel, out_shape=jax.ShapeDtypeStruct(tiles.shape, t...  19.7 us
    add x12, other arithmetic, reduce_scatter(): sent = [have[half:] + more[half:] for have, more in zip(kept, got)]  15.9 us
    pallas_call x4, Pallas kernels, scale_panel(): pl.pallas_call(functools.partial(scale_kernel, factored=factored), out_sh...  14.1 us
    add x12, other arithmetic, reduce_scatter(): kept = [have[:half] + more[:half] for have, more in zip(kept, got)]  10.6 us
  transfers between devices with their start and end apart: 112, of which 48 were waited for; matrix products, arithmetic and copies ran while one was open for 10% of the time, Pallas kernels for 12%

profile of v7, /device:TPU:0, one launch (start us, length us, event | category | flops | bytes accessed | tf_op | source)
XLA Modules:
  0.0 360.2 jit_solution(13820019091436139683)
XLA Ops:
  2.4 4.1 %collective-permute-start.8 = (f32[8,16,128]{2,1,0:T(8,128)S(1)}, f32[8,16,128]{2,1,0:T(8,128)S(1)}, u32[]{:S(2)}, u32[]{:S(2)}) collective-permute-start(f32[8,16,128]{2,1,0:T(8,128)S(1)} %get-tuple-element.159), channel_id=1, source_target_pairs={{0,16},{4,20},{8,24},{12,28},{16,0},{20,4},{24,8},{28,12},{1,17},{... | collective-permute-start | bytes 196616 | tf_op jit(solution)/shard_map/ppermute | solution.py:37
  6.6 2.8 collective-permute-start.4
  10.3 5.2 %collective-permute-start.9 = (f32[16,16,128]{2,1,0:T(8,128)S(1)}, f32[16,16,128]{2,1,0:T(8,128)S(1)}, u32[]{:S(2)}, u32[]{:S(2)}) collective-permute-start(f32[16,16,128]{2,1,0:T(8,128)S(1)} %pad_maximum_fusion.3.refs_8_), channel_id=1, source_target_pairs={{0,8},{4,12},{8,0},{12,4},{16,24},{20,28},{24,16},{28,20},{1,9},{5... | collective-permute-start | bytes 393224 | tf_op jit(solution)/shard_map/ppermute | solution.py:37
  24.9 9.9 %turned_tiles.2.refs_0_ = bf16[512,128,128]{2,1,0:T(8,128)(2,1)} custom-call(bf16[512,128,128]{2,1,0:T(8,128)(2,1)} %bitcast.36), custom_call_target="tpu_custom_call" | custom-call | tf_op jit(solution)/shard_map/turned_tiles/pallas_call | solution.py:240
  34.8 9.9 %turned_tiles.3.refs_16_ = bf16[512,128,128]{2,1,0:T(8,128)(2,1)} custom-call(bf16[512,128,128]{2,1,0:T(8,128)(2,1)} %bitcast.37, bf16[512,128,128]{2,1,0:T(8,128)(2,1)} %turned_tiles.2.refs_0_), custom_call_target="tpu_custom_call", output_to_operand_aliasing={{}: (1, {})} | custom-call | tf_op jit(solution)/shard_map/turned_tiles/pallas_call | solution.py:240
  51.5 2.8 collective-permute-done.11.refs_11_
  56.6 7.5 %shard_map.86 = (f32[32,16,128]{2,1,0:T(8,128)}, f32[32,16,128]{2,1,0:T(8,128)}, f32[32,16,128]{2,1,0:T(8,128)}, f32[32,16,128]{2,1,0:T(8,128)}, f32[32,16,128]{...) custom-call(s32[1]{0:T(128)} %bitcast.31.count, ...), custom_call_target="tpu_custom_call" | custom-call | tf_op jit(solution)/shard_map/pallas_call | solution.py:200
  67.5 8.6 %collective-permute-start.23 = (f32[16,16,128]{2,1,0:T(8,128)S(1)}, f32[16,16,128]{2,1,0:T(8,128)S(1)}, u32[]{:S(2)}, u32[]{:S(2)}) collective-permute-start(f32[16,16,128]{2,1,0:T(8,128)S(1)} %get-tuple-element.134), channel_id=1, source_target_pairs={{0,2},{1,3},{2,0},{3,1},{4,6},{5,7},{6,4},{7,5},{8,10},{9,11},{10,... | collective-permute-start | bytes 393224 | tf_op jit(solution)/shard_map/ppermute | solution.py:37
  79.4 2.0 collective-permute-start.21
  84.1 2.5 collective-permute-done.21.refs_5_
  89.3 3.0 scale_panel.4
  96.4 2.5 collective-permute-done.31.refs_5_
  98.9 2.8 collective-permute-done.34.refs_9_
  101.7 4.2 %collective-permute-done.37.refs_13_ = f32[16,16,128]{2,1,0:T(8,128)S(1)} collective-permute-done((f32[16,16,128]{2,1,0:T(8,128)}, f32[16,16,128]{2,1,0:T(8,128)S(1)}, u32[]{:S(2)}, u32[]{:S(2)}) %collective-permute-start.37) | collective-permute-done | bytes 131104 | tf_op jit(solution)/shard_map/ppermute | solution.py:37
  109.1 7.5 %shard_map.87 = (f32[32,16,128]{2,1,0:T(8,128)}, f32[32,16,128]{2,1,0:T(8,128)}, f32[32,16,128]{2,1,0:T(8,128)}, f32[32,16,128]{2,1,0:T(8,128)}, f32[32,16,128]{...) custom-call(s32[1]{0:T(128)} %bitcast.32.count, ...), custom_call_target="tpu_custom_call" | custom-call | tf_op jit(solution)/shard_map/pallas_call | solution.py:200
  121.5 2.3 collective-permute-done.46
  127.1 4.2 %collective-permute-done.42 = f32[32,16,128]{2,1,0:T(8,128)S(1)} collective-permute-done((f32[32,16,128]{2,1,0:T(8,128)}, f32[32,16,128]{2,1,0:T(8,128)S(1)}, u32[]{:S(2)}, u32[]{:S(2)}) %collective-permute-start.42) | collective-permute-done | bytes 262176 | tf_op jit(solution)/shard_map/ppermute | solution.py:37
  134.8 2.8 collective-permute-done.47
  140.2 2.4 collective-permute-done.43
  142.7 10.1 %collective-permute-start.51 = (f32[8,16,128]{2,1,0:T(8,128)S(1)}, f32[8,16,128]{2,1,0:T(8,128)S(1)}, u32[]{:S(2)}, u32[]{:S(2)}) collective-permute-start(f32[8,16,128]{2,1,0:T(8,128)S(1)} %get-tuple-element.150), channel_id=1, source_target_pairs={{0,16},{4,20},{8,24},{12,28},{16,0},{20,4},{24,8},{28,12},{1,17},{... | collective-permute-start | bytes 196616 | tf_op jit(solution)/shard_map/ppermute | solution.py:37
  153.4 4.8 %collective-permute-start.50 = (f32[8,16,128]{2,1,0:T(8,128)S(1)}, f32[8,16,128]{2,1,0:T(8,128)S(1)}, u32[]{:S(2)}, u32[]{:S(2)}) collective-permute-start(f32[8,16,128]{2,1,0:T(8,128)S(1)} %get-tuple-element.152), channel_id=1, source_target_pairs={{0,16},{4,20},{8,24},{12,28},{16,0},{20,4},{24,8},{28,12},{1,17},{... | collective-permute-start | bytes 196616 | tf_op jit(solution)/shard_map/ppermute | solution.py:37
  158.9 2.9 collective-permute-start.48
  162.0 4.6 %collective-permute-done.30 = f32[32,128]{1,0:T(8,128)S(1)} collective-permute-done((f32[32,128]{1,0:T(8,128)S(1)}, f32[32,128]{1,0:T(8,128)S(1)}, u32[]{:S(2)}, u32[]{:S(2)}) %collective-permute-start.30) | collective-permute-done | bytes 16416 | tf_op jit(solution)/shard_map/ppermute | solution.py:37
  167.2 6.8 %factor.4.refs_0_ = f32[64,64]{1,0:T(8,128)} custom-call(f32[32,128]{1,0:T(8,128)} %add.288.gram_ref), custom_call_target="tpu_custom_call" | custom-call | tf_op jit(solution)/shard_map/factor/pallas_call | solution.py:252
  174.7 3.2 scale_panel.5
  180.2 2.3 collective-permute-start.63
  184.0 2.3 collective-permute-start.59
  203.0 2.3 collective-permute-done.70.refs_15_
  207.4 7.7 %shard_map.88 = (f32[32,16,128]{2,1,0:T(8,128)}, f32[32,16,128]{2,1,0:T(8,128)}, f32[32,16,128]{2,1,0:T(8,128)}, f32[32,16,128]{2,1,0:T(8,128)}, f32[32,16,128]{...) custom-call(s32[1]{0:T(128)} %bitcast.33.count, ...), custom_call_target="tpu_custom_call" | custom-call | tf_op jit(solution)/shard_map/pallas_call | solution.py:200
  216.4 6.7 %collective-permute-start.56 = (f32[32,128]{1,0:T(8,128)S(1)}, f32[32,128]{1,0:T(8,128)S(1)}, u32[]{:S(2)}, u32[]{:S(2)}) collective-permute-start(f32[32,128]{1,0:T(8,128)S(1)} %bitcast.47), channel_id=1, source_target_pairs={{0,2},{1,3},{2,0},{3,1},{4,6},{5,7},{6,4},{7,5},{8,10},{9,11},{10,... | collective-permute-start | bytes 49160 | tf_op jit(solution)/shard_map/ppermute | solution.py:37
  235.2 6.8 %factor.5.refs_0_ = f32[64,64]{1,0:T(8,128)} custom-call(f32[32,128]{1,0:T(8,128)} %add_add_fusion.1.gram_ref), custom_call_target="tpu_custom_call" | custom-call | tf_op jit(solution)/shard_map/factor/pallas_call | solution.py:252
  242.7 4.6 %scale_panel.6 = (f32[16,64,128]{2,1,0:T(8,128)}, f32[18,16,128]{2,1,0:T(8,128)}, f32[16,16,128]{2,1,0:T(8,128)}, f32[16,16,128]{2,1,0:T(8,128)}, f32[16,16,128]{2,1,0:T(8,128)}) custom-call(f32[64,64]{1,0:T(8,128)} %factor.5.refs_0_, f32[16,16,128]{2,1,0:T(8,128)} %get-tuple-element.125.refs_1_, f32[16,16,128]{2,1,0:T(8,128)} %get-tuple-element.123.refs_2_, ...), custom_call_target="tpu_custom_call" | custom-call | tf_op jit(solution)/shard_map/scale_panel/pallas_call | solution.py:287
  251.4 2.5 collective-permute-done.86.refs_5_
  254.0 2.8 collective-permute-done.89.refs_9_
  256.8 4.2 %collective-permute-done.92.refs_13_ = f32[16,16,128]{2,1,0:T(8,128)S(1)} collective-permute-done((f32[16,16,128]{2,1,0:T(8,128)}, f32[16,16,128]{2,1,0:T(8,128)S(1)}, u32[]{:S(2)}, u32[]{:S(2)}) %collective-permute-start.92) | collective-permute-done | bytes 131104 | tf_op jit(solution)/shard_map/ppermute | solution.py:37
  264.1 7.5 %shard_map.89 = (f32[32,16,128]{2,1,0:T(8,128)}, f32[32,16,128]{2,1,0:T(8,128)}, f32[32,16,128]{2,1,0:T(8,128)}, f32[32,16,128]{2,1,0:T(8,128)}, f32[32,16,128]{...) custom-call(s32[1]{0:T(128)} %bitcast.34.count, ...), custom_call_target="tpu_custom_call" | custom-call | tf_op jit(solution)/shard_map/pallas_call | solution.py:200
  276.5 4.5 %collective-permute-done.104 = f32[32,16,128]{2,1,0:T(8,128)S(1)} collective-permute-done((f32[32,16,128]{2,1,0:T(8,128)}, f32[32,16,128]{2,1,0:T(8,128)S(1)}, u32[]{:S(2)}, u32[]{:S(2)}) %collective-permute-start.104) | collective-permute-done | bytes 262176 | tf_op jit(solution)/shard_map/ppermute | solution.py:37
  283.1 6.1 %collective-permute-done.98 = f32[32,16,128]{2,1,0:T(8,128)S(1)} collective-permute-done((f32[32,16,128]{2,1,0:T(8,128)}, f32[32,16,128]{2,1,0:T(8,128)S(1)}, u32[]{:S(2)}, u32[]{:S(2)}) %collective-permute-start.98) | collective-permute-done | bytes 262176 | tf_op jit(solution)/shard_map/ppermute | solution.py:37
  299.1 8.2 %collective-permute-start.106 = (f32[8,16,128]{2,1,0:T(8,128)S(1)}, f32[8,16,128]{2,1,0:T(8,128)S(1)}, u32[]{:S(2)}, u32[]{:S(2)}) collective-permute-start(f32[8,16,128]{2,1,0:T(8,128)S(1)} %get-tuple-element.143), channel_id=1, source_target_pairs={{0,16},{4,20},{8,24},{12,28},{16,0},{20,4},{24,8},{28,12},{1,17},{... | collective-permute-start | bytes 196616 | tf_op jit(solution)/shard_map/ppermute | solution.py:37
  314.6 4.1 %collective-permute-done.85 = f32[32,128]{1,0:T(8,128)S(1)} collective-permute-done((f32[32,128]{1,0:T(8,128)S(1)}, f32[32,128]{1,0:T(8,128)S(1)}, u32[]{:S(2)}, u32[]{:S(2)}) %collective-permute-start.85) | collective-permute-done | bytes 16416 | tf_op jit(solution)/shard_map/ppermute | solution.py:37
  319.3 6.8 %factor.6.inverse_ref.refs_0_ = f32[64,64]{1,0:T(8,128)} custom-call(f32[32,128]{1,0:T(8,128)} %add.328.gram_ref), custom_call_target="tpu_custom_call" | custom-call | tf_op jit(solution)/shard_map/factor/pallas_call | solution.py:252
  326.1 2.4 finish_panel.2
  329.2 3.2 scale_panel.7
  335.7 2.4 collective-permute-done.108
  338.0 2.5 collective-permute-start.109
  342.2 2.2 collective-permute-start.110
  347.1 3.7 %collective-permute-done.111 = f32[32,128]{1,0:T(8,128)S(1)} collective-permute-done((f32[32,128]{1,0:T(8,128)S(1)}, f32[32,128]{1,0:T(8,128)S(1)}, u32[]{:S(2)}, u32[]{:S(2)}) %collective-permute-start.111) | collective-permute-done | bytes 16416 | tf_op jit(solution)/shard_map/ppermute | solution.py:37
  351.4 6.8 %factor.7.inverse_ref = f32[64,64]{1,0:T(8,128)} custom-call(f32[32,128]{1,0:T(8,128)} %add.349.gram_ref), custom_call_target="tpu_custom_call" | custom-call | tf_op jit(solution)/shard_map/factor/pallas_call | solution.py:252
  (404 shorter events, 136.1 us)
Async XLA Ops:
  6.5 10.2 %collective-permute-start.12 = (f32[8,16,128]{2,1,0:T(8,128)S(1)}, f32[8,16,128]{2,1,0:T(8,128)S(1)}, u32[]{:S(2)}, u32[]{:S(2)}) collective-permute-start(f32[8,16,128]{2,1,0:T(8,128)S(1)} %get-tuple-element.158), channel_id=1, source_target_pairs={{0,16},{4,20},{8,24},{12,28},{16,0},{20,4},{24,8},{28,12},{1,17},{... | collective-permute-start | bytes 196616 | tf_op jit(solution)/shard_map/ppermute | solution.py:37
  6.6 13.4 %collective-permute-start.4 = (f32[8,16,128]{2,1,0:T(8,128)S(1)}, f32[8,16,128]{2,1,0:T(8,128)S(1)}, u32[]{:S(2)}, u32[]{:S(2)}) collective-permute-start(f32[8,16,128]{2,1,0:T(8,128)S(1)} %get-tuple-element.160), channel_id=1, source_target_pairs={{0,16},{4,20},{8,24},{12,28},{16,0},{20,4},{24,8},{28,12},{1,17},{... | collective-permute-start | bytes 196616 | tf_op jit(solution)/shard_map/ppermute | solution.py:37
  9.5 9.9 %collective-permute-start = (f32[10,16,128]{2,1,0:T(8,128)S(1)}, f32[10,16,128]{2,1,0:T(8,128)S(1)}, u32[]{:S(2)}, u32[]{:S(2)}) collective-permute-start(f32[10,16,128]{2,1,0:T(8,128)S(1)} %concatenate.27), channel_id=1, source_target_pairs={{0,16},{4,20},{8,24},{12,28},{16,0},{20,4},{24,8},{28,12},{1,17},{... | collective-permute-start | bytes 245768 | tf_op jit(solution)/shard_map/ppermute | solution.py:37
  10.3 11.9 %collective-permute-start.9 = (f32[16,16,128]{2,1,0:T(8,128)S(1)}, f32[16,16,128]{2,1,0:T(8,128)S(1)}, u32[]{:S(2)}, u32[]{:S(2)}) collective-permute-start(f32[16,16,128]{2,1,0:T(8,128)S(1)} %pad_maximum_fusion.3.refs_8_), channel_id=1, source_target_pairs={{0,8},{4,12},{8,0},{12,4},{16,24},{20,28},{24,16},{28,20},{1,9},{5... | collective-permute-start | bytes 393224 | tf_op jit(solution)/shard_map/ppermute | solution.py:37
  19.4 29.5 %collective-permute-start.1 = (f32[18,16,128]{2,1,0:T(8,128)S(1)}, f32[18,16,128]{2,1,0:T(8,128)S(1)}, u32[]{:S(2)}, u32[]{:S(2)}) collective-permute-start(f32[18,16,128]{2,1,0:T(8,128)S(1)} %pad_maximum_fusion.refs_0_), channel_id=1, source_target_pairs={{0,8},{4,12},{8,0},{12,4},{16,24},{20,28},{24,16},{28,20},{1,9},{5... | collective-permute-start | bytes 442376 | tf_op jit(solution)/shard_map/ppermute | solution.py:37
  20.0 24.6 %collective-permute-start.5 = (f32[16,16,128]{2,1,0:T(8,128)S(1)}, f32[16,16,128]{2,1,0:T(8,128)S(1)}, u32[]{:S(2)}, u32[]{:S(2)}) collective-permute-start(f32[16,16,128]{2,1,0:T(8,128)S(1)} %pad_maximum_fusion.2.refs_4_), channel_id=1, source_target_pairs={{0,4},{4,0},{8,12},{12,8},{16,20},{20,16},{24,28},{28,24},{1,5},{5... | collective-permute-start | bytes 393224 | tf_op jit(solution)/shard_map/ppermute | solution.py:37
  21.6 24.9 %collective-permute-start.10 = (f32[16,16,128]{2,1,0:T(8,128)S(1)}, f32[16,16,128]{2,1,0:T(8,128)S(1)}, u32[]{:S(2)}, u32[]{:S(2)}) collective-permute-start(f32[16,16,128]{2,1,0:T(8,128)S(1)} %pad_maximum_fusion.3.refs_8_), channel_id=1, source_target_pairs={{0,4},{4,0},{8,12},{12,8},{16,20},{20,16},{24,28},{28,24},{1,5},{5... | collective-permute-start | bytes 393224 | tf_op jit(solution)/shard_map/ppermute | solution.py:37
  22.2 24.7 %collective-permute-start.14 = (f32[16,16,128]{2,1,0:T(8,128)S(1)}, f32[16,16,128]{2,1,0:T(8,128)S(1)}, u32[]{:S(2)}, u32[]{:S(2)}) collective-permute-start(f32[16,16,128]{2,1,0:T(8,128)S(1)} %pad_maximum_fusion.4.refs_12_), channel_id=1, source_target_pairs={{0,8},{4,12},{8,0},{12,4},{16,24},{20,28},{24,16},{28,20},{1,9},{5... | collective-permute-start | bytes 393224 | tf_op jit(solution)/shard_map/ppermute | solution.py:37
  23.7 24.7 %collective-permute-start.6 = (f32[16,16,128]{2,1,0:T(8,128)S(1)}, f32[16,16,128]{2,1,0:T(8,128)S(1)}, u32[]{:S(2)}, u32[]{:S(2)}) collective-permute-start(f32[16,16,128]{2,1,0:T(8,128)S(1)} %pad_maximum_fusion.2.refs_4_), channel_id=1, source_target_pairs={{0,8},{4,12},{8,0},{12,4},{16,24},{20,28},{24,16},{28,20},{1,9},{5... | collective-permute-start | bytes 393224 | tf_op jit(solution)/shard_map/ppermute | solution.py:37
  64.1 12.0 %collective-permute-start.18 = (f32[32,16,128]{2,1,0:T(8,128)}, f32[32,16,128]{2,1,0:T(8,128)S(1)}, u32[]{:S(2)}, u32[]{:S(2)}) collective-permute-start(f32[32,16,128]{2,1,0:T(8,128)} %get-tuple-element.59), channel_id=1, source_target_pairs={{0,1},{1,0},{2,3},{3,2},{4,5},{5,4},{6,7},{7,6},{8,9},{9,8},{10,11... | collective-permute-start | bytes 786440 | tf_op jit(solution)/shard_map/ppermute | solution.py:37
  64.6 13.2 %collective-permute-start.17 = (f32[32,16,128]{2,1,0:T(8,128)}, f32[32,16,128]{2,1,0:T(8,128)S(1)}, u32[]{:S(2)}, u32[]{:S(2)}) collective-permute-start(f32[32,16,128]{2,1,0:T(8,128)} %get-tuple-element.57), channel_id=1, source_target_pairs={{0,1},{1,0},{2,3},{3,2},{4,5},{5,4},{6,7},{7,6},{8,9},{9,8},{10,11... | collective-permute-start | bytes 786440 | tf_op jit(solution)/shard_map/ppermute | solution.py:37
  64.7 16.8 %collective-permute-start.16 = (f32[32,16,128]{2,1,0:T(8,128)}, f32[32,16,128]{2,1,0:T(8,128)S(1)}, u32[]{:S(2)}, u32[]{:S(2)}) collective-permute-start(f32[32,16,128]{2,1,0:T(8,128)} %get-tuple-element.55), channel_id=1, source_target_pairs={{0,1},{1,0},{2,3},{3,2},{4,5},{5,4},{6,7},{7,6},{8,9},{9,8},{10,11... | collective-permute-start | bytes 786440 | tf_op jit(solution)/shard_map/ppermute | solution.py:37
  67.5 16.2 %collective-permute-start.23 = (f32[16,16,128]{2,1,0:T(8,128)S(1)}, f32[16,16,128]{2,1,0:T(8,128)S(1)}, u32[]{:S(2)}, u32[]{:S(2)}) collective-permute-start(f32[16,16,128]{2,1,0:T(8,128)S(1)} %get-tuple-element.134), channel_id=1, source_target_pairs={{0,2},{1,3},{2,0},{3,1},{4,6},{5,7},{6,4},{7,5},{8,10},{9,11},{10,... | collective-permute-start | bytes 393224 | tf_op jit(solution)/shard_map/ppermute | solution.py:37
  94.4 11.6 %collective-permute-start.24 = (f32[18,16,128]{2,1,0:T(8,128)}, f32[18,16,128]{2,1,0:T(8,128)S(1)}, u32[]{:S(2)}, u32[]{:S(2)}) collective-permute-start(f32[18,16,128]{2,1,0:T(8,128)} %get-tuple-element.62.refs_0_), channel_id=1, source_target_pairs={{0,2},{1,3},{2,0},{3,1},{4,6},{5,7},{6,4},{7,5},{8,10},{9,11},{10,... | collective-permute-start | bytes 442376 | tf_op jit(solution)/shard_map/ppermute | solution.py:37
  95.8 10.2 %collective-permute-start.37 = (f32[16,16,128]{2,1,0:T(8,128)}, f32[16,16,128]{2,1,0:T(8,128)S(1)}, u32[]{:S(2)}, u32[]{:S(2)}) collective-permute-start(f32[16,16,128]{2,1,0:T(8,128)} %get-tuple-element.65.refs_12_), channel_id=1, source_target_pairs={{0,2},{1,3},{2,0},{3,1},{4,6},{5,7},{6,4},{7,5},{8,10},{9,11},{10,... | collective-permute-start | bytes 393224 | tf_op jit(solution)/shard_map/ppermute | solution.py:37
  96.4 10.1 %collective-permute-start.32 = (f32[16,16,128]{2,1,0:T(8,128)}, f32[16,16,128]{2,1,0:T(8,128)S(1)}, u32[]{:S(2)}, u32[]{:S(2)}) collective-permute-start(f32[16,16,128]{2,1,0:T(8,128)} %get-tuple-element.63.refs_4_), channel_id=1, source_target_pairs={{0,1},{1,0},{2,3},{3,2},{4,5},{5,4},{6,7},{7,6},{8,9},{9,8},{10,11... | collective-permute-start | bytes 393224 | tf_op jit(solution)/shard_map/ppermute | solution.py:37
  117.5 41.4 %collective-permute-start.27 = (f32[32,128]{1,0:T(8,128)S(1)}, f32[32,128]{1,0:T(8,128)S(1)}, u32[]{:S(2)}, u32[]{:S(2)}) collective-permute-start(f32[32,128]{1,0:T(8,128)S(1)} %bitcast.41), channel_id=1, source_target_pairs={{0,8},{4,12},{8,0},{12,4},{16,24},{20,28},{24,16},{28,20},{1,9},{5... | collective-permute-start | bytes 49160 | tf_op jit(solution)/shard_map/ppermute | solution.py:37
  119.5 39.4 %collective-permute-start.28 = (f32[32,128]{1,0:T(8,128)S(1)}, f32[32,128]{1,0:T(8,128)S(1)}, u32[]{:S(2)}, u32[]{:S(2)}) collective-permute-start(f32[32,128]{1,0:T(8,128)S(1)} %bitcast.42), channel_id=1, source_target_pairs={{0,4},{4,0},{8,12},{12,8},{16,20},{20,16},{24,28},{28,24},{1,5},{5... | collective-permute-start | bytes 49160 | tf_op jit(solution)/shard_map/ppermute | solution.py:37
  121.5 40.3 %collective-permute-start.29 = (f32[32,128]{1,0:T(8,128)S(1)}, f32[32,128]{1,0:T(8,128)S(1)}, u32[]{:S(2)}, u32[]{:S(2)}) collective-permute-start(f32[32,128]{1,0:T(8,128)S(1)} %bitcast.43), channel_id=1, source_target_pairs={{0,12},{4,8},{8,4},{12,0},{16,28},{20,24},{24,20},{28,16},{1,13},{... | collective-permute-start | bytes 49160 | tf_op jit(solution)/shard_map/ppermute | solution.py:37
  124.8 8.8 %collective-permute-start.40 = (f32[32,16,128]{2,1,0:T(8,128)}, f32[32,16,128]{2,1,0:T(8,128)S(1)}, u32[]{:S(2)}, u32[]{:S(2)}) collective-permute-start(f32[32,16,128]{2,1,0:T(8,128)} %get-tuple-element.67), channel_id=1, source_target_pairs={{0,4},{4,0},{8,12},{12,8},{16,20},{20,16},{24,28},{28,24},{1,5},{5... | collective-permute-start | bytes 786440 | tf_op jit(solution)/shard_map/ppermute | solution.py:37
  139.6 13.8 %collective-permute-start.41 = (f32[16,16,128]{2,1,0:T(8,128)S(1)}, f32[16,16,128]{2,1,0:T(8,128)S(1)}, u32[]{:S(2)}, u32[]{:S(2)}) collective-permute-start(f32[16,16,128]{2,1,0:T(8,128)S(1)} %get-tuple-element.133), channel_id=1, source_target_pairs={{0,8},{4,12},{8,0},{12,4},{16,24},{20,28},{24,16},{28,20},{1,9},{5... | collective-permute-start | bytes 393224 | tf_op jit(solution)/shard_map/ppermute | solution.py:37
  142.7 31.3 %collective-permute-start.51 = (f32[8,16,128]{2,1,0:T(8,128)S(1)}, f32[8,16,128]{2,1,0:T(8,128)S(1)}, u32[]{:S(2)}, u32[]{:S(2)}) collective-permute-start(f32[8,16,128]{2,1,0:T(8,128)S(1)} %get-tuple-element.150), channel_id=1, source_target_pairs={{0,16},{4,20},{8,24},{12,28},{16,0},{20,4},{24,8},{28,12},{1,17},{... | collective-permute-start | bytes 196616 | tf_op jit(solution)/shard_map/ppermute | solution.py:37
  153.4 20.5 %collective-permute-start.50 = (f32[8,16,128]{2,1,0:T(8,128)S(1)}, f32[8,16,128]{2,1,0:T(8,128)S(1)}, u32[]{:S(2)}, u32[]{:S(2)}) collective-permute-start(f32[8,16,128]{2,1,0:T(8,128)S(1)} %get-tuple-element.152), channel_id=1, source_target_pairs={{0,16},{4,20},{8,24},{12,28},{16,0},{20,4},{24,8},{28,12},{1,17},{... | collective-permute-start | bytes 196616 | tf_op jit(solution)/shard_map/ppermute | solution.py:37
  158.9 15.1 %collective-permute-start.49 = (f32[8,16,128]{2,1,0:T(8,128)S(1)}, f32[8,16,128]{2,1,0:T(8,128)S(1)}, u32[]{:S(2)}, u32[]{:S(2)}) collective-permute-start(f32[8,16,128]{2,1,0:T(8,128)S(1)} %get-tuple-element.154), channel_id=1, source_target_pairs={{0,16},{4,20},{8,24},{12,28},{16,0},{20,4},{24,8},{28,12},{1,17},{... | collective-permute-start | bytes 196616 | tf_op jit(solution)/shard_map/ppermute | solution.py:37
  158.9 15.1 %collective-permute-start.48 = (f32[8,16,128]{2,1,0:T(8,128)S(1)}, f32[8,16,128]{2,1,0:T(8,128)S(1)}, u32[]{:S(2)}, u32[]{:S(2)}) collective-permute-start(f32[8,16,128]{2,1,0:T(8,128)S(1)} %get-tuple-element.156), channel_id=1, source_target_pairs={{0,16},{4,20},{8,24},{12,28},{16,0},{20,4},{24,8},{28,12},{1,17},{... | collective-permute-start | bytes 196616 | tf_op jit(solution)/shard_map/ppermute | solution.py:37
  178.7 8.5 %collective-permute-start.67 = (f32[8,16,128]{2,1,0:T(8,128)}, f32[8,16,128]{2,1,0:T(8,128)S(1)}, u32[]{:S(2)}, u32[]{:S(2)}) collective-permute-start(f32[8,16,128]{2,1,0:T(8,128)} %get-tuple-element.77), channel_id=1, source_target_pairs={{0,16},{4,20},{8,24},{12,28},{16,0},{20,4},{24,8},{28,12},{1,17},{... | collective-permute-start | bytes 196616 | tf_op jit(solution)/shard_map/ppermute | solution.py:37
  189.4 10.9 %collective-permute-start.65 = (f32[16,16,128]{2,1,0:T(8,128)S(1)}, f32[16,16,128]{2,1,0:T(8,128)S(1)}, u32[]{:S(2)}, u32[]{:S(2)}) collective-permute-start(f32[16,16,128]{2,1,0:T(8,128)S(1)} %constant_dynamic-update-slice_fusion.2.refs_8_), channel_id=1, source_target_pairs={{0,4},{4,0},{8,12},{12,8},{16,20},{20,16},{24,28},{28,24},{1,5},{5... | collective-permute-start | bytes 393224 | tf_op jit(solution)/shard_map/ppermute | solution.py:37
  215.2 10.2 %collective-permute-start.73 = (f32[32,16,128]{2,1,0:T(8,128)}, f32[32,16,128]{2,1,0:T(8,128)S(1)}, u32[]{:S(2)}, u32[]{:S(2)}) collective-permute-start(f32[32,16,128]{2,1,0:T(8,128)} %get-tuple-element.83), channel_id=1, source_target_pairs={{0,1},{1,0},{2,3},{3,2},{4,5},{5,4},{6,7},{7,6},{8,9},{9,8},{10,11... | collective-permute-start | bytes 786440 | tf_op jit(solution)/shard_map/ppermute | solution.py:37
  216.4 16.1 %collective-permute-start.56 = (f32[32,128]{1,0:T(8,128)S(1)}, f32[32,128]{1,0:T(8,128)S(1)}, u32[]{:S(2)}, u32[]{:S(2)}) collective-permute-start(f32[32,128]{1,0:T(8,128)S(1)} %bitcast.47), channel_id=1, source_target_pairs={{0,2},{1,3},{2,0},{3,1},{4,6},{5,7},{6,4},{7,5},{8,10},{9,11},{10,... | collective-permute-start | bytes 49160 | tf_op jit(solution)/shard_map/ppermute | solution.py:37
  223.1 11.4 %collective-permute-start.57 = (f32[32,128]{1,0:T(8,128)S(1)}, f32[32,128]{1,0:T(8,128)S(1)}, u32[]{:S(2)}, u32[]{:S(2)}) collective-permute-start(f32[32,128]{1,0:T(8,128)S(1)} %bitcast.48), channel_id=1, source_target_pairs={{0,1},{1,0},{2,3},{3,2},{4,5},{5,4},{6,7},{7,6},{8,9},{9,8},{10,11... | collective-permute-start | bytes 49160 | tf_op jit(solution)/shard_map/ppermute | solution.py:37
  223.1 11.4 %collective-permute-start.58 = (f32[32,128]{1,0:T(8,128)S(1)}, f32[32,128]{1,0:T(8,128)S(1)}, u32[]{:S(2)}, u32[]{:S(2)}) collective-permute-start(f32[32,128]{1,0:T(8,128)S(1)} %bitcast.49), channel_id=1, source_target_pairs={{0,3},{1,2},{2,1},{3,0},{4,7},{5,6},{6,5},{7,4},{8,11},{9,10},{10,... | collective-permute-start | bytes 49160 | tf_op jit(solution)/shard_map/ppermute | solution.py:37
  227.2 14.8 %collective-permute-start.78 = (f32[16,16,128]{2,1,0:T(8,128)S(1)}, f32[16,16,128]{2,1,0:T(8,128)S(1)}, u32[]{:S(2)}, u32[]{:S(2)}) collective-permute-start(f32[16,16,128]{2,1,0:T(8,128)S(1)} %get-tuple-element.118), channel_id=1, source_target_pairs={{0,2},{1,3},{2,0},{3,1},{4,6},{5,7},{6,4},{7,5},{8,10},{9,11},{10,... | collective-permute-start | bytes 393224 | tf_op jit(solution)/shard_map/ppermute | solution.py:37
  230.8 11.2 %collective-permute-start.77 = (f32[16,16,128]{2,1,0:T(8,128)S(1)}, f32[16,16,128]{2,1,0:T(8,128)S(1)}, u32[]{:S(2)}, u32[]{:S(2)}) collective-permute-start(f32[16,16,128]{2,1,0:T(8,128)S(1)} %get-tuple-element.120), channel_id=1, source_target_pairs={{0,2},{1,3},{2,0},{3,1},{4,6},{5,7},{6,4},{7,5},{8,10},{9,11},{10,... | collective-permute-start | bytes 393224 | tf_op jit(solution)/shard_map/ppermute | solution.py:37
  232.5 9.4 %collective-permute-start.76 = (f32[16,16,128]{2,1,0:T(8,128)S(1)}, f32[16,16,128]{2,1,0:T(8,128)S(1)}, u32[]{:S(2)}, u32[]{:S(2)}) collective-permute-start(f32[16,16,128]{2,1,0:T(8,128)S(1)} %get-tuple-element.122), channel_id=1, source_target_pairs={{0,2},{1,3},{2,0},{3,1},{4,6},{5,7},{6,4},{7,5},{8,10},{9,11},{10,... | collective-permute-start | bytes 393224 | tf_op jit(solution)/shard_map/ppermute | solution.py:37
  249.4 11.6 %collective-permute-start.79 = (f32[18,16,128]{2,1,0:T(8,128)}, f32[18,16,128]{2,1,0:T(8,128)S(1)}, u32[]{:S(2)}, u32[]{:S(2)}) collective-permute-start(f32[18,16,128]{2,1,0:T(8,128)} %get-tuple-element.86.refs_0_), channel_id=1, source_target_pairs={{0,2},{1,3},{2,0},{3,1},{4,6},{5,7},{6,4},{7,5},{8,10},{9,11},{10,... | collective-permute-start | bytes 442376 | tf_op jit(solution)/shard_map/ppermute | solution.py:37
  251.4 9.6 %collective-permute-start.92 = (f32[16,16,128]{2,1,0:T(8,128)}, f32[16,16,128]{2,1,0:T(8,128)S(1)}, u32[]{:S(2)}, u32[]{:S(2)}) collective-permute-start(f32[16,16,128]{2,1,0:T(8,128)} %get-tuple-element.90.refs_12_), channel_id=1, source_target_pairs={{0,2},{1,3},{2,0},{3,1},{4,6},{5,7},{6,4},{7,5},{8,10},{9,11},{10,... | collective-permute-start | bytes 393224 | tf_op jit(solution)/shard_map/ppermute | solution.py:37
  251.4 10.1 %collective-permute-start.87 = (f32[16,16,128]{2,1,0:T(8,128)}, f32[16,16,128]{2,1,0:T(8,128)S(1)}, u32[]{:S(2)}, u32[]{:S(2)}) collective-permute-start(f32[16,16,128]{2,1,0:T(8,128)} %get-tuple-element.88.refs_4_), channel_id=1, source_target_pairs={{0,1},{1,0},{2,3},{3,2},{4,5},{5,4},{6,7},{7,6},{8,9},{9,8},{10,11... | collective-permute-start | bytes 393224 | tf_op jit(solution)/shard_map/ppermute | solution.py:37
  271.5 9.5 %collective-permute-start.104 = (f32[32,16,128]{2,1,0:T(8,128)}, f32[32,16,128]{2,1,0:T(8,128)S(1)}, u32[]{:S(2)}, u32[]{:S(2)}) collective-permute-start(f32[32,16,128]{2,1,0:T(8,128)} %get-tuple-element.98), channel_id=1, source_target_pairs={{0,8},{4,12},{8,0},{12,4},{16,24},{20,28},{24,16},{28,20},{1,9},{5... | collective-permute-start | bytes 786440 | tf_op jit(solution)/shard_map/ppermute | solution.py:37
  271.6 10.4 %collective-permute-start.101 = (f32[32,16,128]{2,1,0:T(8,128)}, f32[32,16,128]{2,1,0:T(8,128)S(1)}, u32[]{:S(2)}, u32[]{:S(2)}) collective-permute-start(f32[32,16,128]{2,1,0:T(8,128)} %get-tuple-element.96), channel_id=1, source_target_pairs={{0,4},{4,0},{8,12},{12,8},{16,20},{20,16},{24,28},{28,24},{1,5},{5... | collective-permute-start | bytes 786440 | tf_op jit(solution)/shard_map/ppermute | solution.py:37
  272.5 38.2 %collective-permute-start.82 = (f32[32,128]{1,0:T(8,128)S(1)}, f32[32,128]{1,0:T(8,128)S(1)}, u32[]{:S(2)}, u32[]{:S(2)}) collective-permute-start(f32[32,128]{1,0:T(8,128)S(1)} %bitcast.44), channel_id=1, source_target_pairs={{0,8},{4,12},{8,0},{12,4},{16,24},{20,28},{24,16},{28,20},{1,9},{5... | collective-permute-start | bytes 49160 | tf_op jit(solution)/shard_map/ppermute | solution.py:37
  274.5 37.1 %collective-permute-start.83 = (f32[32,128]{1,0:T(8,128)S(1)}, f32[32,128]{1,0:T(8,128)S(1)}, u32[]{:S(2)}, u32[]{:S(2)}) collective-permute-start(f32[32,128]{1,0:T(8,128)S(1)} %bitcast.45), channel_id=1, source_target_pairs={{0,4},{4,0},{8,12},{12,8},{16,20},{20,16},{24,28},{28,24},{1,5},{5... | collective-permute-start | bytes 49160 | tf_op jit(solution)/shard_map/ppermute | solution.py:37
  276.5 37.1 %collective-permute-start.84 = (f32[32,128]{1,0:T(8,128)S(1)}, f32[32,128]{1,0:T(8,128)S(1)}, u32[]{:S(2)}, u32[]{:S(2)}) collective-permute-start(f32[32,128]{1,0:T(8,128)S(1)} %bitcast.46), channel_id=1, source_target_pairs={{0,12},{4,8},{8,4},{12,0},{16,28},{20,24},{24,20},{28,16},{1,13},{... | collective-permute-start | bytes 49160 | tf_op jit(solution)/shard_map/ppermute | solution.py:37
  282.0 8.7 %collective-permute-start.95 = (f32[32,16,128]{2,1,0:T(8,128)}, f32[32,16,128]{2,1,0:T(8,128)S(1)}, u32[]{:S(2)}, u32[]{:S(2)}) collective-permute-start(f32[32,16,128]{2,1,0:T(8,128)} %get-tuple-element.92), channel_id=1, source_target_pairs={{0,4},{4,0},{8,12},{12,8},{16,20},{20,16},{24,28},{28,24},{1,5},{5... | collective-permute-start | bytes 786440 | tf_op jit(solution)/shard_map/ppermute | solution.py:37
  295.7 12.4 %collective-permute-start.96 = (f32[16,16,128]{2,1,0:T(8,128)S(1)}, f32[16,16,128]{2,1,0:T(8,128)S(1)}, u32[]{:S(2)}, u32[]{:S(2)}) collective-permute-start(f32[16,16,128]{2,1,0:T(8,128)S(1)} %get-tuple-element.117), channel_id=1, source_target_pairs={{0,8},{4,12},{8,0},{12,4},{16,24},{20,28},{24,16},{28,20},{1,9},{5... | collective-permute-start | bytes 393224 | tf_op jit(solution)/shard_map/ppermute | solution.py:37
  299.1 29.3 %collective-permute-start.106 = (f32[8,16,128]{2,1,0:T(8,128)S(1)}, f32[8,16,128]{2,1,0:T(8,128)S(1)}, u32[]{:S(2)}, u32[]{:S(2)}) collective-permute-start(f32[8,16,128]{2,1,0:T(8,128)S(1)} %get-tuple-element.143), channel_id=1, source_target_pairs={{0,16},{4,20},{8,24},{12,28},{16,0},{20,4},{24,8},{28,12},{1,17},{... | collective-permute-start | bytes 196616 | tf_op jit(solution)/shard_map/ppermute | solution.py:37
  308.0 20.4 %collective-permute-start.103 = (f32[8,16,128]{2,1,0:T(8,128)S(1)}, f32[8,16,128]{2,1,0:T(8,128)S(1)}, u32[]{:S(2)}, u32[]{:S(2)}) collective-permute-start(f32[8,16,128]{2,1,0:T(8,128)S(1)} %get-tuple-element.145), channel_id=1, source_target_pairs={{0,16},{4,20},{8,24},{12,28},{16,0},{20,4},{24,8},{28,12},{1,17},{... | collective-permute-start | bytes 196616 | tf_op jit(solution)/shard_map/ppermute | solution.py:37
  310.7 17.8 %collective-permute-start.100 = (f32[8,16,128]{2,1,0:T(8,128)S(1)}, f32[8,16,128]{2,1,0:T(8,128)S(1)}, u32[]{:S(2)}, u32[]{:S(2)}) collective-permute-start(f32[8,16,128]{2,1,0:T(8,128)S(1)} %get-tuple-element.147), channel_id=1, source_target_pairs={{0,16},{4,20},{8,24},{12,28},{16,0},{20,4},{24,8},{28,12},{1,17},{... | collective-permute-start | bytes 196616 | tf_op jit(solution)/shard_map/ppermute | solution.py:37
  311.6 16.9 %collective-permute-start.97 = (f32[8,16,128]{2,1,0:T(8,128)S(1)}, f32[8,16,128]{2,1,0:T(8,128)S(1)}, u32[]{:S(2)}, u32[]{:S(2)}) collective-permute-start(f32[8,16,128]{2,1,0:T(8,128)S(1)} %get-tuple-element.149), channel_id=1, source_target_pairs={{0,16},{4,20},{8,24},{12,28},{16,0},{20,4},{24,8},{28,12},{1,17},{... | collective-permute-start | bytes 196616 | tf_op jit(solution)/shard_map/ppermute | solution.py:37
  (140 other events, 859.2 us)

commit v8 on v7

--- a/solution.py
+++ b/solution.py
@@ -20,6 +20,7 @@
 UNROLL = 64
 HIGHEST = lax.Precision.HIGHEST
 VMEM_SPEC = pl.BlockSpec(memory_space=pltpu.VMEM)
+SMALL_KERNEL = pltpu.CompilerParams(vmem_limit_bytes=16 << 20)
 
 
 def gather_order(axis, part):
@@ -184,7 +185,7 @@
     )
     call = pl.pallas_call(
         kernel,
-        out_shape=[jax.ShapeDtypeStruct((half_out, ROWS, TILE), jnp.float32)] * (2 * PARTS),
+        out_shape=[pltpu.VMEM((half_out, ROWS, TILE), jnp.float32)] * (2 * PARTS),
         grid_spec=pltpu.PrefetchScalarGridSpec(
             num_scalar_prefetch=3,
             grid=(tiles.shape[0] // BATCH,),
@@ -196,9 +197,14 @@
                 pltpu.VMEM((2 * half_out + 1, K, TILE), jnp.float32),
             ],
         ),
+        compiler_params=pltpu.CompilerParams(vmem_limit_bytes=20 << 20),
     )
-    out = call(count, source, target, *[piece for part in pieces for piece in part], tiles)
+    out = call(count, source, target, *[in_vmem(piece) for part in pieces for piece in part], tiles)
     return out[:PARTS], out[PARTS:]
+
+
+def in_vmem(value):
+    return pltpu.with_memory_space_constraint(value, pltpu.VMEM)
 
 
 def dot_full(left, right, contract):
@@ -243,6 +249,7 @@
         grid=(blocks,),
         in_specs=[block] + ([] if into is None else [pl.BlockSpec(memory_space=pl.ANY)]),
         out_specs=block,
+        compiler_params=SMALL_KERNEL,
         input_output_aliases={} if into is None else {1: 0},
         name="turned_tiles",
     )(*([tiles] if into is None else [tiles, into]))
@@ -251,11 +258,12 @@
 def inverse_factor(gram, total):
     return pl.pallas_call(
         functools.partial(factor_kernel, total=total),
-        out_shape=jax.ShapeDtypeStruct((K, K), jnp.float32),
+        out_shape=pltpu.VMEM((K, K), jnp.float32),
         in_specs=[VMEM_SPEC],
         out_specs=VMEM_SPEC,
+        compiler_params=SMALL_KERNEL,
         name="factor",
-    )(gram)
+    )(in_vmem(gram))
 
 
 def scale_kernel(*refs, factored):
@@ -287,11 +295,12 @@
     panel, *sent = pl.pallas_call(
         functools.partial(scale_kernel, factored=factored),
         out_shape=[jax.ShapeDtypeStruct((blocks, K, TILE), jnp.float32)]
-        + [jax.ShapeDtypeStruct((blocks + GRAM * (part == 0), ROWS, TILE), jnp.float32) for part in range(PARTS)],
+        + [pltpu.VMEM((blocks + GRAM * (part == 0), ROWS, TILE), jnp.float32) for part in range(PARTS)],
         in_specs=[VMEM_SPEC] * len(operands),
         out_specs=[VMEM_SPEC] * (1 + PARTS),
+        compiler_params=SMALL_KERNEL,
         name="scale_panel",
-    )(*operands)
+    )(*map(in_vmem, operands))
     return panel, sent
 
 
@@ -306,6 +315,7 @@
         out_shape=jax.ShapeDtypeStruct((K, panel.shape[0] * TILE), jnp.float32),
         in_specs=[VMEM_SPEC] * 2,
         out_specs=VMEM_SPEC,
+        compiler_params=SMALL_KERNEL,
         name="finish_panel",
     )(inverse, panel)
 

time: 362 us -> 311 us (0.86)
  Pallas kernels: 95.4 us -> 51.8 us
  other arithmetic: 34.9 us -> 2.59 us
  waiting for transfers between devices: 88.4 us -> 114 us
  local copies, waits for them, and re-layouts: 9.55 us -> 18.4 us
  starting transfers between devices: 130 us -> 122 us
    ppermute x112, waiting for transfers between devices: 88.4 us -> 114 us  [exchange(): lax.ppermute(value, axis, [(at, at ^ bit) for at in range(lax.axis_size(a...]
    pallas_call x8, Pallas kernels: 57.2 us -> 36.4 us  [the longest x4 21.7 us: inverse_factor(): pl.pallas_call(functools.partial(factor_kernel, total=total), out_shape=p...]
    add x12, other arithmetic: 15.9 us -> 0.39 us  [reduce_scatter(): sent = [have[half:] + more[half:] for have, more in zip(kept, got)]]
    pallas_call x2, Pallas kernels: 19.7 us -> 5.33 us  [turned_tiles(): pl.pallas_call(turn_kernel, out_shape=jax.ShapeDtypeStruct(tiles.shape, t...]
    unnamed x156 -> x24, local copies, waits for them, and re-layouts: 7.9 us -> 18.3 us
    add x12, other arithmetic: 10.6 us -> 0.38 us  [reduce_scatter(): kept = [have[:half] + more[:half] for have, more in zip(kept, got)]]
    ppermute x112, starting transfers between devices: 130 us -> 122 us  [exchange(): lax.ppermute(value, axis, [(at, at ^ bit) for at in range(lax.axis_size(a...]
    pallas_call x4, Pallas kernels: 14.1 us -> 7.63 us  [scale_panel(): pl.pallas_call(functools.partial(scale_kernel, factored=factored), out_sh...]
  transfers between devices with their start and end apart: 112 -> 112, of which waited for: 48 -> 54; matrix products, arithmetic and copies ran while one was open for 10% -> 0% of each run, Pallas kernels for 12% -> 7%
where the time goes in v8:
time: 311 us
  starting transfers between devices  122 us (39%)
  waiting for transfers between devices  114 us (37%)
  Pallas kernels  51.8 us (17%)
  local copies, waits for them, and re-layouts  18.4 us (6%)
    ppermute x112, starting transfers between devices, exchange(): lax.ppermute(value, axis, [(at, at ^ bit) for at in range(lax.axis_size(a...  122 us
    ppermute x112, waiting for transfers between devices, exchange(): lax.ppermute(value, axis, [(at, at ^ bit) for at in range(lax.axis_size(a...  114 us
    pallas_call x4, Pallas kernels, inverse_factor(): pl.pallas_call(functools.partial(factor_kernel, total=total), out_shape=p...  21.7 us
    unnamed x24, local copies, waits for them, and re-layouts  18.3 us
    pallas_call x4, Pallas kernels, tiles_product(): call(count, source, target, *[in_vmem(piece) for part in pieces for piece...  14.6 us
    pallas_call x4, Pallas kernels, scale_panel(): pl.pallas_call(functools.partial(scale_kernel, factored=factored), out_sh...  7.63 us
  transfers between devices with their start and end apart: 112, of which 54 were waited for; matrix products, arithmetic and copies ran while one was open for 0% of the time, Pallas kernels for 7%

profile of v8, /device:TPU:0, one launch (start us, length us, event | category | flops | bytes accessed | tf_op | source)
XLA Modules:
  0.0 311.2 jit_solution(4320334533664095430)
XLA Ops:
  2.4 4.1 %collective-permute-start.8 = (f32[8,16,128]{2,1,0:T(8,128)S(1)}, f32[8,16,128]{2,1,0:T(8,128)S(1)}, u32[]{:S(2)}, u32[]{:S(2)}) collective-permute-start(f32[8,16,128]{2,1,0:T(8,128)S(1)} %get-tuple-element.159), channel_id=1, source_target_pairs={{0,16},{4,20},{8,24},{12,28},{16,0},{20,4},{24,8},{28,12},{1,17},{... | collective-permute-start | bytes 196616 | tf_op jit(solution)/shard_map/ppermute | solution.py:38
  6.6 2.8 collective-permute-start.4
  10.2 5.2 %collective-permute-start.9 = (f32[16,16,128]{2,1,0:T(8,128)S(1)}, f32[16,16,128]{2,1,0:T(8,128)S(1)}, u32[]{:S(2)}, u32[]{:S(2)}) collective-permute-start(f32[16,16,128]{2,1,0:T(8,128)S(1)} %pad_maximum_fusion.3.refs_8_), channel_id=1, source_target_pairs={{0,8},{4,12},{8,0},{12,4},{16,24},{20,28},{24,16},{28,20},{1,9},{5... | collective-permute-start | bytes 393224 | tf_op jit(solution)/shard_map/ppermute | solution.py:38
  24.9 5.8 %copy-done = bf16[1,1,512,128,128]{4,3,2,1,0:T(8,128)(2,1)S(1)} copy-done((bf16[1,1,512,128,128]{4,3,2,1,0:T(8,128)(2,1)S(1)}, bf16[1,1,512,128,128]{4,3,2,1,0:T(8,128)(2,1)}, u32[]{:S(2)}) %copy-start) | copy-done | bytes 16777240
  30.6 2.7 turned_tiles.2.refs_0_
  33.4 2.7 turned_tiles.3.refs_16_
  36.0 6.7 %copy-done.1 = bf16[512,128,128]{2,1,0:T(8,128)(2,1)} copy-done((bf16[512,128,128]{2,1,0:T(8,128)(2,1)}, bf16[512,128,128]{2,1,0:T(8,128)(2,1)S(1)}, u32[]{:S(2)}) %copy-start.1) | copy-done | bytes 16777240
  49.4 2.8 collective-permute-done.11.refs_11_
  53.9 5.8 %copy-done.2 = bf16[512,128,128]{2,1,0:T(8,128)(2,1)S(1)} copy-done((bf16[512,128,128]{2,1,0:T(8,128)(2,1)S(1)}, bf16[512,128,128]{2,1,0:T(8,128)(2,1)}, u32[]{:S(2)}) %copy-start.2) | copy-done | bytes 16777240
  59.6 3.6 %shard_map.86 = (f32[32,16,128]{2,1,0:T(8,128)S(1)}, f32[32,16,128]{2,1,0:T(8,128)S(1)}, f32[32,16,128]{2,1,0:T(8,128)S(1)}, f32[32,16,128]{2,1,0:T(8,128)S(1)},...) custom-call(s32[1]{0:T(128)} %bitcast.31.count, ...), custom_call_target="tpu_custom_call" | custom-call | tf_op jit(solution)/shard_map/pallas_call | solution.py:202
  64.9 6.0 %collective-permute-start.23 = (f32[16,16,128]{2,1,0:T(8,128)S(1)}, f32[16,16,128]{2,1,0:T(8,128)S(1)}, u32[]{:S(2)}, u32[]{:S(2)}) collective-permute-start(f32[16,16,128]{2,1,0:T(8,128)S(1)} %get-tuple-element.134), channel_id=1, source_target_pairs={{0,2},{1,3},{2,0},{3,1},{4,6},{5,7},{6,4},{7,5},{8,10},{9,11},{10,... | collective-permute-start | bytes 393224 | tf_op jit(solution)/shard_map/ppermute | solution.py:38
  75.2 2.8 collective-permute-done.22.refs_6_
  78.0 2.8 collective-permute-done.21.refs_5_
  90.9 2.8 collective-permute-done.34.refs_9_
  93.7 4.6 %collective-permute-done.37.refs_13_ = f32[16,16,128]{2,1,0:T(8,128)S(1)} collective-permute-done((f32[16,16,128]{2,1,0:T(8,128)S(1)}, f32[16,16,128]{2,1,0:T(8,128)S(1)}, u32[]{:S(2)}, u32[]{:S(2)}) %collective-permute-start.37) | collective-permute-done | bytes 131104 | tf_op jit(solution)/shard_map/ppermute | solution.py:38
  100.7 3.6 %shard_map.87 = (f32[32,16,128]{2,1,0:T(8,128)S(1)}, f32[32,16,128]{2,1,0:T(8,128)S(1)}, f32[32,16,128]{2,1,0:T(8,128)S(1)}, f32[32,16,128]{2,1,0:T(8,128)S(1)},...) custom-call(s32[1]{0:T(128)} %bitcast.32.count, ...), custom_call_target="tpu_custom_call" | custom-call | tf_op jit(solution)/shard_map/pallas_call | solution.py:202
  108.5 4.8 %collective-permute-done.46 = f32[32,16,128]{2,1,0:T(8,128)S(1)} collective-permute-done((f32[32,16,128]{2,1,0:T(8,128)S(1)}, f32[32,16,128]{2,1,0:T(8,128)S(1)}, u32[]{:S(2)}, u32[]{:S(2)}) %collective-permute-start.46) | collective-permute-done | bytes 262176 | tf_op jit(solution)/shard_map/ppermute | solution.py:38
  113.5 7.5 %collective-permute-done.42 = f32[32,16,128]{2,1,0:T(8,128)S(1)} collective-permute-done((f32[32,16,128]{2,1,0:T(8,128)S(1)}, f32[32,16,128]{2,1,0:T(8,128)S(1)}, u32[]{:S(2)}, u32[]{:S(2)}) %collective-permute-start.42) | collective-permute-done | bytes 262176 | tf_op jit(solution)/shard_map/ppermute | solution.py:38
  131.0 5.8 %collective-permute-start.51 = (f32[8,16,128]{2,1,0:T(8,128)S(1)}, f32[8,16,128]{2,1,0:T(8,128)S(1)}, u32[]{:S(2)}, u32[]{:S(2)}) collective-permute-start(f32[8,16,128]{2,1,0:T(8,128)S(1)} %get-tuple-element.150), channel_id=1, source_target_pairs={{0,16},{4,20},{8,24},{12,28},{16,0},{20,4},{24,8},{28,12},{1,17},{... | collective-permute-start | bytes 196616 | tf_op jit(solution)/shard_map/ppermute | solution.py:38
  136.8 2.7 collective-permute-start.50
  139.9 2.7 collective-permute-start.48
  142.9 4.8 %collective-permute-done.30 = f32[32,128]{1,0:T(8,128)S(1)} collective-permute-done((f32[32,128]{1,0:T(8,128)S(1)}, f32[32,128]{1,0:T(8,128)S(1)}, u32[]{:S(2)}, u32[]{:S(2)}) %collective-permute-start.30) | collective-permute-done | bytes 16416 | tf_op jit(solution)/shard_map/ppermute | solution.py:38
  147.7 5.4 %factor.4.refs_0_ = f32[64,64]{1,0:T(8,128)S(1)} custom-call(f32[32,128]{1,0:T(8,128)S(1)} %add.288.gram_ref), custom_call_target="tpu_custom_call" | custom-call | tf_op jit(solution)/shard_map/factor/pallas_call | solution.py:259
  155.3 2.6 collective-permute-start.63
  160.8 3.0 collective-permute-done.67
  166.9 2.8 collective-permute-start.65
  172.6 3.1 collective-permute-start.54
  176.1 2.9 collective-permute-start.55
  181.0 2.9 collective-permute-done.70.refs_15_
  185.3 3.8 %shard_map.88 = (f32[32,16,128]{2,1,0:T(8,128)S(1)}, f32[32,16,128]{2,1,0:T(8,128)S(1)}, f32[32,16,128]{2,1,0:T(8,128)S(1)}, f32[32,16,128]{2,1,0:T(8,128)S(1)},...) custom-call(s32[1]{0:T(128)} %bitcast.33.count, ...), custom_call_target="tpu_custom_call" | custom-call | tf_op jit(solution)/shard_map/pallas_call | solution.py:202
  197.6 5.4 %factor.5.refs_0_ = f32[64,64]{1,0:T(8,128)S(1)} custom-call(f32[32,128]{1,0:T(8,128)S(1)} %add_add_fusion.1.gram_ref), custom_call_target="tpu_custom_call" | custom-call | tf_op jit(solution)/shard_map/factor/pallas_call | solution.py:259
  207.3 2.6 scale_panel.6
  216.3 2.8 collective-permute-done.89.refs_9_
  219.1 4.3 %collective-permute-done.92.refs_13_ = f32[16,16,128]{2,1,0:T(8,128)S(1)} collective-permute-done((f32[16,16,128]{2,1,0:T(8,128)S(1)}, f32[16,16,128]{2,1,0:T(8,128)S(1)}, u32[]{:S(2)}, u32[]{:S(2)}) %collective-permute-start.92) | collective-permute-done | bytes 131104 | tf_op jit(solution)/shard_map/ppermute | solution.py:38
  225.8 3.6 %shard_map.89 = (f32[32,16,128]{2,1,0:T(8,128)S(1)}, f32[32,16,128]{2,1,0:T(8,128)S(1)}, f32[32,16,128]{2,1,0:T(8,128)S(1)}, f32[32,16,128]{2,1,0:T(8,128)S(1)},...) custom-call(s32[1]{0:T(128)} %bitcast.34.count, ...), custom_call_target="tpu_custom_call" | custom-call | tf_op jit(solution)/shard_map/pallas_call | solution.py:202
  237.4 5.4 %collective-permute-done.98 = f32[32,16,128]{2,1,0:T(8,128)S(1)} collective-permute-done((f32[32,16,128]{2,1,0:T(8,128)S(1)}, f32[32,16,128]{2,1,0:T(8,128)S(1)}, u32[]{:S(2)}, u32[]{:S(2)}) %collective-permute-start.98) | collective-permute-done | bytes 262176 | tf_op jit(solution)/shard_map/ppermute | solution.py:38
  244.6 4.4 %collective-permute-done.105 = f32[16,16,128]{2,1,0:T(8,128)S(1)} collective-permute-done((f32[16,16,128]{2,1,0:T(8,128)S(1)}, f32[16,16,128]{2,1,0:T(8,128)S(1)}, u32[]{:S(2)}, u32[]{:S(2)}) %collective-permute-start.105) | collective-permute-done | bytes 131104 | tf_op jit(solution)/shard_map/ppermute | solution.py:38
  250.5 4.6 %collective-permute-done.99 = f32[16,16,128]{2,1,0:T(8,128)S(1)} collective-permute-done((f32[16,16,128]{2,1,0:T(8,128)S(1)}, f32[16,16,128]{2,1,0:T(8,128)S(1)}, u32[]{:S(2)}, u32[]{:S(2)}) %collective-permute-start.99) | collective-permute-done | bytes 131104 | tf_op jit(solution)/shard_map/ppermute | solution.py:38
  255.1 11.4 %collective-permute-start.106 = (f32[8,16,128]{2,1,0:T(8,128)S(1)}, f32[8,16,128]{2,1,0:T(8,128)S(1)}, u32[]{:S(2)}, u32[]{:S(2)}) collective-permute-start(f32[8,16,128]{2,1,0:T(8,128)S(1)} %get-tuple-element.143), channel_id=1, source_target_pairs={{0,16},{4,20},{8,24},{12,28},{16,0},{20,4},{24,8},{28,12},{1,17},{... | collective-permute-start | bytes 196616 | tf_op jit(solution)/shard_map/ppermute | solution.py:38
  266.6 4.7 %collective-permute-start.103 = (f32[8,16,128]{2,1,0:T(8,128)S(1)}, f32[8,16,128]{2,1,0:T(8,128)S(1)}, u32[]{:S(2)}, u32[]{:S(2)}) collective-permute-start(f32[8,16,128]{2,1,0:T(8,128)S(1)} %get-tuple-element.145), channel_id=1, source_target_pairs={{0,16},{4,20},{8,24},{12,28},{16,0},{20,4},{24,8},{28,12},{1,17},{... | collective-permute-start | bytes 196616 | tf_op jit(solution)/shard_map/ppermute | solution.py:38
  271.4 2.9 collective-permute-start.97
  274.5 4.6 %collective-permute-done.85 = f32[32,128]{1,0:T(8,128)S(1)} collective-permute-done((f32[32,128]{1,0:T(8,128)S(1)}, f32[32,128]{1,0:T(8,128)S(1)}, u32[]{:S(2)}, u32[]{:S(2)}) %collective-permute-start.85) | collective-permute-done | bytes 16416 | tf_op jit(solution)/shard_map/ppermute | solution.py:38
  279.1 5.4 %factor.6.inverse_ref.refs_0_ = f32[64,64]{1,0:T(8,128)S(1)} custom-call(f32[32,128]{1,0:T(8,128)S(1)} %add.328.gram_ref), custom_call_target="tpu_custom_call" | custom-call | tf_op jit(solution)/shard_map/factor/pallas_call | solution.py:259
  288.8 3.7 %collective-permute-done.108 = f32[32,128]{1,0:T(8,128)S(1)} collective-permute-done((f32[32,128]{1,0:T(8,128)S(1)}, f32[32,128]{1,0:T(8,128)S(1)}, u32[]{:S(2)}, u32[]{:S(2)}) %collective-permute-start.108) | collective-permute-done | bytes 16416 | tf_op jit(solution)/shard_map/ppermute | solution.py:38
  292.6 3.7 %collective-permute-done.109 = f32[32,128]{1,0:T(8,128)S(1)} collective-permute-done((f32[32,128]{1,0:T(8,128)S(1)}, f32[32,128]{1,0:T(8,128)S(1)}, u32[]{:S(2)}, u32[]{:S(2)}) %collective-permute-start.109) | collective-permute-done | bytes 16416 | tf_op jit(solution)/shard_map/ppermute | solution.py:38
  296.3 3.7 %collective-permute-done.110 = f32[32,128]{1,0:T(8,128)S(1)} collective-permute-done((f32[32,128]{1,0:T(8,128)S(1)}, f32[32,128]{1,0:T(8,128)S(1)}, u32[]{:S(2)}, u32[]{:S(2)}) %collective-permute-start.110) | collective-permute-done | bytes 16416 | tf_op jit(solution)/shard_map/ppermute | solution.py:38
  300.8 3.9 %collective-permute-done.111 = f32[32,128]{1,0:T(8,128)S(1)} collective-permute-done((f32[32,128]{1,0:T(8,128)S(1)}, f32[32,128]{1,0:T(8,128)S(1)}, u32[]{:S(2)}, u32[]{:S(2)}) %collective-permute-start.111) | collective-permute-done | bytes 16416 | tf_op jit(solution)/shard_map/ppermute | solution.py:38
  304.7 5.4 %factor.7.inverse_ref = f32[64,64]{1,0:T(8,128)S(1)} custom-call(f32[32,128]{1,0:T(8,128)S(1)} %add.349.gram_ref), custom_call_target="tpu_custom_call" | custom-call | tf_op jit(solution)/shard_map/factor/pallas_call | solution.py:259
  (273 shorter events, 107.2 us)
Async XLA Ops:
  6.5 10.2 %collective-permute-start.12 = (f32[8,16,128]{2,1,0:T(8,128)S(1)}, f32[8,16,128]{2,1,0:T(8,128)S(1)}, u32[]{:S(2)}, u32[]{:S(2)}) collective-permute-start(f32[8,16,128]{2,1,0:T(8,128)S(1)} %get-tuple-element.158), channel_id=1, source_target_pairs={{0,16},{4,20},{8,24},{12,28},{16,0},{20,4},{24,8},{28,12},{1,17},{... | collective-permute-start | bytes 196616 | tf_op jit(solution)/shard_map/ppermute | solution.py:38
  6.6 13.4 %collective-permute-start.4 = (f32[8,16,128]{2,1,0:T(8,128)S(1)}, f32[8,16,128]{2,1,0:T(8,128)S(1)}, u32[]{:S(2)}, u32[]{:S(2)}) collective-permute-start(f32[8,16,128]{2,1,0:T(8,128)S(1)} %get-tuple-element.160), channel_id=1, source_target_pairs={{0,16},{4,20},{8,24},{12,28},{16,0},{20,4},{24,8},{28,12},{1,17},{... | collective-permute-start | bytes 196616 | tf_op jit(solution)/shard_map/ppermute | solution.py:38
  9.5 9.9 %collective-permute-start = (f32[10,16,128]{2,1,0:T(8,128)S(1)}, f32[10,16,128]{2,1,0:T(8,128)S(1)}, u32[]{:S(2)}, u32[]{:S(2)}) collective-permute-start(f32[10,16,128]{2,1,0:T(8,128)S(1)} %concatenate.27), channel_id=1, source_target_pairs={{0,16},{4,20},{8,24},{12,28},{16,0},{20,4},{24,8},{28,12},{1,17},{... | collective-permute-start | bytes 245768 | tf_op jit(solution)/shard_map/ppermute | solution.py:38
  10.2 11.9 %collective-permute-start.9 = (f32[16,16,128]{2,1,0:T(8,128)S(1)}, f32[16,16,128]{2,1,0:T(8,128)S(1)}, u32[]{:S(2)}, u32[]{:S(2)}) collective-permute-start(f32[16,16,128]{2,1,0:T(8,128)S(1)} %pad_maximum_fusion.3.refs_8_), channel_id=1, source_target_pairs={{0,8},{4,12},{8,0},{12,4},{16,24},{20,28},{24,16},{28,20},{1,9},{5... | collective-permute-start | bytes 393224 | tf_op jit(solution)/shard_map/ppermute | solution.py:38
  19.4 27.4 %collective-permute-start.1 = (f32[18,16,128]{2,1,0:T(8,128)S(1)}, f32[18,16,128]{2,1,0:T(8,128)S(1)}, u32[]{:S(2)}, u32[]{:S(2)}) collective-permute-start(f32[18,16,128]{2,1,0:T(8,128)S(1)} %pad_maximum_fusion.refs_0_), channel_id=1, source_target_pairs={{0,8},{4,12},{8,0},{12,4},{16,24},{20,28},{24,16},{28,20},{1,9},{5... | collective-permute-start | bytes 442376 | tf_op jit(solution)/shard_map/ppermute | solution.py:38
  20.0 22.7 %collective-permute-start.5 = (f32[16,16,128]{2,1,0:T(8,128)S(1)}, f32[16,16,128]{2,1,0:T(8,128)S(1)}, u32[]{:S(2)}, u32[]{:S(2)}) collective-permute-start(f32[16,16,128]{2,1,0:T(8,128)S(1)} %pad_maximum_fusion.2.refs_4_), channel_id=1, source_target_pairs={{0,4},{4,0},{8,12},{12,8},{16,20},{20,16},{24,28},{28,24},{1,5},{5... | collective-permute-start | bytes 393224 | tf_op jit(solution)/shard_map/ppermute | solution.py:38
  21.6 22.8 %collective-permute-start.10 = (f32[16,16,128]{2,1,0:T(8,128)S(1)}, f32[16,16,128]{2,1,0:T(8,128)S(1)}, u32[]{:S(2)}, u32[]{:S(2)}) collective-permute-start(f32[16,16,128]{2,1,0:T(8,128)S(1)} %pad_maximum_fusion.3.refs_8_), channel_id=1, source_target_pairs={{0,4},{4,0},{8,12},{12,8},{16,20},{20,16},{24,28},{28,24},{1,5},{5... | collective-permute-start | bytes 393224 | tf_op jit(solution)/shard_map/ppermute | solution.py:38
  22.2 22.6 %collective-permute-start.14 = (f32[16,16,128]{2,1,0:T(8,128)S(1)}, f32[16,16,128]{2,1,0:T(8,128)S(1)}, u32[]{:S(2)}, u32[]{:S(2)}) collective-permute-start(f32[16,16,128]{2,1,0:T(8,128)S(1)} %pad_maximum_fusion.4.refs_12_), channel_id=1, source_target_pairs={{0,8},{4,12},{8,0},{12,4},{16,24},{20,28},{24,16},{28,20},{1,9},{5... | collective-permute-start | bytes 393224 | tf_op jit(solution)/shard_map/ppermute | solution.py:38
  23.6 22.6 %collective-permute-start.6 = (f32[16,16,128]{2,1,0:T(8,128)S(1)}, f32[16,16,128]{2,1,0:T(8,128)S(1)}, u32[]{:S(2)}, u32[]{:S(2)}) collective-permute-start(f32[16,16,128]{2,1,0:T(8,128)S(1)} %pad_maximum_fusion.2.refs_4_), channel_id=1, source_target_pairs={{0,8},{4,12},{8,0},{12,4},{16,24},{20,28},{24,16},{28,20},{1,9},{5... | collective-permute-start | bytes 393224 | tf_op jit(solution)/shard_map/ppermute | solution.py:38
  63.9 9.2 %collective-permute-start.16 = (f32[32,16,128]{2,1,0:T(8,128)S(1)}, f32[32,16,128]{2,1,0:T(8,128)S(1)}, u32[]{:S(2)}, u32[]{:S(2)}) collective-permute-start(f32[32,16,128]{2,1,0:T(8,128)S(1)} %get-tuple-element.55), channel_id=1, source_target_pairs={{0,1},{1,0},{2,3},{3,2},{4,5},{5,4},{6,7},{7,6},{8,9},{9,8},{10,11... | collective-permute-start | bytes 786440 | tf_op jit(solution)/shard_map/ppermute | solution.py:38
  64.9 10.3 %collective-permute-start.23 = (f32[16,16,128]{2,1,0:T(8,128)S(1)}, f32[16,16,128]{2,1,0:T(8,128)S(1)}, u32[]{:S(2)}, u32[]{:S(2)}) collective-permute-start(f32[16,16,128]{2,1,0:T(8,128)S(1)} %get-tuple-element.134), channel_id=1, source_target_pairs={{0,2},{1,3},{2,0},{3,1},{4,6},{5,7},{6,4},{7,5},{8,10},{9,11},{10,... | collective-permute-start | bytes 393224 | tf_op jit(solution)/shard_map/ppermute | solution.py:38
  71.3 9.5 %collective-permute-start.21 = (f32[16,16,128]{2,1,0:T(8,128)S(1)}, f32[16,16,128]{2,1,0:T(8,128)S(1)}, u32[]{:S(2)}, u32[]{:S(2)}) collective-permute-start(f32[16,16,128]{2,1,0:T(8,128)S(1)} %get-tuple-element.138), channel_id=1, source_target_pairs={{0,2},{1,3},{2,0},{3,1},{4,6},{5,7},{6,4},{7,5},{8,10},{9,11},{10,... | collective-permute-start | bytes 393224 | tf_op jit(solution)/shard_map/ppermute | solution.py:38
  73.2 9.9 %collective-permute-start.20 = (f32[16,16,128]{2,1,0:T(8,128)S(1)}, f32[16,16,128]{2,1,0:T(8,128)S(1)}, u32[]{:S(2)}, u32[]{:S(2)}) collective-permute-start(f32[16,16,128]{2,1,0:T(8,128)S(1)} %get-tuple-element.140), channel_id=1, source_target_pairs={{0,2},{1,3},{2,0},{3,1},{4,6},{5,7},{6,4},{7,5},{8,10},{9,11},{10,... | collective-permute-start | bytes 393224 | tf_op jit(solution)/shard_map/ppermute | solution.py:38
  86.6 11.7 %collective-permute-start.24 = (f32[18,16,128]{2,1,0:T(8,128)S(1)}, f32[18,16,128]{2,1,0:T(8,128)S(1)}, u32[]{:S(2)}, u32[]{:S(2)}) collective-permute-start(f32[18,16,128]{2,1,0:T(8,128)S(1)} %get-tuple-element.62.refs_0_), channel_id=1, source_target_pairs={{0,2},{1,3},{2,0},{3,1},{4,6},{5,7},{6,4},{7,5},{8,10},{9,11},{10,... | collective-permute-start | bytes 442376 | tf_op jit(solution)/shard_map/ppermute | solution.py:38
  88.3 10.0 %collective-permute-start.37 = (f32[16,16,128]{2,1,0:T(8,128)S(1)}, f32[16,16,128]{2,1,0:T(8,128)S(1)}, u32[]{:S(2)}, u32[]{:S(2)}) collective-permute-start(f32[16,16,128]{2,1,0:T(8,128)S(1)} %get-tuple-element.65.refs_12_), channel_id=1, source_target_pairs={{0,2},{1,3},{2,0},{3,1},{4,6},{5,7},{6,4},{7,5},{8,10},{9,11},{10,... | collective-permute-start | bytes 393224 | tf_op jit(solution)/shard_map/ppermute | solution.py:38
  88.6 10.2 %collective-permute-start.32 = (f32[16,16,128]{2,1,0:T(8,128)S(1)}, f32[16,16,128]{2,1,0:T(8,128)S(1)}, u32[]{:S(2)}, u32[]{:S(2)}) collective-permute-start(f32[16,16,128]{2,1,0:T(8,128)S(1)} %get-tuple-element.63.refs_4_), channel_id=1, source_target_pairs={{0,1},{1,0},{2,3},{3,2},{4,5},{5,4},{6,7},{7,6},{8,9},{9,8},{10,11... | collective-permute-start | bytes 393224 | tf_op jit(solution)/shard_map/ppermute | solution.py:38
  104.4 9.0 %collective-permute-start.46 = (f32[32,16,128]{2,1,0:T(8,128)S(1)}, f32[32,16,128]{2,1,0:T(8,128)S(1)}, u32[]{:S(2)}, u32[]{:S(2)}) collective-permute-start(f32[32,16,128]{2,1,0:T(8,128)S(1)} %get-tuple-element.73), channel_id=1, source_target_pairs={{0,8},{4,12},{8,0},{12,4},{16,24},{20,28},{24,16},{28,20},{1,9},{5... | collective-permute-start | bytes 786440 | tf_op jit(solution)/shard_map/ppermute | solution.py:38
  104.4 9.0 %collective-permute-start.44 = (f32[32,16,128]{2,1,0:T(8,128)S(1)}, f32[32,16,128]{2,1,0:T(8,128)S(1)}, u32[]{:S(2)}, u32[]{:S(2)}) collective-permute-start(f32[32,16,128]{2,1,0:T(8,128)S(1)} %get-tuple-element.71), channel_id=1, source_target_pairs={{0,4},{4,0},{8,12},{12,8},{16,20},{20,16},{24,28},{28,24},{1,5},{5... | collective-permute-start | bytes 786440 | tf_op jit(solution)/shard_map/ppermute | solution.py:38
  104.7 34.9 %collective-permute-start.27 = (f32[32,128]{1,0:T(8,128)S(1)}, f32[32,128]{1,0:T(8,128)S(1)}, u32[]{:S(2)}, u32[]{:S(2)}) collective-permute-start(f32[32,128]{1,0:T(8,128)S(1)} %bitcast.43), channel_id=1, source_target_pairs={{0,8},{4,12},{8,0},{12,4},{16,24},{20,28},{24,16},{28,20},{1,9},{5... | collective-permute-start | bytes 49160 | tf_op jit(solution)/shard_map/ppermute | solution.py:38
  106.6 33.3 %collective-permute-start.28 = (f32[32,128]{1,0:T(8,128)S(1)}, f32[32,128]{1,0:T(8,128)S(1)}, u32[]{:S(2)}, u32[]{:S(2)}) collective-permute-start(f32[32,128]{1,0:T(8,128)S(1)} %bitcast.44), channel_id=1, source_target_pairs={{0,4},{4,0},{8,12},{12,8},{16,20},{20,16},{24,28},{28,24},{1,5},{5... | collective-permute-start | bytes 49160 | tf_op jit(solution)/shard_map/ppermute | solution.py:38
  108.5 34.1 %collective-permute-start.29 = (f32[32,128]{1,0:T(8,128)S(1)}, f32[32,128]{1,0:T(8,128)S(1)}, u32[]{:S(2)}, u32[]{:S(2)}) collective-permute-start(f32[32,128]{1,0:T(8,128)S(1)} %bitcast.45), channel_id=1, source_target_pairs={{0,12},{4,8},{8,4},{12,0},{16,28},{20,24},{24,20},{28,16},{1,13},{... | collective-permute-start | bytes 49160 | tf_op jit(solution)/shard_map/ppermute | solution.py:38
  113.4 8.7 %collective-permute-start.40 = (f32[32,16,128]{2,1,0:T(8,128)S(1)}, f32[32,16,128]{2,1,0:T(8,128)S(1)}, u32[]{:S(2)}, u32[]{:S(2)}) collective-permute-start(f32[32,16,128]{2,1,0:T(8,128)S(1)} %get-tuple-element.67), channel_id=1, source_target_pairs={{0,4},{4,0},{8,12},{12,8},{16,20},{20,16},{24,28},{28,24},{1,5},{5... | collective-permute-start | bytes 786440 | tf_op jit(solution)/shard_map/ppermute | solution.py:38
  127.5 9.3 %collective-permute-start.41 = (f32[16,16,128]{2,1,0:T(8,128)S(1)}, f32[16,16,128]{2,1,0:T(8,128)S(1)}, u32[]{:S(2)}, u32[]{:S(2)}) collective-permute-start(f32[16,16,128]{2,1,0:T(8,128)S(1)} %get-tuple-element.133), channel_id=1, source_target_pairs={{0,8},{4,12},{8,0},{12,4},{16,24},{20,28},{24,16},{28,20},{1,9},{5... | collective-permute-start | bytes 393224 | tf_op jit(solution)/shard_map/ppermute | solution.py:38
  131.0 22.1 %collective-permute-start.51 = (f32[8,16,128]{2,1,0:T(8,128)S(1)}, f32[8,16,128]{2,1,0:T(8,128)S(1)}, u32[]{:S(2)}, u32[]{:S(2)}) collective-permute-start(f32[8,16,128]{2,1,0:T(8,128)S(1)} %get-tuple-element.150), channel_id=1, source_target_pairs={{0,16},{4,20},{8,24},{12,28},{16,0},{20,4},{24,8},{28,12},{1,17},{... | collective-permute-start | bytes 196616 | tf_op jit(solution)/shard_map/ppermute | solution.py:38
  136.8 16.3 %collective-permute-start.50 = (f32[8,16,128]{2,1,0:T(8,128)S(1)}, f32[8,16,128]{2,1,0:T(8,128)S(1)}, u32[]{:S(2)}, u32[]{:S(2)}) collective-permute-start(f32[8,16,128]{2,1,0:T(8,128)S(1)} %get-tuple-element.152), channel_id=1, source_target_pairs={{0,16},{4,20},{8,24},{12,28},{16,0},{20,4},{24,8},{28,12},{1,17},{... | collective-permute-start | bytes 196616 | tf_op jit(solution)/shard_map/ppermute | solution.py:38
  139.6 13.5 %collective-permute-start.49 = (f32[8,16,128]{2,1,0:T(8,128)S(1)}, f32[8,16,128]{2,1,0:T(8,128)S(1)}, u32[]{:S(2)}, u32[]{:S(2)}) collective-permute-start(f32[8,16,128]{2,1,0:T(8,128)S(1)} %get-tuple-element.154), channel_id=1, source_target_pairs={{0,16},{4,20},{8,24},{12,28},{16,0},{20,4},{24,8},{28,12},{1,17},{... | collective-permute-start | bytes 196616 | tf_op jit(solution)/shard_map/ppermute | solution.py:38
  139.9 13.2 %collective-permute-start.48 = (f32[8,16,128]{2,1,0:T(8,128)S(1)}, f32[8,16,128]{2,1,0:T(8,128)S(1)}, u32[]{:S(2)}, u32[]{:S(2)}) collective-permute-start(f32[8,16,128]{2,1,0:T(8,128)S(1)} %get-tuple-element.156), channel_id=1, source_target_pairs={{0,16},{4,20},{8,24},{12,28},{16,0},{20,4},{24,8},{28,12},{1,17},{... | collective-permute-start | bytes 196616 | tf_op jit(solution)/shard_map/ppermute | solution.py:38
  155.0 8.8 %collective-permute-start.67 = (f32[8,16,128]{2,1,0:T(8,128)S(1)}, f32[8,16,128]{2,1,0:T(8,128)S(1)}, u32[]{:S(2)}, u32[]{:S(2)}) collective-permute-start(f32[8,16,128]{2,1,0:T(8,128)S(1)} %get-tuple-element.77), channel_id=1, source_target_pairs={{0,16},{4,20},{8,24},{12,28},{16,0},{20,4},{24,8},{28,12},{1,17},{... | collective-permute-start | bytes 196616 | tf_op jit(solution)/shard_map/ppermute | solution.py:38
  155.3 10.6 %collective-permute-start.63 = (f32[8,16,128]{2,1,0:T(8,128)S(1)}, f32[8,16,128]{2,1,0:T(8,128)S(1)}, u32[]{:S(2)}, u32[]{:S(2)}) collective-permute-start(f32[8,16,128]{2,1,0:T(8,128)S(1)} %get-tuple-element.76), channel_id=1, source_target_pairs={{0,16},{4,20},{8,24},{12,28},{16,0},{20,4},{24,8},{28,12},{1,17},{... | collective-permute-start | bytes 196616 | tf_op jit(solution)/shard_map/ppermute | solution.py:38
  157.9 9.0 %collective-permute-start.52 = (f32[10,16,128]{2,1,0:T(8,128)S(1)}, f32[10,16,128]{2,1,0:T(8,128)S(1)}, u32[]{:S(2)}, u32[]{:S(2)}) collective-permute-start(f32[10,16,128]{2,1,0:T(8,128)S(1)} %get-tuple-element.74), channel_id=1, source_target_pairs={{0,16},{4,20},{8,24},{12,28},{16,0},{20,4},{24,8},{28,12},{1,17},{... | collective-permute-start | bytes 245768 | tf_op jit(solution)/shard_map/ppermute | solution.py:38
  158.2 11.5 %collective-permute-start.59 = (f32[8,16,128]{2,1,0:T(8,128)S(1)}, f32[8,16,128]{2,1,0:T(8,128)S(1)}, u32[]{:S(2)}, u32[]{:S(2)}) collective-permute-start(f32[8,16,128]{2,1,0:T(8,128)S(1)} %get-tuple-element.75), channel_id=1, source_target_pairs={{0,16},{4,20},{8,24},{12,28},{16,0},{20,4},{24,8},{28,12},{1,17},{... | collective-permute-start | bytes 196616 | tf_op jit(solution)/shard_map/ppermute | solution.py:38
  166.9 12.0 %collective-permute-start.65 = (f32[16,16,128]{2,1,0:T(8,128)S(1)}, f32[16,16,128]{2,1,0:T(8,128)S(1)}, u32[]{:S(2)}, u32[]{:S(2)}) collective-permute-start(f32[16,16,128]{2,1,0:T(8,128)S(1)} %constant_dynamic-update-slice_fusion.2.refs_8_), channel_id=1, source_target_pairs={{0,4},{4,0},{8,12},{12,8},{16,20},{20,16},{24,28},{28,24},{1,5},{5... | collective-permute-start | bytes 393224 | tf_op jit(solution)/shard_map/ppermute | solution.py:38
  176.1 9.2 %collective-permute-start.55 = (f32[18,16,128]{2,1,0:T(8,128)S(1)}, f32[18,16,128]{2,1,0:T(8,128)S(1)}, u32[]{:S(2)}, u32[]{:S(2)}) collective-permute-start(f32[18,16,128]{2,1,0:T(8,128)S(1)} %collective-permute-done.53.refs_1_), channel_id=1, source_target_pairs={{0,4},{4,0},{8,12},{12,8},{16,20},{20,16},{24,28},{28,24},{1,5},{5... | collective-permute-start | bytes 442376 | tf_op jit(solution)/shard_map/ppermute | solution.py:38
  193.3 9.7 %collective-permute-start.78 = (f32[16,16,128]{2,1,0:T(8,128)S(1)}, f32[16,16,128]{2,1,0:T(8,128)S(1)}, u32[]{:S(2)}, u32[]{:S(2)}) collective-permute-start(f32[16,16,128]{2,1,0:T(8,128)S(1)} %get-tuple-element.118), channel_id=1, source_target_pairs={{0,2},{1,3},{2,0},{3,1},{4,6},{5,7},{6,4},{7,5},{8,10},{9,11},{10,... | collective-permute-start | bytes 393224 | tf_op jit(solution)/shard_map/ppermute | solution.py:38
  194.3 8.7 %collective-permute-start.77 = (f32[16,16,128]{2,1,0:T(8,128)S(1)}, f32[16,16,128]{2,1,0:T(8,128)S(1)}, u32[]{:S(2)}, u32[]{:S(2)}) collective-permute-start(f32[16,16,128]{2,1,0:T(8,128)S(1)} %get-tuple-element.120), channel_id=1, source_target_pairs={{0,2},{1,3},{2,0},{3,1},{4,6},{5,7},{6,4},{7,5},{8,10},{9,11},{10,... | collective-permute-start | bytes 393224 | tf_op jit(solution)/shard_map/ppermute | solution.py:38
  195.5 9.8 %collective-permute-start.76 = (f32[16,16,128]{2,1,0:T(8,128)S(1)}, f32[16,16,128]{2,1,0:T(8,128)S(1)}, u32[]{:S(2)}, u32[]{:S(2)}) collective-permute-start(f32[16,16,128]{2,1,0:T(8,128)S(1)} %get-tuple-element.122), channel_id=1, source_target_pairs={{0,2},{1,3},{2,0},{3,1},{4,6},{5,7},{6,4},{7,5},{8,10},{9,11},{10,... | collective-permute-start | bytes 393224 | tf_op jit(solution)/shard_map/ppermute | solution.py:38
  196.5 10.8 %collective-permute-start.75 = (f32[16,16,128]{2,1,0:T(8,128)S(1)}, f32[16,16,128]{2,1,0:T(8,128)S(1)}, u32[]{:S(2)}, u32[]{:S(2)}) collective-permute-start(f32[16,16,128]{2,1,0:T(8,128)S(1)} %get-tuple-element.124), channel_id=1, source_target_pairs={{0,2},{1,3},{2,0},{3,1},{4,6},{5,7},{6,4},{7,5},{8,10},{9,11},{10,... | collective-permute-start | bytes 393224 | tf_op jit(solution)/shard_map/ppermute | solution.py:38
  212.0 11.4 %collective-permute-start.79 = (f32[18,16,128]{2,1,0:T(8,128)S(1)}, f32[18,16,128]{2,1,0:T(8,128)S(1)}, u32[]{:S(2)}, u32[]{:S(2)}) collective-permute-start(f32[18,16,128]{2,1,0:T(8,128)S(1)} %get-tuple-element.86.refs_0_), channel_id=1, source_target_pairs={{0,2},{1,3},{2,0},{3,1},{4,6},{5,7},{6,4},{7,5},{8,10},{9,11},{10,... | collective-permute-start | bytes 442376 | tf_op jit(solution)/shard_map/ppermute | solution.py:38
  212.9 10.5 %collective-permute-start.92 = (f32[16,16,128]{2,1,0:T(8,128)S(1)}, f32[16,16,128]{2,1,0:T(8,128)S(1)}, u32[]{:S(2)}, u32[]{:S(2)}) collective-permute-start(f32[16,16,128]{2,1,0:T(8,128)S(1)} %get-tuple-element.90.refs_12_), channel_id=1, source_target_pairs={{0,2},{1,3},{2,0},{3,1},{4,6},{5,7},{6,4},{7,5},{8,10},{9,11},{10,... | collective-permute-start | bytes 393224 | tf_op jit(solution)/shard_map/ppermute | solution.py:38
  214.0 9.9 %collective-permute-start.87 = (f32[16,16,128]{2,1,0:T(8,128)S(1)}, f32[16,16,128]{2,1,0:T(8,128)S(1)}, u32[]{:S(2)}, u32[]{:S(2)}) collective-permute-start(f32[16,16,128]{2,1,0:T(8,128)S(1)} %get-tuple-element.88.refs_4_), channel_id=1, source_target_pairs={{0,1},{1,0},{2,3},{3,2},{4,5},{5,4},{6,7},{7,6},{8,9},{9,8},{10,11... | collective-permute-start | bytes 393224 | tf_op jit(solution)/shard_map/ppermute | solution.py:38
  231.0 40.3 %collective-permute-start.82 = (f32[32,128]{1,0:T(8,128)S(1)}, f32[32,128]{1,0:T(8,128)S(1)}, u32[]{:S(2)}, u32[]{:S(2)}) collective-permute-start(f32[32,128]{1,0:T(8,128)S(1)} %bitcast.46), channel_id=1, source_target_pairs={{0,8},{4,12},{8,0},{12,4},{16,24},{20,28},{24,16},{28,20},{1,9},{5... | collective-permute-start | bytes 49160 | tf_op jit(solution)/shard_map/ppermute | solution.py:38
  233.0 38.5 %collective-permute-start.83 = (f32[32,128]{1,0:T(8,128)S(1)}, f32[32,128]{1,0:T(8,128)S(1)}, u32[]{:S(2)}, u32[]{:S(2)}) collective-permute-start(f32[32,128]{1,0:T(8,128)S(1)} %bitcast.47), channel_id=1, source_target_pairs={{0,4},{4,0},{8,12},{12,8},{16,20},{20,16},{24,28},{28,24},{1,5},{5... | collective-permute-start | bytes 49160 | tf_op jit(solution)/shard_map/ppermute | solution.py:38
  233.5 40.8 %collective-permute-start.84 = (f32[32,128]{1,0:T(8,128)S(1)}, f32[32,128]{1,0:T(8,128)S(1)}, u32[]{:S(2)}, u32[]{:S(2)}) collective-permute-start(f32[32,128]{1,0:T(8,128)S(1)} %bitcast.48), channel_id=1, source_target_pairs={{0,12},{4,8},{8,4},{12,0},{16,28},{20,24},{24,20},{28,16},{1,13},{... | collective-permute-start | bytes 49160 | tf_op jit(solution)/shard_map/ppermute | solution.py:38
  249.6 17.0 %collective-permute-start.96 = (f32[16,16,128]{2,1,0:T(8,128)S(1)}, f32[16,16,128]{2,1,0:T(8,128)S(1)}, u32[]{:S(2)}, u32[]{:S(2)}) collective-permute-start(f32[16,16,128]{2,1,0:T(8,128)S(1)} %get-tuple-element.117), channel_id=1, source_target_pairs={{0,8},{4,12},{8,0},{12,4},{16,24},{20,28},{24,16},{28,20},{1,9},{5... | collective-permute-start | bytes 393224 | tf_op jit(solution)/shard_map/ppermute | solution.py:38
  255.1 30.7 %collective-permute-start.106 = (f32[8,16,128]{2,1,0:T(8,128)S(1)}, f32[8,16,128]{2,1,0:T(8,128)S(1)}, u32[]{:S(2)}, u32[]{:S(2)}) collective-permute-start(f32[8,16,128]{2,1,0:T(8,128)S(1)} %get-tuple-element.143), channel_id=1, source_target_pairs={{0,16},{4,20},{8,24},{12,28},{16,0},{20,4},{24,8},{28,12},{1,17},{... | collective-permute-start | bytes 196616 | tf_op jit(solution)/shard_map/ppermute | solution.py:38
  266.6 19.3 %collective-permute-start.103 = (f32[8,16,128]{2,1,0:T(8,128)S(1)}, f32[8,16,128]{2,1,0:T(8,128)S(1)}, u32[]{:S(2)}, u32[]{:S(2)}) collective-permute-start(f32[8,16,128]{2,1,0:T(8,128)S(1)} %get-tuple-element.145), channel_id=1, source_target_pairs={{0,16},{4,20},{8,24},{12,28},{16,0},{20,4},{24,8},{28,12},{1,17},{... | collective-permute-start | bytes 196616 | tf_op jit(solution)/shard_map/ppermute | solution.py:38
  271.3 14.5 %collective-permute-start.100 = (f32[8,16,128]{2,1,0:T(8,128)S(1)}, f32[8,16,128]{2,1,0:T(8,128)S(1)}, u32[]{:S(2)}, u32[]{:S(2)}) collective-permute-start(f32[8,16,128]{2,1,0:T(8,128)S(1)} %get-tuple-element.147), channel_id=1, source_target_pairs={{0,16},{4,20},{8,24},{12,28},{16,0},{20,4},{24,8},{28,12},{1,17},{... | collective-permute-start | bytes 196616 | tf_op jit(solution)/shard_map/ppermute | solution.py:38
  271.4 14.4 %collective-permute-start.97 = (f32[8,16,128]{2,1,0:T(8,128)S(1)}, f32[8,16,128]{2,1,0:T(8,128)S(1)}, u32[]{:S(2)}, u32[]{:S(2)}) collective-permute-start(f32[8,16,128]{2,1,0:T(8,128)S(1)} %get-tuple-element.149), channel_id=1, source_target_pairs={{0,16},{4,20},{8,24},{12,28},{16,0},{20,4},{24,8},{28,12},{1,17},{... | collective-permute-start | bytes 196616 | tf_op jit(solution)/shard_map/ppermute | solution.py:38
  (74 other events, 657.4 us)

commit v9 on v8

--- a/solution.py
+++ b/solution.py
@@ -234,25 +234,22 @@
     out_ref[...] = work[:, K:] * lax.rsqrt(pivots)
 
 
-def turn_kernel(tile_ref, *refs):
-    out_ref = refs[-1]
+def turn_kernel(tile_ref, out_ref):
     for at in range(tile_ref.shape[0]):
         out_ref[at] = tile_ref[at].T
 
 
-def turned_tiles(tiles, first, blocks, into):
-    size = tiles.shape[0] // 16
-    block = pl.BlockSpec((size, TILE, TILE), lambda step: (step + first, 0, 0))
+def turned_tiles(tiles):
+    block = pl.BlockSpec((tiles.shape[0] // 16, TILE, TILE), lambda step: (step, 0, 0))
     return pl.pallas_call(
         turn_kernel,
-        out_shape=jax.ShapeDtypeStruct(tiles.shape, tiles.dtype),
-        grid=(blocks,),
-        in_specs=[block] + ([] if into is None else [pl.BlockSpec(memory_space=pl.ANY)]),
+        out_shape=pltpu.HBM(tiles.shape, tiles.dtype),
+        grid=(16,),
+        in_specs=[block],
         out_specs=block,
         compiler_params=SMALL_KERNEL,
-        input_output_aliases={} if into is None else {1: 0},
         name="turned_tiles",
-    )(*([tiles] if into is None else [tiles, into]))
+    )(in_vmem(tiles))
 
 
 def inverse_factor(gram, total):
@@ -344,14 +341,14 @@
     start = item_scale[None, :, None, :] * start
     sent = [start[part] for part in range(PARTS)]
     sent[0] = jnp.concatenate([sent[0], jnp.zeros((GRAM, ROWS, TILE), jnp.float32)], axis=0)
-    turned = turned_tiles(tiles, 0, 8, None)
-    turned = turned_tiles(tiles, 8, 8, turned)
+    turned = turned_tiles(tiles)
     item_inverse = None
     for step in range(ITERS):
         pieces = gather(sent, "users")
         if step:
             item_inverse = inverse_factor(gram_sum(pieces, "items"), item_total)
-        kept, out = tiles_product(count, col_at, row_to, pieces, turned, UT, "users", "items")
+        source = turned if step else pltpu.with_memory_space_constraint(turned, pltpu.HBM)
+        kept, out = tiles_product(count, col_at, row_to, pieces, source, UT, "users", "items")
         kept, got = reduce_scatter(kept, out, "items")
         user_raw, sent = scale_panel(item_inverse, kept, got, user_scale)
         pieces = gather(sent, "items")

time: 311 us -> 311 us (level)
  local copies, waits for them, and re-layouts: 18.4 us -> 5.93 us
  Pallas kernels: 51.8 us -> 59.6 us
  waiting for transfers between devices: 114 us -> 118 us
    unnamed x24 -> x28, local copies, waits for them, and re-layouts: 18.3 us -> 5.88 us
    pallas_call x2 -> x1, Pallas kernels: 5.33 us -> 11 us  [turned_tiles(): pl.pallas_call(turn_kernel, out_shape=pltpu.HBM(tiles.shape, tiles.dtype)...]
    ppermute x112, waiting for transfers between devices: 114 us -> 118 us  [exchange(): lax.ppermute(value, axis, [(at, at ^ bit) for at in range(lax.axis_size(a...]
  transfers between devices with their start and end apart: 112 -> 112, of which waited for: 54 -> 47; matrix products, arithmetic and copies ran while one was open for 0% -> 0% of each run, Pallas kernels for 7% -> 9%
where the time goes in v9:
time: 311 us
  starting transfers between devices  123 us (40%)
  waiting for transfers between devices  118 us (38%)
  Pallas kernels  59.6 us (19%)
  local copies, waits for them, and re-layouts  5.93 us (2%)
    ppermute x112, starting transfers between devices, exchange(): lax.ppermute(value, axis, [(at, at ^ bit) for at in range(lax.axis_size(a...  123 us
    ppermute x112, waiting for transfers between devices, exchange(): lax.ppermute(value, axis, [(at, at ^ bit) for at in range(lax.axis_size(a...  118 us
    pallas_call x4, Pallas kernels, inverse_factor(): pl.pallas_call(functools.partial(factor_kernel, total=total), out_shape=p...  21.7 us
    pallas_call x4, Pallas kernels, tiles_product(): call(count, source, target, *[in_vmem(piece) for part in pieces for piece...  16.8 us
    pallas_call x1, Pallas kernels, turned_tiles(): pl.pallas_call(turn_kernel, out_shape=pltpu.HBM(tiles.shape, tiles.dtype)...  11 us
    pallas_call x4, Pallas kernels, scale_panel(): pl.pallas_call(functools.partial(scale_kernel, factored=factored), out_sh...  7.64 us
  transfers between devices with their start and end apart: 112, of which 47 were waited for; matrix products, arithmetic and copies ran while one was open for 0% of the time, Pallas kernels for 9%

profile of v9, /device:TPU:0, one launch (start us, length us, event | category | flops | bytes accessed | tf_op | source)
XLA Modules:
  0.0 311.1 jit_solution(14034372072018548148)
XLA Ops:
  2.4 4.1 %collective-permute-start.4 = (f32[8,16,128]{2,1,0:T(8,128)S(1)}, f32[8,16,128]{2,1,0:T(8,128)S(1)}, u32[]{:S(2)}, u32[]{:S(2)}) collective-permute-start(f32[8,16,128]{2,1,0:T(8,128)S(1)} %get-tuple-element.160), channel_id=1, source_target_pairs={{0,16},{4,20},{8,24},{12,28},{16,0},{20,4},{24,8},{28,12},{1,17},{... | collective-permute-start | bytes 196616 | tf_op jit(solution)/shard_map/ppermute | solution.py:38
  6.6 2.8 collective-permute-start.8
  10.2 5.2 %collective-permute-start.6 = (f32[16,16,128]{2,1,0:T(8,128)S(1)}, f32[16,16,128]{2,1,0:T(8,128)S(1)}, u32[]{:S(2)}, u32[]{:S(2)}) collective-permute-start(f32[16,16,128]{2,1,0:T(8,128)S(1)} %pad_maximum_fusion.2.refs_4_), channel_id=1, source_target_pairs={{0,8},{4,12},{8,0},{12,4},{16,24},{20,28},{24,16},{28,20},{1,9},{5... | collective-permute-start | bytes 393224 | tf_op jit(solution)/shard_map/ppermute | solution.py:38
  24.6 5.8 %copy-done = bf16[1,1,512,128,128]{4,3,2,1,0:T(8,128)(2,1)S(1)} copy-done((bf16[1,1,512,128,128]{4,3,2,1,0:T(8,128)(2,1)S(1)}, bf16[1,1,512,128,128]{4,3,2,1,0:T(8,128)(2,1)}, u32[]{:S(2)}) %copy-start) | copy-done | bytes 16777240
  30.4 11.0 %turned_tiles.1.refs_16_ = bf16[512,128,128]{2,1,0:T(8,128)(2,1)} custom-call(bf16[512,128,128]{2,1,0:T(8,128)(2,1)S(1)} %bitcast.36), custom_call_target="tpu_custom_call" | custom-call | tf_op jit(solution)/shard_map/turned_tiles/pallas_call | solution.py:244
  45.8 2.3 collective-permute-done.2.refs_2_
  48.1 2.8 collective-permute-done.11.refs_11_
  52.8 5.5 %shard_map.86 = (f32[32,16,128]{2,1,0:T(8,128)S(1)}, f32[32,16,128]{2,1,0:T(8,128)S(1)}, f32[32,16,128]{2,1,0:T(8,128)S(1)}, f32[32,16,128]{2,1,0:T(8,128)S(1)},...) custom-call(s32[1]{0:T(128)} %bitcast.31.count, ...), custom_call_target="tpu_custom_call" | custom-call | tf_op jit(solution)/shard_map/pallas_call | solution.py:202
  59.9 8.7 %collective-permute-start.20 = (f32[16,16,128]{2,1,0:T(8,128)S(1)}, f32[16,16,128]{2,1,0:T(8,128)S(1)}, u32[]{:S(2)}, u32[]{:S(2)}) collective-permute-start(f32[16,16,128]{2,1,0:T(8,128)S(1)} %get-tuple-element.140), channel_id=1, source_target_pairs={{0,2},{1,3},{2,0},{3,1},{4,6},{5,7},{6,4},{7,5},{8,10},{9,11},{10,... | collective-permute-start | bytes 393224 | tf_op jit(solution)/shard_map/ppermute | solution.py:38
  73.0 2.8 collective-permute-done.21.refs_5_
  75.8 2.8 collective-permute-done.22.refs_6_
  78.6 2.3 collective-permute-done.23.refs_7_
  86.3 2.4 collective-permute-done.31.refs_5_
  91.8 2.8 collective-permute-done.34.refs_9_
  98.4 3.8 %shard_map.87 = (f32[32,16,128]{2,1,0:T(8,128)S(1)}, f32[32,16,128]{2,1,0:T(8,128)S(1)}, f32[32,16,128]{2,1,0:T(8,128)S(1)}, f32[32,16,128]{2,1,0:T(8,128)S(1)},...) custom-call(s32[1]{0:T(128)} %bitcast.32.count, ...), custom_call_target="tpu_custom_call" | custom-call | tf_op jit(solution)/shard_map/pallas_call | solution.py:202
  106.3 4.2 %collective-permute-done.40 = f32[32,16,128]{2,1,0:T(8,128)S(1)} collective-permute-done((f32[32,16,128]{2,1,0:T(8,128)S(1)}, f32[32,16,128]{2,1,0:T(8,128)S(1)}, u32[]{:S(2)}, u32[]{:S(2)}) %collective-permute-start.40) | collective-permute-done | bytes 262176 | tf_op jit(solution)/shard_map/ppermute | solution.py:38
  110.7 8.9 %collective-permute-done.44 = f32[32,16,128]{2,1,0:T(8,128)S(1)} collective-permute-done((f32[32,16,128]{2,1,0:T(8,128)S(1)}, f32[32,16,128]{2,1,0:T(8,128)S(1)}, u32[]{:S(2)}, u32[]{:S(2)}) %collective-permute-start.44) | collective-permute-done | bytes 262176 | tf_op jit(solution)/shard_map/ppermute | solution.py:38
  121.0 4.1 %collective-permute-done.41 = f32[16,16,128]{2,1,0:T(8,128)S(1)} collective-permute-done((f32[16,16,128]{2,1,0:T(8,128)S(1)}, f32[16,16,128]{2,1,0:T(8,128)S(1)}, u32[]{:S(2)}, u32[]{:S(2)}) %collective-permute-start.41) | collective-permute-done | bytes 131104 | tf_op jit(solution)/shard_map/ppermute | solution.py:38
  127.1 3.0 collective-permute-done.45
  130.1 6.9 %collective-permute-start.48 = (f32[8,16,128]{2,1,0:T(8,128)S(1)}, f32[8,16,128]{2,1,0:T(8,128)S(1)}, u32[]{:S(2)}, u32[]{:S(2)}) collective-permute-start(f32[8,16,128]{2,1,0:T(8,128)S(1)} %get-tuple-element.156), channel_id=1, source_target_pairs={{0,16},{4,20},{8,24},{12,28},{16,0},{20,4},{24,8},{28,12},{1,17},{... | collective-permute-start | bytes 196616 | tf_op jit(solution)/shard_map/ppermute | solution.py:38
  137.2 2.9 collective-permute-start.50
  140.2 2.9 collective-permute-start.30
  143.1 3.3 %collective-permute-done.30 = f32[32,128]{1,0:T(8,128)S(1)} collective-permute-done((f32[32,128]{1,0:T(8,128)S(1)}, f32[32,128]{1,0:T(8,128)S(1)}, u32[]{:S(2)}, u32[]{:S(2)}) %collective-permute-start.30) | collective-permute-done | bytes 16416 | tf_op jit(solution)/shard_map/ppermute | solution.py:38
  146.4 5.4 %factor.4.refs_0_ = f32[64,64]{1,0:T(8,128)S(1)} custom-call(f32[32,128]{1,0:T(8,128)S(1)} %add.288.gram_ref), custom_call_target="tpu_custom_call" | custom-call | tf_op jit(solution)/shard_map/factor/pallas_call | solution.py:256
  159.6 5.9 %collective-permute-done.67 = f32[8,16,128]{2,1,0:T(8,128)S(1)} collective-permute-done((f32[8,16,128]{2,1,0:T(8,128)S(1)}, f32[8,16,128]{2,1,0:T(8,128)S(1)}, u32[]{:S(2)}, u32[]{:S(2)}) %collective-permute-start.67) | collective-permute-done | bytes 65568 | tf_op jit(solution)/shard_map/ppermute | solution.py:38
  180.1 2.5 collective-permute-start.66
  187.6 3.8 %shard_map.88 = (f32[32,16,128]{2,1,0:T(8,128)S(1)}, f32[32,16,128]{2,1,0:T(8,128)S(1)}, f32[32,16,128]{2,1,0:T(8,128)S(1)}, f32[32,16,128]{2,1,0:T(8,128)S(1)},...) custom-call(s32[1]{0:T(128)} %bitcast.33.count, ...), custom_call_target="tpu_custom_call" | custom-call | tf_op jit(solution)/shard_map/pallas_call | solution.py:202
  192.1 5.0 %collective-permute-start.58 = (f32[32,128]{1,0:T(8,128)S(1)}, f32[32,128]{1,0:T(8,128)S(1)}, u32[]{:S(2)}, u32[]{:S(2)}) collective-permute-start(f32[32,128]{1,0:T(8,128)S(1)} %bitcast.51), channel_id=1, source_target_pairs={{0,3},{1,2},{2,1},{3,0},{4,7},{5,6},{6,5},{7,4},{8,11},{9,10},{10,... | collective-permute-start | bytes 49160 | tf_op jit(solution)/shard_map/ppermute | solution.py:38
  203.2 5.4 %factor.5.refs_0_ = f32[64,64]{1,0:T(8,128)S(1)} custom-call(f32[32,128]{1,0:T(8,128)S(1)} %add_add_fusion.1.gram_ref), custom_call_target="tpu_custom_call" | custom-call | tf_op jit(solution)/shard_map/factor/pallas_call | solution.py:256
  210.6 2.2 collective-permute-done.78.refs_8_
  212.9 2.6 scale_panel.6
  219.6 2.4 collective-permute-done.86.refs_5_
  225.1 2.8 collective-permute-done.89.refs_9_
  231.5 3.7 %shard_map.89 = (f32[32,16,128]{2,1,0:T(8,128)S(1)}, f32[32,16,128]{2,1,0:T(8,128)S(1)}, f32[32,16,128]{2,1,0:T(8,128)S(1)}, f32[32,16,128]{2,1,0:T(8,128)S(1)},...) custom-call(s32[1]{0:T(128)} %bitcast.34.count, ...), custom_call_target="tpu_custom_call" | custom-call | tf_op jit(solution)/shard_map/pallas_call | solution.py:202
  239.4 4.7 %collective-permute-done.95 = f32[32,16,128]{2,1,0:T(8,128)S(1)} collective-permute-done((f32[32,16,128]{2,1,0:T(8,128)S(1)}, f32[32,16,128]{2,1,0:T(8,128)S(1)}, u32[]{:S(2)}, u32[]{:S(2)}) %collective-permute-start.95) | collective-permute-done | bytes 262176 | tf_op jit(solution)/shard_map/ppermute | solution.py:38
  244.3 8.5 %collective-permute-done.101 = f32[32,16,128]{2,1,0:T(8,128)S(1)} collective-permute-done((f32[32,16,128]{2,1,0:T(8,128)S(1)}, f32[32,16,128]{2,1,0:T(8,128)S(1)}, u32[]{:S(2)}, u32[]{:S(2)}) %collective-permute-start.101) | collective-permute-done | bytes 262176 | tf_op jit(solution)/shard_map/ppermute | solution.py:38
  254.8 3.0 collective-permute-done.96
  259.8 3.1 collective-permute-done.102
  262.8 6.3 %collective-permute-start.97 = (f32[8,16,128]{2,1,0:T(8,128)S(1)}, f32[8,16,128]{2,1,0:T(8,128)S(1)}, u32[]{:S(2)}, u32[]{:S(2)}) collective-permute-start(f32[8,16,128]{2,1,0:T(8,128)S(1)} %get-tuple-element.149), channel_id=1, source_target_pairs={{0,16},{4,20},{8,24},{12,28},{16,0},{20,4},{24,8},{28,12},{1,17},{... | collective-permute-start | bytes 196616 | tf_op jit(solution)/shard_map/ppermute | solution.py:38
  269.3 2.9 collective-permute-start.103
  272.3 2.9 collective-permute-start.85
  275.2 3.3 %collective-permute-done.85 = f32[32,128]{1,0:T(8,128)S(1)} collective-permute-done((f32[32,128]{1,0:T(8,128)S(1)}, f32[32,128]{1,0:T(8,128)S(1)}, u32[]{:S(2)}, u32[]{:S(2)}) %collective-permute-start.85) | collective-permute-done | bytes 16416 | tf_op jit(solution)/shard_map/ppermute | solution.py:38
  278.5 5.4 %factor.6.inverse_ref.refs_0_ = f32[64,64]{1,0:T(8,128)S(1)} custom-call(f32[32,128]{1,0:T(8,128)S(1)} %add.328.gram_ref), custom_call_target="tpu_custom_call" | custom-call | tf_op jit(solution)/shard_map/factor/pallas_call | solution.py:256
  288.2 2.4 collective-permute-start.108
  292.7 3.4 %collective-permute-done.109 = f32[32,128]{1,0:T(8,128)S(1)} collective-permute-done((f32[32,128]{1,0:T(8,128)S(1)}, f32[32,128]{1,0:T(8,128)S(1)}, u32[]{:S(2)}, u32[]{:S(2)}) %collective-permute-start.109) | collective-permute-done | bytes 16416 | tf_op jit(solution)/shard_map/ppermute | solution.py:38
  296.2 3.7 %collective-permute-done.110 = f32[32,128]{1,0:T(8,128)S(1)} collective-permute-done((f32[32,128]{1,0:T(8,128)S(1)}, f32[32,128]{1,0:T(8,128)S(1)}, u32[]{:S(2)}, u32[]{:S(2)}) %collective-permute-start.110) | collective-permute-done | bytes 16416 | tf_op jit(solution)/shard_map/ppermute | solution.py:38
  301.0 3.5 %collective-permute-done.111 = f32[32,128]{1,0:T(8,128)S(1)} collective-permute-done((f32[32,128]{1,0:T(8,128)S(1)}, f32[32,128]{1,0:T(8,128)S(1)}, u32[]{:S(2)}, u32[]{:S(2)}) %collective-permute-start.111) | collective-permute-done | bytes 16416 | tf_op jit(solution)/shard_map/ppermute | solution.py:38
  304.5 5.4 %factor.7.inverse_ref = f32[64,64]{1,0:T(8,128)S(1)} custom-call(f32[32,128]{1,0:T(8,128)S(1)} %add.349.gram_ref), custom_call_target="tpu_custom_call" | custom-call | tf_op jit(solution)/shard_map/factor/pallas_call | solution.py:256
  (277 shorter events, 107.3 us)
Async XLA Ops:
  6.5 13.4 %collective-permute-start.12 = (f32[8,16,128]{2,1,0:T(8,128)S(1)}, f32[8,16,128]{2,1,0:T(8,128)S(1)}, u32[]{:S(2)}, u32[]{:S(2)}) collective-permute-start(f32[8,16,128]{2,1,0:T(8,128)S(1)} %get-tuple-element.158), channel_id=1, source_target_pairs={{0,16},{4,20},{8,24},{12,28},{16,0},{20,4},{24,8},{28,12},{1,17},{... | collective-permute-start | bytes 196616 | tf_op jit(solution)/shard_map/ppermute | solution.py:38
  6.6 11.5 %collective-permute-start.8 = (f32[8,16,128]{2,1,0:T(8,128)S(1)}, f32[8,16,128]{2,1,0:T(8,128)S(1)}, u32[]{:S(2)}, u32[]{:S(2)}) collective-permute-start(f32[8,16,128]{2,1,0:T(8,128)S(1)} %get-tuple-element.159), channel_id=1, source_target_pairs={{0,16},{4,20},{8,24},{12,28},{16,0},{20,4},{24,8},{28,12},{1,17},{... | collective-permute-start | bytes 196616 | tf_op jit(solution)/shard_map/ppermute | solution.py:38
  9.5 10.3 %collective-permute-start = (f32[10,16,128]{2,1,0:T(8,128)S(1)}, f32[10,16,128]{2,1,0:T(8,128)S(1)}, u32[]{:S(2)}, u32[]{:S(2)}) collective-permute-start(f32[10,16,128]{2,1,0:T(8,128)S(1)} %concatenate.27), channel_id=1, source_target_pairs={{0,16},{4,20},{8,24},{12,28},{16,0},{20,4},{24,8},{28,12},{1,17},{... | collective-permute-start | bytes 245768 | tf_op jit(solution)/shard_map/ppermute | solution.py:38
  10.2 11.9 %collective-permute-start.6 = (f32[16,16,128]{2,1,0:T(8,128)S(1)}, f32[16,16,128]{2,1,0:T(8,128)S(1)}, u32[]{:S(2)}, u32[]{:S(2)}) collective-permute-start(f32[16,16,128]{2,1,0:T(8,128)S(1)} %pad_maximum_fusion.2.refs_4_), channel_id=1, source_target_pairs={{0,8},{4,12},{8,0},{12,4},{16,24},{20,28},{24,16},{28,20},{1,9},{5... | collective-permute-start | bytes 393224 | tf_op jit(solution)/shard_map/ppermute | solution.py:38
  18.2 23.2 %collective-permute-start.10 = (f32[16,16,128]{2,1,0:T(8,128)S(1)}, f32[16,16,128]{2,1,0:T(8,128)S(1)}, u32[]{:S(2)}, u32[]{:S(2)}) collective-permute-start(f32[16,16,128]{2,1,0:T(8,128)S(1)} %pad_maximum_fusion.3.refs_8_), channel_id=1, source_target_pairs={{0,4},{4,0},{8,12},{12,8},{16,20},{20,16},{24,28},{28,24},{1,5},{5... | collective-permute-start | bytes 393224 | tf_op jit(solution)/shard_map/ppermute | solution.py:38
  19.8 21.9 %collective-permute-start.9 = (f32[16,16,128]{2,1,0:T(8,128)S(1)}, f32[16,16,128]{2,1,0:T(8,128)S(1)}, u32[]{:S(2)}, u32[]{:S(2)}) collective-permute-start(f32[16,16,128]{2,1,0:T(8,128)S(1)} %pad_maximum_fusion.3.refs_8_), channel_id=1, source_target_pairs={{0,8},{4,12},{8,0},{12,4},{16,24},{20,28},{24,16},{28,20},{1,9},{5... | collective-permute-start | bytes 393224 | tf_op jit(solution)/shard_map/ppermute | solution.py:38
  19.9 25.5 %collective-permute-start.1 = (f32[18,16,128]{2,1,0:T(8,128)S(1)}, f32[18,16,128]{2,1,0:T(8,128)S(1)}, u32[]{:S(2)}, u32[]{:S(2)}) collective-permute-start(f32[18,16,128]{2,1,0:T(8,128)S(1)} %pad_maximum_fusion.refs_0_), channel_id=1, source_target_pairs={{0,8},{4,12},{8,0},{12,4},{16,24},{20,28},{24,16},{28,20},{1,9},{5... | collective-permute-start | bytes 442376 | tf_op jit(solution)/shard_map/ppermute | solution.py:38
  22.2 21.5 %collective-permute-start.14 = (f32[16,16,128]{2,1,0:T(8,128)S(1)}, f32[16,16,128]{2,1,0:T(8,128)S(1)}, u32[]{:S(2)}, u32[]{:S(2)}) collective-permute-start(f32[16,16,128]{2,1,0:T(8,128)S(1)} %pad_maximum_fusion.4.refs_12_), channel_id=1, source_target_pairs={{0,8},{4,12},{8,0},{12,4},{16,24},{20,28},{24,16},{28,20},{1,9},{5... | collective-permute-start | bytes 393224 | tf_op jit(solution)/shard_map/ppermute | solution.py:38
  22.2 23.2 %collective-permute-start.13 = (f32[16,16,128]{2,1,0:T(8,128)S(1)}, f32[16,16,128]{2,1,0:T(8,128)S(1)}, u32[]{:S(2)}, u32[]{:S(2)}) collective-permute-start(f32[16,16,128]{2,1,0:T(8,128)S(1)} %pad_maximum_fusion.4.refs_12_), channel_id=1, source_target_pairs={{0,4},{4,0},{8,12},{12,8},{16,20},{20,16},{24,28},{28,24},{1,5},{5... | collective-permute-start | bytes 393224 | tf_op jit(solution)/shard_map/ppermute | solution.py:38
  58.4 10.2 %collective-permute-start.17 = (f32[32,16,128]{2,1,0:T(8,128)S(1)}, f32[32,16,128]{2,1,0:T(8,128)S(1)}, u32[]{:S(2)}, u32[]{:S(2)}) collective-permute-start(f32[32,16,128]{2,1,0:T(8,128)S(1)} %get-tuple-element.57), channel_id=1, source_target_pairs={{0,1},{1,0},{2,3},{3,2},{4,5},{5,4},{6,7},{7,6},{8,9},{9,8},{10,11... | collective-permute-start | bytes 786440 | tf_op jit(solution)/shard_map/ppermute | solution.py:38
  58.9 10.1 %collective-permute-start.18 = (f32[32,16,128]{2,1,0:T(8,128)S(1)}, f32[32,16,128]{2,1,0:T(8,128)S(1)}, u32[]{:S(2)}, u32[]{:S(2)}) collective-permute-start(f32[32,16,128]{2,1,0:T(8,128)S(1)} %get-tuple-element.59), channel_id=1, source_target_pairs={{0,1},{1,0},{2,3},{3,2},{4,5},{5,4},{6,7},{7,6},{8,9},{9,8},{10,11... | collective-permute-start | bytes 786440 | tf_op jit(solution)/shard_map/ppermute | solution.py:38
  59.0 11.9 %collective-permute-start.19 = (f32[32,16,128]{2,1,0:T(8,128)S(1)}, f32[32,16,128]{2,1,0:T(8,128)S(1)}, u32[]{:S(2)}, u32[]{:S(2)}) collective-permute-start(f32[32,16,128]{2,1,0:T(8,128)S(1)} %get-tuple-element.61), channel_id=1, source_target_pairs={{0,1},{1,0},{2,3},{3,2},{4,5},{5,4},{6,7},{7,6},{8,9},{9,8},{10,11... | collective-permute-start | bytes 786440 | tf_op jit(solution)/shard_map/ppermute | solution.py:38
  59.9 13.0 %collective-permute-start.20 = (f32[16,16,128]{2,1,0:T(8,128)S(1)}, f32[16,16,128]{2,1,0:T(8,128)S(1)}, u32[]{:S(2)}, u32[]{:S(2)}) collective-permute-start(f32[16,16,128]{2,1,0:T(8,128)S(1)} %get-tuple-element.140), channel_id=1, source_target_pairs={{0,2},{1,3},{2,0},{3,1},{4,6},{5,7},{6,4},{7,5},{8,10},{9,11},{10,... | collective-permute-start | bytes 393224 | tf_op jit(solution)/shard_map/ppermute | solution.py:38
  69.0 9.5 %collective-permute-start.22 = (f32[16,16,128]{2,1,0:T(8,128)S(1)}, f32[16,16,128]{2,1,0:T(8,128)S(1)}, u32[]{:S(2)}, u32[]{:S(2)}) collective-permute-start(f32[16,16,128]{2,1,0:T(8,128)S(1)} %get-tuple-element.136), channel_id=1, source_target_pairs={{0,2},{1,3},{2,0},{3,1},{4,6},{5,7},{6,4},{7,5},{8,10},{9,11},{10,... | collective-permute-start | bytes 393224 | tf_op jit(solution)/shard_map/ppermute | solution.py:38
  70.9 9.9 %collective-permute-start.23 = (f32[16,16,128]{2,1,0:T(8,128)S(1)}, f32[16,16,128]{2,1,0:T(8,128)S(1)}, u32[]{:S(2)}, u32[]{:S(2)}) collective-permute-start(f32[16,16,128]{2,1,0:T(8,128)S(1)} %get-tuple-element.134), channel_id=1, source_target_pairs={{0,2},{1,3},{2,0},{3,1},{4,6},{5,7},{6,4},{7,5},{8,10},{9,11},{10,... | collective-permute-start | bytes 393224 | tf_op jit(solution)/shard_map/ppermute | solution.py:38
  84.3 10.3 %collective-permute-start.34 = (f32[16,16,128]{2,1,0:T(8,128)S(1)}, f32[16,16,128]{2,1,0:T(8,128)S(1)}, u32[]{:S(2)}, u32[]{:S(2)}) collective-permute-start(f32[16,16,128]{2,1,0:T(8,128)S(1)} %get-tuple-element.64.refs_8_), channel_id=1, source_target_pairs={{0,2},{1,3},{2,0},{3,1},{4,6},{5,7},{6,4},{7,5},{8,10},{9,11},{10,... | collective-permute-start | bytes 393224 | tf_op jit(solution)/shard_map/ppermute | solution.py:38
  102.4 34.9 %collective-permute-start.28 = (f32[32,128]{1,0:T(8,128)S(1)}, f32[32,128]{1,0:T(8,128)S(1)}, u32[]{:S(2)}, u32[]{:S(2)}) collective-permute-start(f32[32,128]{1,0:T(8,128)S(1)} %bitcast.44), channel_id=1, source_target_pairs={{0,4},{4,0},{8,12},{12,8},{16,20},{20,16},{24,28},{28,24},{1,5},{5... | collective-permute-start | bytes 49160 | tf_op jit(solution)/shard_map/ppermute | solution.py:38
  104.4 35.8 %collective-permute-start.29 = (f32[32,128]{1,0:T(8,128)S(1)}, f32[32,128]{1,0:T(8,128)S(1)}, u32[]{:S(2)}, u32[]{:S(2)}) collective-permute-start(f32[32,128]{1,0:T(8,128)S(1)} %bitcast.45), channel_id=1, source_target_pairs={{0,12},{4,8},{8,4},{12,0},{16,28},{20,24},{24,20},{28,16},{1,13},{... | collective-permute-start | bytes 49160 | tf_op jit(solution)/shard_map/ppermute | solution.py:38
  105.8 34.4 %collective-permute-start.27 = (f32[32,128]{1,0:T(8,128)S(1)}, f32[32,128]{1,0:T(8,128)S(1)}, u32[]{:S(2)}, u32[]{:S(2)}) collective-permute-start(f32[32,128]{1,0:T(8,128)S(1)} %bitcast.46), channel_id=1, source_target_pairs={{0,8},{4,12},{8,0},{12,4},{16,24},{20,28},{24,16},{28,20},{1,9},{5... | collective-permute-start | bytes 49160 | tf_op jit(solution)/shard_map/ppermute | solution.py:38
  110.6 9.1 %collective-permute-start.44 = (f32[32,16,128]{2,1,0:T(8,128)S(1)}, f32[32,16,128]{2,1,0:T(8,128)S(1)}, u32[]{:S(2)}, u32[]{:S(2)}) collective-permute-start(f32[32,16,128]{2,1,0:T(8,128)S(1)} %get-tuple-element.71), channel_id=1, source_target_pairs={{0,4},{4,0},{8,12},{12,8},{16,20},{20,16},{24,28},{28,24},{1,5},{5... | collective-permute-start | bytes 786440 | tf_op jit(solution)/shard_map/ppermute | solution.py:38
  110.6 9.1 %collective-permute-start.46 = (f32[32,16,128]{2,1,0:T(8,128)S(1)}, f32[32,16,128]{2,1,0:T(8,128)S(1)}, u32[]{:S(2)}, u32[]{:S(2)}) collective-permute-start(f32[32,16,128]{2,1,0:T(8,128)S(1)} %get-tuple-element.73), channel_id=1, source_target_pairs={{0,8},{4,12},{8,0},{12,4},{16,24},{20,28},{24,16},{28,20},{1,9},{5... | collective-permute-start | bytes 786440 | tf_op jit(solution)/shard_map/ppermute | solution.py:38
  125.5 11.5 %collective-permute-start.47 = (f32[16,16,128]{2,1,0:T(8,128)S(1)}, f32[16,16,128]{2,1,0:T(8,128)S(1)}, u32[]{:S(2)}, u32[]{:S(2)}) collective-permute-start(f32[16,16,128]{2,1,0:T(8,128)S(1)} %get-tuple-element.127), channel_id=1, source_target_pairs={{0,4},{4,0},{8,12},{12,8},{16,20},{20,16},{24,28},{28,24},{1,5},{5... | collective-permute-start | bytes 393224 | tf_op jit(solution)/shard_map/ppermute | solution.py:38
  130.1 21.7 %collective-permute-start.48 = (f32[8,16,128]{2,1,0:T(8,128)S(1)}, f32[8,16,128]{2,1,0:T(8,128)S(1)}, u32[]{:S(2)}, u32[]{:S(2)}) collective-permute-start(f32[8,16,128]{2,1,0:T(8,128)S(1)} %get-tuple-element.156), channel_id=1, source_target_pairs={{0,16},{4,20},{8,24},{12,28},{16,0},{20,4},{24,8},{28,12},{1,17},{... | collective-permute-start | bytes 196616 | tf_op jit(solution)/shard_map/ppermute | solution.py:38
  137.0 14.8 %collective-permute-start.49 = (f32[8,16,128]{2,1,0:T(8,128)S(1)}, f32[8,16,128]{2,1,0:T(8,128)S(1)}, u32[]{:S(2)}, u32[]{:S(2)}) collective-permute-start(f32[8,16,128]{2,1,0:T(8,128)S(1)} %get-tuple-element.154), channel_id=1, source_target_pairs={{0,16},{4,20},{8,24},{12,28},{16,0},{20,4},{24,8},{28,12},{1,17},{... | collective-permute-start | bytes 196616 | tf_op jit(solution)/shard_map/ppermute | solution.py:38
  137.2 14.7 %collective-permute-start.50 = (f32[8,16,128]{2,1,0:T(8,128)S(1)}, f32[8,16,128]{2,1,0:T(8,128)S(1)}, u32[]{:S(2)}, u32[]{:S(2)}) collective-permute-start(f32[8,16,128]{2,1,0:T(8,128)S(1)} %get-tuple-element.152), channel_id=1, source_target_pairs={{0,16},{4,20},{8,24},{12,28},{16,0},{20,4},{24,8},{28,12},{1,17},{... | collective-permute-start | bytes 196616 | tf_op jit(solution)/shard_map/ppermute | solution.py:38
  140.1 11.8 %collective-permute-start.51 = (f32[8,16,128]{2,1,0:T(8,128)S(1)}, f32[8,16,128]{2,1,0:T(8,128)S(1)}, u32[]{:S(2)}, u32[]{:S(2)}) collective-permute-start(f32[8,16,128]{2,1,0:T(8,128)S(1)} %get-tuple-element.150), channel_id=1, source_target_pairs={{0,16},{4,20},{8,24},{12,28},{16,0},{20,4},{24,8},{28,12},{1,17},{... | collective-permute-start | bytes 196616 | tf_op jit(solution)/shard_map/ppermute | solution.py:38
  153.7 14.0 %collective-permute-start.52 = (f32[10,16,128]{2,1,0:T(8,128)S(1)}, f32[10,16,128]{2,1,0:T(8,128)S(1)}, u32[]{:S(2)}, u32[]{:S(2)}) collective-permute-start(f32[10,16,128]{2,1,0:T(8,128)S(1)} %get-tuple-element.74), channel_id=1, source_target_pairs={{0,16},{4,20},{8,24},{12,28},{16,0},{20,4},{24,8},{28,12},{1,17},{... | collective-permute-start | bytes 245768 | tf_op jit(solution)/shard_map/ppermute | solution.py:38
  155.0 14.6 %collective-permute-start.59 = (f32[8,16,128]{2,1,0:T(8,128)S(1)}, f32[8,16,128]{2,1,0:T(8,128)S(1)}, u32[]{:S(2)}, u32[]{:S(2)}) collective-permute-start(f32[8,16,128]{2,1,0:T(8,128)S(1)} %get-tuple-element.75), channel_id=1, source_target_pairs={{0,16},{4,20},{8,24},{12,28},{16,0},{20,4},{24,8},{28,12},{1,17},{... | collective-permute-start | bytes 196616 | tf_op jit(solution)/shard_map/ppermute | solution.py:38
  156.6 10.9 %collective-permute-start.63 = (f32[8,16,128]{2,1,0:T(8,128)S(1)}, f32[8,16,128]{2,1,0:T(8,128)S(1)}, u32[]{:S(2)}, u32[]{:S(2)}) collective-permute-start(f32[8,16,128]{2,1,0:T(8,128)S(1)} %get-tuple-element.76), channel_id=1, source_target_pairs={{0,16},{4,20},{8,24},{12,28},{16,0},{20,4},{24,8},{28,12},{1,17},{... | collective-permute-start | bytes 196616 | tf_op jit(solution)/shard_map/ppermute | solution.py:38
  167.7 12.1 %collective-permute-start.64 = (f32[16,16,128]{2,1,0:T(8,128)S(1)}, f32[16,16,128]{2,1,0:T(8,128)S(1)}, u32[]{:S(2)}, u32[]{:S(2)}) collective-permute-start(f32[16,16,128]{2,1,0:T(8,128)S(1)} %constant_dynamic-update-slice_fusion.2.refs_8_), channel_id=1, source_target_pairs={{0,8},{4,12},{8,0},{12,4},{16,24},{20,28},{24,16},{28,20},{1,9},{5... | collective-permute-start | bytes 393224 | tf_op jit(solution)/shard_map/ppermute | solution.py:38
  171.9 10.7 %collective-permute-start.60 = (f32[16,16,128]{2,1,0:T(8,128)S(1)}, f32[16,16,128]{2,1,0:T(8,128)S(1)}, u32[]{:S(2)}, u32[]{:S(2)}) collective-permute-start(f32[16,16,128]{2,1,0:T(8,128)S(1)} %constant_dynamic-update-slice_fusion.refs_4_), channel_id=1, source_target_pairs={{0,4},{4,0},{8,12},{12,8},{16,20},{20,16},{24,28},{28,24},{1,5},{5... | collective-permute-start | bytes 393224 | tf_op jit(solution)/shard_map/ppermute | solution.py:38
  177.6 10.0 %collective-permute-start.55 = (f32[18,16,128]{2,1,0:T(8,128)S(1)}, f32[18,16,128]{2,1,0:T(8,128)S(1)}, u32[]{:S(2)}, u32[]{:S(2)}) collective-permute-start(f32[18,16,128]{2,1,0:T(8,128)S(1)} %collective-permute-done.53.refs_1_), channel_id=1, source_target_pairs={{0,4},{4,0},{8,12},{12,8},{16,20},{20,16},{24,28},{28,24},{1,5},{5... | collective-permute-start | bytes 442376 | tf_op jit(solution)/shard_map/ppermute | solution.py:38
  192.0 9.1 %collective-permute-start.57 = (f32[32,128]{1,0:T(8,128)S(1)}, f32[32,128]{1,0:T(8,128)S(1)}, u32[]{:S(2)}, u32[]{:S(2)}) collective-permute-start(f32[32,128]{1,0:T(8,128)S(1)} %bitcast.50), channel_id=1, source_target_pairs={{0,1},{1,0},{2,3},{3,2},{4,5},{5,4},{6,7},{7,6},{8,9},{9,8},{10,11... | collective-permute-start | bytes 49160 | tf_op jit(solution)/shard_map/ppermute | solution.py:38
  192.1 10.8 %collective-permute-start.58 = (f32[32,128]{1,0:T(8,128)S(1)}, f32[32,128]{1,0:T(8,128)S(1)}, u32[]{:S(2)}, u32[]{:S(2)}) collective-permute-start(f32[32,128]{1,0:T(8,128)S(1)} %bitcast.51), channel_id=1, source_target_pairs={{0,3},{1,2},{2,1},{3,0},{4,7},{5,6},{6,5},{7,4},{8,11},{9,10},{10,... | collective-permute-start | bytes 49160 | tf_op jit(solution)/shard_map/ppermute | solution.py:38
  198.7 10.0 %collective-permute-start.75 = (f32[16,16,128]{2,1,0:T(8,128)S(1)}, f32[16,16,128]{2,1,0:T(8,128)S(1)}, u32[]{:S(2)}, u32[]{:S(2)}) collective-permute-start(f32[16,16,128]{2,1,0:T(8,128)S(1)} %get-tuple-element.124), channel_id=1, source_target_pairs={{0,2},{1,3},{2,0},{3,1},{4,6},{5,7},{6,4},{7,5},{8,10},{9,11},{10,... | collective-permute-start | bytes 393224 | tf_op jit(solution)/shard_map/ppermute | solution.py:38
  201.1 9.6 %collective-permute-start.77 = (f32[16,16,128]{2,1,0:T(8,128)S(1)}, f32[16,16,128]{2,1,0:T(8,128)S(1)}, u32[]{:S(2)}, u32[]{:S(2)}) collective-permute-start(f32[16,16,128]{2,1,0:T(8,128)S(1)} %get-tuple-element.120), channel_id=1, source_target_pairs={{0,2},{1,3},{2,0},{3,1},{4,6},{5,7},{6,4},{7,5},{8,10},{9,11},{10,... | collective-permute-start | bytes 393224 | tf_op jit(solution)/shard_map/ppermute | solution.py:38
  202.9 10.0 %collective-permute-start.78 = (f32[16,16,128]{2,1,0:T(8,128)S(1)}, f32[16,16,128]{2,1,0:T(8,128)S(1)}, u32[]{:S(2)}, u32[]{:S(2)}) collective-permute-start(f32[16,16,128]{2,1,0:T(8,128)S(1)} %get-tuple-element.118), channel_id=1, source_target_pairs={{0,2},{1,3},{2,0},{3,1},{4,6},{5,7},{6,4},{7,5},{8,10},{9,11},{10,... | collective-permute-start | bytes 393224 | tf_op jit(solution)/shard_map/ppermute | solution.py:38
  217.6 10.3 %collective-permute-start.89 = (f32[16,16,128]{2,1,0:T(8,128)S(1)}, f32[16,16,128]{2,1,0:T(8,128)S(1)}, u32[]{:S(2)}, u32[]{:S(2)}) collective-permute-start(f32[16,16,128]{2,1,0:T(8,128)S(1)} %get-tuple-element.89.refs_8_), channel_id=1, source_target_pairs={{0,2},{1,3},{2,0},{3,1},{4,6},{5,7},{6,4},{7,5},{8,10},{9,11},{10,... | collective-permute-start | bytes 393224 | tf_op jit(solution)/shard_map/ppermute | solution.py:38
  235.3 8.9 %collective-permute-start.95 = (f32[32,16,128]{2,1,0:T(8,128)S(1)}, f32[32,16,128]{2,1,0:T(8,128)S(1)}, u32[]{:S(2)}, u32[]{:S(2)}) collective-permute-start(f32[32,16,128]{2,1,0:T(8,128)S(1)} %get-tuple-element.92), channel_id=1, source_target_pairs={{0,4},{4,0},{8,12},{12,8},{16,20},{20,16},{24,28},{28,24},{1,5},{5... | collective-permute-start | bytes 786440 | tf_op jit(solution)/shard_map/ppermute | solution.py:38
  235.5 33.8 %collective-permute-start.83 = (f32[32,128]{1,0:T(8,128)S(1)}, f32[32,128]{1,0:T(8,128)S(1)}, u32[]{:S(2)}, u32[]{:S(2)}) collective-permute-start(f32[32,128]{1,0:T(8,128)S(1)} %bitcast.47), channel_id=1, source_target_pairs={{0,4},{4,0},{8,12},{12,8},{16,20},{20,16},{24,28},{28,24},{1,5},{5... | collective-permute-start | bytes 49160 | tf_op jit(solution)/shard_map/ppermute | solution.py:38
  237.5 34.7 %collective-permute-start.84 = (f32[32,128]{1,0:T(8,128)S(1)}, f32[32,128]{1,0:T(8,128)S(1)}, u32[]{:S(2)}, u32[]{:S(2)}) collective-permute-start(f32[32,128]{1,0:T(8,128)S(1)} %bitcast.48), channel_id=1, source_target_pairs={{0,12},{4,8},{8,4},{12,0},{16,28},{20,24},{24,20},{28,16},{1,13},{... | collective-permute-start | bytes 49160 | tf_op jit(solution)/shard_map/ppermute | solution.py:38
  238.9 33.3 %collective-permute-start.82 = (f32[32,128]{1,0:T(8,128)S(1)}, f32[32,128]{1,0:T(8,128)S(1)}, u32[]{:S(2)}, u32[]{:S(2)}) collective-permute-start(f32[32,128]{1,0:T(8,128)S(1)} %bitcast.49), channel_id=1, source_target_pairs={{0,8},{4,12},{8,0},{12,4},{16,24},{20,28},{24,16},{28,20},{1,9},{5... | collective-permute-start | bytes 49160 | tf_op jit(solution)/shard_map/ppermute | solution.py:38
  244.2 8.8 %collective-permute-start.104 = (f32[32,16,128]{2,1,0:T(8,128)S(1)}, f32[32,16,128]{2,1,0:T(8,128)S(1)}, u32[]{:S(2)}, u32[]{:S(2)}) collective-permute-start(f32[32,16,128]{2,1,0:T(8,128)S(1)} %get-tuple-element.98), channel_id=1, source_target_pairs={{0,8},{4,12},{8,0},{12,4},{16,24},{20,28},{24,16},{28,20},{1,9},{5... | collective-permute-start | bytes 786440 | tf_op jit(solution)/shard_map/ppermute | solution.py:38
  258.2 10.9 %collective-permute-start.105 = (f32[16,16,128]{2,1,0:T(8,128)S(1)}, f32[16,16,128]{2,1,0:T(8,128)S(1)}, u32[]{:S(2)}, u32[]{:S(2)}) collective-permute-start(f32[16,16,128]{2,1,0:T(8,128)S(1)} %get-tuple-element.111), channel_id=1, source_target_pairs={{0,4},{4,0},{8,12},{12,8},{16,20},{20,16},{24,28},{28,24},{1,5},{5... | collective-permute-start | bytes 393224 | tf_op jit(solution)/shard_map/ppermute | solution.py:38
  262.8 22.5 %collective-permute-start.97 = (f32[8,16,128]{2,1,0:T(8,128)S(1)}, f32[8,16,128]{2,1,0:T(8,128)S(1)}, u32[]{:S(2)}, u32[]{:S(2)}) collective-permute-start(f32[8,16,128]{2,1,0:T(8,128)S(1)} %get-tuple-element.149), channel_id=1, source_target_pairs={{0,16},{4,20},{8,24},{12,28},{16,0},{20,4},{24,8},{28,12},{1,17},{... | collective-permute-start | bytes 196616 | tf_op jit(solution)/shard_map/ppermute | solution.py:38
  269.1 16.2 %collective-permute-start.100 = (f32[8,16,128]{2,1,0:T(8,128)S(1)}, f32[8,16,128]{2,1,0:T(8,128)S(1)}, u32[]{:S(2)}, u32[]{:S(2)}) collective-permute-start(f32[8,16,128]{2,1,0:T(8,128)S(1)} %get-tuple-element.147), channel_id=1, source_target_pairs={{0,16},{4,20},{8,24},{12,28},{16,0},{20,4},{24,8},{28,12},{1,17},{... | collective-permute-start | bytes 196616 | tf_op jit(solution)/shard_map/ppermute | solution.py:38
  269.3 16.0 %collective-permute-start.103 = (f32[8,16,128]{2,1,0:T(8,128)S(1)}, f32[8,16,128]{2,1,0:T(8,128)S(1)}, u32[]{:S(2)}, u32[]{:S(2)}) collective-permute-start(f32[8,16,128]{2,1,0:T(8,128)S(1)} %get-tuple-element.145), channel_id=1, source_target_pairs={{0,16},{4,20},{8,24},{12,28},{16,0},{20,4},{24,8},{28,12},{1,17},{... | collective-permute-start | bytes 196616 | tf_op jit(solution)/shard_map/ppermute | solution.py:38
  272.2 13.1 %collective-permute-start.106 = (f32[8,16,128]{2,1,0:T(8,128)S(1)}, f32[8,16,128]{2,1,0:T(8,128)S(1)}, u32[]{:S(2)}, u32[]{:S(2)}) collective-permute-start(f32[8,16,128]{2,1,0:T(8,128)S(1)} %get-tuple-element.143), channel_id=1, source_target_pairs={{0,16},{4,20},{8,24},{12,28},{16,0},{20,4},{24,8},{28,12},{1,17},{... | collective-permute-start | bytes 196616 | tf_op jit(solution)/shard_map/ppermute | solution.py:38
  (76 other events, 1082.3 us)

commit v10 on v9

--- a/solution.py
+++ b/solution.py
@@ -104,7 +104,7 @@
     return [at * quarter for at in ((0, 2, 1, 3) if swapped else (0, 1, 2, 3))], quarter
 
 
-def tiles_kernel(count, source, target, *refs, places_in, places_out):
+def tiles_kernel(count, source, target, *refs, contract, places_in, places_out):
     piece_refs, refs = [refs[4 * part : 4 * part + 4] for part in range(PARTS)], refs[4 * PARTS :]
     tile_ref, keep_refs, send_refs = refs[0], refs[1 : 1 + PARTS], refs[1 + PARTS : 1 + 2 * PARTS]
     pieces, total = refs[1 + 2 * PARTS :]
@@ -144,8 +144,8 @@
             products.append(
                 lax.dot_general(
                     pieces[source[step * BATCH + first + slot]],
-                    jnp.concatenate([tile, tile], axis=0),
-                    (((1,), (0,)), ((), ())),
+                    jnp.concatenate([tile, tile], axis=contract),
+                    (((1,), (contract,)), ((), ())),
                     preferred_element_type=jnp.float32,
                 )
             )
@@ -171,7 +171,7 @@
                 lax.fori_loop(0, quarter, finish, 0, unroll=4)
 
 
-def tiles_product(count, source, target, pieces, tiles, blocks_out, axis_in, axis_out):
+def tiles_product(count, source, target, pieces, tiles, blocks_out, axis_in, axis_out, contract):
     quarter_in = pieces[-1][0].shape[0]
     half_out = blocks_out // 2
 
@@ -180,6 +180,7 @@
 
     kernel = functools.partial(
         tiles_kernel,
+        contract=contract,
         places_in=[part_places(axis_in, part, 4 * quarter_in) for part in range(PARTS)],
         places_out=[part_places(axis_out, part, 2 * half_out) for part in range(PARTS)],
     )
@@ -234,24 +235,6 @@
     out_ref[...] = work[:, K:] * lax.rsqrt(pivots)
 
 
-def turn_kernel(tile_ref, out_ref):
-    for at in range(tile_ref.shape[0]):
-        out_ref[at] = tile_ref[at].T
-
-
-def turned_tiles(tiles):
-    block = pl.BlockSpec((tiles.shape[0] // 16, TILE, TILE), lambda step: (step, 0, 0))
-    return pl.pallas_call(
-        turn_kernel,
-        out_shape=pltpu.HBM(tiles.shape, tiles.dtype),
-        grid=(16,),
-        in_specs=[block],
-        out_specs=block,
-        compiler_params=SMALL_KERNEL,
-        name="turned_tiles",
-    )(in_vmem(tiles))
-
-
 def inverse_factor(gram, total):
     return pl.pallas_call(
         functools.partial(factor_kernel, total=total),
@@ -341,19 +324,17 @@
     start = item_scale[None, :, None, :] * start
     sent = [start[part] for part in range(PARTS)]
     sent[0] = jnp.concatenate([sent[0], jnp.zeros((GRAM, ROWS, TILE), jnp.float32)], axis=0)
-    turned = turned_tiles(tiles)
     item_inverse = None
     for step in range(ITERS):
         pieces = gather(sent, "users")
         if step:
             item_inverse = inverse_factor(gram_sum(pieces, "items"), item_total)
-        source = turned if step else pltpu.with_memory_space_constraint(turned, pltpu.HBM)
-        kept, out = tiles_product(count, col_at, row_to, pieces, source, UT, "users", "items")
+        kept, out = tiles_product(count, col_at, row_to, pieces, tiles, UT, "users", "items", 1)
         kept, got = reduce_scatter(kept, out, "items")
         user_raw, sent = scale_panel(item_inverse, kept, got, user_scale)
         pieces = gather(sent, "items")
         user_inverse = inverse_factor(gram_sum(pieces, "users"), user_total)
-        kept, out = tiles_product(count, row_at, col_to, pieces, tiles, IT, "items", "users")
+        kept, out = tiles_product(count, row_at, col_to, pieces, tiles, IT, "items", "users", 0)
         kept, got = reduce_scatter(kept, out, "users")
         if step == ITERS - 1:
             user_panel = finish_panel(user_inverse, user_raw)

time: 311 us -> 311 us (level)
  Pallas kernels: 59.6 us -> 50.2 us
  starting transfers between devices: 123 us -> 129 us
    pallas_call x1 -> x0, Pallas kernels: 11 us -> none  [turned_tiles(): pl.pallas_call(turn_kernel, out_shape=pltpu.HBM(tiles.shape, tiles.dtype)...]
    ppermute x112, starting transfers between devices: 123 us -> 129 us  [exchange(): lax.ppermute(value, axis, [(at, at ^ bit) for at in range(lax.axis_size(a...]
  transfers between devices with their start and end apart: 112 -> 112, of which waited for: 47 -> 55; matrix products, arithmetic and copies ran while one was open for 0% -> 1% of each run, Pallas kernels for 9% -> 6%
where the time goes in v10:
time: 311 us
  starting transfers between devices  129 us (41%)
  waiting for transfers between devices  121 us (39%)
  Pallas kernels  50.2 us (16%)
  local copies, waits for them, and re-layouts  5.9 us (2%)
  other arithmetic  3.26 us (1%)
    ppermute x112, starting transfers between devices, exchange(): lax.ppermute(value, axis, [(at, at ^ bit) for at in range(lax.axis_size(a...  129 us
    ppermute x112, waiting for transfers between devices, exchange(): lax.ppermute(value, axis, [(at, at ^ bit) for at in range(lax.axis_size(a...  121 us
    pallas_call x4, Pallas kernels, inverse_factor(): pl.pallas_call(functools.partial(factor_kernel, total=total), out_shape=p...  21.7 us
    pallas_call x4, Pallas kernels, tiles_product(): call(count, source, target, *[in_vmem(piece) for part in pieces for piece...  18.4 us
    pallas_call x4, Pallas kernels, scale_panel(): pl.pallas_call(functools.partial(scale_kernel, factored=factored), out_sh...  7.64 us
  transfers between devices with their start and end apart: 112, of which 55 were waited for; matrix products, arithmetic and copies ran while one was open for 1% of the time, Pallas kernels for 6%

profile of v10, /device:TPU:0, one launch (start us, length us, event | category | flops | bytes accessed | tf_op | source)
XLA Modules:
  0.0 310.9 jit_solution(3648416213606569303)
XLA Ops:
  2.4 4.1 %collective-permute-start.8 = (f32[8,16,128]{2,1,0:T(8,128)S(1)}, f32[8,16,128]{2,1,0:T(8,128)S(1)}, u32[]{:S(2)}, u32[]{:S(2)}) collective-permute-start(f32[8,16,128]{2,1,0:T(8,128)S(1)} %get-tuple-element.159), channel_id=1, source_target_pairs={{0,16},{4,20},{8,24},{12,28},{16,0},{20,4},{24,8},{28,12},{1,17},{... | collective-permute-start | bytes 196616 | tf_op jit(solution)/shard_map/ppermute | solution.py:38
  6.6 2.8 collective-permute-start.4
  10.3 5.2 %collective-permute-start.9 = (f32[16,16,128]{2,1,0:T(8,128)S(1)}, f32[16,16,128]{2,1,0:T(8,128)S(1)}, u32[]{:S(2)}, u32[]{:S(2)}) collective-permute-start(f32[16,16,128]{2,1,0:T(8,128)S(1)} %pad_maximum_fusion.3.refs_8_), channel_id=1, source_target_pairs={{0,8},{4,12},{8,0},{12,4},{16,24},{20,28},{24,16},{28,20},{1,9},{5... | collective-permute-start | bytes 393224 | tf_op jit(solution)/shard_map/ppermute | solution.py:38
  37.7 5.8 %copy-done = bf16[1,1,512,128,128]{4,3,2,1,0:T(8,128)(2,1)S(1)} copy-done((bf16[1,1,512,128,128]{4,3,2,1,0:T(8,128)(2,1)S(1)}, bf16[1,1,512,128,128]{4,3,2,1,0:T(8,128)(2,1)}, u32[]{:S(2)}) %copy-start) | copy-done | bytes 16777240
  43.5 5.4 %shard_map.86 = (f32[32,16,128]{2,1,0:T(8,128)S(1)}, f32[32,16,128]{2,1,0:T(8,128)S(1)}, f32[32,16,128]{2,1,0:T(8,128)S(1)}, f32[32,16,128]{2,1,0:T(8,128)S(1)},...) custom-call(s32[1]{0:T(128)} %bitcast.31.count, ...), custom_call_target="tpu_custom_call" | custom-call | tf_op jit(solution)/shard_map/pallas_call | solution.py:203
  50.6 11.2 %collective-permute-start.23 = (f32[16,16,128]{2,1,0:T(8,128)S(1)}, f32[16,16,128]{2,1,0:T(8,128)S(1)}, u32[]{:S(2)}, u32[]{:S(2)}) collective-permute-start(f32[16,16,128]{2,1,0:T(8,128)S(1)} %get-tuple-element.134), channel_id=1, source_target_pairs={{0,2},{1,3},{2,0},{3,1},{4,6},{5,7},{6,4},{7,5},{8,10},{9,11},{10,... | collective-permute-start | bytes 393224 | tf_op jit(solution)/shard_map/ppermute | solution.py:38
  66.1 2.8 collective-permute-done.22.refs_6_
  68.9 2.8 collective-permute-done.21.refs_5_
  71.7 2.3 collective-permute-done.20.refs_4_
  79.5 2.3 collective-permute-done.31.refs_5_
  81.8 2.8 collective-permute-done.34.refs_9_
  84.6 4.6 %collective-permute-done.37.refs_13_ = f32[16,16,128]{2,1,0:T(8,128)S(1)} collective-permute-done((f32[16,16,128]{2,1,0:T(8,128)S(1)}, f32[16,16,128]{2,1,0:T(8,128)S(1)}, u32[]{:S(2)}, u32[]{:S(2)}) %collective-permute-start.37) | collective-permute-done | bytes 131104 | tf_op jit(solution)/shard_map/ppermute | solution.py:38
  91.6 3.7 %shard_map.87 = (f32[32,16,128]{2,1,0:T(8,128)S(1)}, f32[32,16,128]{2,1,0:T(8,128)S(1)}, f32[32,16,128]{2,1,0:T(8,128)S(1)}, f32[32,16,128]{2,1,0:T(8,128)S(1)},...) custom-call(s32[1]{0:T(128)} %bitcast.32.count, ...), custom_call_target="tpu_custom_call" | custom-call | tf_op jit(solution)/shard_map/pallas_call | solution.py:203
  99.4 3.3 %collective-permute-done.46 = f32[32,16,128]{2,1,0:T(8,128)S(1)} collective-permute-done((f32[32,16,128]{2,1,0:T(8,128)S(1)}, f32[32,16,128]{2,1,0:T(8,128)S(1)}, u32[]{:S(2)}, u32[]{:S(2)}) %collective-permute-start.46) | collective-permute-done | bytes 262176 | tf_op jit(solution)/shard_map/ppermute | solution.py:38
  103.1 7.7 %collective-permute-done.42 = f32[32,16,128]{2,1,0:T(8,128)S(1)} collective-permute-done((f32[32,16,128]{2,1,0:T(8,128)S(1)}, f32[32,16,128]{2,1,0:T(8,128)S(1)}, u32[]{:S(2)}, u32[]{:S(2)}) %collective-permute-start.42) | collective-permute-done | bytes 262176 | tf_op jit(solution)/shard_map/ppermute | solution.py:38
  112.7 4.4 %collective-permute-done.47 = f32[16,16,128]{2,1,0:T(8,128)S(1)} collective-permute-done((f32[16,16,128]{2,1,0:T(8,128)S(1)}, f32[16,16,128]{2,1,0:T(8,128)S(1)}, u32[]{:S(2)}, u32[]{:S(2)}) %collective-permute-start.47) | collective-permute-done | bytes 131104 | tf_op jit(solution)/shard_map/ppermute | solution.py:38
  118.4 4.1 %collective-permute-done.43 = f32[16,16,128]{2,1,0:T(8,128)S(1)} collective-permute-done((f32[16,16,128]{2,1,0:T(8,128)S(1)}, f32[16,16,128]{2,1,0:T(8,128)S(1)}, u32[]{:S(2)}, u32[]{:S(2)}) %collective-permute-start.43) | collective-permute-done | bytes 131104 | tf_op jit(solution)/shard_map/ppermute | solution.py:38
  122.5 7.4 %collective-permute-start.51 = (f32[8,16,128]{2,1,0:T(8,128)S(1)}, f32[8,16,128]{2,1,0:T(8,128)S(1)}, u32[]{:S(2)}, u32[]{:S(2)}) collective-permute-start(f32[8,16,128]{2,1,0:T(8,128)S(1)} %get-tuple-element.150), channel_id=1, source_target_pairs={{0,16},{4,20},{8,24},{12,28},{16,0},{20,4},{24,8},{28,12},{1,17},{... | collective-permute-start | bytes 196616 | tf_op jit(solution)/shard_map/ppermute | solution.py:38
  130.4 2.7 collective-permute-start.49
  133.4 2.7 collective-permute-start.30
  136.0 3.6 %collective-permute-done.30 = f32[32,128]{1,0:T(8,128)S(1)} collective-permute-done((f32[32,128]{1,0:T(8,128)S(1)}, f32[32,128]{1,0:T(8,128)S(1)}, u32[]{:S(2)}, u32[]{:S(2)}) %collective-permute-start.30) | collective-permute-done | bytes 16416 | tf_op jit(solution)/shard_map/ppermute | solution.py:38
  139.7 5.4 %factor.4.refs_0_ = f32[64,64]{1,0:T(8,128)S(1)} custom-call(f32[32,128]{1,0:T(8,128)S(1)} %add.288.gram_ref), custom_call_target="tpu_custom_call" | custom-call | tf_op jit(solution)/shard_map/factor/pallas_call | solution.py:239
  152.8 3.9 %collective-permute-done.67 = f32[8,16,128]{2,1,0:T(8,128)S(1)} collective-permute-done((f32[8,16,128]{2,1,0:T(8,128)S(1)}, f32[8,16,128]{2,1,0:T(8,128)S(1)}, u32[]{:S(2)}, u32[]{:S(2)}) %collective-permute-start.67) | collective-permute-done | bytes 65568 | tf_op jit(solution)/shard_map/ppermute | solution.py:38
  156.7 2.9 collective-permute-start.68
  162.7 2.4 collective-permute-start.60
  169.3 2.7 collective-permute-start.55
  174.2 2.9 collective-permute-done.70.refs_15_
  178.4 5.6 %shard_map.88 = (f32[32,16,128]{2,1,0:T(8,128)S(1)}, f32[32,16,128]{2,1,0:T(8,128)S(1)}, f32[32,16,128]{2,1,0:T(8,128)S(1)}, f32[32,16,128]{2,1,0:T(8,128)S(1)},...) custom-call(s32[1]{0:T(128)} %bitcast.33.count, ...), custom_call_target="tpu_custom_call" | custom-call | tf_op jit(solution)/shard_map/pallas_call | solution.py:203
  184.6 6.4 %collective-permute-start.56 = (f32[32,128]{1,0:T(8,128)S(1)}, f32[32,128]{1,0:T(8,128)S(1)}, u32[]{:S(2)}, u32[]{:S(2)}) collective-permute-start(f32[32,128]{1,0:T(8,128)S(1)} %bitcast.47), channel_id=1, source_target_pairs={{0,2},{1,3},{2,0},{3,1},{4,6},{5,7},{6,4},{7,5},{8,10},{9,11},{10,... | collective-permute-start | bytes 49160 | tf_op jit(solution)/shard_map/ppermute | solution.py:38
  197.2 5.4 %factor.5.refs_0_ = f32[64,64]{1,0:T(8,128)S(1)} custom-call(f32[32,128]{1,0:T(8,128)S(1)} %add_add_fusion.1.gram_ref), custom_call_target="tpu_custom_call" | custom-call | tf_op jit(solution)/shard_map/factor/pallas_call | solution.py:239
  206.9 2.6 scale_panel.6
  213.6 2.3 collective-permute-done.86.refs_5_
  215.9 2.8 collective-permute-done.89.refs_9_
  218.7 4.5 %collective-permute-done.92.refs_13_ = f32[16,16,128]{2,1,0:T(8,128)S(1)} collective-permute-done((f32[16,16,128]{2,1,0:T(8,128)S(1)}, f32[16,16,128]{2,1,0:T(8,128)S(1)}, u32[]{:S(2)}, u32[]{:S(2)}) %collective-permute-start.92) | collective-permute-done | bytes 131104 | tf_op jit(solution)/shard_map/ppermute | solution.py:38
  225.6 3.7 %shard_map.89 = (f32[32,16,128]{2,1,0:T(8,128)S(1)}, f32[32,16,128]{2,1,0:T(8,128)S(1)}, f32[32,16,128]{2,1,0:T(8,128)S(1)}, f32[32,16,128]{2,1,0:T(8,128)S(1)},...) custom-call(s32[1]{0:T(128)} %bitcast.34.count, ...), custom_call_target="tpu_custom_call" | custom-call | tf_op jit(solution)/shard_map/pallas_call | solution.py:203
  237.1 7.0 %collective-permute-done.98 = f32[32,16,128]{2,1,0:T(8,128)S(1)} collective-permute-done((f32[32,16,128]{2,1,0:T(8,128)S(1)}, f32[32,16,128]{2,1,0:T(8,128)S(1)}, u32[]{:S(2)}, u32[]{:S(2)}) %collective-permute-start.98) | collective-permute-done | bytes 262176 | tf_op jit(solution)/shard_map/ppermute | solution.py:38
  245.5 4.7 %collective-permute-done.105 = f32[16,16,128]{2,1,0:T(8,128)S(1)} collective-permute-done((f32[16,16,128]{2,1,0:T(8,128)S(1)}, f32[16,16,128]{2,1,0:T(8,128)S(1)}, u32[]{:S(2)}, u32[]{:S(2)}) %collective-permute-start.105) | collective-permute-done | bytes 131104 | tf_op jit(solution)/shard_map/ppermute | solution.py:38
  250.5 5.2 %collective-permute-done.99 = f32[16,16,128]{2,1,0:T(8,128)S(1)} collective-permute-done((f32[16,16,128]{2,1,0:T(8,128)S(1)}, f32[16,16,128]{2,1,0:T(8,128)S(1)}, u32[]{:S(2)}, u32[]{:S(2)}) %collective-permute-start.99) | collective-permute-done | bytes 131104 | tf_op jit(solution)/shard_map/ppermute | solution.py:38
  255.7 10.5 %collective-permute-start.106 = (f32[8,16,128]{2,1,0:T(8,128)S(1)}, f32[8,16,128]{2,1,0:T(8,128)S(1)}, u32[]{:S(2)}, u32[]{:S(2)}) collective-permute-start(f32[8,16,128]{2,1,0:T(8,128)S(1)} %get-tuple-element.143), channel_id=1, source_target_pairs={{0,16},{4,20},{8,24},{12,28},{16,0},{20,4},{24,8},{28,12},{1,17},{... | collective-permute-start | bytes 196616 | tf_op jit(solution)/shard_map/ppermute | solution.py:38
  266.3 4.7 %collective-permute-start.103 = (f32[8,16,128]{2,1,0:T(8,128)S(1)}, f32[8,16,128]{2,1,0:T(8,128)S(1)}, u32[]{:S(2)}, u32[]{:S(2)}) collective-permute-start(f32[8,16,128]{2,1,0:T(8,128)S(1)} %get-tuple-element.145), channel_id=1, source_target_pairs={{0,16},{4,20},{8,24},{12,28},{16,0},{20,4},{24,8},{28,12},{1,17},{... | collective-permute-start | bytes 196616 | tf_op jit(solution)/shard_map/ppermute | solution.py:38
  271.1 2.9 collective-permute-start.97
  274.2 4.6 %collective-permute-done.85 = f32[32,128]{1,0:T(8,128)S(1)} collective-permute-done((f32[32,128]{1,0:T(8,128)S(1)}, f32[32,128]{1,0:T(8,128)S(1)}, u32[]{:S(2)}, u32[]{:S(2)}) %collective-permute-start.85) | collective-permute-done | bytes 16416 | tf_op jit(solution)/shard_map/ppermute | solution.py:38
  278.7 5.4 %factor.6.inverse_ref.refs_0_ = f32[64,64]{1,0:T(8,128)S(1)} custom-call(f32[32,128]{1,0:T(8,128)S(1)} %add.328.gram_ref), custom_call_target="tpu_custom_call" | custom-call | tf_op jit(solution)/shard_map/factor/pallas_call | solution.py:239
  288.5 3.7 %collective-permute-done.108 = f32[32,128]{1,0:T(8,128)S(1)} collective-permute-done((f32[32,128]{1,0:T(8,128)S(1)}, f32[32,128]{1,0:T(8,128)S(1)}, u32[]{:S(2)}, u32[]{:S(2)}) %collective-permute-start.108) | collective-permute-done | bytes 16416 | tf_op jit(solution)/shard_map/ppermute | solution.py:38
  292.2 3.7 %collective-permute-done.109 = f32[32,128]{1,0:T(8,128)S(1)} collective-permute-done((f32[32,128]{1,0:T(8,128)S(1)}, f32[32,128]{1,0:T(8,128)S(1)}, u32[]{:S(2)}, u32[]{:S(2)}) %collective-permute-start.109) | collective-permute-done | bytes 16416 | tf_op jit(solution)/shard_map/ppermute | solution.py:38
  296.0 3.7 %collective-permute-done.110 = f32[32,128]{1,0:T(8,128)S(1)} collective-permute-done((f32[32,128]{1,0:T(8,128)S(1)}, f32[32,128]{1,0:T(8,128)S(1)}, u32[]{:S(2)}, u32[]{:S(2)}) %collective-permute-start.110) | collective-permute-done | bytes 16416 | tf_op jit(solution)/shard_map/ppermute | solution.py:38
  300.5 3.9 %collective-permute-done.111 = f32[32,128]{1,0:T(8,128)S(1)} collective-permute-done((f32[32,128]{1,0:T(8,128)S(1)}, f32[32,128]{1,0:T(8,128)S(1)}, u32[]{:S(2)}, u32[]{:S(2)}) %collective-permute-start.111) | collective-permute-done | bytes 16416 | tf_op jit(solution)/shard_map/ppermute | solution.py:38
  304.4 5.4 %factor.7.inverse_ref = f32[64,64]{1,0:T(8,128)S(1)} custom-call(f32[32,128]{1,0:T(8,128)S(1)} %add.349.gram_ref), custom_call_target="tpu_custom_call" | custom-call | tf_op jit(solution)/shard_map/factor/pallas_call | solution.py:239
  (256 shorter events, 98.3 us)
Async XLA Ops:
  6.5 10.2 %collective-permute-start.12 = (f32[8,16,128]{2,1,0:T(8,128)S(1)}, f32[8,16,128]{2,1,0:T(8,128)S(1)}, u32[]{:S(2)}, u32[]{:S(2)}) collective-permute-start(f32[8,16,128]{2,1,0:T(8,128)S(1)} %get-tuple-element.158), channel_id=1, source_target_pairs={{0,16},{4,20},{8,24},{12,28},{16,0},{20,4},{24,8},{28,12},{1,17},{... | collective-permute-start | bytes 196616 | tf_op jit(solution)/shard_map/ppermute | solution.py:38
  6.6 13.4 %collective-permute-start.4 = (f32[8,16,128]{2,1,0:T(8,128)S(1)}, f32[8,16,128]{2,1,0:T(8,128)S(1)}, u32[]{:S(2)}, u32[]{:S(2)}) collective-permute-start(f32[8,16,128]{2,1,0:T(8,128)S(1)} %get-tuple-element.160), channel_id=1, source_target_pairs={{0,16},{4,20},{8,24},{12,28},{16,0},{20,4},{24,8},{28,12},{1,17},{... | collective-permute-start | bytes 196616 | tf_op jit(solution)/shard_map/ppermute | solution.py:38
  9.5 9.9 %collective-permute-start = (f32[10,16,128]{2,1,0:T(8,128)S(1)}, f32[10,16,128]{2,1,0:T(8,128)S(1)}, u32[]{:S(2)}, u32[]{:S(2)}) collective-permute-start(f32[10,16,128]{2,1,0:T(8,128)S(1)} %concatenate.27), channel_id=1, source_target_pairs={{0,16},{4,20},{8,24},{12,28},{16,0},{20,4},{24,8},{28,12},{1,17},{... | collective-permute-start | bytes 245768 | tf_op jit(solution)/shard_map/ppermute | solution.py:38
  10.3 11.9 %collective-permute-start.9 = (f32[16,16,128]{2,1,0:T(8,128)S(1)}, f32[16,16,128]{2,1,0:T(8,128)S(1)}, u32[]{:S(2)}, u32[]{:S(2)}) collective-permute-start(f32[16,16,128]{2,1,0:T(8,128)S(1)} %pad_maximum_fusion.3.refs_8_), channel_id=1, source_target_pairs={{0,8},{4,12},{8,0},{12,4},{16,24},{20,28},{24,16},{28,20},{1,9},{5... | collective-permute-start | bytes 393224 | tf_op jit(solution)/shard_map/ppermute | solution.py:38
  19.4 13.2 %collective-permute-start.1 = (f32[18,16,128]{2,1,0:T(8,128)S(1)}, f32[18,16,128]{2,1,0:T(8,128)S(1)}, u32[]{:S(2)}, u32[]{:S(2)}) collective-permute-start(f32[18,16,128]{2,1,0:T(8,128)S(1)} %pad_maximum_fusion.refs_0_), channel_id=1, source_target_pairs={{0,8},{4,12},{8,0},{12,4},{16,24},{20,28},{24,16},{28,20},{1,9},{5... | collective-permute-start | bytes 442376 | tf_op jit(solution)/shard_map/ppermute | solution.py:38
  22.2 8.2 %collective-permute-start.14 = (f32[16,16,128]{2,1,0:T(8,128)S(1)}, f32[16,16,128]{2,1,0:T(8,128)S(1)}, u32[]{:S(2)}, u32[]{:S(2)}) collective-permute-start(f32[16,16,128]{2,1,0:T(8,128)S(1)} %pad_maximum_fusion.4.refs_12_), channel_id=1, source_target_pairs={{0,8},{4,12},{8,0},{12,4},{16,24},{20,28},{24,16},{28,20},{1,9},{5... | collective-permute-start | bytes 393224 | tf_op jit(solution)/shard_map/ppermute | solution.py:38
  23.6 8.9 %collective-permute-start.6 = (f32[16,16,128]{2,1,0:T(8,128)S(1)}, f32[16,16,128]{2,1,0:T(8,128)S(1)}, u32[]{:S(2)}, u32[]{:S(2)}) collective-permute-start(f32[16,16,128]{2,1,0:T(8,128)S(1)} %pad_maximum_fusion.2.refs_4_), channel_id=1, source_target_pairs={{0,8},{4,12},{8,0},{12,4},{16,24},{20,28},{24,16},{28,20},{1,9},{5... | collective-permute-start | bytes 393224 | tf_op jit(solution)/shard_map/ppermute | solution.py:38
  49.0 12.7 %collective-permute-start.18 = (f32[32,16,128]{2,1,0:T(8,128)S(1)}, f32[32,16,128]{2,1,0:T(8,128)S(1)}, u32[]{:S(2)}, u32[]{:S(2)}) collective-permute-start(f32[32,16,128]{2,1,0:T(8,128)S(1)} %get-tuple-element.59), channel_id=1, source_target_pairs={{0,1},{1,0},{2,3},{3,2},{4,5},{5,4},{6,7},{7,6},{8,9},{9,8},{10,11... | collective-permute-start | bytes 786440 | tf_op jit(solution)/shard_map/ppermute | solution.py:38
  49.5 12.6 %collective-permute-start.17 = (f32[32,16,128]{2,1,0:T(8,128)S(1)}, f32[32,16,128]{2,1,0:T(8,128)S(1)}, u32[]{:S(2)}, u32[]{:S(2)}) collective-permute-start(f32[32,16,128]{2,1,0:T(8,128)S(1)} %get-tuple-element.57), channel_id=1, source_target_pairs={{0,1},{1,0},{2,3},{3,2},{4,5},{5,4},{6,7},{7,6},{8,9},{9,8},{10,11... | collective-permute-start | bytes 786440 | tf_op jit(solution)/shard_map/ppermute | solution.py:38
  49.6 14.4 %collective-permute-start.16 = (f32[32,16,128]{2,1,0:T(8,128)S(1)}, f32[32,16,128]{2,1,0:T(8,128)S(1)}, u32[]{:S(2)}, u32[]{:S(2)}) collective-permute-start(f32[32,16,128]{2,1,0:T(8,128)S(1)} %get-tuple-element.55), channel_id=1, source_target_pairs={{0,1},{1,0},{2,3},{3,2},{4,5},{5,4},{6,7},{7,6},{8,9},{9,8},{10,11... | collective-permute-start | bytes 786440 | tf_op jit(solution)/shard_map/ppermute | solution.py:38
  50.6 15.5 %collective-permute-start.23 = (f32[16,16,128]{2,1,0:T(8,128)S(1)}, f32[16,16,128]{2,1,0:T(8,128)S(1)}, u32[]{:S(2)}, u32[]{:S(2)}) collective-permute-start(f32[16,16,128]{2,1,0:T(8,128)S(1)} %get-tuple-element.134), channel_id=1, source_target_pairs={{0,2},{1,3},{2,0},{3,1},{4,6},{5,7},{6,4},{7,5},{8,10},{9,11},{10,... | collective-permute-start | bytes 393224 | tf_op jit(solution)/shard_map/ppermute | solution.py:38
  62.2 9.5 %collective-permute-start.21 = (f32[16,16,128]{2,1,0:T(8,128)S(1)}, f32[16,16,128]{2,1,0:T(8,128)S(1)}, u32[]{:S(2)}, u32[]{:S(2)}) collective-permute-start(f32[16,16,128]{2,1,0:T(8,128)S(1)} %get-tuple-element.138), channel_id=1, source_target_pairs={{0,2},{1,3},{2,0},{3,1},{4,6},{5,7},{6,4},{7,5},{8,10},{9,11},{10,... | collective-permute-start | bytes 393224 | tf_op jit(solution)/shard_map/ppermute | solution.py:38
  64.0 9.9 %collective-permute-start.20 = (f32[16,16,128]{2,1,0:T(8,128)S(1)}, f32[16,16,128]{2,1,0:T(8,128)S(1)}, u32[]{:S(2)}, u32[]{:S(2)}) collective-permute-start(f32[16,16,128]{2,1,0:T(8,128)S(1)} %get-tuple-element.140), channel_id=1, source_target_pairs={{0,2},{1,3},{2,0},{3,1},{4,6},{5,7},{6,4},{7,5},{8,10},{9,11},{10,... | collective-permute-start | bytes 393224 | tf_op jit(solution)/shard_map/ppermute | solution.py:38
  77.5 11.7 %collective-permute-start.24 = (f32[18,16,128]{2,1,0:T(8,128)S(1)}, f32[18,16,128]{2,1,0:T(8,128)S(1)}, u32[]{:S(2)}, u32[]{:S(2)}) collective-permute-start(f32[18,16,128]{2,1,0:T(8,128)S(1)} %get-tuple-element.62.refs_0_), channel_id=1, source_target_pairs={{0,2},{1,3},{2,0},{3,1},{4,6},{5,7},{6,4},{7,5},{8,10},{9,11},{10,... | collective-permute-start | bytes 442376 | tf_op jit(solution)/shard_map/ppermute | solution.py:38
  79.2 10.0 %collective-permute-start.37 = (f32[16,16,128]{2,1,0:T(8,128)S(1)}, f32[16,16,128]{2,1,0:T(8,128)S(1)}, u32[]{:S(2)}, u32[]{:S(2)}) collective-permute-start(f32[16,16,128]{2,1,0:T(8,128)S(1)} %get-tuple-element.65.refs_12_), channel_id=1, source_target_pairs={{0,2},{1,3},{2,0},{3,1},{4,6},{5,7},{6,4},{7,5},{8,10},{9,11},{10,... | collective-permute-start | bytes 393224 | tf_op jit(solution)/shard_map/ppermute | solution.py:38
  79.5 10.2 %collective-permute-start.32 = (f32[16,16,128]{2,1,0:T(8,128)S(1)}, f32[16,16,128]{2,1,0:T(8,128)S(1)}, u32[]{:S(2)}, u32[]{:S(2)}) collective-permute-start(f32[16,16,128]{2,1,0:T(8,128)S(1)} %get-tuple-element.63.refs_4_), channel_id=1, source_target_pairs={{0,1},{1,0},{2,3},{3,2},{4,5},{5,4},{6,7},{7,6},{8,9},{9,8},{10,11... | collective-permute-start | bytes 393224 | tf_op jit(solution)/shard_map/ppermute | solution.py:38
  95.5 34.8 %collective-permute-start.27 = (f32[32,128]{1,0:T(8,128)S(1)}, f32[32,128]{1,0:T(8,128)S(1)}, u32[]{:S(2)}, u32[]{:S(2)}) collective-permute-start(f32[32,128]{1,0:T(8,128)S(1)} %bitcast.41), channel_id=1, source_target_pairs={{0,8},{4,12},{8,0},{12,4},{16,24},{20,28},{24,16},{28,20},{1,9},{5... | collective-permute-start | bytes 49160 | tf_op jit(solution)/shard_map/ppermute | solution.py:38
  97.5 35.5 %collective-permute-start.28 = (f32[32,128]{1,0:T(8,128)S(1)}, f32[32,128]{1,0:T(8,128)S(1)}, u32[]{:S(2)}, u32[]{:S(2)}) collective-permute-start(f32[32,128]{1,0:T(8,128)S(1)} %bitcast.42), channel_id=1, source_target_pairs={{0,4},{4,0},{8,12},{12,8},{16,20},{20,16},{24,28},{28,24},{1,5},{5... | collective-permute-start | bytes 49160 | tf_op jit(solution)/shard_map/ppermute | solution.py:38
  99.4 33.9 %collective-permute-start.29 = (f32[32,128]{1,0:T(8,128)S(1)}, f32[32,128]{1,0:T(8,128)S(1)}, u32[]{:S(2)}, u32[]{:S(2)}) collective-permute-start(f32[32,128]{1,0:T(8,128)S(1)} %bitcast.43), channel_id=1, source_target_pairs={{0,12},{4,8},{8,4},{12,0},{16,28},{20,24},{24,20},{28,16},{1,13},{... | collective-permute-start | bytes 49160 | tf_op jit(solution)/shard_map/ppermute | solution.py:38
  102.7 8.1 %collective-permute-start.42 = (f32[32,16,128]{2,1,0:T(8,128)S(1)}, f32[32,16,128]{2,1,0:T(8,128)S(1)}, u32[]{:S(2)}, u32[]{:S(2)}) collective-permute-start(f32[32,16,128]{2,1,0:T(8,128)S(1)} %get-tuple-element.69), channel_id=1, source_target_pairs={{0,8},{4,12},{8,0},{12,4},{16,24},{20,28},{24,16},{28,20},{1,9},{5... | collective-permute-start | bytes 786440 | tf_op jit(solution)/shard_map/ppermute | solution.py:38
  102.8 8.1 %collective-permute-start.40 = (f32[32,16,128]{2,1,0:T(8,128)S(1)}, f32[32,16,128]{2,1,0:T(8,128)S(1)}, u32[]{:S(2)}, u32[]{:S(2)}) collective-permute-start(f32[32,16,128]{2,1,0:T(8,128)S(1)} %get-tuple-element.67), channel_id=1, source_target_pairs={{0,4},{4,0},{8,12},{12,8},{16,20},{20,16},{24,28},{28,24},{1,5},{5... | collective-permute-start | bytes 786440 | tf_op jit(solution)/shard_map/ppermute | solution.py:38
  117.1 12.8 %collective-permute-start.41 = (f32[16,16,128]{2,1,0:T(8,128)S(1)}, f32[16,16,128]{2,1,0:T(8,128)S(1)}, u32[]{:S(2)}, u32[]{:S(2)}) collective-permute-start(f32[16,16,128]{2,1,0:T(8,128)S(1)} %get-tuple-element.133), channel_id=1, source_target_pairs={{0,8},{4,12},{8,0},{12,4},{16,24},{20,28},{24,16},{28,20},{1,9},{5... | collective-permute-start | bytes 393224 | tf_op jit(solution)/shard_map/ppermute | solution.py:38
  122.5 22.6 %collective-permute-start.51 = (f32[8,16,128]{2,1,0:T(8,128)S(1)}, f32[8,16,128]{2,1,0:T(8,128)S(1)}, u32[]{:S(2)}, u32[]{:S(2)}) collective-permute-start(f32[8,16,128]{2,1,0:T(8,128)S(1)} %get-tuple-element.150), channel_id=1, source_target_pairs={{0,16},{4,20},{8,24},{12,28},{16,0},{20,4},{24,8},{28,12},{1,17},{... | collective-permute-start | bytes 196616 | tf_op jit(solution)/shard_map/ppermute | solution.py:38
  129.9 15.2 %collective-permute-start.50 = (f32[8,16,128]{2,1,0:T(8,128)S(1)}, f32[8,16,128]{2,1,0:T(8,128)S(1)}, u32[]{:S(2)}, u32[]{:S(2)}) collective-permute-start(f32[8,16,128]{2,1,0:T(8,128)S(1)} %get-tuple-element.152), channel_id=1, source_target_pairs={{0,16},{4,20},{8,24},{12,28},{16,0},{20,4},{24,8},{28,12},{1,17},{... | collective-permute-start | bytes 196616 | tf_op jit(solution)/shard_map/ppermute | solution.py:38
  130.4 14.8 %collective-permute-start.49 = (f32[8,16,128]{2,1,0:T(8,128)S(1)}, f32[8,16,128]{2,1,0:T(8,128)S(1)}, u32[]{:S(2)}, u32[]{:S(2)}) collective-permute-start(f32[8,16,128]{2,1,0:T(8,128)S(1)} %get-tuple-element.154), channel_id=1, source_target_pairs={{0,16},{4,20},{8,24},{12,28},{16,0},{20,4},{24,8},{28,12},{1,17},{... | collective-permute-start | bytes 196616 | tf_op jit(solution)/shard_map/ppermute | solution.py:38
  133.0 12.1 %collective-permute-start.48 = (f32[8,16,128]{2,1,0:T(8,128)S(1)}, f32[8,16,128]{2,1,0:T(8,128)S(1)}, u32[]{:S(2)}, u32[]{:S(2)}) collective-permute-start(f32[8,16,128]{2,1,0:T(8,128)S(1)} %get-tuple-element.156), channel_id=1, source_target_pairs={{0,16},{4,20},{8,24},{12,28},{16,0},{20,4},{24,8},{28,12},{1,17},{... | collective-permute-start | bytes 196616 | tf_op jit(solution)/shard_map/ppermute | solution.py:38
  147.0 9.8 %collective-permute-start.67 = (f32[8,16,128]{2,1,0:T(8,128)S(1)}, f32[8,16,128]{2,1,0:T(8,128)S(1)}, u32[]{:S(2)}, u32[]{:S(2)}) collective-permute-start(f32[8,16,128]{2,1,0:T(8,128)S(1)} %get-tuple-element.77), channel_id=1, source_target_pairs={{0,16},{4,20},{8,24},{12,28},{16,0},{20,4},{24,8},{28,12},{1,17},{... | collective-permute-start | bytes 196616 | tf_op jit(solution)/shard_map/ppermute | solution.py:38
  148.1 11.6 %collective-permute-start.63 = (f32[8,16,128]{2,1,0:T(8,128)S(1)}, f32[8,16,128]{2,1,0:T(8,128)S(1)}, u32[]{:S(2)}, u32[]{:S(2)}) collective-permute-start(f32[8,16,128]{2,1,0:T(8,128)S(1)} %get-tuple-element.76), channel_id=1, source_target_pairs={{0,16},{4,20},{8,24},{12,28},{16,0},{20,4},{24,8},{28,12},{1,17},{... | collective-permute-start | bytes 196616 | tf_op jit(solution)/shard_map/ppermute | solution.py:38
  149.9 11.9 %collective-permute-start.52 = (f32[10,16,128]{2,1,0:T(8,128)S(1)}, f32[10,16,128]{2,1,0:T(8,128)S(1)}, u32[]{:S(2)}, u32[]{:S(2)}) collective-permute-start(f32[10,16,128]{2,1,0:T(8,128)S(1)} %get-tuple-element.74), channel_id=1, source_target_pairs={{0,16},{4,20},{8,24},{12,28},{16,0},{20,4},{24,8},{28,12},{1,17},{... | collective-permute-start | bytes 245768 | tf_op jit(solution)/shard_map/ppermute | solution.py:38
  151.0 10.9 %collective-permute-start.59 = (f32[8,16,128]{2,1,0:T(8,128)S(1)}, f32[8,16,128]{2,1,0:T(8,128)S(1)}, u32[]{:S(2)}, u32[]{:S(2)}) collective-permute-start(f32[8,16,128]{2,1,0:T(8,128)S(1)} %get-tuple-element.75), channel_id=1, source_target_pairs={{0,16},{4,20},{8,24},{12,28},{16,0},{20,4},{24,8},{28,12},{1,17},{... | collective-permute-start | bytes 196616 | tf_op jit(solution)/shard_map/ppermute | solution.py:38
  161.8 10.3 %collective-permute-start.65 = (f32[16,16,128]{2,1,0:T(8,128)S(1)}, f32[16,16,128]{2,1,0:T(8,128)S(1)}, u32[]{:S(2)}, u32[]{:S(2)}) collective-permute-start(f32[16,16,128]{2,1,0:T(8,128)S(1)} %constant_dynamic-update-slice_fusion.2.refs_8_), channel_id=1, source_target_pairs={{0,4},{4,0},{8,12},{12,8},{16,20},{20,16},{24,28},{28,24},{1,5},{5... | collective-permute-start | bytes 393224 | tf_op jit(solution)/shard_map/ppermute | solution.py:38
  162.7 9.4 %collective-permute-start.60 = (f32[16,16,128]{2,1,0:T(8,128)S(1)}, f32[16,16,128]{2,1,0:T(8,128)S(1)}, u32[]{:S(2)}, u32[]{:S(2)}) collective-permute-start(f32[16,16,128]{2,1,0:T(8,128)S(1)} %constant_dynamic-update-slice_fusion.refs_4_), channel_id=1, source_target_pairs={{0,4},{4,0},{8,12},{12,8},{16,20},{20,16},{24,28},{28,24},{1,5},{5... | collective-permute-start | bytes 393224 | tf_op jit(solution)/shard_map/ppermute | solution.py:38
  169.3 9.1 %collective-permute-start.55 = (f32[18,16,128]{2,1,0:T(8,128)S(1)}, f32[18,16,128]{2,1,0:T(8,128)S(1)}, u32[]{:S(2)}, u32[]{:S(2)}) collective-permute-start(f32[18,16,128]{2,1,0:T(8,128)S(1)} %collective-permute-done.53.refs_1_), channel_id=1, source_target_pairs={{0,4},{4,0},{8,12},{12,8},{16,20},{20,16},{24,28},{28,24},{1,5},{5... | collective-permute-start | bytes 442376 | tf_op jit(solution)/shard_map/ppermute | solution.py:38
  184.6 10.5 %collective-permute-start.56 = (f32[32,128]{1,0:T(8,128)S(1)}, f32[32,128]{1,0:T(8,128)S(1)}, u32[]{:S(2)}, u32[]{:S(2)}) collective-permute-start(f32[32,128]{1,0:T(8,128)S(1)} %bitcast.47), channel_id=1, source_target_pairs={{0,2},{1,3},{2,0},{3,1},{4,6},{5,7},{6,4},{7,5},{8,10},{9,11},{10,... | collective-permute-start | bytes 49160 | tf_op jit(solution)/shard_map/ppermute | solution.py:38
  192.7 9.9 %collective-permute-start.78 = (f32[16,16,128]{2,1,0:T(8,128)S(1)}, f32[16,16,128]{2,1,0:T(8,128)S(1)}, u32[]{:S(2)}, u32[]{:S(2)}) collective-permute-start(f32[16,16,128]{2,1,0:T(8,128)S(1)} %get-tuple-element.118), channel_id=1, source_target_pairs={{0,2},{1,3},{2,0},{3,1},{4,6},{5,7},{6,4},{7,5},{8,10},{9,11},{10,... | collective-permute-start | bytes 393224 | tf_op jit(solution)/shard_map/ppermute | solution.py:38
  195.1 9.6 %collective-permute-start.76 = (f32[16,16,128]{2,1,0:T(8,128)S(1)}, f32[16,16,128]{2,1,0:T(8,128)S(1)}, u32[]{:S(2)}, u32[]{:S(2)}) collective-permute-start(f32[16,16,128]{2,1,0:T(8,128)S(1)} %get-tuple-element.122), channel_id=1, source_target_pairs={{0,2},{1,3},{2,0},{3,1},{4,6},{5,7},{6,4},{7,5},{8,10},{9,11},{10,... | collective-permute-start | bytes 393224 | tf_op jit(solution)/shard_map/ppermute | solution.py:38
  197.0 10.0 %collective-permute-start.75 = (f32[16,16,128]{2,1,0:T(8,128)S(1)}, f32[16,16,128]{2,1,0:T(8,128)S(1)}, u32[]{:S(2)}, u32[]{:S(2)}) collective-permute-start(f32[16,16,128]{2,1,0:T(8,128)S(1)} %get-tuple-element.124), channel_id=1, source_target_pairs={{0,2},{1,3},{2,0},{3,1},{4,6},{5,7},{6,4},{7,5},{8,10},{9,11},{10,... | collective-permute-start | bytes 393224 | tf_op jit(solution)/shard_map/ppermute | solution.py:38
  211.6 11.6 %collective-permute-start.79 = (f32[18,16,128]{2,1,0:T(8,128)S(1)}, f32[18,16,128]{2,1,0:T(8,128)S(1)}, u32[]{:S(2)}, u32[]{:S(2)}) collective-permute-start(f32[18,16,128]{2,1,0:T(8,128)S(1)} %get-tuple-element.86.refs_0_), channel_id=1, source_target_pairs={{0,2},{1,3},{2,0},{3,1},{4,6},{5,7},{6,4},{7,5},{8,10},{9,11},{10,... | collective-permute-start | bytes 442376 | tf_op jit(solution)/shard_map/ppermute | solution.py:38
  213.3 9.9 %collective-permute-start.92 = (f32[16,16,128]{2,1,0:T(8,128)S(1)}, f32[16,16,128]{2,1,0:T(8,128)S(1)}, u32[]{:S(2)}, u32[]{:S(2)}) collective-permute-start(f32[16,16,128]{2,1,0:T(8,128)S(1)} %get-tuple-element.90.refs_12_), channel_id=1, source_target_pairs={{0,2},{1,3},{2,0},{3,1},{4,6},{5,7},{6,4},{7,5},{8,10},{9,11},{10,... | collective-permute-start | bytes 393224 | tf_op jit(solution)/shard_map/ppermute | solution.py:38
  213.6 10.1 %collective-permute-start.87 = (f32[16,16,128]{2,1,0:T(8,128)S(1)}, f32[16,16,128]{2,1,0:T(8,128)S(1)}, u32[]{:S(2)}, u32[]{:S(2)}) collective-permute-start(f32[16,16,128]{2,1,0:T(8,128)S(1)} %get-tuple-element.88.refs_4_), channel_id=1, source_target_pairs={{0,1},{1,0},{2,3},{3,2},{4,5},{5,4},{6,7},{7,6},{8,9},{9,8},{10,11... | collective-permute-start | bytes 393224 | tf_op jit(solution)/shard_map/ppermute | solution.py:38
  230.5 40.5 %collective-permute-start.82 = (f32[32,128]{1,0:T(8,128)S(1)}, f32[32,128]{1,0:T(8,128)S(1)}, u32[]{:S(2)}, u32[]{:S(2)}) collective-permute-start(f32[32,128]{1,0:T(8,128)S(1)} %bitcast.44), channel_id=1, source_target_pairs={{0,8},{4,12},{8,0},{12,4},{16,24},{20,28},{24,16},{28,20},{1,9},{5... | collective-permute-start | bytes 49160 | tf_op jit(solution)/shard_map/ppermute | solution.py:38
  232.5 38.6 %collective-permute-start.83 = (f32[32,128]{1,0:T(8,128)S(1)}, f32[32,128]{1,0:T(8,128)S(1)}, u32[]{:S(2)}, u32[]{:S(2)}) collective-permute-start(f32[32,128]{1,0:T(8,128)S(1)} %bitcast.45), channel_id=1, source_target_pairs={{0,4},{4,0},{8,12},{12,8},{16,20},{20,16},{24,28},{28,24},{1,5},{5... | collective-permute-start | bytes 49160 | tf_op jit(solution)/shard_map/ppermute | solution.py:38
  233.5 40.5 %collective-permute-start.84 = (f32[32,128]{1,0:T(8,128)S(1)}, f32[32,128]{1,0:T(8,128)S(1)}, u32[]{:S(2)}, u32[]{:S(2)}) collective-permute-start(f32[32,128]{1,0:T(8,128)S(1)} %bitcast.46), channel_id=1, source_target_pairs={{0,12},{4,8},{8,4},{12,0},{16,28},{20,24},{24,20},{28,16},{1,13},{... | collective-permute-start | bytes 49160 | tf_op jit(solution)/shard_map/ppermute | solution.py:38
  250.3 16.0 %collective-permute-start.96 = (f32[16,16,128]{2,1,0:T(8,128)S(1)}, f32[16,16,128]{2,1,0:T(8,128)S(1)}, u32[]{:S(2)}, u32[]{:S(2)}) collective-permute-start(f32[16,16,128]{2,1,0:T(8,128)S(1)} %get-tuple-element.117), channel_id=1, source_target_pairs={{0,8},{4,12},{8,0},{12,4},{16,24},{20,28},{24,16},{28,20},{1,9},{5... | collective-permute-start | bytes 393224 | tf_op jit(solution)/shard_map/ppermute | solution.py:38
  255.7 29.8 %collective-permute-start.106 = (f32[8,16,128]{2,1,0:T(8,128)S(1)}, f32[8,16,128]{2,1,0:T(8,128)S(1)}, u32[]{:S(2)}, u32[]{:S(2)}) collective-permute-start(f32[8,16,128]{2,1,0:T(8,128)S(1)} %get-tuple-element.143), channel_id=1, source_target_pairs={{0,16},{4,20},{8,24},{12,28},{16,0},{20,4},{24,8},{28,12},{1,17},{... | collective-permute-start | bytes 196616 | tf_op jit(solution)/shard_map/ppermute | solution.py:38
  266.3 19.3 %collective-permute-start.103 = (f32[8,16,128]{2,1,0:T(8,128)S(1)}, f32[8,16,128]{2,1,0:T(8,128)S(1)}, u32[]{:S(2)}, u32[]{:S(2)}) collective-permute-start(f32[8,16,128]{2,1,0:T(8,128)S(1)} %get-tuple-element.145), channel_id=1, source_target_pairs={{0,16},{4,20},{8,24},{12,28},{16,0},{20,4},{24,8},{28,12},{1,17},{... | collective-permute-start | bytes 196616 | tf_op jit(solution)/shard_map/ppermute | solution.py:38
  271.0 14.5 %collective-permute-start.100 = (f32[8,16,128]{2,1,0:T(8,128)S(1)}, f32[8,16,128]{2,1,0:T(8,128)S(1)}, u32[]{:S(2)}, u32[]{:S(2)}) collective-permute-start(f32[8,16,128]{2,1,0:T(8,128)S(1)} %get-tuple-element.147), channel_id=1, source_target_pairs={{0,16},{4,20},{8,24},{12,28},{16,0},{20,4},{24,8},{28,12},{1,17},{... | collective-permute-start | bytes 196616 | tf_op jit(solution)/shard_map/ppermute | solution.py:38
  271.1 14.4 %collective-permute-start.97 = (f32[8,16,128]{2,1,0:T(8,128)S(1)}, f32[8,16,128]{2,1,0:T(8,128)S(1)}, u32[]{:S(2)}, u32[]{:S(2)}) collective-permute-start(f32[8,16,128]{2,1,0:T(8,128)S(1)} %get-tuple-element.149), channel_id=1, source_target_pairs={{0,16},{4,20},{8,24},{12,28},{16,0},{20,4},{24,8},{28,12},{1,17},{... | collective-permute-start | bytes 196616 | tf_op jit(solution)/shard_map/ppermute | solution.py:38
  (67 other events, 458.6 us)

commit v11 on v10

--- a/solution.py
+++ b/solution.py
@@ -9,7 +9,7 @@
 
 
 K = 64
-PARTS = 4
+PARTS = 2
 ROWS = K // PARTS
 TILE = 128
 GRAM = K // 2 // ROWS
@@ -329,7 +329,8 @@
         pieces = gather(sent, "users")
         if step:
             item_inverse = inverse_factor(gram_sum(pieces, "items"), item_total)
-        kept, out = tiles_product(count, col_at, row_to, pieces, tiles, UT, "users", "items", 1)
+        source = tiles if step else pltpu.with_memory_space_constraint(tiles, pltpu.HBM)
+        kept, out = tiles_product(count, col_at, row_to, pieces, source, UT, "users", "items", 1)
         kept, got = reduce_scatter(kept, out, "items")
         user_raw, sent = scale_panel(item_inverse, kept, got, user_scale)
         pieces = gather(sent, "items")

time: 311 us -> 303 us (0.974)
  starting transfers between devices: 129 us -> 84 us
  waiting for transfers between devices: 121 us -> 163 us
  local copies, waits for them, and re-layouts: 5.9 us -> 0.13 us
    ppermute x112 -> x64, starting transfers between devices: 129 us -> 84 us  [exchange(): lax.ppermute(value, axis, [(at, at ^ bit) for at in range(lax.axis_size(a...]
    ppermute x112 -> x64, waiting for transfers between devices: 121 us -> 163 us  [exchange(): lax.ppermute(value, axis, [(at, at ^ bit) for at in range(lax.axis_size(a...]
    unnamed x10 -> x6, local copies, waits for them, and re-layouts: 5.84 us -> 0.07 us
  transfers between devices with their start and end apart: 112 -> 64, of which waited for: 55 -> 37; matrix products, arithmetic and copies ran while one was open for 1% -> 1% of each run, Pallas kernels for 6% -> 6%
where the time goes in v11:
time: 303 us
  waiting for transfers between devices  163 us (54%)
  starting transfers between devices  84 us (28%)
  Pallas kernels  50.3 us (17%)
  other arithmetic  3.47 us (1%)
    ppermute x64, waiting for transfers between devices, exchange(): lax.ppermute(value, axis, [(at, at ^ bit) for at in range(lax.axis_size(a...  163 us
    ppermute x64, starting transfers between devices, exchange(): lax.ppermute(value, axis, [(at, at ^ bit) for at in range(lax.axis_size(a...  84 us
    pallas_call x4, Pallas kernels, inverse_factor(): pl.pallas_call(functools.partial(factor_kernel, total=total), out_shape=p...  21.7 us
    pallas_call x4, Pallas kernels, tiles_product(): call(count, source, target, *[in_vmem(piece) for part in pieces for piece...  18.4 us
    pallas_call x4, Pallas kernels, scale_panel(): pl.pallas_call(functools.partial(scale_kernel, factored=factored), out_sh...  7.68 us
  transfers between devices with their start and end apart: 64, of which 37 were waited for; matrix products, arithmetic and copies ran while one was open for 1% of the time, Pallas kernels for 6%

profile of v11, /device:TPU:0, one launch (start us, length us, event | category | flops | bytes accessed | tf_op | source)
XLA Modules:
  0.0 302.6 jit_solution(17350880042152623564)
XLA Ops:
  2.4 4.1 %collective-permute-start = (f32[9,32,128]{2,1,0:T(8,128)S(1)}, f32[9,32,128]{2,1,0:T(8,128)S(1)}, u32[]{:S(2)}, u32[]{:S(2)}) collective-permute-start(f32[9,32,128]{2,1,0:T(8,128)S(1)} %concatenate.15), channel_id=1, source_target_pairs={{0,16},{4,20},{8,24},{12,28},{16,0},{20,4},{24,8},{28,12},{1,17},{... | collective-permute-start | bytes 442376 | tf_op jit(solution)/shard_map/ppermute | solution.py:38
  6.6 10.6 %collective-permute-done = f32[9,32,128]{2,1,0:T(8,128)S(1)} collective-permute-done((f32[9,32,128]{2,1,0:T(8,128)S(1)}, f32[9,32,128]{2,1,0:T(8,128)S(1)}, u32[]{:S(2)}, u32[]{:S(2)}) %collective-permute-start) | collective-permute-done | bytes 147488 | tf_op jit(solution)/shard_map/ppermute | solution.py:38
  17.3 1.9 collective-permute-done.4
  21.4 3.8 %collective-permute-done.1.refs_1_ = f32[17,32,128]{2,1,0:T(8,128)S(1)} collective-permute-done((f32[17,32,128]{2,1,0:T(8,128)S(1)}, f32[17,32,128]{2,1,0:T(8,128)S(1)}, u32[]{:S(2)}, u32[]{:S(2)}) %collective-permute-start.1) | collective-permute-done | bytes 278560 | tf_op jit(solution)/shard_map/ppermute | solution.py:38
  30.7 4.9 %collective-permute-done.6.refs_6_ = f32[16,32,128]{2,1,0:T(8,128)S(1)} collective-permute-done((f32[16,32,128]{2,1,0:T(8,128)S(1)}, f32[16,32,128]{2,1,0:T(8,128)S(1)}, u32[]{:S(2)}, u32[]{:S(2)}) %collective-permute-start.6) | collective-permute-done | bytes 262176 | tf_op jit(solution)/shard_map/ppermute | solution.py:38
  35.6 2.8 collective-permute-done.7.refs_7_
  38.7 6.6 %shard_map.86 = (f32[32,32,128]{2,1,0:T(8,128)S(1)}, f32[32,32,128]{2,1,0:T(8,128)S(1)}, f32[32,32,128]{2,1,0:T(8,128)S(1)}, f32[32,32,128]{2,1,0:T(8,128)S(1)}) custom-call(s32[1]{0:T(128)} %bitcast.29.count, s32[512]{0:T(512)S(1)} %get-tuple-element.59.source, s32[512]{0:T(512)S(1)} %get-tuple-element.88.target, ...), custom_call_target="tpu_custom_call" | custom-call | tf_op jit(solution)/shard_map/pallas_call | solution.py:203
  47.3 10.7 %collective-permute-start.11 = (f32[16,32,128]{2,1,0:T(8,128)S(1)}, f32[16,32,128]{2,1,0:T(8,128)S(1)}, u32[]{:S(2)}, u32[]{:S(2)}) collective-permute-start(f32[16,32,128]{2,1,0:T(8,128)S(1)} %get-tuple-element.74), channel_id=1, source_target_pairs={{0,2},{1,3},{2,0},{3,1},{4,6},{5,7},{6,4},{7,5},{8,10},{9,11},{10,... | collective-permute-start | bytes 786440 | tf_op jit(solution)/shard_map/ppermute | solution.py:38
  58.8 6.4 %collective-permute-done.11.refs_3_ = f32[16,32,128]{2,1,0:T(8,128)S(1)} collective-permute-done((f32[16,32,128]{2,1,0:T(8,128)S(1)}, f32[16,32,128]{2,1,0:T(8,128)S(1)}, u32[]{:S(2)}, u32[]{:S(2)}) %collective-permute-start.11) | collective-permute-done | bytes 262176 | tf_op jit(solution)/shard_map/ppermute | solution.py:38
  65.2 5.1 %collective-permute-done.10.refs_2_ = f32[16,32,128]{2,1,0:T(8,128)S(1)} collective-permute-done((f32[16,32,128]{2,1,0:T(8,128)S(1)}, f32[16,32,128]{2,1,0:T(8,128)S(1)}, u32[]{:S(2)}, u32[]{:S(2)}) %collective-permute-start.10) | collective-permute-done | bytes 262176 | tf_op jit(solution)/shard_map/ppermute | solution.py:38
  73.7 7.5 %collective-permute-done.12.refs_1_ = f32[17,32,128]{2,1,0:T(8,128)S(1)} collective-permute-done((f32[17,32,128]{2,1,0:T(8,128)S(1)}, f32[17,32,128]{2,1,0:T(8,128)S(1)}, u32[]{:S(2)}, u32[]{:S(2)}) %collective-permute-start.12) | collective-permute-done | bytes 278560 | tf_op jit(solution)/shard_map/ppermute | solution.py:38
  81.7 3.7 %collective-permute-done.19.refs_5_ = f32[16,32,128]{2,1,0:T(8,128)S(1)} collective-permute-done((f32[16,32,128]{2,1,0:T(8,128)S(1)}, f32[16,32,128]{2,1,0:T(8,128)S(1)}, u32[]{:S(2)}, u32[]{:S(2)}) %collective-permute-start.19) | collective-permute-done | bytes 262176 | tf_op jit(solution)/shard_map/ppermute | solution.py:38
  87.0 3.3 %shard_map.87 = (f32[32,32,128]{2,1,0:T(8,128)S(1)}, f32[32,32,128]{2,1,0:T(8,128)S(1)}, f32[32,32,128]{2,1,0:T(8,128)S(1)}, f32[32,32,128]{2,1,0:T(8,128)S(1)}) custom-call(s32[1]{0:T(128)} %bitcast.30.count, s32[512]{0:T(512)S(1)} %get-tuple-element.89.source, s32[512]{0:T(512)S(1)} %get-tuple-element.58.target, ...), custom_call_target="tpu_custom_call" | custom-call | tf_op jit(solution)/shard_map/pallas_call | solution.py:203
  90.6 11.7 %collective-permute-done.24 = f32[32,32,128]{2,1,0:T(8,128)S(1)} collective-permute-done((f32[32,32,128]{2,1,0:T(8,128)S(1)}, f32[32,32,128]{2,1,0:T(8,128)S(1)}, u32[]{:S(2)}, u32[]{:S(2)}) %collective-permute-start.24) | collective-permute-done | bytes 524320 | tf_op jit(solution)/shard_map/ppermute | solution.py:38
  102.5 2.1 collective-permute-start.23
  104.8 1.9 collective-permute-start.16
  109.9 10.5 %collective-permute-start.27 = (f32[8,32,128]{2,1,0:T(8,128)S(1)}, f32[8,32,128]{2,1,0:T(8,128)S(1)}, u32[]{:S(2)}, u32[]{:S(2)}) collective-permute-start(f32[8,32,128]{2,1,0:T(8,128)S(1)} %get-tuple-element.82), channel_id=1, source_target_pairs={{0,16},{4,20},{8,24},{12,28},{16,0},{20,4},{24,8},{28,12},{1,17},{... | collective-permute-start | bytes 393224 | tf_op jit(solution)/shard_map/ppermute | solution.py:38
  123.5 8.1 %collective-permute-done.18 = f32[32,128]{1,0:T(8,128)S(1)} collective-permute-done((f32[32,128]{1,0:T(8,128)S(1)}, f32[32,128]{1,0:T(8,128)S(1)}, u32[]{:S(2)}, u32[]{:S(2)}) %collective-permute-start.18) | collective-permute-done | bytes 16416 | tf_op jit(solution)/shard_map/ppermute | solution.py:38
  131.6 5.4 %factor.4.refs_0_ = f32[64,64]{1,0:T(8,128)S(1)} custom-call(f32[32,128]{1,0:T(8,128)S(1)} %add.212.gram_ref), custom_call_target="tpu_custom_call" | custom-call | tf_op jit(solution)/shard_map/factor/pallas_call | solution.py:239
  137.1 1.8 scale_panel.5
  138.9 3.0 collective-permute-start.35
  141.9 9.7 %collective-permute-done.28 = f32[9,32,128]{2,1,0:T(8,128)S(1)} collective-permute-done((f32[9,32,128]{2,1,0:T(8,128)S(1)}, f32[9,32,128]{2,1,0:T(8,128)S(1)}, u32[]{:S(2)}, u32[]{:S(2)}) %collective-permute-start.28) | collective-permute-done | bytes 147488 | tf_op jit(solution)/shard_map/ppermute | solution.py:38
  155.1 3.8 %collective-permute-done.29.refs_1_ = f32[17,32,128]{2,1,0:T(8,128)S(1)} collective-permute-done((f32[17,32,128]{2,1,0:T(8,128)S(1)}, f32[17,32,128]{2,1,0:T(8,128)S(1)}, u32[]{:S(2)}, u32[]{:S(2)}) %collective-permute-start.29) | collective-permute-done | bytes 278560 | tf_op jit(solution)/shard_map/ppermute | solution.py:38
  159.6 2.7 collective-permute-done.36.refs_5_
  163.0 5.0 %collective-permute-done.37.refs_6_ = f32[16,32,128]{2,1,0:T(8,128)S(1)} collective-permute-done((f32[16,32,128]{2,1,0:T(8,128)S(1)}, f32[16,32,128]{2,1,0:T(8,128)S(1)}, u32[]{:S(2)}, u32[]{:S(2)}) %collective-permute-start.37) | collective-permute-done | bytes 262176 | tf_op jit(solution)/shard_map/ppermute | solution.py:38
  168.3 2.6 collective-permute-done.38.refs_7_
  171.3 5.2 %shard_map.88 = (f32[32,32,128]{2,1,0:T(8,128)S(1)}, f32[32,32,128]{2,1,0:T(8,128)S(1)}, f32[32,32,128]{2,1,0:T(8,128)S(1)}, f32[32,32,128]{2,1,0:T(8,128)S(1)}) custom-call(s32[1]{0:T(128)} %bitcast.31.count, s32[512]{0:T(512)S(1)} %get-tuple-element.59.source, s32[512]{0:T(512)S(1)} %get-tuple-element.88.target, ...), custom_call_target="tpu_custom_call" | custom-call | tf_op jit(solution)/shard_map/pallas_call | solution.py:203
  178.6 10.6 %collective-permute-start.42 = (f32[16,32,128]{2,1,0:T(8,128)S(1)}, f32[16,32,128]{2,1,0:T(8,128)S(1)}, u32[]{:S(2)}, u32[]{:S(2)}) collective-permute-start(f32[16,32,128]{2,1,0:T(8,128)S(1)} %get-tuple-element.66), channel_id=1, source_target_pairs={{0,2},{1,3},{2,0},{3,1},{4,6},{5,7},{6,4},{7,5},{8,10},{9,11},{10,... | collective-permute-start | bytes 786440 | tf_op jit(solution)/shard_map/ppermute | solution.py:38
  192.0 9.9 %collective-permute-done.32 = f32[32,128]{1,0:T(8,128)S(1)} collective-permute-done((f32[32,128]{1,0:T(8,128)S(1)}, f32[32,128]{1,0:T(8,128)S(1)}, u32[]{:S(2)}, u32[]{:S(2)}) %collective-permute-start.32) | collective-permute-done | bytes 16416 | tf_op jit(solution)/shard_map/ppermute | solution.py:38
  201.9 5.4 %factor.5.refs_0_ = f32[64,64]{1,0:T(8,128)S(1)} custom-call(f32[32,128]{1,0:T(8,128)S(1)} %add_add_fusion.1.gram_ref), custom_call_target="tpu_custom_call" | custom-call | tf_op jit(solution)/shard_map/factor/pallas_call | solution.py:239
  207.3 2.6 scale_panel.6
  210.0 1.8 collective-permute-start.43
  212.0 7.5 %collective-permute-done.43.refs_1_ = f32[17,32,128]{2,1,0:T(8,128)S(1)} collective-permute-done((f32[17,32,128]{2,1,0:T(8,128)S(1)}, f32[17,32,128]{2,1,0:T(8,128)S(1)}, u32[]{:S(2)}, u32[]{:S(2)}) %collective-permute-start.43) | collective-permute-done | bytes 278560 | tf_op jit(solution)/shard_map/ppermute | solution.py:38
  220.0 4.2 %collective-permute-done.50.refs_5_ = f32[16,32,128]{2,1,0:T(8,128)S(1)} collective-permute-done((f32[16,32,128]{2,1,0:T(8,128)S(1)}, f32[16,32,128]{2,1,0:T(8,128)S(1)}, u32[]{:S(2)}, u32[]{:S(2)}) %collective-permute-start.50) | collective-permute-done | bytes 262176 | tf_op jit(solution)/shard_map/ppermute | solution.py:38
  225.8 3.3 %shard_map.89 = (f32[32,32,128]{2,1,0:T(8,128)S(1)}, f32[32,32,128]{2,1,0:T(8,128)S(1)}, f32[32,32,128]{2,1,0:T(8,128)S(1)}, f32[32,32,128]{2,1,0:T(8,128)S(1)}) custom-call(s32[1]{0:T(128)} %bitcast.32.count, s32[512]{0:T(512)S(1)} %get-tuple-element.89.source, s32[512]{0:T(512)S(1)} %get-tuple-element.58.target, ...), custom_call_target="tpu_custom_call" | custom-call | tf_op jit(solution)/shard_map/pallas_call | solution.py:203
  229.6 13.8 %collective-permute-done.56 = f32[32,32,128]{2,1,0:T(8,128)S(1)} collective-permute-done((f32[32,32,128]{2,1,0:T(8,128)S(1)}, f32[32,32,128]{2,1,0:T(8,128)S(1)}, u32[]{:S(2)}, u32[]{:S(2)}) %collective-permute-start.56) | collective-permute-done | bytes 524320 | tf_op jit(solution)/shard_map/ppermute | solution.py:38
  245.8 2.0 collective-permute-start.47
  247.8 4.5 %collective-permute-done.57 = f32[16,32,128]{2,1,0:T(8,128)S(1)} collective-permute-done((f32[16,32,128]{2,1,0:T(8,128)S(1)}, f32[16,32,128]{2,1,0:T(8,128)S(1)}, u32[]{:S(2)}, u32[]{:S(2)}) %collective-permute-start.57) | collective-permute-done | bytes 262176 | tf_op jit(solution)/shard_map/ppermute | solution.py:38
  252.4 6.9 %collective-permute-start.58 = (f32[8,32,128]{2,1,0:T(8,128)S(1)}, f32[8,32,128]{2,1,0:T(8,128)S(1)}, u32[]{:S(2)}, u32[]{:S(2)}) collective-permute-start(f32[8,32,128]{2,1,0:T(8,128)S(1)} %get-tuple-element.79), channel_id=1, source_target_pairs={{0,16},{4,20},{8,24},{12,28},{16,0},{20,4},{24,8},{28,12},{1,17},{... | collective-permute-start | bytes 393224 | tf_op jit(solution)/shard_map/ppermute | solution.py:38
  260.6 1.8 collective-permute-start.49
  262.4 8.0 %collective-permute-done.49 = f32[32,128]{1,0:T(8,128)S(1)} collective-permute-done((f32[32,128]{1,0:T(8,128)S(1)}, f32[32,128]{1,0:T(8,128)S(1)}, u32[]{:S(2)}, u32[]{:S(2)}) %collective-permute-start.49) | collective-permute-done | bytes 16416 | tf_op jit(solution)/shard_map/ppermute | solution.py:38
  270.4 5.4 %factor.6.inverse_ref.refs_0_ = f32[64,64]{1,0:T(8,128)S(1)} custom-call(f32[32,128]{1,0:T(8,128)S(1)} %add.240.gram_ref), custom_call_target="tpu_custom_call" | custom-call | tf_op jit(solution)/shard_map/factor/pallas_call | solution.py:239
  280.8 3.1 %collective-permute-done.60 = f32[32,128]{1,0:T(8,128)S(1)} collective-permute-done((f32[32,128]{1,0:T(8,128)S(1)}, f32[32,128]{1,0:T(8,128)S(1)}, u32[]{:S(2)}, u32[]{:S(2)}) %collective-permute-start.60) | collective-permute-done | bytes 16416 | tf_op jit(solution)/shard_map/ppermute | solution.py:38
  284.5 3.2 %collective-permute-done.61 = f32[32,128]{1,0:T(8,128)S(1)} collective-permute-done((f32[32,128]{1,0:T(8,128)S(1)}, f32[32,128]{1,0:T(8,128)S(1)}, u32[]{:S(2)}, u32[]{:S(2)}) %collective-permute-start.61) | collective-permute-done | bytes 16416 | tf_op jit(solution)/shard_map/ppermute | solution.py:38
  288.1 3.3 %collective-permute-done.62 = f32[32,128]{1,0:T(8,128)S(1)} collective-permute-done((f32[32,128]{1,0:T(8,128)S(1)}, f32[32,128]{1,0:T(8,128)S(1)}, u32[]{:S(2)}, u32[]{:S(2)}) %collective-permute-start.62) | collective-permute-done | bytes 16416 | tf_op jit(solution)/shard_map/ppermute | solution.py:38
  291.4 1.8 collective-permute-start.63
  293.2 2.8 collective-permute-done.63
  296.1 5.4 %factor.7.inverse_ref = f32[64,64]{1,0:T(8,128)S(1)} custom-call(f32[32,128]{1,0:T(8,128)S(1)} %add.253.gram_ref), custom_call_target="tpu_custom_call" | custom-call | tf_op jit(solution)/shard_map/factor/pallas_call | solution.py:239
  (140 shorter events, 48.5 us)
Async XLA Ops:
  2.4 14.8 %collective-permute-start = (f32[9,32,128]{2,1,0:T(8,128)S(1)}, f32[9,32,128]{2,1,0:T(8,128)S(1)}, u32[]{:S(2)}, u32[]{:S(2)}) collective-permute-start(f32[9,32,128]{2,1,0:T(8,128)S(1)} %concatenate.15), channel_id=1, source_target_pairs={{0,16},{4,20},{8,24},{12,28},{16,0},{20,4},{24,8},{28,12},{1,17},{... | collective-permute-start | bytes 442376 | tf_op jit(solution)/shard_map/ppermute | solution.py:38
  6.6 12.7 %collective-permute-start.4 = (f32[8,32,128]{2,1,0:T(8,128)S(1)}, f32[8,32,128]{2,1,0:T(8,128)S(1)}, u32[]{:S(2)}, u32[]{:S(2)}) collective-permute-start(f32[8,32,128]{2,1,0:T(8,128)S(1)} %get-tuple-element.86), channel_id=1, source_target_pairs={{0,16},{4,20},{8,24},{12,28},{16,0},{20,4},{24,8},{28,12},{1,17},{... | collective-permute-start | bytes 393224 | tf_op jit(solution)/shard_map/ppermute | solution.py:38
  19.3 9.2 %collective-permute-start.5 = (f32[16,32,128]{2,1,0:T(8,128)S(1)}, f32[16,32,128]{2,1,0:T(8,128)S(1)}, u32[]{:S(2)}, u32[]{:S(2)}) collective-permute-start(f32[16,32,128]{2,1,0:T(8,128)S(1)} %pad_maximum_fusion.2.refs_4_), channel_id=1, source_target_pairs={{0,4},{4,0},{8,12},{12,8},{16,20},{20,16},{24,28},{28,24},{1,5},{5... | collective-permute-start | bytes 786440 | tf_op jit(solution)/shard_map/ppermute | solution.py:38
  20.9 14.7 %collective-permute-start.2 = (f32[17,32,128]{2,1,0:T(8,128)S(1)}, f32[17,32,128]{2,1,0:T(8,128)S(1)}, u32[]{:S(2)}, u32[]{:S(2)}) collective-permute-start(f32[17,32,128]{2,1,0:T(8,128)S(1)} %pad_maximum_fusion.refs_0_), channel_id=1, source_target_pairs={{0,4},{4,0},{8,12},{12,8},{16,20},{20,16},{24,28},{28,24},{1,5},{5... | collective-permute-start | bytes 835592 | tf_op jit(solution)/shard_map/ppermute | solution.py:38
  25.2 13.5 %collective-permute-start.3 = (f32[17,32,128]{2,1,0:T(8,128)S(1)}, f32[17,32,128]{2,1,0:T(8,128)S(1)}, u32[]{:S(2)}, u32[]{:S(2)}) collective-permute-start(f32[17,32,128]{2,1,0:T(8,128)S(1)} %collective-permute-done.1.refs_1_), channel_id=1, source_target_pairs={{0,4},{4,0},{8,12},{12,8},{16,20},{20,16},{24,28},{28,24},{1,5},{5... | collective-permute-start | bytes 835592 | tf_op jit(solution)/shard_map/ppermute | solution.py:38
  26.7 8.9 %collective-permute-start.6 = (f32[16,32,128]{2,1,0:T(8,128)S(1)}, f32[16,32,128]{2,1,0:T(8,128)S(1)}, u32[]{:S(2)}, u32[]{:S(2)}) collective-permute-start(f32[16,32,128]{2,1,0:T(8,128)S(1)} %pad_maximum_fusion.2.refs_4_), channel_id=1, source_target_pairs={{0,8},{4,12},{8,0},{12,4},{16,24},{20,28},{24,16},{28,20},{1,9},{5... | collective-permute-start | bytes 786440 | tf_op jit(solution)/shard_map/ppermute | solution.py:38
  28.5 9.9 %collective-permute-start.7 = (f32[16,32,128]{2,1,0:T(8,128)S(1)}, f32[16,32,128]{2,1,0:T(8,128)S(1)}, u32[]{:S(2)}, u32[]{:S(2)}) collective-permute-start(f32[16,32,128]{2,1,0:T(8,128)S(1)} %collective-permute-done.5.refs_5_), channel_id=1, source_target_pairs={{0,8},{4,12},{8,0},{12,4},{16,24},{20,28},{24,16},{28,20},{1,9},{5... | collective-permute-start | bytes 786440 | tf_op jit(solution)/shard_map/ppermute | solution.py:38
  45.3 12.7 %collective-permute-start.8 = (f32[32,32,128]{2,1,0:T(8,128)S(1)}, f32[32,32,128]{2,1,0:T(8,128)S(1)}, u32[]{:S(2)}, u32[]{:S(2)}) collective-permute-start(f32[32,32,128]{2,1,0:T(8,128)S(1)} %get-tuple-element.31), channel_id=1, source_target_pairs={{0,1},{1,0},{2,3},{3,2},{4,5},{5,4},{6,7},{7,6},{8,9},{9,8},{10,11... | collective-permute-start | bytes 1572872 | tf_op jit(solution)/shard_map/ppermute | solution.py:38
  47.3 17.8 %collective-permute-start.11 = (f32[16,32,128]{2,1,0:T(8,128)S(1)}, f32[16,32,128]{2,1,0:T(8,128)S(1)}, u32[]{:S(2)}, u32[]{:S(2)}) collective-permute-start(f32[16,32,128]{2,1,0:T(8,128)S(1)} %get-tuple-element.74), channel_id=1, source_target_pairs={{0,2},{1,3},{2,0},{3,1},{4,6},{5,7},{6,4},{7,5},{8,10},{9,11},{10,... | collective-permute-start | bytes 786440 | tf_op jit(solution)/shard_map/ppermute | solution.py:38
  58.1 12.1 %collective-permute-start.10 = (f32[16,32,128]{2,1,0:T(8,128)S(1)}, f32[16,32,128]{2,1,0:T(8,128)S(1)}, u32[]{:S(2)}, u32[]{:S(2)}) collective-permute-start(f32[16,32,128]{2,1,0:T(8,128)S(1)} %get-tuple-element.76), channel_id=1, source_target_pairs={{0,2},{1,3},{2,0},{3,1},{4,6},{5,7},{6,4},{7,5},{8,10},{9,11},{10,... | collective-permute-start | bytes 786440 | tf_op jit(solution)/shard_map/ppermute | solution.py:38
  71.7 9.5 %collective-permute-start.12 = (f32[17,32,128]{2,1,0:T(8,128)S(1)}, f32[17,32,128]{2,1,0:T(8,128)S(1)}, u32[]{:S(2)}, u32[]{:S(2)}) collective-permute-start(f32[17,32,128]{2,1,0:T(8,128)S(1)} %get-tuple-element.34.refs_0_), channel_id=1, source_target_pairs={{0,2},{1,3},{2,0},{3,1},{4,6},{5,7},{6,4},{7,5},{8,10},{9,11},{10,... | collective-permute-start | bytes 835592 | tf_op jit(solution)/shard_map/ppermute | solution.py:38
  73.4 12.0 %collective-permute-start.19 = (f32[16,32,128]{2,1,0:T(8,128)S(1)}, f32[16,32,128]{2,1,0:T(8,128)S(1)}, u32[]{:S(2)}, u32[]{:S(2)}) collective-permute-start(f32[16,32,128]{2,1,0:T(8,128)S(1)} %get-tuple-element.35.refs_4_), channel_id=1, source_target_pairs={{0,2},{1,3},{2,0},{3,1},{4,6},{5,7},{6,4},{7,5},{8,10},{9,11},{10,... | collective-permute-start | bytes 786440 | tf_op jit(solution)/shard_map/ppermute | solution.py:38
  73.7 11.7 %collective-permute-start.13 = (f32[17,32,128]{2,1,0:T(8,128)S(1)}, f32[17,32,128]{2,1,0:T(8,128)S(1)}, u32[]{:S(2)}, u32[]{:S(2)}) collective-permute-start(f32[17,32,128]{2,1,0:T(8,128)S(1)} %get-tuple-element.34.refs_0_), channel_id=1, source_target_pairs={{0,1},{1,0},{2,3},{3,2},{4,5},{5,4},{6,7},{7,6},{8,9},{9,8},{10,11... | collective-permute-start | bytes 835592 | tf_op jit(solution)/shard_map/ppermute | solution.py:38
  90.3 11.9 %collective-permute-start.24 = (f32[32,32,128]{2,1,0:T(8,128)S(1)}, f32[32,32,128]{2,1,0:T(8,128)S(1)}, u32[]{:S(2)}, u32[]{:S(2)}) collective-permute-start(f32[32,32,128]{2,1,0:T(8,128)S(1)} %get-tuple-element.39), channel_id=1, source_target_pairs={{0,8},{4,12},{8,0},{12,4},{16,24},{20,28},{24,16},{28,20},{1,9},{5... | collective-permute-start | bytes 1572872 | tf_op jit(solution)/shard_map/ppermute | solution.py:38
  90.6 11.9 %collective-permute-start.22 = (f32[32,32,128]{2,1,0:T(8,128)S(1)}, f32[32,32,128]{2,1,0:T(8,128)S(1)}, u32[]{:S(2)}, u32[]{:S(2)}) collective-permute-start(f32[32,32,128]{2,1,0:T(8,128)S(1)} %get-tuple-element.37), channel_id=1, source_target_pairs={{0,4},{4,0},{8,12},{12,8},{16,20},{20,16},{24,28},{28,24},{1,5},{5... | collective-permute-start | bytes 1572872 | tf_op jit(solution)/shard_map/ppermute | solution.py:38
  102.5 17.8 %collective-permute-start.23 = (f32[16,32,128]{2,1,0:T(8,128)S(1)}, f32[16,32,128]{2,1,0:T(8,128)S(1)}, u32[]{:S(2)}, u32[]{:S(2)}) collective-permute-start(f32[16,32,128]{2,1,0:T(8,128)S(1)} %get-tuple-element.73), channel_id=1, source_target_pairs={{0,8},{4,12},{8,0},{12,4},{16,24},{20,28},{24,16},{28,20},{1,9},{5... | collective-permute-start | bytes 786440 | tf_op jit(solution)/shard_map/ppermute | solution.py:38
  104.7 17.2 %collective-permute-start.15 = (f32[32,128]{1,0:T(8,128)S(1)}, f32[32,128]{1,0:T(8,128)S(1)}, u32[]{:S(2)}, u32[]{:S(2)}) collective-permute-start(f32[32,128]{1,0:T(8,128)S(1)} %fusion.6), channel_id=1, source_target_pairs={{0,8},{4,12},{8,0},{12,4},{16,24},{20,28},{24,16},{28,20},{1,9},{5... | collective-permute-start | bytes 49160 | tf_op jit(solution)/shard_map/ppermute | solution.py:38
  104.8 17.2 %collective-permute-start.16 = (f32[32,128]{1,0:T(8,128)S(1)}, f32[32,128]{1,0:T(8,128)S(1)}, u32[]{:S(2)}, u32[]{:S(2)}) collective-permute-start(f32[32,128]{1,0:T(8,128)S(1)} %fusion.6), channel_id=1, source_target_pairs={{0,4},{4,0},{8,12},{12,8},{16,20},{20,16},{24,28},{28,24},{1,5},{5... | collective-permute-start | bytes 49160 | tf_op jit(solution)/shard_map/ppermute | solution.py:38
  106.6 15.3 %collective-permute-start.17 = (f32[32,128]{1,0:T(8,128)S(1)}, f32[32,128]{1,0:T(8,128)S(1)}, u32[]{:S(2)}, u32[]{:S(2)}) collective-permute-start(f32[32,128]{1,0:T(8,128)S(1)} %fusion.6), channel_id=1, source_target_pairs={{0,12},{4,8},{8,4},{12,0},{16,28},{20,24},{24,20},{28,16},{1,13},{... | collective-permute-start | bytes 49160 | tf_op jit(solution)/shard_map/ppermute | solution.py:38
  109.9 27.2 %collective-permute-start.27 = (f32[8,32,128]{2,1,0:T(8,128)S(1)}, f32[8,32,128]{2,1,0:T(8,128)S(1)}, u32[]{:S(2)}, u32[]{:S(2)}) collective-permute-start(f32[8,32,128]{2,1,0:T(8,128)S(1)} %get-tuple-element.82), channel_id=1, source_target_pairs={{0,16},{4,20},{8,24},{12,28},{16,0},{20,4},{24,8},{28,12},{1,17},{... | collective-permute-start | bytes 393224 | tf_op jit(solution)/shard_map/ppermute | solution.py:38
  120.4 16.7 %collective-permute-start.26 = (f32[8,32,128]{2,1,0:T(8,128)S(1)}, f32[8,32,128]{2,1,0:T(8,128)S(1)}, u32[]{:S(2)}, u32[]{:S(2)}) collective-permute-start(f32[8,32,128]{2,1,0:T(8,128)S(1)} %get-tuple-element.84), channel_id=1, source_target_pairs={{0,16},{4,20},{8,24},{12,28},{16,0},{20,4},{24,8},{28,12},{1,17},{... | collective-permute-start | bytes 393224 | tf_op jit(solution)/shard_map/ppermute | solution.py:38
  121.9 9.7 %collective-permute-start.18 = (f32[32,128]{1,0:T(8,128)S(1)}, f32[32,128]{1,0:T(8,128)S(1)}, u32[]{:S(2)}, u32[]{:S(2)}) collective-permute-start(f32[32,128]{1,0:T(8,128)S(1)} %add_add_fusion.2), channel_id=1, source_target_pairs={{0,16},{4,20},{8,24},{12,28},{16,0},{20,4},{24,8},{28,12},{1,17},{... | collective-permute-start | bytes 49160 | tf_op jit(solution)/shard_map/ppermute | solution.py:38
  138.9 12.8 %collective-permute-start.28 = (f32[9,32,128]{2,1,0:T(8,128)S(1)}, f32[9,32,128]{2,1,0:T(8,128)S(1)}, u32[]{:S(2)}, u32[]{:S(2)}) collective-permute-start(f32[9,32,128]{2,1,0:T(8,128)S(1)} %get-tuple-element.40), channel_id=1, source_target_pairs={{0,16},{4,20},{8,24},{12,28},{16,0},{20,4},{24,8},{28,12},{1,17},{... | collective-permute-start | bytes 442376 | tf_op jit(solution)/shard_map/ppermute | solution.py:38
  138.9 14.1 %collective-permute-start.35 = (f32[8,32,128]{2,1,0:T(8,128)S(1)}, f32[8,32,128]{2,1,0:T(8,128)S(1)}, u32[]{:S(2)}, u32[]{:S(2)}) collective-permute-start(f32[8,32,128]{2,1,0:T(8,128)S(1)} %get-tuple-element.41), channel_id=1, source_target_pairs={{0,16},{4,20},{8,24},{12,28},{16,0},{20,4},{24,8},{28,12},{1,17},{... | collective-permute-start | bytes 393224 | tf_op jit(solution)/shard_map/ppermute | solution.py:38
  153.1 9.2 %collective-permute-start.36 = (f32[16,32,128]{2,1,0:T(8,128)S(1)}, f32[16,32,128]{2,1,0:T(8,128)S(1)}, u32[]{:S(2)}, u32[]{:S(2)}) collective-permute-start(f32[16,32,128]{2,1,0:T(8,128)S(1)} %constant_dynamic-update-slice_fusion.refs_4_), channel_id=1, source_target_pairs={{0,4},{4,0},{8,12},{12,8},{16,20},{20,16},{24,28},{28,24},{1,5},{5... | collective-permute-start | bytes 786440 | tf_op jit(solution)/shard_map/ppermute | solution.py:38
  153.8 14.5 %collective-permute-start.30 = (f32[17,32,128]{2,1,0:T(8,128)S(1)}, f32[17,32,128]{2,1,0:T(8,128)S(1)}, u32[]{:S(2)}, u32[]{:S(2)}) collective-permute-start(f32[17,32,128]{2,1,0:T(8,128)S(1)} %pad_maximum_fusion.1.refs_0_), channel_id=1, source_target_pairs={{0,4},{4,0},{8,12},{12,8},{16,20},{20,16},{24,28},{28,24},{1,5},{5... | collective-permute-start | bytes 835592 | tf_op jit(solution)/shard_map/ppermute | solution.py:38
  158.9 12.4 %collective-permute-start.31 = (f32[17,32,128]{2,1,0:T(8,128)S(1)}, f32[17,32,128]{2,1,0:T(8,128)S(1)}, u32[]{:S(2)}, u32[]{:S(2)}) collective-permute-start(f32[17,32,128]{2,1,0:T(8,128)S(1)} %collective-permute-done.29.refs_1_), channel_id=1, source_target_pairs={{0,4},{4,0},{8,12},{12,8},{16,20},{20,16},{24,28},{28,24},{1,5},{5... | collective-permute-start | bytes 835592 | tf_op jit(solution)/shard_map/ppermute | solution.py:38
  159.5 8.5 %collective-permute-start.37 = (f32[16,32,128]{2,1,0:T(8,128)S(1)}, f32[16,32,128]{2,1,0:T(8,128)S(1)}, u32[]{:S(2)}, u32[]{:S(2)}) collective-permute-start(f32[16,32,128]{2,1,0:T(8,128)S(1)} %constant_dynamic-update-slice_fusion.refs_4_), channel_id=1, source_target_pairs={{0,8},{4,12},{8,0},{12,4},{16,24},{20,28},{24,16},{28,20},{1,9},{5... | collective-permute-start | bytes 786440 | tf_op jit(solution)/shard_map/ppermute | solution.py:38
  162.3 8.5 %collective-permute-start.38 = (f32[16,32,128]{2,1,0:T(8,128)S(1)}, f32[16,32,128]{2,1,0:T(8,128)S(1)}, u32[]{:S(2)}, u32[]{:S(2)}) collective-permute-start(f32[16,32,128]{2,1,0:T(8,128)S(1)} %collective-permute-done.36.refs_5_), channel_id=1, source_target_pairs={{0,8},{4,12},{8,0},{12,4},{16,24},{20,28},{24,16},{28,20},{1,9},{5... | collective-permute-start | bytes 786440 | tf_op jit(solution)/shard_map/ppermute | solution.py:38
  176.6 12.6 %collective-permute-start.39 = (f32[32,32,128]{2,1,0:T(8,128)S(1)}, f32[32,32,128]{2,1,0:T(8,128)S(1)}, u32[]{:S(2)}, u32[]{:S(2)}) collective-permute-start(f32[32,32,128]{2,1,0:T(8,128)S(1)} %get-tuple-element.43), channel_id=1, source_target_pairs={{0,1},{1,0},{2,3},{3,2},{4,5},{5,4},{6,7},{7,6},{8,9},{9,8},{10,11... | collective-permute-start | bytes 1572872 | tf_op jit(solution)/shard_map/ppermute | solution.py:38
  178.6 28.8 %collective-permute-start.42 = (f32[16,32,128]{2,1,0:T(8,128)S(1)}, f32[16,32,128]{2,1,0:T(8,128)S(1)}, u32[]{:S(2)}, u32[]{:S(2)}) collective-permute-start(f32[16,32,128]{2,1,0:T(8,128)S(1)} %get-tuple-element.66), channel_id=1, source_target_pairs={{0,2},{1,3},{2,0},{3,1},{4,6},{5,7},{6,4},{7,5},{8,10},{9,11},{10,... | collective-permute-start | bytes 786440 | tf_op jit(solution)/shard_map/ppermute | solution.py:38
  189.2 18.1 %collective-permute-start.41 = (f32[16,32,128]{2,1,0:T(8,128)S(1)}, f32[16,32,128]{2,1,0:T(8,128)S(1)}, u32[]{:S(2)}, u32[]{:S(2)}) collective-permute-start(f32[16,32,128]{2,1,0:T(8,128)S(1)} %get-tuple-element.68), channel_id=1, source_target_pairs={{0,2},{1,3},{2,0},{3,1},{4,6},{5,7},{6,4},{7,5},{8,10},{9,11},{10,... | collective-permute-start | bytes 786440 | tf_op jit(solution)/shard_map/ppermute | solution.py:38
  189.9 12.0 %collective-permute-start.32 = (f32[32,128]{1,0:T(8,128)S(1)}, f32[32,128]{1,0:T(8,128)S(1)}, u32[]{:S(2)}, u32[]{:S(2)}) collective-permute-start(f32[32,128]{1,0:T(8,128)S(1)} %fusion.4), channel_id=1, source_target_pairs={{0,2},{1,3},{2,0},{3,1},{4,6},{5,7},{6,4},{7,5},{8,10},{9,11},{10,... | collective-permute-start | bytes 49160 | tf_op jit(solution)/shard_map/ppermute | solution.py:38
  191.3 10.6 %collective-permute-start.33 = (f32[32,128]{1,0:T(8,128)S(1)}, f32[32,128]{1,0:T(8,128)S(1)}, u32[]{:S(2)}, u32[]{:S(2)}) collective-permute-start(f32[32,128]{1,0:T(8,128)S(1)} %fusion.4), channel_id=1, source_target_pairs={{0,1},{1,0},{2,3},{3,2},{4,5},{5,4},{6,7},{7,6},{8,9},{9,8},{10,11... | collective-permute-start | bytes 49160 | tf_op jit(solution)/shard_map/ppermute | solution.py:38
  191.3 10.6 %collective-permute-start.34 = (f32[32,128]{1,0:T(8,128)S(1)}, f32[32,128]{1,0:T(8,128)S(1)}, u32[]{:S(2)}, u32[]{:S(2)}) collective-permute-start(f32[32,128]{1,0:T(8,128)S(1)} %fusion.4), channel_id=1, source_target_pairs={{0,3},{1,2},{2,1},{3,0},{4,7},{5,6},{6,5},{7,4},{8,11},{9,10},{10,... | collective-permute-start | bytes 49160 | tf_op jit(solution)/shard_map/ppermute | solution.py:38
  210.0 9.6 %collective-permute-start.43 = (f32[17,32,128]{2,1,0:T(8,128)S(1)}, f32[17,32,128]{2,1,0:T(8,128)S(1)}, u32[]{:S(2)}, u32[]{:S(2)}) collective-permute-start(f32[17,32,128]{2,1,0:T(8,128)S(1)} %get-tuple-element.46.refs_0_), channel_id=1, source_target_pairs={{0,2},{1,3},{2,0},{3,1},{4,6},{5,7},{6,4},{7,5},{8,10},{9,11},{10,... | collective-permute-start | bytes 835592 | tf_op jit(solution)/shard_map/ppermute | solution.py:38
  211.7 12.5 %collective-permute-start.50 = (f32[16,32,128]{2,1,0:T(8,128)S(1)}, f32[16,32,128]{2,1,0:T(8,128)S(1)}, u32[]{:S(2)}, u32[]{:S(2)}) collective-permute-start(f32[16,32,128]{2,1,0:T(8,128)S(1)} %get-tuple-element.48.refs_4_), channel_id=1, source_target_pairs={{0,2},{1,3},{2,0},{3,1},{4,6},{5,7},{6,4},{7,5},{8,10},{9,11},{10,... | collective-permute-start | bytes 786440 | tf_op jit(solution)/shard_map/ppermute | solution.py:38
  212.0 12.3 %collective-permute-start.44 = (f32[17,32,128]{2,1,0:T(8,128)S(1)}, f32[17,32,128]{2,1,0:T(8,128)S(1)}, u32[]{:S(2)}, u32[]{:S(2)}) collective-permute-start(f32[17,32,128]{2,1,0:T(8,128)S(1)} %get-tuple-element.46.refs_0_), channel_id=1, source_target_pairs={{0,1},{1,0},{2,3},{3,2},{4,5},{5,4},{6,7},{7,6},{8,9},{9,8},{10,11... | collective-permute-start | bytes 835592 | tf_op jit(solution)/shard_map/ppermute | solution.py:38
  229.2 14.3 %collective-permute-start.56 = (f32[32,32,128]{2,1,0:T(8,128)S(1)}, f32[32,32,128]{2,1,0:T(8,128)S(1)}, u32[]{:S(2)}, u32[]{:S(2)}) collective-permute-start(f32[32,32,128]{2,1,0:T(8,128)S(1)} %get-tuple-element.52), channel_id=1, source_target_pairs={{0,8},{4,12},{8,0},{12,4},{16,24},{20,28},{24,16},{28,20},{1,9},{5... | collective-permute-start | bytes 1572872 | tf_op jit(solution)/shard_map/ppermute | solution.py:38
  229.2 14.4 %collective-permute-start.53 = (f32[32,32,128]{2,1,0:T(8,128)S(1)}, f32[32,32,128]{2,1,0:T(8,128)S(1)}, u32[]{:S(2)}, u32[]{:S(2)}) collective-permute-start(f32[32,32,128]{2,1,0:T(8,128)S(1)} %get-tuple-element.50), channel_id=1, source_target_pairs={{0,4},{4,0},{8,12},{12,8},{16,20},{20,16},{24,28},{28,24},{1,5},{5... | collective-permute-start | bytes 1572872 | tf_op jit(solution)/shard_map/ppermute | solution.py:38
  243.6 8.8 %collective-permute-start.57 = (f32[16,32,128]{2,1,0:T(8,128)S(1)}, f32[16,32,128]{2,1,0:T(8,128)S(1)}, u32[]{:S(2)}, u32[]{:S(2)}) collective-permute-start(f32[16,32,128]{2,1,0:T(8,128)S(1)} %get-tuple-element.63), channel_id=1, source_target_pairs={{0,4},{4,0},{8,12},{12,8},{16,20},{20,16},{24,28},{28,24},{1,5},{5... | collective-permute-start | bytes 786440 | tf_op jit(solution)/shard_map/ppermute | solution.py:38
  243.7 15.6 %collective-permute-start.54 = (f32[16,32,128]{2,1,0:T(8,128)S(1)}, f32[16,32,128]{2,1,0:T(8,128)S(1)}, u32[]{:S(2)}, u32[]{:S(2)}) collective-permute-start(f32[16,32,128]{2,1,0:T(8,128)S(1)} %get-tuple-element.65), channel_id=1, source_target_pairs={{0,8},{4,12},{8,0},{12,4},{16,24},{20,28},{24,16},{28,20},{1,9},{5... | collective-permute-start | bytes 786440 | tf_op jit(solution)/shard_map/ppermute | solution.py:38
  244.2 16.4 %collective-permute-start.46 = (f32[32,128]{1,0:T(8,128)S(1)}, f32[32,128]{1,0:T(8,128)S(1)}, u32[]{:S(2)}, u32[]{:S(2)}) collective-permute-start(f32[32,128]{1,0:T(8,128)S(1)} %fusion.2), channel_id=1, source_target_pairs={{0,8},{4,12},{8,0},{12,4},{16,24},{20,28},{24,16},{28,20},{1,9},{5... | collective-permute-start | bytes 49160 | tf_op jit(solution)/shard_map/ppermute | solution.py:38
  245.8 14.8 %collective-permute-start.47 = (f32[32,128]{1,0:T(8,128)S(1)}, f32[32,128]{1,0:T(8,128)S(1)}, u32[]{:S(2)}, u32[]{:S(2)}) collective-permute-start(f32[32,128]{1,0:T(8,128)S(1)} %fusion.2), channel_id=1, source_target_pairs={{0,4},{4,0},{8,12},{12,8},{16,20},{20,16},{24,28},{28,24},{1,5},{5... | collective-permute-start | bytes 49160 | tf_op jit(solution)/shard_map/ppermute | solution.py:38
  247.8 12.8 %collective-permute-start.48 = (f32[32,128]{1,0:T(8,128)S(1)}, f32[32,128]{1,0:T(8,128)S(1)}, u32[]{:S(2)}, u32[]{:S(2)}) collective-permute-start(f32[32,128]{1,0:T(8,128)S(1)} %fusion.2), channel_id=1, source_target_pairs={{0,12},{4,8},{8,4},{12,0},{16,28},{20,24},{24,20},{28,16},{1,13},{... | collective-permute-start | bytes 49160 | tf_op jit(solution)/shard_map/ppermute | solution.py:38
  252.4 24.8 %collective-permute-start.58 = (f32[8,32,128]{2,1,0:T(8,128)S(1)}, f32[8,32,128]{2,1,0:T(8,128)S(1)}, u32[]{:S(2)}, u32[]{:S(2)}) collective-permute-start(f32[8,32,128]{2,1,0:T(8,128)S(1)} %get-tuple-element.79), channel_id=1, source_target_pairs={{0,16},{4,20},{8,24},{12,28},{16,0},{20,4},{24,8},{28,12},{1,17},{... | collective-permute-start | bytes 393224 | tf_op jit(solution)/shard_map/ppermute | solution.py:38
  259.3 17.9 %collective-permute-start.55 = (f32[8,32,128]{2,1,0:T(8,128)S(1)}, f32[8,32,128]{2,1,0:T(8,128)S(1)}, u32[]{:S(2)}, u32[]{:S(2)}) collective-permute-start(f32[8,32,128]{2,1,0:T(8,128)S(1)} %get-tuple-element.81), channel_id=1, source_target_pairs={{0,16},{4,20},{8,24},{12,28},{16,0},{20,4},{24,8},{28,12},{1,17},{... | collective-permute-start | bytes 393224 | tf_op jit(solution)/shard_map/ppermute | solution.py:38
  260.6 9.8 %collective-permute-start.49 = (f32[32,128]{1,0:T(8,128)S(1)}, f32[32,128]{1,0:T(8,128)S(1)}, u32[]{:S(2)}, u32[]{:S(2)}) collective-permute-start(f32[32,128]{1,0:T(8,128)S(1)} %add_add_fusion), channel_id=1, source_target_pairs={{0,16},{4,20},{8,24},{12,28},{16,0},{20,4},{24,8},{28,12},{1,17},{... | collective-permute-start | bytes 49160 | tf_op jit(solution)/shard_map/ppermute | solution.py:38
  (18 other events, 183.0 us)
